TPU v7x, 32 devices: a whole 2x2x4 slice. The times are simulated.
32 devices in a mesh: batch: 8 (over z, x), rows: 4 (over y, core).
Axes of the slice: x: 2, y: 2, z: 4, core: 2. Of those that a mesh axis runs over, the one named last changes fastest.
Arguments:
- pixels: int32 [12, 16, 16, 1024], P(None, 'rows', None, 'batch'), may hold values from 0 to 255
- valid_mask: int32 [16, 16, 1024], P('rows', None, 'batch'), may hold values from 0 to 1, as said below
- vectors: float32 [2960], replicated, may hold values from -0.8 to 0.8
- vectors_first: float32 [2960], replicated, may hold values from -7.6293945e-06 to 7.6293945e-06
- vectors_second: float32 [2960], replicated, may hold values from 6.357699e-14 to 5.0861594e-13
- entry_taps: float32 [9, 18, 512], replicated, may hold values from -0.625 to 0.625
- entry_first: float32 [9, 18, 512], replicated, may hold values from -1.4305115e-06 to 1.4305115e-06
- entry_second: float32 [9, 18, 512], replicated, may hold values from 3.1788496e-15 to 2.5430797e-14
- middle: float32 [2, 512, 512], replicated, may hold values from -0.25 to 0.25
- middle_first: float32 [2, 512, 512], replicated, may hold values from -7.6293945e-06 to 7.6293945e-06
- middle_second: float32 [2, 512, 512], replicated, may hold values from 6.357699e-14 to 5.0861594e-13
- exit_taps: float32 [9, 36, 512], replicated, may hold values from -0.046875 to 0.046875
- exit_first: float32 [9, 36, 512], replicated, may hold values from -7.6293945e-06 to 7.6293945e-06
- exit_second: float32 [9, 36, 512], replicated, may hold values from 6.357699e-14 to 5.0861594e-13
- prior_taps: float32 [9, 48, 24], replicated, may hold values from -0.21875 to 0.21875
- prior_first: float32 [9, 48, 24], replicated, may hold values from -7.6293945e-06 to 7.6293945e-06
- prior_second: float32 [9, 48, 24], replicated, may hold values from 6.357699e-14 to 5.0861594e-13
Outputs:
- loss: float32 [], replicated
- grad_norm: float32 [], replicated
- vectors_new: float32 [2960], replicated
- vectors_grad: float32 [2960], replicated
- vectors_moment: float32 [2960], replicated
- entry_new: float32 [9, 18, 512], replicated
- entry_grad: float32 [9, 18, 512], replicated
- entry_moment: float32 [9, 18, 512], replicated
- middle_new: float32 [2, 512, 512], replicated
- middle_grad: float32 [2, 512, 512], replicated
- middle_moment: float32 [2, 512, 512], replicated
- exit_new: float32 [9, 36, 512], replicated
- exit_grad: float32 [9, 36, 512], replicated
- exit_moment: float32 [9, 36, 512], replicated
- prior_new: float32 [9, 48, 24], replicated
- prior_grad: float32 [9, 48, 24], replicated
- prior_moment: float32 [9, 48, 24], replicated
- bias_grads: float32 [4, 512], replicated
Inputs may be any that keep to these rules, and one draw needn't show every extreme that they name: `valid_mask`: 0 or 1; the first pixel (row 0, column 0) of every image is 1.
All inputs are finite; a program needn't handle non-finite values.
Results may differ from a plain program's by a relative error of at most 0.0055.
The roundings to bfloat16 on the way count: a program that leaves them out, or rounds other values in their place, can miss the bound.
Values may be sent and summed in bfloat16 or wider, within the bound.
No kernel may reach another device: no remote copies, remote signals or barrier semaphores. Data moves between devices by JAX's collectives and lax.ppermute only.
A program may use at most 448 MiB of HBM per device.

v0:
```python
import math

import jax
import jax.numpy as jnp
from jax import lax
from jax.sharding import PartitionSpec as P

HID = 512
CH = 12


HIGH = lax.Precision.HIGHEST
LOG_TWO_PI = math.log(2.0 * math.pi)
LEARN_RATE = 0.05
BETA_ONE = 0.9
BETA_TWO = 0.999
ADAM_EPS = 1e-08
WEIGHT_DECAY = 0.01
CLIP_NORM = 0.01
ADAM_STEP = 10


def padded_2(shard, sides, width):
    for axis, dim in sides:
        size, length = (lax.axis_size(axis), shard.shape[dim])
        up = [(i, (i + 1) % size) for i in range(size - 1)]
        down = [(j, i) for i, j in up]
        last = lax.slice_in_dim(shard, length - width, length, axis=dim)
        first = lax.slice_in_dim(shard, 0, width, axis=dim)
        before = lax.ppermute(last, axis, up)
        after = lax.ppermute(first, axis, down)
        shard = jnp.concatenate([before, shard, after], axis=dim)
    return shard


def conv_taps(source, weight):
    row_count = source.shape[1] - 2
    col_count = source.shape[2]
    padded = jnp.pad(source, ((0, 0), (0, 0), (1, 1), (0, 0)))
    total = None
    for tap_index in range(9):
        shift_row, shift_col = (tap_index // 3, tap_index % 3)
        window = padded[:, shift_row : shift_row + row_count, shift_col : shift_col + col_count, :]
        term = lax.dot_general(
            weight[tap_index], window, (((1,), (0,)), ((), ())), preferred_element_type=jnp.float32
        )
        total = term if total is None else total + term
    return total


def tap_grads(source, grad):
    row_count, col_count = (grad.shape[1], grad.shape[2])
    padded = jnp.pad(source, ((0, 0), (0, 0), (1, 1), (0, 0)))
    pieces = []
    for tap_index in range(9):
        shift_row, shift_col = (tap_index // 3, tap_index % 3)
        window = padded[:, shift_row : shift_row + row_count, shift_col : shift_col + col_count, :]
        pieces.append(
            lax.dot_general(
                grad, window, (((1, 2, 3), (1, 2, 3)), ((), ())), preferred_element_type=jnp.float32
            )
        )
    return jnp.stack(pieces)


def turn_taps(weight):
    return jnp.swapaxes(weight[::-1], 1, 2)


def stretch(field):
    return padded_2(field, (("rows", 1),), 2)


def stretch_back(field):
    return padded_2(field, (("rows", 1),), 2)


def edge_rows(row_count):
    first_row = lax.axis_index("rows") * row_count
    total_rows = row_count * lax.axis_size("rows")
    placed = first_row + jnp.arange(row_count + 2) - 1
    return ((placed >= 0) & (placed < total_rows)).astype(jnp.float32)


def level_params(vectors, entry_taps, middle, exit_taps, level_index):
    chans = CH * (level_index + 1)
    half_size = chans // 2
    offset = 0 if level_index == 0 else 4 * CH + 2 * HID + CH * CH
    segment = vectors[offset : offset + 4 * chans + 2 * HID + chans * chans]
    first_in = 0 if level_index == 0 else CH // 2
    first_out = 0 if level_index == 0 else CH
    return {
        "chan": segment[: 4 * chans].reshape(4, chans),
        "bias_a": segment[4 * chans : 4 * chans + HID],
        "bias_b": segment[4 * chans + HID : 4 * chans + 2 * HID],
        "lu_mix": segment[4 * chans + 2 * HID :].reshape(chans, chans),
        "weight_a": jnp.swapaxes(entry_taps[:, first_in : first_in + half_size], 1, 2).astype(
            jnp.bfloat16
        ),
        "weight_b": middle[level_index].astype(jnp.bfloat16),
        "weight_c": exit_taps[:, first_out : first_out + chans].astype(jnp.bfloat16),
    }


def hidden_biases(vector_grad):
    second_start = 4 * CH + 2 * HID + CH * CH
    first_part = vector_grad[4 * CH : 4 * CH + 2 * HID]
    second_part = vector_grad[second_start + 8 * CH : second_start + 8 * CH + 2 * HID]
    return jnp.concatenate([first_part, second_part]).reshape(4, HID)


def mix_channels(source, chan, lu_mix):
    chans = lu_mix.shape[0]
    shifted = (source + chan[0][:, None, None, None]) * jnp.exp(chan[1])[:, None, None, None]
    lower = jnp.tril(lu_mix, -1) + jnp.eye(chans, dtype=jnp.float32)
    upper = jnp.triu(lu_mix, 1) + jnp.diag(jnp.exp(chan[2]))
    matrix = jnp.dot(lower, upper, precision=HIGH)[::-1]
    mixed = jnp.tensordot(matrix, shifted, axes=1, precision=HIGH)
    return (mixed, jnp.sum(chan[1]) + jnp.sum(chan[2]))


def affine_head(second_half, output):
    half_size = second_half.shape[0]
    scale_log = jax.nn.log_sigmoid(output[half_size:] + 2.0)
    result = (second_half + output[:half_size]) * jnp.exp(scale_log)
    return (result, jnp.sum(scale_log, axis=0))


def gauss_log(dropped, prior):
    half_size = dropped.shape[0]
    mean_part, log_part = (prior[:half_size], prior[half_size:])
    scaled = (dropped - mean_part) * jnp.exp(-log_part)
    return jnp.sum(-0.5 * LOG_TWO_PI - log_part - 0.5 * scaled * scaled, axis=0)


def squeeze(field):
    chans, row_count, col_count = (field.shape[0], field.shape[1], field.shape[2])
    rest = field.shape[3:]
    parted = field.reshape((chans, row_count // 2, 2, col_count // 2, 2) + rest)
    moved = jnp.moveaxis(parted, (2, 4), (1, 2))
    return moved.reshape((chans * 4, row_count // 2, col_count // 2) + rest)


def unsqueeze(field):
    chans = field.shape[0] // 4
    parted = field.reshape((chans, 2, 2) + field.shape[1:])
    moved = jnp.moveaxis(parted, (1, 2), (2, 4))
    return moved.reshape((chans, field.shape[1] * 2, field.shape[2] * 2) + field.shape[3:])


def couple_forward(mixed, params):
    half_size = mixed.shape[0] // 2
    row_count = mixed.shape[1]
    inner_ext = stretch(mixed[:half_size].astype(jnp.bfloat16))
    pre_one = conv_taps(inner_ext, params["weight_a"]) + params["bias_a"][:, None, None, None]
    hidden_one = jnp.maximum(pre_one, 0.0).astype(jnp.bfloat16)
    pre_two = (
        lax.dot_general(
            params["weight_b"],
            hidden_one,
            (((1,), (0,)), ((), ())),
            preferred_element_type=jnp.float32,
        )
        + params["bias_b"][:, None, None, None]
    )
    inside = edge_rows(row_count)[None, :, None, None]
    hidden_two = (jnp.maximum(pre_two, 0.0) * inside).astype(jnp.bfloat16)
    output = conv_taps(hidden_two, params["weight_c"]) + params["chan"][3][:, None, None, None]
    (result, step_log), head_back = jax.vjp(affine_head, mixed[half_size:], output)
    return (
        jnp.concatenate([mixed[:half_size], result]),
        step_log,
        (inner_ext, hidden_one, hidden_two, head_back),
    )


def couple_backward(grad_out, grad_log, saved, params):
    inner_ext, hidden_one, hidden_two, head_back = saved
    half_size = grad_out.shape[0] // 2
    row_count = grad_out.shape[1]
    grad_second, grad_output = head_back((grad_out[half_size:], grad_log))
    output_low = grad_output.astype(jnp.bfloat16)
    bias_c = jnp.sum(output_low.astype(jnp.float32), axis=(1, 2, 3))
    taps_c = tap_grads(hidden_two, output_low)
    output_ext = stretch_back(output_low)
    grad_hidden_two = conv_taps(output_ext, turn_taps(params["weight_c"]))
    pre_two_low = jnp.where(hidden_two > 0, grad_hidden_two, 0.0).astype(jnp.bfloat16)
    own_two = pre_two_low[:, 1 : row_count + 1]
    bias_b = jnp.sum(own_two.astype(jnp.float32), axis=(1, 2, 3))
    weight_b = lax.dot_general(
        own_two,
        hidden_one[:, 1 : row_count + 1],
        (((1, 2, 3), (1, 2, 3)), ((), ())),
        preferred_element_type=jnp.float32,
    )
    grad_hidden_one = lax.dot_general(
        params["weight_b"],
        pre_two_low,
        (((0,), (0,)), ((), ())),
        preferred_element_type=jnp.float32,
    )
    pre_one_low = jnp.where(hidden_one > 0, grad_hidden_one, 0.0).astype(jnp.bfloat16)
    own_one = pre_one_low[:, 1 : row_count + 1]
    bias_a = jnp.sum(own_one.astype(jnp.float32), axis=(1, 2, 3))
    taps_a = jnp.swapaxes(tap_grads(inner_ext[:, 1 : row_count + 3], own_one), 1, 2)
    grad_first = grad_out[:half_size] + conv_taps(pre_one_low, turn_taps(params["weight_a"]))
    grads = {
        "bias_a": bias_a,
        "bias_b": bias_b,
        "bias_c": bias_c,
        "taps_a": taps_a,
        "weight_b": weight_b,
        "taps_c": taps_c,
    }
    return (jnp.concatenate([grad_first, grad_second]), grads)


def pack_level(chan_grad, lu_grad, grads):
    chan_full = chan_grad.at[3].add(grads["bias_c"])
    return jnp.concatenate(
        [chan_full.reshape(-1), grads["bias_a"], grads["bias_b"], lu_grad.reshape(-1)]
    )


def adamw(weight, grad, first, second):
    first_new = BETA_ONE * first + (1.0 - BETA_ONE) * grad
    second_new = BETA_TWO * second + (1.0 - BETA_TWO) * grad * grad
    first_hat = first_new / (1.0 - BETA_ONE**ADAM_STEP)
    second_hat = second_new / (1.0 - BETA_TWO**ADAM_STEP)
    updated = weight - LEARN_RATE * (
        first_hat / (jnp.sqrt(second_hat) + ADAM_EPS) + WEIGHT_DECAY * weight
    )
    return (updated, second_new)


def on_device(
    pixels,
    valid_mask,
    vectors,
    vectors_first,
    vectors_second,
    entry_taps,
    entry_first,
    entry_second,
    middle,
    middle_first,
    middle_second,
    exit_taps,
    exit_first,
    exit_second,
    prior_taps,
    prior_first,
    prior_second,
):
    source = (pixels.astype(jnp.float32) + 0.5) / 256.0 - 0.5
    mask_one = valid_mask.astype(jnp.float32)
    first_params = level_params(vectors, entry_taps, middle, exit_taps, 0)
    second_params = level_params(vectors, entry_taps, middle, exit_taps, 1)
    prior_low_taps = prior_taps.astype(jnp.bfloat16)
    (mixed_one, const_one), mix_back_one = jax.vjp(
        mix_channels, source, first_params["chan"], first_params["lu_mix"]
    )
    out_one, step_one, saved_one = couple_forward(mixed_one, first_params)
    folded = squeeze(out_one)
    keep_part, drop_part = (folded[: 2 * CH], folded[2 * CH :])
    row_count, col_count = (mask_one.shape[0], mask_one.shape[1])
    mask_two = jnp.min(mask_one.reshape(row_count // 2, 2, col_count // 2, 2, -1), axis=(1, 3))
    keep_ext = stretch(keep_part.astype(jnp.bfloat16))[:, 1:-1]
    prior = conv_taps(keep_ext, prior_low_taps) + vectors[-4 * CH :][:, None, None, None]
    drop_log, prior_back = jax.vjp(gauss_log, drop_part, prior)
    level_input, level_mask = (keep_part, mask_two)
    (mixed_two, const_two), mix_back_two = jax.vjp(
        mix_channels, level_input, second_params["chan"], second_params["lu_mix"]
    )
    out_two, step_two, saved_two = couple_forward(mixed_two, second_params)
    top_log = jnp.sum(-0.5 * (LOG_TWO_PI + out_two * out_two), axis=0)
    local_total = (
        jnp.sum(mask_one * (const_one + step_one))
        + jnp.sum(mask_two * drop_log)
        + jnp.sum(level_mask * (const_two + step_two + top_log))
    )
    total, count = lax.psum((local_total, jnp.sum(mask_one)), ("batch", "rows"))
    coef = -1.0 / (CH * count * math.log(2.0))
    loss = coef * total + 8.0
    grad_top = -coef * level_mask[None] * out_two
    grad_mixed_two, level_two_grads = couple_backward(
        grad_top, coef * level_mask, saved_two, second_params
    )
    grad_input_two, chan_two, lu_two = mix_back_two((grad_mixed_two, coef * jnp.sum(level_mask)))
    grad_drop, grad_prior = prior_back(coef * mask_two)
    prior_low = grad_prior.astype(jnp.bfloat16)
    prior_bias = jnp.sum(prior_low.astype(jnp.float32), axis=(1, 2, 3))
    prior_grad = tap_grads(keep_ext, prior_low)
    prior_ext = stretch_back(prior_low)[:, 1:-1]
    grad_keep = grad_input_two + conv_taps(prior_ext, turn_taps(prior_low_taps))
    vector_two = jnp.concatenate([pack_level(chan_two, lu_two, level_two_grads), prior_bias])
    entry_two = level_two_grads["taps_a"]
    middle_two = level_two_grads["weight_b"]
    exit_two = level_two_grads["taps_c"]
    unfolded = unsqueeze(jnp.concatenate([grad_keep, grad_drop]))
    grad_mixed_one, level_one_grads = couple_backward(
        unfolded, coef * mask_one, saved_one, first_params
    )
    ignored, chan_one, lu_one = mix_back_one((grad_mixed_one, coef * jnp.sum(mask_one)))
    vector_one = pack_level(chan_one, lu_one, level_one_grads)
    entry_one = level_one_grads["taps_a"]
    middle_one = level_one_grads["weight_b"]
    exit_one = level_one_grads["taps_c"]
    (
        vector_one,
        entry_one,
        middle_one,
        exit_one,
        vector_two,
        entry_two,
        middle_two,
        exit_two,
        prior_grad,
    ) = lax.psum(
        (
            vector_one,
            entry_one,
            middle_one,
            exit_one,
            vector_two,
            entry_two,
            middle_two,
            exit_two,
            prior_grad,
        ),
        ("batch", "rows"),
    )
    grads = (
        jnp.concatenate([vector_one, vector_two]),
        jnp.concatenate([entry_one, entry_two], axis=1),
        jnp.stack([middle_one, middle_two]),
        jnp.concatenate([exit_one, exit_two], axis=1),
        prior_grad,
    )
    grad_norm = jnp.sqrt(sum((jnp.sum(grad * grad) for grad in grads)))
    clip = jnp.minimum(1.0, CLIP_NORM / (grad_norm + 1e-06))
    weights = (vectors, entry_taps, middle, exit_taps, prior_taps)
    firsts = (vectors_first, entry_first, middle_first, exit_first, prior_first)
    seconds = (vectors_second, entry_second, middle_second, exit_second, prior_second)
    results = [loss, grad_norm]
    for weight, grad, first, second in zip(weights, grads, firsts, seconds):
        clipped = grad * clip
        updated, second_new = adamw(weight, clipped, first, second)
        results.extend([updated, clipped, second_new])
    results.append(hidden_biases(grads[0] * clip))
    return tuple(results)


def solution(mesh):
    return jax.shard_map(
        on_device,
        mesh=mesh,
        in_specs=(
            P(None, "rows", None, "batch"),
            P("rows", None, "batch"),
            P(),
            P(),
            P(),
            P(),
            P(),
            P(),
            P(),
            P(),
            P(),
            P(),
            P(),
            P(),
            P(),
            P(),
            P(),
        ),
        out_specs=(
            P(),
            P(),
            P(),
            P(),
            P(),
            P(),
            P(),
            P(),
            P(),
            P(),
            P(),
            P(),
            P(),
            P(),
            P(),
            P(),
            P(),
            P(),
        ),
        check_vma=False,
    )
```

profile of v0, /device:TPU:0, one launch (start us, length us, event | category | flops | bytes accessed | tf_op | source)
XLA Modules:
  0.0 892.2 jit_solution(1426610579824177648)
XLA Ops:
  38.3 10.3 %fusion.347 = f32[6,16,128,512]{3,2,1,0:T(8,128)} fusion(bf16[9,512,6]{1,2,0:T(8,128)(2,1)S(1)} %slice_bitcast_fusion.7, bf16[6,2,16,128]{3,0,2,1:T(8,128)(2,1)S(1)} %collective-permute-done.1, bf16[6,4,16,128]{3,0,2,1:T(8,128)(2,1)S(1)} %slice.1746, bf16[6,2,16,128]{3,0,2,1:T(8,128)(2,1)S(1)} %collective-permute-done), kind=kOutput, calls=%fused_computation.561 | convolution fusion | flops 71368704 | bytes 25436160 | tf_op jit(solution)/shard_map/dot_general | solution.py:44
  48.6 10.2 %fusion.349 = f32[6,16,128,512]{3,2,1,0:T(8,128)} fusion(bf16[9,512,6]{1,2,0:T(8,128)(2,1)S(1)} %slice_bitcast_fusion.7, bf16[6,2,16,128]{3,0,2,1:T(8,128)(2,1)S(1)} %collective-permute-done.1, bf16[6,4,16,128]{3,0,2,1:T(8,128)(2,1)S(1)} %slice.1746, bf16[6,2,16,128]{3,0,2,1:T(8,128)(2,1)S(1)} %collective-permute-done), kind=kOutput, calls=%fused_computation.565 | convolution fusion | flops 76087296 | bytes 25436160 | tf_op jit(solution)/shard_map/dot_general | solution.py:44
  58.8 10.1 %fusion.352 = f32[6,16,128,512]{3,2,1,0:T(8,128)} fusion(bf16[9,512,6]{1,2,0:T(8,128)(2,1)S(1)} %slice_bitcast_fusion.7, bf16[6,2,16,128]{3,0,2,1:T(8,128)(2,1)S(1)} %collective-permute-done.1, bf16[6,4,16,128]{3,0,2,1:T(8,128)(2,1)S(1)} %slice.1746, bf16[6,2,16,128]{3,0,2,1:T(8,128)(2,1)S(1)} %collective-permute-done), kind=kOutput, calls=%fused_computation.572 | convolution fusion | flops 71368704 | bytes 25436160 | tf_op jit(solution)/shard_map/dot_general | solution.py:44
  68.9 10.1 %fusion.351 = f32[6,16,128,512]{3,2,1,0:T(8,128)} fusion(bf16[9,512,6]{1,2,0:T(8,128)(2,1)S(1)} %slice_bitcast_fusion.7, bf16[6,2,16,128]{3,0,2,1:T(8,128)(2,1)S(1)} %collective-permute-done.1, bf16[6,4,16,128]{3,0,2,1:T(8,128)(2,1)S(1)} %slice.1746, bf16[6,2,16,128]{3,0,2,1:T(8,128)(2,1)S(1)} %collective-permute-done), kind=kOutput, calls=%fused_computation.569 | convolution fusion | flops 71368704 | bytes 25436160 | tf_op jit(solution)/shard_map/dot_general | solution.py:44
  79.0 10.2 %fusion.350 = f32[6,16,128,512]{3,2,1,0:T(8,128)} fusion(bf16[9,512,6]{1,2,0:T(8,128)(2,1)S(1)} %slice_bitcast_fusion.7, bf16[6,2,16,128]{3,0,2,1:T(8,128)(2,1)S(1)} %collective-permute-done.1, bf16[6,4,16,128]{3,0,2,1:T(8,128)(2,1)S(1)} %slice.1746, bf16[6,2,16,128]{3,0,2,1:T(8,128)(2,1)S(1)} %collective-permute-done), kind=kOutput, calls=%fused_computation.567 | convolution fusion | flops 71368704 | bytes 25436160 | tf_op jit(solution)/shard_map/dot_general | solution.py:44
  89.1 10.1 %fusion.348 = f32[6,16,128,512]{3,2,1,0:T(8,128)} fusion(bf16[9,512,6]{1,2,0:T(8,128)(2,1)S(1)} %slice_bitcast_fusion.7, bf16[6,2,16,128]{3,0,2,1:T(8,128)(2,1)S(1)} %collective-permute-done.1, bf16[6,4,16,128]{3,0,2,1:T(8,128)(2,1)S(1)} %slice.1746, bf16[6,2,16,128]{3,0,2,1:T(8,128)(2,1)S(1)} %collective-permute-done), kind=kOutput, calls=%fused_computation.563 | convolution fusion | flops 71368704 | bytes 25436160 | tf_op jit(solution)/shard_map/dot_general | solution.py:44
  99.2 10.1 %fusion.222 = f32[6,16,128,512]{3,2,1,0:T(8,128)} fusion(bf16[6,2,16,128]{3,0,2,1:T(8,128)(2,1)S(1)} %collective-permute-done.1, bf16[6,4,16,128]{3,0,2,1:T(8,128)(2,1)S(1)} %slice.1746, bf16[9,512,6]{1,2,0:T(8,128)(2,1)S(1)} %slice_bitcast_fusion.7), kind=kOutput, calls=%fused_computation.332 | convolution fusion | flops 75571200 | bytes 25370624 | tf_op jit(solution)/shard_map/dot_general | solution.py:44
  109.4 10.3 %fusion.218 = f32[6,16,128,512]{3,2,1,0:T(8,128)} fusion(bf16[6,4,16,128]{3,0,2,1:T(8,128)(2,1)S(1)} %slice.1746, bf16[6,2,16,128]{3,0,2,1:T(8,128)(2,1)S(1)} %collective-permute-done, bf16[9,512,6]{1,2,0:T(8,128)(2,1)S(1)} %slice_bitcast_fusion.7), kind=kOutput, calls=%fused_computation.328 | convolution fusion | flops 75571200 | bytes 25370624 | tf_op jit(solution)/shard_map/dot_general | solution.py:44
  119.7 65.1 %fusion.3 = bf16[512,6,16,128]{0,3,2,1:T(8,128)(2,1)} fusion(f32[512]{0:T(512)S(1)} %get-tuple-element.133, f32[6,16,128,512]{3,2,1,0:T(8,128)} %fusion.222, f32[6,16,128,512]{3,2,1,0:T(8,128)} %fusion.347, f32[6,16,128,512]{3,2,1,0:T(8,128)} %fusion.348, f32[6,16,128,512]{3,2,1,0:T(8,128)} %fusion.349, f32[6,16,128,512]{3,2,1,0:T(8,128)} %fusion.350, ...), kind=kOutput, calls=%fused_computation.9 | convolution fusion | flops 140574720 | bytes 214181888 | tf_op jit(solution)/shard_map/dot_general | solution.py:44
  184.7 12.1 %fusion.2 = bf16[512,6,16,128]{0,3,2,1:T(8,128)(2,1)S(1)} fusion(f32[6]{0:T(128)S(1)} %and_convert_fusion.1, f32[512]{0:T(512)S(1)} %get-tuple-element.132, bf16[512,6,16,128]{0,3,2,1:T(8,128)(2,1)} %fusion.3, bf16[2,512,512]{2,1,0:T(8,128)(2,1)S(1)} %convert.15), kind=kOutput, calls=%fused_computation.8 | convolution fusion | flops 6467616768 | bytes 25692672 | tf_op jit(solution)/shard_map/dot_general | solution.py:158
  218.1 44.1 %psum.77 = f32[]{:T(128)} all-reduce(f32[]{:T(128)} %get-tuple-element.47), channel_id=1, replica_groups=mesh['batch'=8,'rows'=4] {'batch','rows'}, use_global_device_ids=true, to_apply=%region_1.2 | all-reduce | flops 1 | bytes 8 | tf_op jit(solution)/shard_map/psum | solution.py:282
  281.6 4.5 fusion.329
  286.1 4.5 fusion.328
  290.6 4.5 fusion.327
  295.1 4.5 fusion.325
  299.6 4.5 fusion.268
  304.1 4.6 fusion.272
  308.6 19.3 %fusion.21 = bf16[512,4,8,128]{0,3,2,1:T(8,128)(2,1)} fusion(f32[512]{0:T(512)} %get-tuple-element.130, f32[4,8,128,512]{3,2,1,0:T(8,128)} %fusion.272, f32[4,8,128,512]{3,2,1,0:T(8,128)S(1)} %fusion.324, f32[4,8,128,512]{3,2,1,0:T(8,128)} %fusion.325, f32[4,8,128,512]{3,2,1,0:T(8,128)S(1)} %fusion.326, f32[4,8,128,512]{3,2,1,0:T(8,128)} %fusion.327, ...), kind=kOutput, calls=%fused_computation.45 | convolution fusion | flops 67551232 | bytes 71518208 | tf_op jit(solution)/shard_map/dot_general | solution.py:44
  327.9 4.8 fusion.20
  345.3 4.3 collective-permute-start.6
  351.8 5.3 collective-permute-start.8
  370.6 4.5 fusion.311
  375.1 4.5 fusion.310
  379.7 4.5 fusion.309
  384.2 4.6 fusion.307
  388.8 4.5 fusion.306
  393.3 4.5 fusion.234
  397.8 4.6 fusion.238
  402.4 32.5 %fusion.13 = bf16[512,4,8,128]{0,3,2,1:T(8,128)(2,1)} fusion(f32[4,8,128,512]{3,2,1,0:T(8,128)} %fusion.238, f32[4,8,128,512]{3,2,1,0:T(8,128)} %fusion.306, f32[4,8,128,512]{3,2,1,0:T(8,128)} %fusion.307, f32[4,8,128,512]{3,2,1,0:T(8,128)S(1)} %fusion.308, f32[4,8,128,512]{3,2,1,0:T(8,128)} %fusion.309, f32[4,8,128,512]{3,2,1,0:T(8,128)} %fusion.310, ...), kind=kOutput, calls=%fused_computation.27 | convolution fusion | flops 112033792 | bytes 75816960 | tf_op jit(solution)/shard_map/dot_general | solution.py:44
  436.8 4.5 fusion.37
  441.3 6.1 fusion.12
  498.3 10.6 %fusion.318 = f32[6,16,128,512]{3,2,1,0:T(8,128)} fusion(bf16[9,512,12]{1,2,0:T(8,128)(2,1)S(1)} %copy-done.31, bf16[12,2,16,128]{3,0,2,1:T(8,128)(2,1)S(1)} %collective-permute-done.11, bf16[12,4,16,128]{3,0,2,1:T(8,128)(2,1)S(1)} %get-tuple-element.81, bf16[12,2,16,128]{3,0,2,1:T(8,128)(2,1)S(1)} %collective-permute-done.10), kind=kOutput, calls=%fused_computation.481 | convolution fusion | flops 152174592 | bytes 25706496 | tf_op jit(solution)/shard_map/dot_general | solution.py:44
  508.9 10.1 %fusion.321 = f32[6,16,128,512]{3,2,1,0:T(8,128)} fusion(bf16[9,512,12]{1,2,0:T(8,128)(2,1)S(1)} %copy-done.31, bf16[12,2,16,128]{3,0,2,1:T(8,128)(2,1)S(1)} %collective-permute-done.11, bf16[12,4,16,128]{3,0,2,1:T(8,128)(2,1)S(1)} %get-tuple-element.81, bf16[12,2,16,128]{3,0,2,1:T(8,128)(2,1)S(1)} %collective-permute-done.10), kind=kOutput, calls=%fused_computation.488 | convolution fusion | flops 142737408 | bytes 25706496 | tf_op jit(solution)/shard_map/dot_general | solution.py:44
  519.0 10.1 %fusion.320 = f32[6,16,128,512]{3,2,1,0:T(8,128)} fusion(bf16[9,512,12]{1,2,0:T(8,128)(2,1)S(1)} %copy-done.31, bf16[12,2,16,128]{3,0,2,1:T(8,128)(2,1)S(1)} %collective-permute-done.11, bf16[12,4,16,128]{3,0,2,1:T(8,128)(2,1)S(1)} %get-tuple-element.81, bf16[12,2,16,128]{3,0,2,1:T(8,128)(2,1)S(1)} %collective-permute-done.10), kind=kOutput, calls=%fused_computation.485 | convolution fusion | flops 142737408 | bytes 25706496 | tf_op jit(solution)/shard_map/dot_general | solution.py:44
  529.1 10.1 %fusion.319 = f32[6,16,128,512]{3,2,1,0:T(8,128)} fusion(bf16[9,512,12]{1,2,0:T(8,128)(2,1)S(1)} %copy-done.31, bf16[12,2,16,128]{3,0,2,1:T(8,128)(2,1)S(1)} %collective-permute-done.11, bf16[12,4,16,128]{3,0,2,1:T(8,128)(2,1)S(1)} %get-tuple-element.81, bf16[12,2,16,128]{3,0,2,1:T(8,128)(2,1)S(1)} %collective-permute-done.10), kind=kOutput, calls=%fused_computation.483 | convolution fusion | flops 142737408 | bytes 25706496 | tf_op jit(solution)/shard_map/dot_general | solution.py:44
  539.2 10.1 %fusion.317 = f32[6,16,128,512]{3,2,1,0:T(8,128)} fusion(bf16[9,512,12]{1,2,0:T(8,128)(2,1)S(1)} %copy-done.31, bf16[12,2,16,128]{3,0,2,1:T(8,128)(2,1)S(1)} %collective-permute-done.11, bf16[12,4,16,128]{3,0,2,1:T(8,128)(2,1)S(1)} %get-tuple-element.81, bf16[12,2,16,128]{3,0,2,1:T(8,128)(2,1)S(1)} %collective-permute-done.10), kind=kOutput, calls=%fused_computation.479 | convolution fusion | flops 142737408 | bytes 25706496 | tf_op jit(solution)/shard_map/dot_general | solution.py:44
  549.3 10.0 %fusion.316 = f32[6,16,128,512]{3,2,1,0:T(8,128)} fusion(bf16[9,512,12]{1,2,0:T(8,128)(2,1)S(1)} %copy-done.31, bf16[12,2,16,128]{3,0,2,1:T(8,128)(2,1)S(1)} %collective-permute-done.11, bf16[12,4,16,128]{3,0,2,1:T(8,128)(2,1)S(1)} %get-tuple-element.81, bf16[12,2,16,128]{3,0,2,1:T(8,128)(2,1)S(1)} %collective-permute-done.10), kind=kOutput, calls=%fused_computation.477 | convolution fusion | flops 142737408 | bytes 25706496 | tf_op jit(solution)/shard_map/dot_general | solution.py:44
  559.3 10.1 %fusion.186 = f32[6,16,128,512]{3,2,1,0:T(8,128)} fusion(bf16[12,2,16,128]{3,0,2,1:T(8,128)(2,1)S(1)} %collective-permute-done.11, bf16[12,4,16,128]{3,0,2,1:T(8,128)(2,1)S(1)} %get-tuple-element.81, bf16[9,512,12]{1,2,0:T(8,128)(2,1)S(1)} %copy-done.31), kind=kOutput, calls=%fused_computation.276 | convolution fusion | flops 151142400 | bytes 25575424 | tf_op jit(solution)/shard_map/dot_general | solution.py:44
  569.5 10.2 %fusion.182 = f32[6,16,128,512]{3,2,1,0:T(8,128)} fusion(bf16[12,4,16,128]{3,0,2,1:T(8,128)(2,1)S(1)} %get-tuple-element.81, bf16[12,2,16,128]{3,0,2,1:T(8,128)(2,1)S(1)} %collective-permute-done.10, bf16[9,512,12]{1,2,0:T(8,128)(2,1)S(1)} %copy-done.31), kind=kOutput, calls=%fused_computation.272 | convolution fusion | flops 151142400 | bytes 25575424 | tf_op jit(solution)/shard_map/dot_general | solution.py:44
  579.7 68.6 %fusion.1 = bf16[512,6,16,128]{0,3,2,1:T(8,128)(2,1)} fusion(f32[6,16,128,512]{3,2,1,0:T(8,128)} %fusion.186, f32[6,16,128,512]{3,2,1,0:T(8,128)} %fusion.316, f32[6,16,128,512]{3,2,1,0:T(8,128)} %fusion.317, f32[6,16,128,512]{3,2,1,0:T(8,128)} %fusion.318, f32[6,16,128,512]{3,2,1,0:T(8,128)} %fusion.319, f32[6,16,128,512]{3,2,1,0:T(8,128)} %fusion.320, ...), kind=kOutput, calls=%fused_computation.3 | convolution fusion | flops 211943424 | bytes 227033088 | tf_op jit(solution)/shard_map/dot_general | solution.py:44
  648.2 11.3 %fusion.40 = f32[1,512,512]{2,1,0:T(8,128)} fusion(bf16[512,6,16,128]{0,3,2,1:T(8,128)(2,1)} %fusion.1, bf16[512,6,16,128]{0,3,2,1:T(8,128)(2,1)} %fusion.3), kind=kOutput, calls=%fused_computation.65 | convolution fusion | flops 4294967296 | bytes 22020096 | tf_op jit(solution)/shard_map/dot_general | solution.py:190
  659.6 16.3 %fusion = bf16[512,6,16,128]{0,3,2,1:T(8,128)(2,1)} fusion(bf16[512,6,16,128]{0,3,2,1:T(8,128)(2,1)} %fusion.3, bf16[512,6,16,128]{0,3,2,1:T(8,128)(2,1)} %fusion.1, bf16[2,512,512]{2,1,0:T(8,128)(2,1)S(1)} %copy-done.22), kind=kOutput, calls=%fused_computation.1 | convolution fusion | flops 6461325312 | bytes 38273024 | tf_op jit(solution)/shard_map/dot_general | solution.py:196
  675.9 5.8 fusion.344
  681.7 5.8 fusion.343
  717.1 4.6 convert_reduce_fusion
  721.7 5.0 convert_reduce_fusion.1
  726.8 42.3 %all-reduce.28 = (f32[]{:T(128)}, f32[1744]{0:T(1024)S(1)}, f32[1216]{0:T(1024)S(1)}, f32[9,48,24]{1,2,0:T(8,128)S(1)}) all-reduce(f32[]{:T(128)S(6)} %add.843, f32[1744]{0:T(1024)S(1)} %copy-done.57, f32[1216]{0:T(1024)S(1)} %concatenate.123, f32[9,48,24]{1,2,0:T(8,128)} %fusion.151), channel_id=1, replica_groups=mesh['batch'=8,'rows'=4] {'batch','rows'}, use_global_device_ids=true, to_apply=%region_14.15 | all-reduce | flops 13329 | bytes 106632 | tf_op jit(solution)/shard_map/psum | solution.py:282
  771.0 86.9 %all-reduce.32.cloned.1.call-done = (f32[9,12,512]{2,1,0:T(8,128)}, f32[9,6,512]{2,1,0:T(8,128)}, f32[1,512,512]{2,1,0:T(8,128)}, f32[1,512,512]{2,1,0:T(8,128)}...) async-done(((f32[9,12,512]{2,1,0:T(8,128)}, f32[9,6,512]{2,1,0:T(8,128)}, f32[1,512,512]{2,1,0:T(8,128)}, f32[1,512,512]{2,1,0:T(8,128)}, f32[9,24,512]{2,1,0:T(8,128)}, ...) | async-done | bytes 3092496 | tf_op jit(solution)/shard_map/psum | solution.py:319
  (427 shorter events, 197.5 us)
Async XLA Ops:
  7.2 850.7 %all-reduce.32.cloned.1.call-start = ((), (), s32[]{:S(2)}) async-start(), calls=%async_computation | async-start | bytes 6553600 | tf_op jit(solution)/shard_map/psum | solution.py:319
  14.7 262.6 %copy-start.4 = (bf16[6,4,16,128]{3,0,2,1:T(8,128)(2,1)}, bf16[6,4,16,128]{3,0,2,1:T(8,128)(2,1)S(1)}, u32[]{:S(2)}) copy-start(bf16[6,4,16,128]{3,0,2,1:T(8,128)(2,1)S(1)} %slice.1746) | copy-start | bytes 294916
  14.7 23.5 %collective-permute-start = (bf16[6,2,16,128]{3,0,2,1:T(8,128)(2,1)S(1)}, bf16[6,2,16,128]{3,0,2,1:T(8,128)(2,1)S(1)}, u32[]{:S(2)}, u32[]{:S(2)}) collective-permute-start(bf16[6,2,16,128]{3,0,2,1:T(8,128)(2,1)S(1)} %get-tuple-element.110), channel_id=1, source_target_pairs={{0,1},{1,2},{2,3},{4,5},{5,6},{6,7},{8,9},{9,10},{10,11},{12,13},{... | collective-permute-start | bytes 147464 | tf_op jit(solution)/shard_map/ppermute | solution.py:30
  17.1 21.2 %collective-permute-start.1 = (bf16[6,2,16,128]{3,0,2,1:T(8,128)(2,1)S(1)}, bf16[6,2,16,128]{3,0,2,1:T(8,128)(2,1)S(1)}, u32[]{:S(2)}, u32[]{:S(2)}) collective-permute-start(bf16[6,2,16,128]{3,0,2,1:T(8,128)(2,1)S(1)} %get-tuple-element.111), channel_id=1, source_target_pairs={{1,0},{2,1},{3,2},{5,4},{6,5},{7,6},{9,8},{10,9},{11,10},{13,12},{... | collective-permute-start | bytes 147464 | tf_op jit(solution)/shard_map/ppermute | solution.py:31
  22.5 26.1 %copy-start.19 = (bf16[9,512,12]{1,2,0:T(8,128)(2,1)}, bf16[9,512,12]{1,2,0:T(8,128)(2,1)S(1)}, u32[]{:S(2)}) copy-start(bf16[9,512,12]{1,2,0:T(8,128)(2,1)S(1)} %slice_bitcast_fusion.6) | copy-start | bytes 331780
  26.4 7.4 copy-start.33
  36.3 148.4 %copy-start.21 = (bf16[2,512,512]{2,1,0:T(8,128)(2,1)}, bf16[2,512,512]{2,1,0:T(8,128)(2,1)S(1)}, u32[]{:S(2)}) copy-start(bf16[2,512,512]{2,1,0:T(8,128)(2,1)S(1)} %convert.15) | copy-start | bytes 3145732
  38.3 239.1 %copy-start.9 = (bf16[6,2,16,128]{3,0,2,1:T(8,128)(2,1)}, bf16[6,2,16,128]{3,0,2,1:T(8,128)(2,1)S(1)}, u32[]{:S(2)}) copy-start(bf16[6,2,16,128]{3,0,2,1:T(8,128)(2,1)S(1)} %collective-permute-done) | copy-start | bytes 147460
  38.3 239.1 %copy-start.7 = (bf16[6,2,16,128]{3,0,2,1:T(8,128)(2,1)}, bf16[6,2,16,128]{3,0,2,1:T(8,128)(2,1)S(1)}, u32[]{:S(2)}) copy-start(bf16[6,2,16,128]{3,0,2,1:T(8,128)(2,1)S(1)} %collective-permute-done.1) | copy-start | bytes 147460
  196.8 18.2 %copy-start = (bf16[512,6,16,128]{0,3,2,1:T(8,128)(2,1)}, bf16[512,6,16,128]{0,3,2,1:T(8,128)(2,1)S(1)}, u32[]{:S(2)}) copy-start(bf16[512,6,16,128]{0,3,2,1:T(8,128)(2,1)S(1)} %fusion.2) | copy-start | bytes 37748740
  214.9 55.3 %copy-start.43 = (f32[24,24]{1,0:T(8,128)S(1)}, f32[24,24]{1,0:T(8,128)}, u32[]{:S(2)}) copy-start(f32[24,24]{1,0:T(8,128)} %rev.28) | copy-start | bytes 6916
  214.9 55.3 %copy-start.59 = (f32[24]{0:T(128)S(1)}, f32[24]{0:T(128)}, u32[]{:S(2)}) copy-start(f32[24]{0:T(128)} %get-tuple-element.127) | copy-start | bytes 292
  214.9 55.3 %copy-start.62 = (f32[24]{0:T(128)S(1)}, f32[24]{0:T(128)}, u32[]{:S(2)}) copy-start(f32[24]{0:T(128)} %get-tuple-element.129) | copy-start | bytes 292
  214.9 61.2 %copy-start.49 = (f32[2,8,128]{2,1,0:T(8,128)S(1)}, f32[2,8,128]{2,1,0:T(8,128)}, u32[]{:S(2)}) copy-start(f32[2,8,128]{2,1,0:T(8,128)} %reduce_min.9) | copy-start | bytes 24580
  215.0 64.1 %copy-start.20 = (bf16[9,512,12]{1,2,0:T(8,128)(2,1)S(1)}, bf16[9,512,12]{1,2,0:T(8,128)(2,1)}, u32[]{:S(2)}) copy-start(bf16[9,512,12]{1,2,0:T(8,128)(2,1)} %copy-done.19) | copy-start | bytes 331780
  265.2 73.6 %collective-permute-start.3 = (bf16[24,2,8,128]{3,0,2,1:T(8,128)(2,1)S(1)}, bf16[24,2,8,128]{3,0,2,1:T(8,128)(2,1)}, u32[]{:S(2)}, u32[]{:S(2)}) collective-permute-start(bf16[24,2,8,128]{3,0,2,1:T(8,128)(2,1)S(1)} %copy.686), channel_id=1, source_target_pairs={{1,0},{2,1},{3,2},{5,4},{6,5},{7,6},{9,8},{10,9},{11,10},{13,12},{... | collective-permute-start | bytes 294920 | tf_op jit(solution)/shard_map/ppermute | solution.py:31
  266.5 72.3 %collective-permute-start.2 = (bf16[24,2,8,128]{3,0,2,1:T(8,128)(2,1)S(1)}, bf16[24,2,8,128]{3,0,2,1:T(8,128)(2,1)}, u32[]{:S(2)}, u32[]{:S(2)}) collective-permute-start(bf16[24,2,8,128]{3,0,2,1:T(8,128)(2,1)S(1)} %copy.686), channel_id=1, source_target_pairs={{0,1},{1,2},{2,3},{4,5},{5,6},{6,7},{8,9},{9,10},{10,11},{12,13},{... | collective-permute-start | bytes 294920 | tf_op jit(solution)/shard_map/ppermute | solution.py:30
  270.6 8.4 collective-permute-start.5
  271.9 7.1 collective-permute-start.4
  336.0 7.1 copy-start.78
  336.7 6.7 copy-start.27
  336.7 6.7 copy-start.54
  336.7 6.7 copy-start.55
  336.7 6.7 copy-start.56
  340.7 24.6 %copy-start.39 = (bf16[9,24,48]{2,1,0:T(8,128)(2,1)S(1)}, bf16[9,24,48]{2,1,0:T(8,128)(2,1)}, u32[]{:S(2)}) copy-start(bf16[9,24,48]{2,1,0:T(8,128)(2,1)} %reverse_bitcast_fusion.4) | copy-start | bytes 62212
  344.0 24.5 %collective-permute-start.7 = (bf16[24,2,8,128]{3,0,2,1:T(8,128)(2,1)S(1)}, bf16[24,2,8,128]{3,0,2,1:T(8,128)(2,1)S(1)}, u32[]{:S(2)}, u32[]{:S(2)}) collective-permute-start(bf16[24,2,8,128]{3,0,2,1:T(8,128)(2,1)S(1)} %get-tuple-element.89), channel_id=1, source_target_pairs={{1,0},{2,1},{3,2},{5,4},{6,5},{7,6},{9,8},{10,9},{11,10},{13,12},{... | collective-permute-start | bytes 294920 | tf_op jit(solution)/shard_map/ppermute | solution.py:31
  345.3 24.0 %collective-permute-start.6 = (bf16[24,2,8,128]{3,0,2,1:T(8,128)(2,1)S(1)}, bf16[24,2,8,128]{3,0,2,1:T(8,128)(2,1)S(1)}, u32[]{:S(2)}, u32[]{:S(2)}) collective-permute-start(bf16[24,2,8,128]{3,0,2,1:T(8,128)(2,1)S(1)} %get-tuple-element.89), channel_id=1, source_target_pairs={{0,1},{1,2},{2,3},{4,5},{5,6},{6,7},{8,9},{9,10},{10,11},{12,13},{... | collective-permute-start | bytes 294920 | tf_op jit(solution)/shard_map/ppermute | solution.py:30
  350.5 123.1 %collective-permute-start.9 = (bf16[48,2,8,128]{3,0,2,1:T(8,128)(2,1)S(1)}, bf16[48,2,8,128]{3,0,2,1:T(8,128)(2,1)}, u32[]{:S(2)}, u32[]{:S(2)}) collective-permute-start(bf16[48,2,8,128]{3,0,2,1:T(8,128)(2,1)S(1)} %get-tuple-element.83), channel_id=1, source_target_pairs={{1,0},{2,1},{3,2},{5,4},{6,5},{7,6},{9,8},{10,9},{11,10},{13,12},{... | collective-permute-start | bytes 589832 | tf_op jit(solution)/shard_map/ppermute | solution.py:31
  351.8 121.8 %collective-permute-start.8 = (bf16[48,2,8,128]{3,0,2,1:T(8,128)(2,1)S(1)}, bf16[48,2,8,128]{3,0,2,1:T(8,128)(2,1)}, u32[]{:S(2)}, u32[]{:S(2)}) collective-permute-start(bf16[48,2,8,128]{3,0,2,1:T(8,128)(2,1)S(1)} %get-tuple-element.83), channel_id=1, source_target_pairs={{0,1},{1,2},{2,3},{4,5},{5,6},{6,7},{8,9},{9,10},{10,11},{12,13},{... | collective-permute-start | bytes 589832 | tf_op jit(solution)/shard_map/ppermute | solution.py:30
  449.6 8.2 copy-start.50
  466.9 12.4 %copy-start.41 = (f32[4,16,128]{2,1,0:T(8,128)S(1)}, f32[4,16,128]{2,1,0:T(8,128)}, u32[]{:S(2)}) copy-start(f32[4,16,128]{2,1,0:T(8,128)} %broadcast_multiply_fusion.2) | copy-start | bytes 98308
  471.5 17.4 %slice-start = ((s8[12582912]{0:T(1024)(128)(4,1)}), s8[4194304]{0:T(1024)(128)(4,1)S(1)}, s32[]{:S(2)}) async-start(s8[12582912]{0:T(1024)(128)(4,1)} %bitcast.1259), calls=%async_computation.1 | async-start | bytes 8388608
  478.2 10.6 %slice-start.1 = ((s8[12582912]{0:T(1024)(128)(4,1)}), s8[4194304]{0:T(1024)(128)(4,1)S(1)}, s32[]{:S(2)}) async-start(s8[12582912]{0:T(1024)(128)(4,1)} %bitcast.1259), calls=%async_computation.2 | async-start | bytes 8388608
  479.6 10.5 %copy-start.23 = (f32[6,4,16,128]{3,0,2,1:T(8,128)}, f32[6,4,16,128]{3,0,2,1:T(8,128)S(1)}, u32[]{:S(2)}) copy-start(f32[6,4,16,128]{3,0,2,1:T(8,128)S(1)} %get-tuple-element.91) | copy-start | bytes 589828
  480.4 8.5 slice-start.2
  484.6 13.7 %collective-permute-start.10 = (bf16[12,2,16,128]{3,0,2,1:T(8,128)(2,1)S(1)}, bf16[12,2,16,128]{3,0,2,1:T(8,128)(2,1)S(1)}, u32[]{:S(2)}, u32[]{:S(2)}) collective-permute-start(bf16[12,2,16,128]{3,0,2,1:T(8,128)(2,1)S(1)} %get-tuple-element.103), channel_id=1, source_target_pairs={{0,1},{1,2},{2,3},{4,5},{5,6},{6,7},{8,9},{9,10},{10,11},{12,13},{... | collective-permute-start | bytes 294920 | tf_op jit(solution)/shard_map/ppermute | solution.py:30
  487.6 10.7 %collective-permute-start.11 = (bf16[12,2,16,128]{3,0,2,1:T(8,128)(2,1)S(1)}, bf16[12,2,16,128]{3,0,2,1:T(8,128)(2,1)S(1)}, u32[]{:S(2)}, u32[]{:S(2)}) collective-permute-start(bf16[12,2,16,128]{3,0,2,1:T(8,128)(2,1)S(1)} %get-tuple-element.104), channel_id=1, source_target_pairs={{1,0},{2,1},{3,2},{5,4},{6,5},{7,6},{9,8},{10,9},{11,10},{13,12},{... | collective-permute-start | bytes 294920 | tf_op jit(solution)/shard_map/ppermute | solution.py:31
  498.3 10.6 %copy-start.36 = (f32[9,12,512]{2,1,0:T(8,128)}, f32[9,12,512]{2,1,0:T(8,128)S(1)}, u32[]{:S(2)}) copy-start(f32[9,12,512]{2,1,0:T(8,128)S(1)} %fusion.104) | copy-start | bytes 663556
  648.2 11.3 %copy-start.22 = (bf16[2,512,512]{2,1,0:T(8,128)(2,1)S(1)}, bf16[2,512,512]{2,1,0:T(8,128)(2,1)}, u32[]{:S(2)}) copy-start(bf16[2,512,512]{2,1,0:T(8,128)(2,1)} %copy-done.21) | copy-start | bytes 3145732
  659.6 16.3 %copy-start.38 = (bf16[9,6,512]{2,1,0:T(8,128)(2,1)S(1)}, bf16[9,6,512]{2,1,0:T(8,128)(2,1)}, u32[]{:S(2)}) copy-start(bf16[9,6,512]{2,1,0:T(8,128)(2,1)} %reverse_bitcast_fusion.3) | copy-start | bytes 165892
  675.9 11.6 %copy-start.1 = (bf16[512,6,16,128]{0,3,2,1:T(8,128)(2,1)S(1)}, bf16[512,6,16,128]{0,3,2,1:T(8,128)(2,1)}, u32[]{:S(2)}) copy-start(bf16[512,6,16,128]{0,3,2,1:T(8,128)(2,1)} %fusion) | copy-start | bytes 37748740
  717.1 9.7 %copy-start.57 = (f32[1744]{0:T(1024)S(1)}, f32[1744]{0:T(1024)}, u32[]{:S(2)}) copy-start(f32[1744]{0:T(1024)} %concatenate.124) | copy-start | bytes 20932
  721.6 151.8 %copy-start.18 = (f32[9,18,512]{2,1,0:T(8,128)S(1)}, f32[9,18,512]{2,1,0:T(8,128)}, u32[]{:S(2)}) copy-start(f32[9,18,512]{2,1,0:T(8,128)} %param.26) | copy-start | bytes 995332
  721.6 154.3 %copy-start.15 = (f32[9,36,512]{2,1,0:T(8,128)S(1)}, f32[9,36,512]{2,1,0:T(8,128)}, u32[]{:S(2)}) copy-start(f32[9,36,512]{2,1,0:T(8,128)} %param.32) | copy-start | bytes 1990660
  857.9 15.5 %copy-start.30 = (f32[9,6,512]{2,1,0:T(8,128)S(1)}, f32[9,6,512]{2,1,0:T(8,128)}, u32[]{:S(2)}) copy-start(f32[9,6,512]{2,1,0:T(8,128)} %get-tuple-element.60) | copy-start | bytes 331780
  870.8 8.3 copy-start.6
  870.8 8.3 copy-start.16
  870.8 8.3 copy-start.17
  (47 other events, 168.6 us)
Sparse Core Ops, SparseCore 0:
  717.1 140.8 all-reduce.31
where the time goes:
time: 897 us; the launch traced here: 892 us
  matrix products  587 us (65%)
  waiting for transfers between devices  87 us (10%)
  blocking collectives  86.4 us (10%)
  other arithmetic  51.2 us (6%)
  starting transfers between devices  30.5 us (3%)
  between operations  28.8 us (3%)
  local copies, waits for them, and re-layouts  21.7 us (2%)
    dot_general x90, matrix products, conv_taps(): lax.dot_general(weight[tap_index], window, (((1,), (0,)), ((), ())), pref...  477 us
    psum x1, waiting for transfers between devices, on_device(): lax.psum((vector_one, entry_one, middle_one, exit_one, vector_two, entry_...  86.9 us
    psum x2, blocking collectives, on_device(): total, count = lax.psum((local_total, jnp.sum(mask_one)), ('batch', 'rows'))  86.4 us
    dot_general x45, matrix products, tap_grads(): lax.dot_general(grad, window, (((1, 2, 3), (1, 2, 3)), ((), ())), preferr...  48.2 us
    ppermute x6, starting transfers between devices, padded_2(): before = lax.ppermute(last, axis, up)  22.7 us
    dot_general x2, matrix products, couple_backward(): lax.dot_general(params['weight_b'], pre_two_low, (((0,), (0,)), ((), ()))...  22.3 us
  transfers between devices with their start and end apart: 13, of which 1 were waited for; matrix products, arithmetic and copies ran while one was open for 24% of the time, Pallas kernels for 0%

commit v1 on v0

v1 whole, which is shorter than its diff:
```python
import functools
import math

import jax
import jax.numpy as jnp
from jax import lax
from jax.experimental import pallas as pl
from jax.experimental.pallas import tpu as pltpu
from jax.sharding import PartitionSpec as P

HID = 512
CH = 12

F32 = jnp.float32
BF16 = jnp.bfloat16
HIGH = lax.Precision.HIGHEST
LOG_TWO_PI = math.log(2.0 * math.pi)
LEARN_RATE = 0.05
BETA_ONE = 0.9
BETA_TWO = 0.999
ADAM_EPS = 1e-08
WEIGHT_DECAY = 0.01
CLIP_NORM = 0.01
ADAM_STEP = 10
LANES = 128
VMEM_LIMIT = 60 * 2**20


def dot(left, right):
    return lax.dot_general(left, right, (((1,), (0,)), ((), ())), preferred_element_type=F32)


def dot_nt(left, right):
    return lax.dot_general(left, right, (((1,), (1,)), ((), ())), preferred_element_type=F32)


def lane_band(bands, height=1):
    return lax.broadcasted_iota(jnp.int32, (height, LANES), 1) // (LANES // bands)


def pack_kernel(bands, index_ref, pixels_ref, mask_ref, *out_refs):
    own = index_ref[0]
    width = LANES // bands
    rows = pixels_ref.shape[0] // bands
    extra = mask_ref.shape[0] // bands
    band = lane_band(bands)
    parts = [pixels_ref[pl.ds(e, rows, stride=bands), :].astype(F32) for e in range(bands)]
    masks = [mask_ref[pl.ds(e, extra, stride=bands), :].astype(F32) for e in range(bands)]
    for d, out_ref in enumerate(out_refs):
        target = own ^ d
        for source, first, size in ((parts, 0, rows), (masks, rows, extra)):
            total = jnp.zeros((size, LANES), F32)
            for e in range(bands):
                shift = lax.rem(e - target + bands, bands) * width
                total = jnp.where(band == e, pltpu.roll(source[e], shift, 1), total)
            out_ref[first : first + size, :] = total.astype(BF16)


def fill_ext(ext_ref, field, rows, cols, bands, pattern):
    width = LANES // bands
    band = lane_band(bands)
    stride = (cols + 2) * LANES
    height = ext_ref.shape[0]
    pads = jnp.broadcast_to(pattern, (height, LANES))
    for block in range(ext_ref.shape[1] // LANES):
        ext_ref[:, block * LANES : (block + 1) * LANES] = pads
    for row in range(rows):
        start = (row + 1) * stride + LANES
        ext_ref[:, start : start + cols * LANES] = field[:, row * cols * LANES : (row + 1) * cols * LANES]
    last = (rows - 1) * cols * LANES
    for col in range(cols):
        above = pltpu.roll(field[:, last + col * LANES : last + (col + 1) * LANES], width, 1)
        start = LANES + col * LANES
        ext_ref[:, start : start + LANES] = jnp.where(band >= 1, above, pads)
        below = pltpu.roll(field[:, col * LANES : (col + 1) * LANES], LANES - width, 1)
        start = (rows + 1) * stride + LANES + col * LANES
        ext_ref[:, start : start + LANES] = jnp.where(band < bands - 1, below, pads)


def fold_ext(ext_ref, rows, cols, bands):
    width = LANES // bands
    band = lane_band(bands)
    stride = (cols + 2) * LANES
    pieces = []
    for row in range(rows):
        start = (row + 1) * stride + LANES
        piece = ext_ref[:, start : start + cols * LANES]
        if row == 0:
            blocks = []
            for col in range(cols):
                start = (rows + 1) * stride + LANES + col * LANES
                moved = pltpu.roll(ext_ref[:, start : start + LANES], width, 1)
                blocks.append(jnp.where(band >= 1, moved, 0.0))
            piece = piece + jnp.concatenate(blocks, axis=1)
        if row == rows - 1:
            blocks = []
            for col in range(cols):
                start = LANES + col * LANES
                moved = pltpu.roll(ext_ref[:, start : start + LANES], LANES - width, 1)
                blocks.append(jnp.where(band < bands - 1, moved, 0.0))
            piece = piece + jnp.concatenate(blocks, axis=1)
        pieces.append(piece)
    return pieces


def window(cols, row, first_col, tap, turned=False):
    dy, dx = tap // 3, tap % 3
    if turned:
        dy, dx = 2 - dy, 2 - dx
    return ((row + dy) * (cols + 2) + first_col + dx) * LANES


def gather_cols(ext_ref, cols, row, first_col, size, turned=False):
    starts = [window(cols, row, first_col, tap, turned) for tap in range(9)]
    starts = [s if isinstance(s, int) else pl.multiple_of(s, LANES) for s in starts]
    return jnp.concatenate([ext_ref[:, pl.ds(s, size)] for s in starts], axis=0).astype(BF16)


def scatter_cols(ext_ref, values, cols, row, first_col, size, turned=False):
    height = ext_ref.shape[0]
    for tap in range(9):
        start = window(cols, row, first_col, tap, turned)
        if not isinstance(start, int):
            start = pl.multiple_of(start, LANES)
        at = pl.ds(start, size)
        ext_ref[:, at] = ext_ref[:, at] + values[tap * height : (tap + 1) * height]


def mix(matrix_ref, field_ref, start, size, pairs):
    total = None
    for j in pairs:
        term = matrix_ref[:, j : j + 1] * field_ref[j : j + 1, start : start + size]
        total = term if total is None else total + term
    return total


def log_sigmoid(value):
    return jnp.minimum(value, 0.0) - jnp.log1p(jnp.exp(-jnp.abs(value)))


def sigmoid_minus(value):
    power = jnp.exp(-jnp.abs(value))
    return jnp.where(value >= 0.0, power, 1.0) / (1.0 + power)


def row_mask(height, period, valid):
    return lax.rem(lax.broadcasted_iota(jnp.int32, (height, 1), 0), period) < valid


def fold_lanes(value):
    total = value[:, :LANES]
    for start in range(LANES, value.shape[1], LANES):
        total = total + value[:, start : start + LANES]
    return total


def couple_two_forward(
    dims,
    index_ref,
    b0,
    b1,
    b2,
    b3,
    chan1_ref,
    m1_ref,
    chan2_ref,
    m2_ref,
    et_ref,
    wb_ref,
    f_ref,
    bias_ref,
    y1_ref,
    mix1_ref,
    mask_ref,
    mask2_ref,
    keep_ref,
    y2_ref,
    out2_ref,
    t2_ref,
    xcol_ref,
    h1_ref,
    h2_ref,
    loss_ref,
    bufs,
    xs,
    ext,
    oacc,
):
    rows, cols, bands = dims
    own = index_ref[0]
    width = LANES // bands
    band = lane_band(bands)
    groups = cols // bands
    for d, ref in enumerate((b0, b1, b2, b3)):
        bufs[d, :, :] = ref[...].astype(F32)
    xs[...] = jnp.zeros_like(xs)
    for s in range(rows):
        for a in range(groups):
            loads = [bufs[d, pl.ds(s * groups + a, CH + 1, stride=rows * groups), :] for d in range(bands)]
            for e in range(bands):
                total = jnp.zeros((CH + 1, LANES), F32)
                for d in range(bands):
                    origin = own ^ d
                    shift = lax.rem(origin - e + bands, bands) * width
                    total = jnp.where(band == origin, pltpu.roll(loads[d], shift, 1), total)
                start = (s * cols + bands * a + e) * LANES
                xs[0 : CH + 1, start : start + LANES] = total
    line = cols * LANES
    for s in range(rows):
        at = slice(s * line, (s + 1) * line)
        mask_ref[:, at] = xs[CH : CH + 1, at]
        raw = xs[:, at]
        source = (raw + 0.5) / 256.0 - 0.5
        y1_ref[:, at] = (source + chan1_ref[:, 0:1]) * chan1_ref[:, 1:2]
    for s in range(rows):
        at = slice(s * line, (s + 1) * line)
        mix1_ref[:, at] = mix(m1_ref, y1_ref, s * line, line, range(CH))
    half_rows, half_cols = rows // 2, cols // 2
    for i in range(half_rows):
        for j in range(half_cols):
            at = slice((i * half_cols + j) * LANES, (i * half_cols + j + 1) * LANES)
            masks = None
            for p in range(4):
                di, dj = p // 2, p % 2
                start = ((2 * i + di) * cols + 2 * j + dj) * LANES
                keep_ref[p * 8 : p * 8 + 8, at] = mix1_ref[0:8, start : start + LANES]
                block = mask_ref[:, start : start + LANES]
                masks = block if masks is None else jnp.minimum(masks, block)
            mask2_ref[:, at] = masks
    size = half_rows * half_cols * LANES
    y2_ref[...] = (keep_ref[...] + chan2_ref[:, 0:1]) * chan2_ref[:, 1:2]
    pairs = [j for j in range(32) if j % 8 < 6]
    mixed = mix(m2_ref, y2_ref, 0, size, pairs)
    out2_ref[...] = mixed
    iota = lax.broadcasted_iota(jnp.int32, (16, 1), 0)
    ones = jnp.where(iota == CH, 1.0, 0.0)
    fill_ext(ext, mixed[:16] + ones, half_rows, half_cols, bands, ones)
    oacc[...] = jnp.zeros_like(oacc)
    chunk = half_cols * LANES
    for i in range(half_rows):
        at = slice(i * chunk, (i + 1) * chunk)
        xcol = gather_cols(ext, half_cols, i, 0, chunk)
        xcol_ref[:, at] = xcol
        hidden = jnp.maximum(dot(et_ref[...], xcol), 0.0).astype(BF16)
        h1_ref[:, at] = hidden
        hidden = jnp.maximum(dot(wb_ref[...], hidden) + bias_ref[...], 0.0).astype(BF16)
        h2_ref[:, at] = hidden
        scatter_cols(oacc, dot(f_ref[...], hidden), half_cols, i, 0, chunk, True)
    output = jnp.concatenate(fold_ext(oacc, half_rows, half_cols, bands), axis=1) + chan2_ref[:, 2:3]
    second = output[16:] + 2.0
    t2_ref[...] = second
    scale_log = log_sigmoid(second)
    result = (mixed[16:] + output[:16]) * jnp.exp(scale_log)
    out2_ref[16:, :] = result
    valid = row_mask(16, 16, CH)
    per_pixel = jnp.where(valid, scale_log - 0.5 * (mixed[:16] * mixed[:16] + result * result), 0.0)
    mask2 = mask2_ref[...]
    loss_ref[...] = jnp.zeros_like(loss_ref)
    loss_ref[0:1, :] = jnp.sum(fold_lanes(per_pixel * mask2), axis=0, keepdims=True)
    loss_ref[1:2, :] = fold_lanes(mask2)
    loss_ref[2:3, :] = fold_lanes(mask_ref[...])


def gram(left, right_ref, pairs, acc_ref):
    for j in pairs:
        acc_ref[j, :, :] = acc_ref[j, :, :] + fold_lanes(left * right_ref[j : j + 1, :])


def couple_two_backward(
    dims,
    coef_ref,
    mask2_ref,
    y2_ref,
    out2_ref,
    t2_ref,
    xcol_ref,
    h1_ref,
    h2_ref,
    chan2_ref,
    m2t_ref,
    e_ref,
    wbt_ref,
    ft_ref,
    ge_ref,
    gwb_ref,
    gf_ref,
    gbb_ref,
    gm_ref,
    gsum_ref,
    gbc_ref,
    gkeep_ref,
    ext,
    gacc,
    gmix,
    bacc,
):
    rows, cols, bands = dims
    coef = coef_ref[0]
    mask2 = mask2_ref[...]
    weight = coef * mask2
    second = t2_ref[...]
    result = out2_ref[16:, :]
    g_result = -weight * result
    g_log = g_result * result + weight
    g_second = g_log * sigmoid_minus(second)
    g_half = g_result * jnp.exp(log_sigmoid(second))
    gmix[0:16, :] = -weight * out2_ref[0:16, :]
    gmix[16:32, :] = g_half
    valid = row_mask(16, 16, CH)
    g_out = jnp.concatenate([g_half, jnp.where(valid, g_second, 0.0)], axis=0)
    g_out = g_out.astype(BF16).astype(F32)
    gbc_ref[...] = fold_lanes(g_out)
    fill_ext(ext, g_out, rows, cols, bands, jnp.zeros((32, 1), F32))
    gacc[...] = jnp.zeros_like(gacc)
    chunk = cols * LANES
    for i in range(rows):
        at = slice(i * chunk, (i + 1) * chunk)
        gcol = gather_cols(ext, cols, i, 0, chunk, True)
        hidden_two = h2_ref[:, at]
        hidden_one = h1_ref[:, at]
        g_pre = jnp.where(hidden_two > 0, dot(ft_ref[...], gcol), 0.0).astype(BF16)
        g_f = dot_nt(gcol, hidden_two)
        g_wb = dot_nt(g_pre, hidden_one)
        folded = fold_lanes(g_pre.astype(F32))
        g_pre = jnp.where(hidden_one > 0, dot(wbt_ref[...], g_pre), 0.0).astype(BF16)
        g_e = dot_nt(xcol_ref[:, at], g_pre)
        scatter_cols(gacc, dot(e_ref[...], g_pre), cols, i, 0, chunk)
        if i == 0:
            gf_ref[...], gwb_ref[...], ge_ref[...], bacc[...] = g_f, g_wb, g_e, folded
        else:
            gf_ref[...] += g_f
            gwb_ref[...] += g_wb
            ge_ref[...] += g_e
            bacc[...] += folded
    gbb_ref[...] = lax.dot_general(
        jnp.ones((8, LANES), F32), bacc[...], (((1,), (1,)), ((), ())), precision=HIGH, preferred_element_type=F32
    )
    gmix[0:16, :] += jnp.concatenate(fold_ext(gacc, rows, cols, bands), axis=1)
    pairs = [j for j in range(32) if j % 8 < 6]
    g_mixed = gmix[...]
    gm_ref[...] = jnp.zeros_like(gm_ref)
    gram(g_mixed, y2_ref, pairs, gm_ref)
    gsum_ref[...] = fold_lanes(g_mixed)
    valid_rows = [j for j in range(32) if j % 16 < CH]
    gkeep_ref[...] = mix(m2t_ref, gmix, 0, rows * chunk, valid_rows) * chan2_ref[:, 1:2]


def couple_one_forward(
    dims,
    chunk,
    coef_ref,
    mix1_ref,
    mask_ref,
    mask2_ref,
    keep_ref,
    gkeep_in_ref,
    chan1_ref,
    et_ref,
    wb_ref,
    f_ref,
    bias_ref,
    wp_ref,
    wpt_ref,
    pbias_ref,
    xcol_ref,
    h1_ref,
    h2_ref,
    res_ref,
    t_ref,
    gout_ref,
    gwp_ref,
    gpb_ref,
    loss_ref,
    ext,
    oacc,
    kext,
    kcol,
    gkacc,
    drop,
):
    rows, cols, bands = dims
    step = pl.program_id(0)
    per_row = cols * LANES // chunk
    iota = lax.broadcasted_iota(jnp.int32, (8, 1), 0)
    ones = jnp.where(iota == CH // 2, 1.0, 0.0)

    @pl.when(step == 0)
    def _():
        fill_ext(ext, mix1_ref[0:8, :] + ones, rows, cols, bands, ones)
        oacc[...] = jnp.zeros_like(oacc)

    row = step // per_row
    col = (step % per_row) * (chunk // LANES)
    xcol = gather_cols(ext, cols, row, col, chunk)
    xcol_ref[...] = xcol
    hidden = jnp.maximum(dot(et_ref[...], xcol), 0.0).astype(BF16)
    h1_ref[...] = hidden
    hidden = jnp.maximum(dot(wb_ref[...], hidden) + bias_ref[...], 0.0).astype(BF16)
    h2_ref[...] = hidden
    scatter_cols(oacc, dot(f_ref[...], hidden), cols, row, col, chunk, True)

    @pl.when(step == pl.num_programs(0) - 1)
    def _():
        line = cols * LANES
        valid = row_mask(8, 8, CH // 2)
        step_total = None
        half_rows, half_cols = rows // 2, cols // 2
        for s, piece in enumerate(fold_ext(oacc, rows, cols, bands)):
            at = slice(s * line, (s + 1) * line)
            output = piece + chan1_ref[:, 2:3]
            second = output[8:] + 2.0
            t_ref[:, at] = second
            scale_log = log_sigmoid(second)
            result = (mix1_ref[8:16, at] + output[:8]) * jnp.exp(scale_log)
            res_ref[:, at] = result
            part = fold_lanes(jnp.where(valid, scale_log, 0.0) * mask_ref[:, at])
            step_total = part if step_total is None else step_total + part
        for i in range(half_rows):
            for j in range(half_cols):
                at = slice((i * half_cols + j) * LANES, (i * half_cols + j + 1) * LANES)
                for p in range(4):
                    start = ((2 * i + p // 2) * cols + 2 * j + p % 2) * LANES
                    drop[p * 8 : p * 8 + 8, at] = res_ref[:, start : start + LANES]
        part_iota = lax.broadcasted_iota(jnp.int32, (32, 1), 0)
        part_ones = jnp.where(part_iota == CH // 2, 1.0, 0.0)
        fill_ext(kext, keep_ref[...] + part_ones, half_rows, half_cols, bands, part_ones)
        part_line = half_cols * LANES
        gkacc[...] = jnp.zeros_like(gkacc)
        weight = coef_ref[0] * mask2_ref[...]
        valid = row_mask(32, 8, CH // 2)
        prior_total = None
        for i in range(half_rows):
            at = slice(i * part_line, (i + 1) * part_line)
            columns = gather_cols(kext, half_cols, i, 0, part_line)
            kcol[...] = columns
            prior = dot(wp_ref[...], columns) + pbias_ref[...]
            mean, logs = prior[:32], prior[32:]
            inverse = jnp.exp(-logs)
            scaled = (drop[:, at] - mean) * inverse
            part = fold_lanes((-logs - 0.5 * scaled * scaled) * mask2_ref[:, at])
            prior_total = part if prior_total is None else prior_total + part
            g_mean = weight[:, at] * scaled * inverse
            g_logs = jnp.where(valid, weight[:, at] * (scaled * scaled - 1.0), 0.0)
            drop[:, at] = -g_mean
            g_prior = jnp.concatenate([g_mean, g_logs], axis=0).astype(BF16)
            g_wp = dot_nt(g_prior, kcol[...])
            if i == 0:
                gwp_ref[...] = g_wp
                gpb_ref[...] = fold_lanes(g_prior.astype(F32))
            else:
                gwp_ref[...] += g_wp
                gpb_ref[...] += fold_lanes(g_prior.astype(F32))
            scatter_cols(gkacc, dot(wpt_ref[...], g_prior), half_cols, i, 0, part_line)
        loss_ref[...] = jnp.zeros_like(loss_ref)
        loss_ref[0:1, :] = jnp.sum(step_total, axis=0, keepdims=True) + jnp.sum(prior_total, axis=0, keepdims=True)
        for i, piece in enumerate(fold_ext(gkacc, half_rows, half_cols, bands)):
            at = slice(i * part_line, (i + 1) * part_line)
            g_keep = piece + gkeep_in_ref[:, at]
            g_drop = drop[:, at]
            for j in range(half_cols):
                inner = slice(j * LANES, (j + 1) * LANES)
                for p in range(4):
                    start = ((2 * i + p // 2) * cols + 2 * j + p % 2) * LANES
                    gout_ref[0:8, start : start + LANES] = g_keep[p * 8 : p * 8 + 8, inner]
                    gout_ref[8:16, start : start + LANES] = g_drop[p * 8 : p * 8 + 8, inner]


def couple_one_backward(
    dims,
    chunk,
    coef_ref,
    mask_ref,
    y1_ref,
    res_ref,
    t_ref,
    gout_ref,
    e_ref,
    wbt_ref,
    ft_ref,
    xcol_ref,
    h1_ref,
    h2_ref,
    ge_ref,
    gwb_ref,
    gf_ref,
    gbb_ref,
    gm_ref,
    gsum_ref,
    gbc_ref,
    ext,
    gacc,
    gmix,
    bacc,
):
    rows, cols, bands = dims
    step = pl.program_id(0)
    per_row = cols * LANES // chunk

    @pl.when(step == 0)
    def _():
        weight = coef_ref[0] * mask_ref[...]
        second = t_ref[...]
        result = res_ref[...]
        g_result = gout_ref[8:16, :]
        g_log = g_result * result + weight
        g_second = g_log * sigmoid_minus(second)
        g_half = g_result * jnp.exp(log_sigmoid(second))
        gmix[0:8, :] = gout_ref[0:8, :]
        gmix[8:16, :] = g_half
        valid = row_mask(8, 8, CH // 2)
        g_out = jnp.concatenate([g_half, jnp.where(valid, g_second, 0.0)], axis=0)
        g_out = g_out.astype(BF16).astype(F32)
        gbc_ref[...] = fold_lanes(g_out)
        fill_ext(ext, g_out, rows, cols, bands, jnp.zeros((16, 1), F32))
        gacc[...] = jnp.zeros_like(gacc)
        gf_ref[...] = jnp.zeros_like(gf_ref)
        gwb_ref[...] = jnp.zeros_like(gwb_ref)
        ge_ref[...] = jnp.zeros_like(ge_ref)
        bacc[...] = jnp.zeros_like(bacc)

    row = step // per_row
    col = (step % per_row) * (chunk // LANES)
    gcol = gather_cols(ext, cols, row, col, chunk, True)
    hidden_two = h2_ref[...]
    hidden_one = h1_ref[...]
    g_pre = jnp.where(hidden_two > 0, dot(ft_ref[...], gcol), 0.0).astype(BF16)
    gf_ref[...] += dot_nt(gcol, hidden_two)
    gwb_ref[...] += dot_nt(g_pre, hidden_one)
    bacc[...] += fold_lanes(g_pre.astype(F32))
    g_pre = jnp.where(hidden_one > 0, dot(wbt_ref[...], g_pre), 0.0).astype(BF16)
    ge_ref[...] += dot_nt(xcol_ref[...], g_pre)
    scatter_cols(gacc, dot(e_ref[...], g_pre), cols, row, col, chunk)

    @pl.when(step == pl.num_programs(0) - 1)
    def _():
        gbb_ref[...] = lax.dot_general(
            jnp.ones((8, LANES), F32), bacc[...], (((1,), (1,)), ((), ())), precision=HIGH, preferred_element_type=F32
        )
        gmix[0:8, :] += jnp.concatenate(fold_ext(gacc, rows, cols, bands), axis=1)
        g_mixed = gmix[...]
        gm_ref[...] = jnp.zeros_like(gm_ref)
        gram(g_mixed, y1_ref, range(CH), gm_ref)
        gsum_ref[...] = fold_lanes(g_mixed)


def call(kernel, inputs, outputs, scratch, flops, grid=None, in_specs=None, out_specs=None):
    whole = pl.BlockSpec(memory_space=pltpu.VMEM)
    smem = pl.BlockSpec(memory_space=pltpu.SMEM)
    if in_specs is None:
        in_specs = [smem if x.ndim == 1 else whole for x in inputs]
        out_specs = [whole for _ in outputs]
    spec = {} if grid is None else {"grid": grid}
    traffic = sum(x.size * x.dtype.itemsize for x in list(inputs) + list(outputs))
    return pl.pallas_call(
        kernel,
        out_shape=outputs,
        in_specs=in_specs,
        out_specs=out_specs,
        scratch_shapes=scratch,
        compiler_params=pltpu.CompilerParams(vmem_limit_bytes=VMEM_LIMIT),
        cost_estimate=pl.CostEstimate(flops=flops, bytes_accessed=traffic, transcendentals=0),
        **spec,
    )(*inputs)


def shape(dims, dtype=F32):
    return jax.ShapeDtypeStruct(tuple(dims), dtype)


def split_three(value):
    high = lax.reduce_precision(value, 8, 7)
    middle = lax.reduce_precision(value - high, 8, 7)
    return high, middle, value - high - middle


def mixing_matrix(chan, lu_mix):
    chans = lu_mix.shape[0]
    lower = jnp.tril(lu_mix, -1) + jnp.eye(chans, dtype=F32)
    upper = jnp.triu(lu_mix, 1) + jnp.diag(jnp.exp(chan[2]))
    return jnp.dot(lower, upper, precision=HIGH)[::-1]


def spread_one(value):
    parted = value.reshape((2, CH // 2) + value.shape[1:])
    return jnp.pad(parted, ((0, 0), (0, 2)) + ((0, 0),) * (value.ndim - 1)).reshape((16,) + value.shape[1:])


def spread_two(value):
    parted = value.reshape((2, CH) + value.shape[1:])
    return jnp.pad(parted, ((0, 0), (0, 4)) + ((0, 0),) * (value.ndim - 1)).reshape((32,) + value.shape[1:])


def spread_keep(value):
    parted = jnp.swapaxes(value.reshape((CH // 2, 4) + value.shape[1:]), 0, 1)
    return jnp.pad(parted, ((0, 0), (0, 2)) + ((0, 0),) * (value.ndim - 1)).reshape((32,) + value.shape[1:])


def gather_keep(value):
    parted = value.reshape((4, 8) + value.shape[1:])[:, : CH // 2]
    return jnp.swapaxes(parted, 0, 1).reshape((24,) + value.shape[1:])


def entry_matrix(taps, bias, height):
    count = taps.shape[1]
    padded = jnp.pad(taps, ((0, 0), (0, height - count), (0, 0)))
    for tap, piece in enumerate(split_three(bias)):
        padded = padded.at[tap, count].set(piece)
    return padded.reshape(9 * height, HID).astype(BF16)


def exit_matrix(taps, height):
    half = taps.shape[1] // 2
    parted = jnp.pad(taps.reshape(9, 2, half, HID), ((0, 0), (0, 0), (0, height - half), (0, 0)))
    return parted.reshape(18 * height, HID).astype(BF16)


def level_params(vectors, entry_taps, middle, exit_taps, level_index):
    chans = CH * (level_index + 1)
    half_size = chans // 2
    offset = 0 if level_index == 0 else 4 * CH + 2 * HID + CH * CH
    segment = vectors[offset : offset + 4 * chans + 2 * HID + chans * chans]
    first_in = 0 if level_index == 0 else CH // 2
    first_out = 0 if level_index == 0 else CH
    return {
        "chan": segment[: 4 * chans].reshape(4, chans),
        "bias_a": segment[4 * chans : 4 * chans + HID],
        "bias_b": segment[4 * chans + HID : 4 * chans + 2 * HID],
        "lu_mix": segment[4 * chans + 2 * HID :].reshape(chans, chans),
        "taps_a": entry_taps[:, first_in : first_in + half_size],
        "weight_b": middle[level_index].astype(BF16),
        "taps_c": exit_taps[:, first_out : first_out + chans],
    }


def hidden_biases(vector_grad):
    second_start = 4 * CH + 2 * HID + CH * CH
    first_part = vector_grad[4 * CH : 4 * CH + 2 * HID]
    second_part = vector_grad[second_start + 8 * CH : second_start + 8 * CH + 2 * HID]
    return jnp.concatenate([first_part, second_part]).reshape(4, HID)


def adamw(weight, grad, first, second):
    first_new = BETA_ONE * first + (1.0 - BETA_ONE) * grad
    second_new = BETA_TWO * second + (1.0 - BETA_TWO) * grad * grad
    first_hat = first_new / (1.0 - BETA_ONE**ADAM_STEP)
    second_hat = second_new / (1.0 - BETA_TWO**ADAM_STEP)
    updated = weight - LEARN_RATE * (first_hat / (jnp.sqrt(second_hat) + ADAM_EPS) + WEIGHT_DECAY * weight)
    return (updated, second_new)


def chan_grads(params, grad_matrix, grad_mixed_sum, output_bias, coef_mask):
    chan, lu_mix = params["chan"], params["lu_mix"]
    matrix, back = jax.vjp(mixing_matrix, chan, lu_mix)
    from_matrix, lu_grad = back(grad_matrix)
    shifted_sum = jnp.dot(grad_mixed_sum, matrix, precision=HIGH)
    bias = shifted_sum * jnp.exp(chan[1])
    scale = jnp.sum(matrix * grad_matrix, axis=0) + coef_mask
    rows = jnp.stack([bias, scale, from_matrix[2] + coef_mask, output_bias])
    return rows, lu_grad


def total_over(value, axes):
    for axis in axes:
        size = lax.axis_size(axis)
        distance = 1
        while distance < size:
            value = value + lax.ppermute(value, axis, [(i, i ^ distance) for i in range(size)])
            distance *= 2
    return value


def on_device(
    pixels,
    valid_mask,
    vectors,
    vectors_first,
    vectors_second,
    entry_taps,
    entry_first,
    entry_second,
    middle,
    middle_first,
    middle_second,
    exit_taps,
    exit_first,
    exit_second,
    prior_taps,
    prior_first,
    prior_second,
):
    bands = lax.axis_size("rows")
    rows, cols = valid_mask.shape[0], valid_mask.shape[1]
    dims = (rows, cols, bands)
    half_dims = (rows // 2, cols // 2, bands)
    size = rows * cols * LANES
    part = size // 4
    local_count = jnp.sum(valid_mask.astype(F32))
    own = lax.axis_index("rows").astype(jnp.int32).reshape(1)
    piece_rows = (CH + 1) * rows * cols // bands
    pieces = call(
        functools.partial(pack_kernel, bands),
        (own, pixels.reshape(-1, LANES), valid_mask.reshape(-1, LANES)),
        [shape((piece_rows, LANES), BF16)] * bands,
        [],
        1000,
    )
    count = total_over(local_count, ("batch", "rows"))
    bufs = [pieces[0]]
    for d in range(1, bands):
        bufs.append(lax.ppermute(pieces[d], "rows", [(i, i ^ d) for i in range(bands)]))
    coef = (-1.0 / (CH * count * math.log(2.0))).reshape(1)

    one = level_params(vectors, entry_taps, middle, exit_taps, 0)
    two = level_params(vectors, entry_taps, middle, exit_taps, 1)
    e_one = entry_matrix(one["taps_a"], one["bias_a"], 8)
    e_two = entry_matrix(two["taps_a"], two["bias_a"], 16)
    f_one = exit_matrix(one["taps_c"], 8)
    f_two = exit_matrix(two["taps_c"], 16)
    m_one = jnp.pad(spread_one(mixing_matrix(one["chan"], one["lu_mix"])), ((0, 0), (0, 4)))
    m_two = spread_keep(spread_two(mixing_matrix(two["chan"], two["lu_mix"])).T).T
    chan_one = jnp.stack(
        [
            jnp.pad(one["chan"][0], (0, 4)),
            jnp.pad(jnp.exp(one["chan"][1]), (0, 4)),
            spread_one(one["chan"][3]),
        ],
        axis=1,
    )
    chan_two = jnp.stack(
        [spread_keep(two["chan"][0]), spread_keep(jnp.exp(two["chan"][1])), spread_two(two["chan"][3])], axis=1
    )
    prior_parts = prior_taps.astype(BF16).reshape(9, 2, CH // 2, 4, CH // 2, 4)
    prior_parts = jnp.pad(
        prior_parts.transpose(1, 3, 2, 0, 5, 4), ((0, 0), (0, 0), (0, 2), (0, 0), (0, 0), (0, 2))
    )
    wp = prior_parts.reshape(64, 288)
    prior_bias = vectors[-4 * CH :].reshape(2, 24)
    prior_bias = jnp.concatenate([spread_keep(prior_bias[0]), spread_keep(prior_bias[1])])[:, None]

    ext_lanes = (rows // 2 + 2) * (cols // 2 + 2) * LANES
    (y1, mixed_one, mask, mask2, keep, y2, out_two, t_two, xcol_two, h1_two, h2_two, loss_two) = call(
        functools.partial(couple_two_forward, dims),
        (
            own,
            *bufs,
            chan_one,
            m_one,
            chan_two,
            m_two,
            e_two.T,
            two["weight_b"],
            f_two,
            two["bias_b"][:, None],
        ),
        [
            shape((16, size)),
            shape((16, size)),
            shape((1, size)),
            shape((1, part)),
            shape((32, part)),
            shape((32, part)),
            shape((32, part)),
            shape((16, part)),
            shape((144, part), BF16),
            shape((HID, part), BF16),
            shape((HID, part), BF16),
            shape((8, LANES)),
        ],
        [
            pltpu.VMEM((bands, piece_rows, LANES), F32),
            pltpu.VMEM((16, size), F32),
            pltpu.VMEM((16, ext_lanes), F32),
            pltpu.VMEM((32, ext_lanes), F32),
        ],
        2 * HID * part * (144 + HID + 288),
    )
    (ge_two, gwb_two, gf_two, gbb_two, gm_two, gsum_two, gbc_two, gkeep_two) = call(
        functools.partial(couple_two_backward, half_dims),
        (
            coef,
            mask2,
            y2,
            out_two,
            t_two,
            xcol_two,
            h1_two,
            h2_two,
            chan_two,
            m_two.T,
            e_two,
            two["weight_b"].T,
            f_two.T,
        ),
        [
            shape((144, HID)),
            shape((HID, HID)),
            shape((288, HID)),
            shape((8, HID)),
            shape((32, 32, LANES)),
            shape((32, LANES)),
            shape((32, LANES)),
            shape((32, part)),
        ],
        [
            pltpu.VMEM((32, ext_lanes), F32),
            pltpu.VMEM((16, ext_lanes), F32),
            pltpu.VMEM((32, part), F32),
            pltpu.VMEM((HID, LANES), F32),
        ],
        4 * HID * part * (144 + HID + 288),
    )
    whole_lanes = (rows + 2) * (cols + 2) * LANES
    chunk = 1024
    steps = size // chunk
    vmem = pl.BlockSpec(memory_space=pltpu.VMEM)
    smem = pl.BlockSpec(memory_space=pltpu.SMEM)

    def fixed(value):
        rank = len(value.shape)
        return pl.BlockSpec(value.shape, lambda j: (0,) * rank)

    def moving(height):
        return pl.BlockSpec((height, chunk), lambda j: (0, j))

    fwd_in = (
        coef,
        mixed_one,
        mask,
        mask2,
        keep,
        gkeep_two,
        chan_one,
        e_one.T,
        one["weight_b"],
        f_one,
        one["bias_b"][:, None],
        wp,
        wp.T,
        prior_bias,
    )
    fwd_out = [
        shape((72, size), BF16),
        shape((HID, size), BF16),
        shape((HID, size), BF16),
        shape((8, size)),
        shape((8, size)),
        shape((16, size)),
        shape((64, 288)),
        shape((64, LANES)),
        shape((8, LANES)),
    ]
    (xcol_one, h1_one, h2_one, res_one, t_one, gout_one, gwp, gpb, loss_one) = call(
        functools.partial(couple_one_forward, dims, chunk),
        fwd_in,
        fwd_out,
        [
            pltpu.VMEM((8, whole_lanes), F32),
            pltpu.VMEM((16, whole_lanes), F32),
            pltpu.VMEM((32, ext_lanes), F32),
            pltpu.VMEM((288, cols // 2 * LANES), BF16),
            pltpu.VMEM((32, ext_lanes), F32),
            pltpu.VMEM((32, part), F32),
        ],
        2 * HID * size * (72 + HID + 144),
        grid=(steps,),
        in_specs=[smem] + [fixed(x) for x in fwd_in[1:]],
        out_specs=[moving(72), moving(HID), moving(HID)] + [fixed(x) for x in fwd_out[3:]],
    )
    bwd_in = (
        coef,
        mask,
        y1,
        res_one,
        t_one,
        gout_one,
        e_one,
        one["weight_b"].T,
        f_one.T,
        xcol_one,
        h1_one,
        h2_one,
    )
    bwd_out = [
        shape((72, HID)),
        shape((HID, HID)),
        shape((144, HID)),
        shape((8, HID)),
        shape((CH, 16, LANES)),
        shape((16, LANES)),
        shape((16, LANES)),
    ]
    (ge_one, gwb_one, gf_one, gbb_one, gm_one, gsum_one, gbc_one) = call(
        functools.partial(couple_one_backward, dims, chunk),
        bwd_in,
        bwd_out,
        [
            pltpu.VMEM((16, whole_lanes), F32),
            pltpu.VMEM((8, whole_lanes), F32),
            pltpu.VMEM((16, size), F32),
            pltpu.VMEM((HID, LANES), F32),
        ],
        4 * HID * size * (72 + HID + 144),
        grid=(steps,),
        in_specs=[smem] + [fixed(x) for x in bwd_in[1:9]] + [moving(72), moving(HID), moving(HID)],
        out_specs=[fixed(x) for x in bwd_out],
    )

    def unpad_one(value, axis=0):
        parted = value.reshape(value.shape[:axis] + (2, 8) + value.shape[axis + 1 :])
        parted = lax.slice_in_dim(parted, 0, 6, axis=axis + 1)
        return parted.reshape(value.shape[:axis] + (12,) + value.shape[axis + 1 :])

    def unpad_two(value, axis=0):
        parted = value.reshape(value.shape[:axis] + (2, 16) + value.shape[axis + 1 :])
        parted = lax.slice_in_dim(parted, 0, 12, axis=axis + 1)
        return parted.reshape(value.shape[:axis] + (24,) + value.shape[axis + 1 :])

    entry_one = ge_one.reshape(9, 8, HID)
    entry_two = ge_two.reshape(9, 16, HID)
    exit_one = unpad_one(gf_one.reshape(9, 16, HID), 1)
    exit_two = unpad_two(gf_two.reshape(9, 32, HID), 1)
    prior_grad = gwp.reshape(2, 4, 8, 9, 4, 8)[:, :, :6, :, :, :6].transpose(3, 0, 2, 1, 5, 4).reshape(9, 48, 24)
    pieces_small = (
        unpad_one(jnp.sum(gm_one, axis=2).T),
        unpad_one(jnp.sum(gsum_one, axis=1)),
        unpad_one(jnp.sum(gbc_one, axis=1)),
        gather_keep(unpad_two(jnp.sum(gm_two, axis=2).T).T).T,
        unpad_two(jnp.sum(gsum_two, axis=1)),
        unpad_two(jnp.sum(gbc_two, axis=1)),
        gather_keep(jnp.sum(gpb[:32], axis=1)),
        gather_keep(jnp.sum(gpb[32:], axis=1)),
        entry_one[0, 6],
        gbb_one[0],
        entry_two[0, 12],
        gbb_two[0],
        jnp.sum(loss_one[0]) + jnp.sum(loss_two[0]),
        jnp.sum(loss_two[1]),
    )
    big = (entry_one[:, :6], gwb_one, exit_one, entry_two[:, :12], gwb_two, exit_two, prior_grad)
    pieces_small, big = lax.psum((pieces_small, big), ("batch", "rows"))
    (gm1, gs1, gc1, gm2, gs2, gc2, gp0, gp1, ga1, gb1, ga2, gb2, log_total, count_two) = pieces_small
    (entry_one, middle_one, exit_one, entry_two, middle_two, exit_two, prior_grad) = big
    const_one = jnp.sum(one["chan"][1]) + jnp.sum(one["chan"][2])
    const_two = jnp.sum(two["chan"][1]) + jnp.sum(two["chan"][2])
    total = log_total + const_one * count + count_two * (const_two - 48 * 0.5 * LOG_TWO_PI)
    loss = coef[0] * total + 8.0
    chan1, lu1 = chan_grads(one, gm1, gs1, gc1, coef[0] * count)
    chan2, lu2 = chan_grads(two, gm2, gs2, gc2, coef[0] * count_two)
    vector_grad = jnp.concatenate(
        [chan1.reshape(-1), ga1, gb1, lu1.reshape(-1), chan2.reshape(-1), ga2, gb2, lu2.reshape(-1), gp0, gp1]
    )
    grads = (
        vector_grad,
        jnp.concatenate([entry_one, entry_two], axis=1),
        jnp.stack([middle_one, middle_two]),
        jnp.concatenate([exit_one, exit_two], axis=1),
        prior_grad,
    )
    grad_norm = jnp.sqrt(sum((jnp.sum(grad * grad) for grad in grads)))
    clip = jnp.minimum(1.0, CLIP_NORM / (grad_norm + 1e-06))
    weights = (vectors, entry_taps, middle, exit_taps, prior_taps)
    firsts = (vectors_first, entry_first, middle_first, exit_first, prior_first)
    seconds = (vectors_second, entry_second, middle_second, exit_second, prior_second)
    results = [loss, grad_norm]
    for weight, grad, first, second in zip(weights, grads, firsts, seconds):
        clipped = grad * clip
        updated, second_new = adamw(weight, clipped, first, second)
        results.extend([updated, clipped, second_new])
    results.append(hidden_biases(grads[0] * clip))
    return tuple(results)


def solution(mesh):
    replicated = (P(),) * 15
    return jax.shard_map(
        on_device,
        mesh=mesh,
        in_specs=(P(None, "rows", None, "batch"), P("rows", None, "batch")) + replicated,
        out_specs=(P(),) * 18,
        check_vma=False,
    )
```

time: 897 us -> 376 us (0.42)
  matrix products: 587 us -> 1.35 us
  Pallas kernels: 0 us -> 62.6 us
  waiting for transfers between devices: 87 us -> 137 us
  blocking collectives: 86.4 us -> 43.8 us
  local copies, waits for them, and re-layouts: 21.7 us -> 47.8 us
  other arithmetic: 51.2 us -> 35.5 us
  starting transfers between devices: 30.5 us -> 15.5 us
    dot_general x153 -> x8, matrix products: 587 us -> 1.35 us  [the longest x6 1.11 us: mixing_matrix(): return jnp.dot(lower, upper, precision=HIGH)[::-1]]
    pallas_call x0 -> x5, Pallas kernels: none -> 62.6 us  [call(): pl.pallas_call(kernel, out_shape=outputs, in_specs=in_specs, out_specs=ou...]
    psum x1, waiting for transfers between devices: 86.9 us -> 135 us  [on_device(): pieces_small, big = lax.psum((pieces_small, big), ('batch', 'rows'))]
    psum x2 -> x1, blocking collectives: 86.4 us -> 43.8 us  [on_device(): pieces_small, big = lax.psum((pieces_small, big), ('batch', 'rows'))]
    ppermute x12 -> x8, starting transfers between devices: 30.5 us -> 15.5 us  [the longest x5 13.6 us: total_over(): lax.ppermute(value, axis, [(i, i ^ distance) for i in range(size)])]
  transfers between devices with their start and end apart: 13 -> 9, of which waited for: 1 -> 5; matrix products, arithmetic and copies ran while one was open for 24% -> 11% of each run, Pallas kernels for 0% -> 1%
where the time goes in v1:
time: 376 us; the launch traced here: 374 us
  waiting for transfers between devices  137 us (36%)
  Pallas kernels  62.6 us (17%)
  local copies, waits for them, and re-layouts  47.8 us (13%)
  blocking collectives  43.8 us (12%)
  other arithmetic  35.5 us (9%)
  between operations  30.5 us (8%)
  starting transfers between devices  15.5 us (4%)
    psum x1, waiting for transfers between devices, on_device(): pieces_small, big = lax.psum((pieces_small, big), ('batch', 'rows'))  135 us
    pallas_call x5, Pallas kernels, call(): pl.pallas_call(kernel, out_shape=outputs, in_specs=in_specs, out_specs=ou...  62.6 us
    psum x1, blocking collectives, on_device(): pieces_small, big = lax.psum((pieces_small, big), ('batch', 'rows'))  43.8 us
    ppermute x5, starting transfers between devices, total_over(): lax.ppermute(value, axis, [(i, i ^ distance) for i in range(size)])  13.6 us
    sub x5, other arithmetic, adamw(): weight - LEARN_RATE * (first_hat / (jnp.sqrt(second_hat) + ADAM_EPS) + WE...  10.9 us
  transfers between devices with their start and end apart: 9, of which 5 were waited for; matrix products, arithmetic and copies ran while one was open for 11% of the time, Pallas kernels for 1%

profile of v1, /device:TPU:0, one launch (start us, length us, event | category | flops | bytes accessed | tf_op | source)
XLA Modules:
  0.0 373.8 jit_solution(16934733158530742435)
XLA Ops:
  7.2 1.4 convert_reduce_fusion
  8.6 2.9 collective-permute-start
  11.5 1.9 shard_map.304
  13.4 1.5 collective-permute-start.6
  15.3 0.9 slice_exponential_fusion.2
  16.2 0.9 fusion.55
  17.2 0.9 fusion.56
  25.1 1.0 slice.390
  26.2 1.0 slice_select_fusion
  27.2 1.8 copy.240
  29.0 1.1 slice_bitcast_fusion.1
  30.9 2.0 broadcast_select_fusion
  32.9 2.0 broadcast_select_fusion.1
  40.0 1.3 scatter.25
  42.5 1.2 copy.282
  45.1 0.9 copy.257.bias_ref
  45.9 1.3 scatter.20
  48.4 0.9 copy.246.bias_ref
  50.3 0.9 copy.247
  51.2 1.0 copy.256.wb_ref
  52.2 1.0 copy.245.wb_ref
  54.6 2.9 collective-permute-start.1
  58.8 4.0 %collective-permute-start.2 = (f32[]{:T(128)}, f32[]{:T(128)}, u32[]{:S(2)}, u32[]{:S(2)}) collective-permute-start(f32[]{:T(128)} %add.351), channel_id=1, source_target_pairs={{0,16},{4,20},{8,24},{12,28},{16,0},{20,4},{24,8},{28,12},{1,17},{... | collective-permute-start | bytes 20 | tf_op jit(solution)/shard_map/ppermute | solution.py:667
  64.0 0.9 collective-permute-start.3
  65.8 2.9 collective-permute-start.4
  70.2 8.0 %shard_map.305 = (f32[16,8192]{1,0:T(8,128)}, f32[16,8192]{1,0:T(8,128)}, f32[1,8192]{1,0:T(1,128)}, f32[1,2048]{1,0:T(1,128)}, f32[32,2048]{1,0:T(8,128)}, /*in...) custom-call(s32[1]{0:T(128)} %bitcast.1.index_ref, ...), custom_call_target="tpu_custom_call" | custom-call | flops 1979711488 | bytes 7982660 | tf_op jit(solution)/shard_map/pallas_call | solution.py:554
  78.2 1.4 slice_reduce_fusion.2
  79.6 10.4 %shard_map.306 = (f32[144,512]{1,0:T(8,128)}, f32[512,512]{1,0:T(8,128)}, f32[288,512]{1,0:T(8,128)}, f32[8,512]{1,0:T(8,128)}, f32[32,32,128]{2,1,0:T(8,128)}, ...) custom-call(f32[1]{0:T(128)} %bitcast.coef_ref, f32[1,2048]{1,0:T(1,128)} %get-tuple-element.136.mask2_ref, ...), custom_call_target="tpu_custom_call" | custom-call | flops 3959422976 | bytes 9187716 | tf_op jit(solution)/shard_map/pallas_call | solution.py:554
  93.1 1.3 slice.441
  94.5 1.3 slice.421
  95.8 1.2 reduce_sum.253
  97.9 15.2 %shard_map.307 = (bf16[72,8192]{1,0:T(8,128)(2,1)}, bf16[512,8192]{1,0:T(8,128)(2,1)}, bf16[512,8192]{1,0:T(8,128)(2,1)}, f32[8,8192]{1,0:T(8,128)}, f32[8,8192]...) custom-call(f32[1]{0:T(128)} %bitcast.coef_ref, ...), custom_call_target="tpu_custom_call" | custom-call | flops 6106906624 | bytes 21027268 | tf_op jit(solution)/shard_map/pallas_call | solution.py:554
  113.0 1.3 slice_reduce_fusion.4
  114.3 0.8 slice_reduce_fusion
  116.8 27.1 %shard_map.308 = (f32[72,512]{1,0:T(8,128)}, f32[512,512]{1,0:T(8,128)}, f32[144,512]{1,0:T(8,128)}, f32[8,512]{1,0:T(8,128)}, f32[12,16,128]{2,1,0:T(8,128)}, /*index=5*/f32[16,128]{1,0:T(8,128)}, f32[16,128]{1,0:T(8,128)}) custom-call(f32[1]{0:T(128)} %bitcast.coef_ref, f32[1,8192]{1,0:T(1,128)} %get-tuple-element.135.mask_ref, ...), custom_call_target="tpu_custom_call" | custom-call | flops 12213813248 | bytes 21929988 | tf_op jit(solution)/shard_map/pallas_call | solution.py:554
  146.2 1.0 reduce_sum.248
  147.9 1.3 slice.438
  149.2 1.3 slice.415
  151.4 1.3 copy.275
  154.3 43.8 %all-reduce.15 = (f32[]{:T(128)}, f32[]{:T(128)}, f32[1,12]{1,0:T(1,128)S(1)}, f32[12,12]{1,0:T(8,128)S(1)}, f32[12]{0:T(128)S(1)}, /*index=5*/f32[512]{0:T(512)...) all-reduce(f32[]{:T(128)S(6)} %add.367, ...), channel_id=1, replica_groups=mesh['batch'=8,'rows'=4] {'batch','rows'}, use_global_device_ids=true, to_apply=%region_5.6 | all-reduce | flops 13258 | bytes 106064 | tf_op jit(solution)/shard_map/psum | solution.py:940
  208.8 134.6 %all-reduce.19.cloned.1.call-done = (f32[9,12,512]{2,1,0:T(8,128)}, f32[9,6,512]{2,1,0:T(8,128)}, f32[1,512,512]{2,1,0:T(8,128)}, f32[1,512,512]{2,1,0:T(8,128)}...) async-done(((f32[9,12,512]{2,1,0:T(8,128)}, f32[9,6,512]{2,1,0:T(8,128)}, f32[1,512,512]{2,1,0:T(8,128)}, f32[1,512,512]{2,1,0:T(8,128)}, f32[9,24,512]{2,1,0:T(8,128)}, ...) | async-done | bytes 3092496 | tf_op jit(solution)/shard_map/psum | solution.py:940
  343.4 1.4 constant_dynamic-update-slice_fusion.1
  345.0 1.1 multiply_reduce_fusion
  351.0 1.4 multiply_subtract_fusion.4
  353.7 1.7 multiply_subtract_fusion.3
  355.4 2.7 multiply_subtract_fusion.2
  358.2 1.6 multiply_subtract_fusion.1
  361.2 3.5 multiply_subtract_fusion
  (276 shorter events, 39.9 us)
Async XLA Ops:
  8.6 44.7 %collective-permute-start = (f32[]{:T(128)}, f32[]{:T(128)}, u32[]{:S(2)}, u32[]{:S(2)}) collective-permute-start(f32[]{:T(128)} %convert_reduce_fusion), channel_id=1, source_target_pairs={{0,4},{4,0},{8,12},{12,8},{16,20},{20,16},{24,28},{28,24},{1,5},{5... | collective-permute-start | bytes 20 | tf_op jit(solution)/shard_map/ppermute | solution.py:667
  13.4 56.7 %collective-permute-start.5 = (bf16[208,128]{1,0:T(8,128)(2,1)}, bf16[208,128]{1,0:T(8,128)(2,1)}, u32[]{:S(2)}, u32[]{:S(2)}) collective-permute-start(bf16[208,128]{1,0:T(8,128)(2,1)} %get-tuple-element.131), channel_id=1, source_target_pairs={{0,1},{1,0},{2,3},{3,2},{4,5},{5,4},{6,7},{7,6},{8,9},{9,8},{10,11... | collective-permute-start | bytes 159752 | tf_op jit(solution)/shard_map/ppermute | solution.py:710
  13.4 56.7 %collective-permute-start.6 = (bf16[208,128]{1,0:T(8,128)(2,1)}, bf16[208,128]{1,0:T(8,128)(2,1)}, u32[]{:S(2)}, u32[]{:S(2)}) collective-permute-start(bf16[208,128]{1,0:T(8,128)(2,1)} %get-tuple-element.132), channel_id=1, source_target_pairs={{0,2},{1,3},{2,0},{3,1},{4,6},{5,7},{6,4},{7,5},{8,10},{9,11},{10,... | collective-permute-start | bytes 159752 | tf_op jit(solution)/shard_map/ppermute | solution.py:710
  14.9 55.2 %collective-permute-start.7 = (bf16[208,128]{1,0:T(8,128)(2,1)}, bf16[208,128]{1,0:T(8,128)(2,1)}, u32[]{:S(2)}, u32[]{:S(2)}) collective-permute-start(bf16[208,128]{1,0:T(8,128)(2,1)} %get-tuple-element.133), channel_id=1, source_target_pairs={{0,3},{1,2},{2,1},{3,0},{4,7},{5,6},{6,5},{7,4},{8,11},{9,10},{10,... | collective-permute-start | bytes 159752 | tf_op jit(solution)/shard_map/ppermute | solution.py:710
  15.3 4.1 %copy-start.35 = (s32[12]{0:T(128)}, s32[12]{0:T(128)S(1)}, u32[]{:S(2)}) copy-start(s32[12]{0:T(128)S(1)} %iota_add_fusion.1) | copy-start | bytes 148
  15.3 4.5 %copy-start.31 = (s32[24]{0:T(128)}, s32[24]{0:T(128)S(1)}, u32[]{:S(2)}) copy-start(s32[24]{0:T(128)S(1)} %iota_add_fusion) | copy-start | bytes 292
  16.2 12.7 %copy-start.37 = (f32[12]{0:T(128)}, f32[12]{0:T(128)S(1)}, u32[]{:S(2)}) copy-start(f32[12]{0:T(128)S(1)} %get-tuple-element.298) | copy-start | bytes 148
  17.1 6.1 %copy-start.33 = (f32[24]{0:T(128)}, f32[24]{0:T(128)S(1)}, u32[]{:S(2)}) copy-start(f32[24]{0:T(128)S(1)} %get-tuple-element.285) | copy-start | bytes 292
  29.0 6.0 %copy-start.1 = (f32[9,36,512]{2,1,0:T(8,128)S(1)}, f32[9,36,512]{2,1,0:T(8,128)}, u32[]{:S(2)}) copy-start(f32[9,36,512]{2,1,0:T(8,128)} %param.40) | copy-start | bytes 1990660
  29.0 11.0 %copy-start.16 = (f32[9,48,24]{1,2,0:T(8,128)S(1)}, f32[9,48,24]{1,2,0:T(8,128)}, u32[]{:S(2)}) copy-start(f32[9,48,24]{1,2,0:T(8,128)} %param.43) | copy-start | bytes 124420
  41.4 7.9 %copy-start.17 = (bf16[9,8,512]{2,1,0:T(8,128)(2,1)}, bf16[9,8,512]{2,1,0:T(8,128)(2,1)S(1)}, u32[]{:S(2)}) copy-start(bf16[9,8,512]{2,1,0:T(8,128)(2,1)S(1)} %scatter.29) | copy-start | bytes 221188
  44.3 7.9 %copy-start.19 = (bf16[64,288]{1,0:T(8,128)(2,1)}, bf16[64,288]{1,0:T(8,128)(2,1)S(1)}, u32[]{:S(2)}) copy-start(bf16[64,288]{1,0:T(8,128)(2,1)S(1)} %reshape.622.wp_ref) | copy-start | bytes 110596
  47.5 4.7 %copy-start.14 = (bf16[9,16,512]{2,1,0:T(8,128)(2,1)}, bf16[9,16,512]{2,1,0:T(8,128)(2,1)S(1)}, u32[]{:S(2)}) copy-start(bf16[9,16,512]{2,1,0:T(8,128)(2,1)S(1)} %scatter.24) | copy-start | bytes 442372
  49.4 3.9 %copy-start.13 = (bf16[9,2,8,512]{3,2,1,0:T(8,128)(2,1)}, bf16[9,2,8,512]{3,2,1,0:T(8,128)(2,1)S(1)}, u32[]{:S(2)}) copy-start(bf16[9,2,8,512]{3,2,1,0:T(8,128)(2,1)S(1)} %pad.99) | copy-start | bytes 442372
  49.5 20.7 %copy-start.6 = (bf16[9,2,16,512]{3,2,1,0:T(8,128)(2,1)}, bf16[9,2,16,512]{3,2,1,0:T(8,128)(2,1)S(1)}, u32[]{:S(2)}) copy-start(bf16[9,2,16,512]{3,2,1,0:T(8,128)(2,1)S(1)} %pad.97) | copy-start | bytes 884740
  54.6 3.6 collective-permute-start.1
  58.8 4.5 %collective-permute-start.2 = (f32[]{:T(128)}, f32[]{:T(128)}, u32[]{:S(2)}, u32[]{:S(2)}) collective-permute-start(f32[]{:T(128)} %add.351), channel_id=1, source_target_pairs={{0,16},{4,20},{8,24},{12,28},{16,0},{20,4},{24,8},{28,12},{1,17},{... | collective-permute-start | bytes 20 | tf_op jit(solution)/shard_map/ppermute | solution.py:667
  64.0 1.2 collective-permute-start.3
  65.8 3.6 collective-permute-start.4
  116.8 33.7 %copy-start.23 = (f32[64,288]{1,0:T(8,128)S(1)}, f32[64,288]{1,0:T(8,128)}, u32[]{:S(2)}) copy-start(f32[64,288]{1,0:T(8,128)} %get-tuple-element.169) | copy-start | bytes 221188
  149.2 194.1 %all-reduce.19.cloned.1.call-start = ((), (), s32[]{:S(2)}) async-start(), calls=%async_computation | async-start | bytes 6553600 | tf_op jit(solution)/shard_map/psum | solution.py:940
  151.1 3.0 copy-start.27
  151.1 47.0 %copy-start.15 = (f32[288,512]{1,0:T(8,128)S(1)}, f32[288,512]{1,0:T(8,128)}, u32[]{:S(2)}) copy-start(f32[288,512]{1,0:T(8,128)} %get-tuple-element.168) | copy-start | bytes 1769476
  151.2 3.0 copy-start.25
  151.2 3.0 copy-start.28
  151.2 3.0 copy-start.29
  151.3 2.9 copy-start.30
  151.3 2.9 copy-start.39
  151.3 2.9 copy-start.40
  151.3 2.9 copy-start.41
  151.3 2.9 copy-start.42
  151.3 2.9 copy-start.43
  151.3 2.9 copy-start.44
  151.3 47.6 %copy-start.18 = (f32[144,512]{1,0:T(8,128)S(1)}, f32[144,512]{1,0:T(8,128)}, u32[]{:S(2)}) copy-start(f32[144,512]{1,0:T(8,128)} %get-tuple-element.167) | copy-start | bytes 884740
  151.3 49.0 %copy-start.24 = (f32[12,12]{0,1:T(8,128)S(1)}, f32[12,12]{0,1:T(8,128)}, u32[]{:S(2)}) copy-start(f32[12,12]{0,1:T(8,128)} %copy.261) | copy-start | bytes 1732
  151.4 49.0 %copy-start.36 = (s32[12]{0:T(128)S(1)}, s32[12]{0:T(128)}, u32[]{:S(2)}) copy-start(s32[12]{0:T(128)} %copy-done.35) | copy-start | bytes 148
  151.4 49.3 %copy-start.38 = (f32[12]{0:T(128)S(1)}, f32[12]{0:T(128)}, u32[]{:S(2)}) copy-start(f32[12]{0:T(128)} %copy-done.37) | copy-start | bytes 148
  199.0 4.3 %copy-start.21 = (f32[24,24]{0,1:T(8,128)S(1)}, f32[24,24]{0,1:T(8,128)}, u32[]{:S(2)}) copy-start(f32[24,24]{0,1:T(8,128)} %copy.269) | copy-start | bytes 6916
  199.0 4.3 %copy-start.32 = (s32[24]{0:T(128)S(1)}, s32[24]{0:T(128)}, u32[]{:S(2)}) copy-start(s32[24]{0:T(128)} %copy-done.31) | copy-start | bytes 292
  199.0 4.5 %copy-start.34 = (f32[24]{0:T(128)S(1)}, f32[24]{0:T(128)}, u32[]{:S(2)}) copy-start(f32[24]{0:T(128)} %copy-done.33) | copy-start | bytes 292
  207.5 135.8 %copy-start.22 = (f32[2960]{0:T(1024)}, f32[2960]{0:T(1024)S(1)}, u32[]{:S(2)}) copy-start(f32[2960]{0:T(1024)S(1)} %concatenate.45) | copy-start | bytes 35524
  344.9 2.0 copy-start.12
  353.0 5.1 %copy-start.8 = (f32[9,12,512]{2,1,0:T(8,128)S(1)}, f32[9,12,512]{2,1,0:T(8,128)}, u32[]{:S(2)}) copy-start(f32[9,12,512]{2,1,0:T(8,128)} %get-tuple-element.252) | copy-start | bytes 663556
  353.0 5.1 %copy-start.10 = (f32[9,36,512]{2,1,0:T(8,128)S(1)}, f32[9,36,512]{2,1,0:T(8,128)}, u32[]{:S(2)}) copy-start(f32[9,36,512]{2,1,0:T(8,128)} %param.41) | copy-start | bytes 1990660
  353.0 5.1 %copy-start.11 = (f32[9,36,512]{2,1,0:T(8,128)S(1)}, f32[9,36,512]{2,1,0:T(8,128)}, u32[]{:S(2)}) copy-start(f32[9,36,512]{2,1,0:T(8,128)} %param.42) | copy-start | bytes 1990660
  355.4 4.4 %copy-start.3 = (f32[2,512,512]{2,1,0:T(8,128)S(1)}, f32[2,512,512]{2,1,0:T(8,128)}, u32[]{:S(2)}) copy-start(f32[2,512,512]{2,1,0:T(8,128)} %param.39) | copy-start | bytes 6291460
  358.1 2.4 copy-start
  358.1 3.0 copy-start.2
  (9 other events, 11.5 us)
Sparse Core Ops, SparseCore 0:
  203.2 140.1 all-reduce.18

commit v2 on v1

v2 whole, which is shorter than its diff:
```python
import functools
import math

import jax
import jax.numpy as jnp
from jax import lax
from jax.experimental import pallas as pl
from jax.experimental.pallas import tpu as pltpu
from jax.sharding import PartitionSpec as P

HID = 512
CH = 12

F32 = jnp.float32
BF16 = jnp.bfloat16
HIGH = lax.Precision.HIGHEST
LOG_TWO_PI = math.log(2.0 * math.pi)
LEARN_RATE = 0.05
BETA_ONE = 0.9
BETA_TWO = 0.999
ADAM_EPS = 1e-08
WEIGHT_DECAY = 0.01
CLIP_NORM = 0.01
ADAM_STEP = 10
LANES = 128
VMEM_LIMIT = 20 * 2**20
ONE_START = 4 * CH
TWO_START = 4 * CH + 2 * HID + CH * CH
PRIOR_START = TWO_START + 8 * CH + 2 * HID + 4 * CH * CH
VEC = PRIOR_START + 4 * CH
FLAT_ROWS = -(-VEC // (8 * LANES)) * 8
WB_ROWS = 4 * HID
TWO_F, TWO_E = WB_ROWS, WB_ROWS + 4 * 216
TWO_B = TWO_E + 4 * 144
TWO_SMALL = TWO_B + 8
TWO_ROWS = 3584
ONE_F = WB_ROWS
ONE_P = ONE_F + 4 * 112
ONE_B = ONE_P + 3 * 64
ONE_LOSS = ONE_B + 8
ONE_ROWS = 2816
PART_A = 1536
REST_A = 4 * 56
REST_SMALL = REST_A + 8
REST_ROWS = 256


def dot(left, right):
    return lax.dot_general(left, right, (((1,), (0,)), ((), ())), preferred_element_type=F32)


def dot_nt(left, right):
    return lax.dot_general(left, right, (((1,), (1,)), ((), ())), preferred_element_type=F32)


def lane_band(bands, height=1):
    return lax.broadcasted_iota(jnp.int32, (height, LANES), 1) // (LANES // bands)


def pack_kernel(bands, index_ref, pixels_ref, mask_ref, *out_refs):
    own = index_ref[0]
    count = jnp.sum(mask_ref[...].astype(F32), axis=0, keepdims=True)
    count = jnp.where(lax.broadcasted_iota(jnp.int32, (16, 1), 0) == 0, count, 0.0).astype(BF16)
    width = LANES // bands
    rows = pixels_ref.shape[0] // bands
    extra = mask_ref.shape[0] // bands
    band = lane_band(bands)
    parts = [pixels_ref[pl.ds(e, rows, stride=bands), :].astype(F32) for e in range(bands)]
    masks = [mask_ref[pl.ds(e, extra, stride=bands), :].astype(F32) for e in range(bands)]
    for d, out_ref in enumerate(out_refs):
        target = own ^ d
        for source, first, size in ((parts, 0, rows), (masks, rows, extra)):
            total = jnp.zeros((size, LANES), F32)
            for e in range(bands):
                shift = lax.rem(e - target + bands, bands) * width
                total = jnp.where(band == e, pltpu.roll(source[e], shift, 1), total)
            out_ref[first : first + size, :] = total.astype(BF16)
        out_ref[rows + extra :, :] = count


def fill_ext(ext_ref, field, rows, cols, bands, pattern):
    width = LANES // bands
    band = lane_band(bands)
    stride = (cols + 2) * LANES
    height = ext_ref.shape[0]
    pads = jnp.broadcast_to(pattern, (height, LANES))
    for block in range(ext_ref.shape[1] // LANES):
        ext_ref[:, block * LANES : (block + 1) * LANES] = pads
    for row in range(rows):
        start = (row + 1) * stride + LANES
        ext_ref[:, start : start + cols * LANES] = field[:, row * cols * LANES : (row + 1) * cols * LANES]
    last = (rows - 1) * cols * LANES
    for col in range(cols):
        above = pltpu.roll(field[:, last + col * LANES : last + (col + 1) * LANES], width, 1)
        start = LANES + col * LANES
        ext_ref[:, start : start + LANES] = jnp.where(band >= 1, above, pads)
        below = pltpu.roll(field[:, col * LANES : (col + 1) * LANES], LANES - width, 1)
        start = (rows + 1) * stride + LANES + col * LANES
        ext_ref[:, start : start + LANES] = jnp.where(band < bands - 1, below, pads)


def fold_ext(ext_ref, rows, cols, bands):
    width = LANES // bands
    band = lane_band(bands)
    stride = (cols + 2) * LANES
    pieces = []
    for row in range(rows):
        start = (row + 1) * stride + LANES
        piece = ext_ref[:, start : start + cols * LANES]
        if row == 0:
            blocks = []
            for col in range(cols):
                start = (rows + 1) * stride + LANES + col * LANES
                moved = pltpu.roll(ext_ref[:, start : start + LANES], width, 1)
                blocks.append(jnp.where(band >= 1, moved, 0.0))
            piece = piece + jnp.concatenate(blocks, axis=1)
        if row == rows - 1:
            blocks = []
            for col in range(cols):
                start = LANES + col * LANES
                moved = pltpu.roll(ext_ref[:, start : start + LANES], LANES - width, 1)
                blocks.append(jnp.where(band < bands - 1, moved, 0.0))
            piece = piece + jnp.concatenate(blocks, axis=1)
        pieces.append(piece)
    return pieces


def window(cols, row, first_col, tap, turned=False):
    dy, dx = tap // 3, tap % 3
    if turned:
        dy, dx = 2 - dy, 2 - dx
    return ((row + dy) * (cols + 2) + first_col + dx) * LANES


def gather_cols(ext_ref, cols, row, first_col, size, turned=False):
    starts = [window(cols, row, first_col, tap, turned) for tap in range(9)]
    starts = [s if isinstance(s, int) else pl.multiple_of(s, LANES) for s in starts]
    return jnp.concatenate([ext_ref[:, pl.ds(s, size)] for s in starts], axis=0).astype(BF16)


def scatter_cols(ext_ref, values, cols, row, first_col, size, turned=False):
    height = ext_ref.shape[0]
    for tap in range(9):
        start = window(cols, row, first_col, tap, turned)
        if not isinstance(start, int):
            start = pl.multiple_of(start, LANES)
        at = pl.ds(start, size)
        ext_ref[:, at] = ext_ref[:, at] + values[tap * height : (tap + 1) * height]


def mix(matrix_ref, field_ref, start, size, pairs):
    total = None
    for j in pairs:
        term = matrix_ref[:, j : j + 1] * field_ref[j : j + 1, start : start + size]
        total = term if total is None else total + term
    return total


def log_sigmoid(value):
    return jnp.minimum(value, 0.0) - jnp.log1p(jnp.exp(-jnp.abs(value)))


def sigmoid_minus(value):
    power = jnp.exp(-jnp.abs(value))
    return jnp.where(value >= 0.0, power, 1.0) / (1.0 + power)


def row_mask(height, period, valid):
    return lax.rem(lax.broadcasted_iota(jnp.int32, (height, 1), 0), period) < valid


def fold_lanes(value):
    total = value[:, :LANES]
    for start in range(LANES, value.shape[1], LANES):
        total = total + value[:, start : start + LANES]
    return total


def coef_of(count_ref):
    return -1.0 / (CH * jnp.sum(count_ref[...], keepdims=True) * math.log(2.0))


def unpack_kernel(
    dims,
    index_ref,
    b0,
    b1,
    b2,
    b3,
    chan1_ref,
    m1_ref,
    chan2_ref,
    m2_ref,
    y1_ref,
    mix1_ref,
    mask_ref,
    mask2_ref,
    keep_ref,
    y2_ref,
    mix2_ref,
    bufs,
    xs,
):
    rows, cols, bands = dims
    own = index_ref[0]
    width = LANES // bands
    band = lane_band(bands)
    groups = cols // bands
    for d, ref in enumerate((b0, b1, b2, b3)):
        bufs[d, :, :] = ref[...].astype(F32)
    xs[...] = jnp.zeros_like(xs)
    for s in range(rows):
        for a in range(groups):
            loads = [bufs[d, pl.ds(s * groups + a, CH + 1, stride=rows * groups), :] for d in range(bands)]
            for e in range(bands):
                total = jnp.zeros((CH + 1, LANES), F32)
                for d in range(bands):
                    origin = own ^ d
                    shift = lax.rem(origin - e + bands, bands) * width
                    total = jnp.where(band == origin, pltpu.roll(loads[d], shift, 1), total)
                start = (s * cols + bands * a + e) * LANES
                xs[0 : CH + 1, start : start + LANES] = total
    line = cols * LANES
    for s in range(rows):
        at = slice(s * line, (s + 1) * line)
        mask_ref[:, at] = xs[CH : CH + 1, at]
        raw = xs[:, at]
        source = (raw + 0.5) / 256.0 - 0.5
        y1_ref[:, at] = (source + chan1_ref[:, 0:1]) * chan1_ref[:, 1:2]
    for s in range(rows):
        at = slice(s * line, (s + 1) * line)
        mix1_ref[:, at] = mix(m1_ref, y1_ref, s * line, line, range(CH))
    half_rows, half_cols = rows // 2, cols // 2
    for i in range(half_rows):
        for j in range(half_cols):
            at = slice((i * half_cols + j) * LANES, (i * half_cols + j + 1) * LANES)
            masks = None
            for p in range(4):
                di, dj = p // 2, p % 2
                start = ((2 * i + di) * cols + 2 * j + dj) * LANES
                keep_ref[p * 8 : p * 8 + 8, at] = mix1_ref[0:8, start : start + LANES]
                block = mask_ref[:, start : start + LANES]
                masks = block if masks is None else jnp.minimum(masks, block)
            mask2_ref[:, at] = masks
    size = half_rows * half_cols * LANES
    y2_ref[...] = (keep_ref[...] + chan2_ref[:, 0:1]) * chan2_ref[:, 1:2]
    pairs = [j for j in range(32) if j % 8 < 6]
    mix2_ref[...] = mix(m2_ref, y2_ref, 0, size, pairs)


def couple_two_forward(
    dims,
    mix2_ref,
    mask_ref,
    mask2_ref,
    chan2_ref,
    et_ref,
    wb_ref,
    f_ref,
    bias_ref,
    out2_ref,
    t2_ref,
    xcol_ref,
    h1_ref,
    h2_ref,
    loss_ref,
    ext,
    oacc,
):
    half_rows, half_cols, bands = dims
    mixed = mix2_ref[...]
    out2_ref[0:16, :] = mixed[:16]
    iota = lax.broadcasted_iota(jnp.int32, (16, 1), 0)
    ones = jnp.where(iota == CH, 1.0, 0.0)
    fill_ext(ext, mixed[:16] + ones, half_rows, half_cols, bands, ones)
    oacc[...] = jnp.zeros_like(oacc)
    chunk = half_cols * LANES
    for i in range(half_rows):
        at = slice(i * chunk, (i + 1) * chunk)
        xcol = gather_cols(ext, half_cols, i, 0, chunk)
        xcol_ref[:, at] = xcol
        hidden = jnp.maximum(dot(et_ref[...], xcol), 0.0).astype(BF16)
        h1_ref[:, at] = hidden
        hidden = jnp.maximum(dot(wb_ref[...], hidden) + bias_ref[...], 0.0).astype(BF16)
        h2_ref[:, at] = hidden
        scatter_cols(oacc, dot(f_ref[...], hidden), half_cols, i, 0, chunk, True)
    output = jnp.concatenate(fold_ext(oacc, half_rows, half_cols, bands), axis=1) + chan2_ref[:, 2:3]
    second = output[16:] + 2.0
    t2_ref[...] = second
    scale_log = log_sigmoid(second)
    result = (mixed[16:] + output[:16]) * jnp.exp(scale_log)
    out2_ref[16:, :] = result
    valid = row_mask(16, 16, CH)
    per_pixel = jnp.where(valid, scale_log - 0.5 * (mixed[:16] * mixed[:16] + result * result), 0.0)
    mask2 = mask2_ref[...]
    loss_ref[...] = jnp.zeros_like(loss_ref)
    loss_ref[0:1, :] = jnp.sum(fold_lanes(per_pixel * mask2), axis=0, keepdims=True)
    loss_ref[1:2, :] = fold_lanes(mask2)
    loss_ref[2:3, :] = fold_lanes(mask_ref[...])


def part_out(slab_ref, first, size, index, bit, kept_ref, sent_ref):
    half = size // 2
    high = lax.rem(index // bit, 2)
    kept_ref[...] = slab_ref[pl.ds(pl.multiple_of(first + high * half, 8), half), :]
    sent_ref[...] = slab_ref[pl.ds(pl.multiple_of(first + (1 - high) * half, 8), half), :]


def gram(left, right_ref, pairs, acc_ref):
    for j in pairs:
        acc_ref[j, :, :] = acc_ref[j, :, :] + fold_lanes(left * right_ref[j : j + 1, :])


def couple_two_backward(
    dims,
    index_ref,
    count_ref,
    mask2_ref,
    y2_ref,
    out2_ref,
    t2_ref,
    xcol_ref,
    h1_ref,
    h2_ref,
    chan2_ref,
    m2t_ref,
    e_ref,
    wbt_ref,
    ft_ref,
    kept_ref,
    sent_ref,
    gkeep_ref,
    ext,
    gacc,
    gmix,
    bacc,
    ge,
    gf,
    acc,
    slab_ref,
):
    rows, cols, bands = dims
    coef = coef_of(count_ref)
    mask2 = mask2_ref[...]
    weight = coef * mask2
    second = t2_ref[...]
    result = out2_ref[16:, :]
    g_result = -weight * result
    g_log = g_result * result + weight
    g_second = g_log * sigmoid_minus(second)
    g_half = g_result * jnp.exp(log_sigmoid(second))
    gmix[0:16, :] = -weight * out2_ref[0:16, :]
    gmix[16:32, :] = g_half
    valid = row_mask(16, 16, CH)
    g_out = jnp.concatenate([g_half, jnp.where(valid, g_second, 0.0)], axis=0)
    g_out = g_out.astype(BF16).astype(F32)
    out_sums = fold_lanes(g_out)
    fill_ext(ext, g_out, rows, cols, bands, jnp.zeros((32, 1), F32))
    gacc[...] = jnp.zeros_like(gacc)
    chunk = cols * LANES
    for i in range(rows):
        at = slice(i * chunk, (i + 1) * chunk)
        gcol = gather_cols(ext, cols, i, 0, chunk, True)
        hidden_two = h2_ref[:, at]
        hidden_one = h1_ref[:, at]
        g_pre = jnp.where(hidden_two > 0, dot(ft_ref[...], gcol), 0.0).astype(BF16)
        g_f = dot_nt(gcol, hidden_two)
        g_wb = dot_nt(g_pre, hidden_one)
        folded = fold_lanes(g_pre.astype(F32))
        g_pre = jnp.where(hidden_one > 0, dot(wbt_ref[...], g_pre), 0.0).astype(BF16)
        g_e = dot_nt(xcol_ref[:, at], g_pre)
        scatter_cols(gacc, dot(e_ref[...], g_pre), cols, i, 0, chunk)
        if i == 0:
            gf[...], ge[...], bacc[...] = g_f, g_e, folded
        else:
            gf[...] += g_f
            ge[...] += g_e
            bacc[...] += folded
        for block in range(HID // LANES):
            at = slice(block * HID, (block + 1) * HID)
            part = g_wb[:, block * LANES : (block + 1) * LANES]
            slab_ref[at, :] = part if i == 0 else slab_ref[at, :] + part
    slab_ref[TWO_B:TWO_ROWS, :] = jnp.zeros((TWO_ROWS - TWO_B, LANES), F32)
    put_rows(slab_ref, lambda block: TWO_B + block, ones_sum(bacc), 0, 1)
    for piece in range(18):
        put_rows(slab_ref, lambda block: TWO_F + block * 216 + piece * CH, gf, piece * 16, CH)
    put_rows(slab_ref, lambda block: TWO_E + block * 144, ge, 0, 144)
    gmix[0:16, :] += jnp.concatenate(fold_ext(gacc, rows, cols, bands), axis=1)
    pairs = [j for j in range(32) if j % 8 < 6]
    g_mixed = gmix[...]
    acc[...] = jnp.zeros_like(acc)
    gram(g_mixed, y2_ref, pairs, acc)
    stack = [(j, acc[j]) for j in pairs] + [(32, fold_lanes(g_mixed)), (33, out_sums)]
    slab_ref[TWO_SMALL : TWO_SMALL + 32, :] = lane_sums(stack, 32)
    part_out(slab_ref, 0, TWO_ROWS, index_ref[1], 1, kept_ref, sent_ref)
    valid_rows = [j for j in range(32) if j % 16 < CH]
    gkeep_ref[...] = mix(m2t_ref, gmix, 0, rows * chunk, valid_rows) * chan2_ref[:, 1:2]


def couple_one_forward(
    dims,
    chunk,
    count_ref,
    mix1_ref,
    mask_ref,
    mask2_ref,
    keep_ref,
    gkeep_in_ref,
    chan1_ref,
    et_ref,
    wb_ref,
    f_ref,
    bias_ref,
    wp_ref,
    wpt_ref,
    pbias_ref,
    xcol_ref,
    h1_ref,
    h2_ref,
    res_ref,
    t_ref,
    gout_ref,
    gwp_ref,
    loss_ref,
    ext,
    oacc,
    kext,
    kcol,
    gkacc,
    drop,
):
    rows, cols, bands = dims
    step = pl.program_id(0)
    per_row = cols * LANES // chunk
    iota = lax.broadcasted_iota(jnp.int32, (8, 1), 0)
    ones = jnp.where(iota == CH // 2, 1.0, 0.0)

    @pl.when(step == 0)
    def _():
        fill_ext(ext, mix1_ref[0:8, :] + ones, rows, cols, bands, ones)
        oacc[...] = jnp.zeros_like(oacc)

    row = step // per_row
    col = (step % per_row) * (chunk // LANES)
    xcol = gather_cols(ext, cols, row, col, chunk)
    xcol_ref[...] = xcol
    hidden = jnp.maximum(dot(et_ref[...], xcol), 0.0).astype(BF16)
    h1_ref[...] = hidden
    hidden = jnp.maximum(dot(wb_ref[...], hidden) + bias_ref[...], 0.0).astype(BF16)
    h2_ref[...] = hidden
    scatter_cols(oacc, dot(f_ref[...], hidden), cols, row, col, chunk, True)

    @pl.when(step == pl.num_programs(0) - 1)
    def _():
        line = cols * LANES
        valid = row_mask(8, 8, CH // 2)
        step_total = None
        half_rows, half_cols = rows // 2, cols // 2
        for s, piece in enumerate(fold_ext(oacc, rows, cols, bands)):
            at = slice(s * line, (s + 1) * line)
            output = piece + chan1_ref[:, 2:3]
            second = output[8:] + 2.0
            t_ref[:, at] = second
            scale_log = log_sigmoid(second)
            result = (mix1_ref[8:16, at] + output[:8]) * jnp.exp(scale_log)
            res_ref[:, at] = result
            part = fold_lanes(jnp.where(valid, scale_log, 0.0) * mask_ref[:, at])
            step_total = part if step_total is None else step_total + part
        for i in range(half_rows):
            for j in range(half_cols):
                at = slice((i * half_cols + j) * LANES, (i * half_cols + j + 1) * LANES)
                for p in range(4):
                    start = ((2 * i + p // 2) * cols + 2 * j + p % 2) * LANES
                    drop[p * 8 : p * 8 + 8, at] = res_ref[:, start : start + LANES]
        part_iota = lax.broadcasted_iota(jnp.int32, (32, 1), 0)
        part_ones = jnp.where(part_iota == CH // 2, 1.0, 0.0)
        fill_ext(kext, keep_ref[...] + part_ones, half_rows, half_cols, bands, part_ones)
        part_line = half_cols * LANES
        gkacc[...] = jnp.zeros_like(gkacc)
        weight = coef_of(count_ref) * mask2_ref[...]
        valid = row_mask(32, 8, CH // 2)
        prior_total = None
        for i in range(half_rows):
            at = slice(i * part_line, (i + 1) * part_line)
            columns = gather_cols(kext, half_cols, i, 0, part_line)
            kcol[...] = columns
            prior = dot(wp_ref[...], columns) + pbias_ref[...]
            mean, logs = prior[:32], prior[32:]
            inverse = jnp.exp(-logs)
            scaled = (drop[:, at] - mean) * inverse
            part = fold_lanes((-logs - 0.5 * scaled * scaled) * mask2_ref[:, at])
            prior_total = part if prior_total is None else prior_total + part
            g_mean = weight[:, at] * scaled * inverse
            g_logs = jnp.where(valid, weight[:, at] * (scaled * scaled - 1.0), 0.0)
            drop[:, at] = -g_mean
            g_prior = jnp.concatenate([g_mean, g_logs], axis=0).astype(BF16)
            g_wp = dot_nt(g_prior, kcol[...])
            if i == 0:
                gwp_ref[...] = g_wp
            else:
                gwp_ref[...] += g_wp
            scatter_cols(gkacc, dot(wpt_ref[...], g_prior), half_cols, i, 0, part_line)
        loss_ref[...] = jnp.zeros_like(loss_ref)
        loss_ref[0:1, :] = jnp.sum(step_total, axis=0, keepdims=True) + jnp.sum(prior_total, axis=0, keepdims=True)
        for i, piece in enumerate(fold_ext(gkacc, half_rows, half_cols, bands)):
            at = slice(i * part_line, (i + 1) * part_line)
            g_keep = piece + gkeep_in_ref[:, at]
            g_drop = drop[:, at]
            for j in range(half_cols):
                inner = slice(j * LANES, (j + 1) * LANES)
                for p in range(4):
                    start = ((2 * i + p // 2) * cols + 2 * j + p % 2) * LANES
                    gout_ref[0:8, start : start + LANES] = g_keep[p * 8 : p * 8 + 8, inner]
                    gout_ref[8:16, start : start + LANES] = g_drop[p * 8 : p * 8 + 8, inner]


def put_rows(slab_ref, first, values, row, count):
    for block in range(HID // LANES):
        start = first(block)
        slab_ref[start : start + count, :] = values[row : row + count, block * LANES : (block + 1) * LANES]


def lane_sums(stack, width):
    lane = lax.broadcasted_iota(jnp.int32, (1, LANES), 1)
    total = jnp.zeros(stack[0][1].shape, F32)
    for j, value in stack:
        total = total + jnp.where(lane == j, jnp.sum(value, axis=1, keepdims=True), 0.0)
    return total


def ones_sum(value_ref):
    return lax.dot_general(
        jnp.ones((8, LANES), F32), value_ref[...], (((1,), (1,)), ((), ())), precision=HIGH, preferred_element_type=F32
    )


def one_backward_top(
    dims,
    chunk,
    bits,
    index_ref,
    count_ref,
    mask_ref,
    res_ref,
    t_ref,
    gout_ref,
    ft_ref,
    gwp_ref,
    loss_one_ref,
    loss_two_ref,
    h1_ref,
    h2_ref,
    kept_a,
    sent_a,
    kept_b,
    sent_b,
    ghalf_ref,
    gbc_ref,
    gpre_ref,
    ext,
    gf,
    bacc,
    slab_ref,
):
    rows, cols, bands = dims
    step = pl.program_id(0)
    per_row = cols * LANES // chunk

    @pl.when(step == 0)
    def _():
        weight = coef_of(count_ref) * mask_ref[...]
        second = t_ref[...]
        result = res_ref[...]
        g_result = gout_ref[8:16, :]
        g_log = g_result * result + weight
        g_second = g_log * sigmoid_minus(second)
        g_half = g_result * jnp.exp(log_sigmoid(second))
        ghalf_ref[...] = g_half
        valid = row_mask(8, 8, CH // 2)
        g_out = jnp.concatenate([g_half, jnp.where(valid, g_second, 0.0)], axis=0)
        g_out = g_out.astype(BF16).astype(F32)
        gbc_ref[...] = fold_lanes(g_out)
        fill_ext(ext, g_out, rows, cols, bands, jnp.zeros((16, 1), F32))
        gf[...] = jnp.zeros_like(gf)
        slab_ref[...] = jnp.zeros_like(slab_ref)
        bacc[...] = jnp.zeros_like(bacc)

    row = step // per_row
    col = (step % per_row) * (chunk // LANES)
    gcol = gather_cols(ext, cols, row, col, chunk, True)
    hidden_two = h2_ref[...]
    g_pre = jnp.where(hidden_two > 0, dot(ft_ref[...], gcol), 0.0).astype(BF16)
    gpre_ref[...] = g_pre
    gf[...] += dot_nt(gcol, hidden_two)
    g_wb = dot_nt(g_pre, h1_ref[...])
    for block in range(HID // LANES):
        slab_ref[block * HID : (block + 1) * HID, :] += g_wb[:, block * LANES : (block + 1) * LANES]
    bacc[...] += fold_lanes(g_pre.astype(F32))

    @pl.when(step == pl.num_programs(0) - 1)
    def _():
        bias = ones_sum(bacc)
        put_rows(slab_ref, lambda block: ONE_B + block, bias, 0, 1)
        for piece in range(18):
            put_rows(slab_ref, lambda block: ONE_F + block * 112 + piece * 6, gf, piece * 8, 6)
        for block in range(3):
            width = min(LANES, 288 - block * LANES)
            slab_ref[ONE_P + block * 64 : ONE_P + block * 64 + 64, 0:width] = gwp_ref[
                :, block * LANES : block * LANES + width
            ]
        slab_ref[ONE_LOSS : ONE_LOSS + 1, :] = loss_one_ref[0:1, :] + loss_two_ref[0:1, :]
        slab_ref[ONE_LOSS + 1 : ONE_LOSS + 2, :] = loss_two_ref[1:2, :]
        part_out(slab_ref, 0, PART_A, index_ref[1], bits[0], kept_a, sent_a)
        part_out(slab_ref, PART_A, ONE_ROWS - PART_A, index_ref[1], bits[1], kept_b, sent_b)


def one_backward_bottom(
    dims,
    chunk,
    y1_ref,
    ghalf_ref,
    gbc_ref,
    gout_ref,
    e_ref,
    wbt_ref,
    xcol_ref,
    h1_ref,
    gpre_ref,
    slab_ref,
    gacc,
    gmix,
    ge,
    acc,
):
    rows, cols, bands = dims
    step = pl.program_id(0)
    per_row = cols * LANES // chunk

    @pl.when(step == 0)
    def _():
        gacc[...] = jnp.zeros_like(gacc)
        ge[...] = jnp.zeros_like(ge)
        slab_ref[...] = jnp.zeros_like(slab_ref)

    row = step // per_row
    col = (step % per_row) * (chunk // LANES)
    g_pre = jnp.where(h1_ref[...] > 0, dot(wbt_ref[...], gpre_ref[...]), 0.0).astype(BF16)
    ge[...] += dot_nt(xcol_ref[...], g_pre)
    scatter_cols(gacc, dot(e_ref[...], g_pre), cols, row, col, chunk)

    @pl.when(step == pl.num_programs(0) - 1)
    def _():
        gmix[0:8, :] = gout_ref[0:8, :] + jnp.concatenate(fold_ext(gacc, rows, cols, bands), axis=1)
        gmix[8:16, :] = ghalf_ref[...]
        g_mixed = gmix[...]
        acc[...] = jnp.zeros_like(acc)
        gram(g_mixed, y1_ref, range(CH), acc)
        stack = [(j, acc[j]) for j in range(CH)] + [(16, fold_lanes(g_mixed)), (17, gbc_ref[...])]
        slab_ref[REST_SMALL : REST_SMALL + 16, :] = lane_sums(stack, CH)
        for tap in range(9):
            put_rows(slab_ref, lambda block: block * 56 + tap * 6, ge, tap * 8, 6)
        put_rows(slab_ref, lambda block: REST_A + block, ge, 6, 1)


def call(kernel, inputs, outputs, scratch, flops, grid=None, in_specs=None, out_specs=None):
    whole = pl.BlockSpec(memory_space=pltpu.VMEM)
    smem = pl.BlockSpec(memory_space=pltpu.SMEM)
    if in_specs is None:
        in_specs = [smem if x.dtype == jnp.int32 and x.ndim == 1 else whole for x in inputs]
        out_specs = [whole for _ in outputs]
    spec = {} if grid is None else {"grid": grid}
    traffic = sum(x.size * x.dtype.itemsize for x in list(inputs) + list(outputs))
    return pl.pallas_call(
        kernel,
        out_shape=outputs,
        in_specs=in_specs,
        out_specs=out_specs,
        scratch_shapes=scratch,
        compiler_params=pltpu.CompilerParams(vmem_limit_bytes=VMEM_LIMIT),
        cost_estimate=pl.CostEstimate(flops=flops, bytes_accessed=traffic, transcendentals=0),
        **spec,
    )(*inputs)


def shape(dims, dtype=F32):
    return jax.ShapeDtypeStruct(tuple(dims), dtype)


def high_dot(left, right, contract=(1, 0)):
    return lax.dot_general(
        left, right, (((contract[0],), (contract[1],)), ((), ())), precision=HIGH, preferred_element_type=F32
    )


def iotas(height, width=LANES):
    return (
        lax.broadcasted_iota(jnp.int32, (height, width), 0),
        lax.broadcasted_iota(jnp.int32, (height, width), 1),
    )


def take_flat(flat_ref, start, length):
    row, offset = divmod(start, LANES)
    lane = lax.broadcasted_iota(jnp.int32, (1, LANES), 1)
    value = flat_ref[row : row + 1, :]
    if offset:
        value = pltpu.roll(value, LANES - offset, 1)
        if offset + length > LANES:
            after = pltpu.roll(flat_ref[row + 1 : row + 2, :], LANES - offset, 1)
            value = jnp.where(lane < LANES - offset, value, after)
    return jnp.where(lane < length, value, 0.0) if length < LANES else value


def put_flat(pieces, start, value, length):
    row, offset = divmod(start, LANES)
    lane = lax.broadcasted_iota(jnp.int32, (1, LANES), 1)
    if length < LANES:
        value = jnp.where(lane < length, value, 0.0)
    if offset:
        value = pltpu.roll(value, offset, 1)
    if offset + length > LANES:
        pieces.setdefault(row + 1, []).append(jnp.where(lane < offset, value, 0.0))
        value = jnp.where(lane >= offset, value, 0.0)
    pieces.setdefault(row, []).append(value)


def level_tables(flat_ref, level, lu):
    chans = CH * (level + 1)
    start = ONE_START - 4 * CH if level == 0 else TWO_START
    chan = [take_flat(flat_ref, start + k * chans, chans) for k in range(4)]
    first = start + 4 * chans + 2 * HID
    lu[...] = jnp.zeros_like(lu)
    for i in range(chans):
        lu[i : i + 1, :] = take_flat(flat_ref, first + i * chans, chans)
    row, lane = iotas(LANES)
    value = lu[...]
    inside = row < chans
    lower = jnp.where(row > lane, value, 0.0) + jnp.where((row == lane) & inside, 1.0, 0.0)
    upper = jnp.where(row < lane, value, 0.0) + jnp.where((row == lane) & inside, jnp.exp(chan[2]), 0.0)
    return chans, start, chan, lower, upper


def natural_row(level, row):
    height, half = (8, CH // 2) if level == 0 else (16, CH)
    return (row // height) * half + lax.rem(row, height), lax.rem(row, height) < half


def natural_keep(row):
    return 4 * lax.rem(row, 8) + row // 8, lax.rem(row, 8) < CH // 2


def pick(condition, value):
    return jnp.sum(jnp.where(condition, value, 0.0), axis=1, keepdims=True)


def prior_places():
    row, lane = iotas(64, 4 * CH)
    inner = lax.rem(row, 32)
    natural, valid = natural_keep(inner)
    return ((lane == natural + (row // 32) * 2 * CH) & valid).astype(F32).astype(BF16)


def prior_lanes(tap):
    row, lane = iotas(2 * CH)
    inner = lane - (tap * 32) % LANES
    natural = 4 * lax.rem(inner, 8) + inner // 8
    valid = (inner >= 0) & (inner < 32) & (lax.rem(inner, 8) < CH // 2)
    return ((row == natural) & valid).astype(F32).astype(BF16)


def prepare_level(level, flat_ref, entry_ref, middle_ref, exit_ref, outs, wide):
    e_ref, et_ref, f_ref, ft_ref, wb_ref, wbt_ref, bb_ref = outs
    chans = CH * (level + 1)
    start = 0 if level == 0 else TWO_START
    half, tall = chans // 2, 8 * (level + 1)
    first_in, first_out = (0, 0) if level == 0 else (CH // 2, CH)
    wide[...] = jnp.zeros_like(wide)
    for tap in range(9):
        wide[tap * tall : tap * tall + half, :] = entry_ref[tap, first_in : first_in + half, :]
    row, lane = iotas(LANES)
    for block in range(HID // LANES):
        at = slice(block * LANES, (block + 1) * LANES)
        value = take_flat(flat_ref, start + 4 * chans + block * LANES, LANES)
        for tap in range(3):
            part = value.astype(BF16).astype(F32)
            wide[tap * tall + half : tap * tall + half + 1, at] = part
            value = value - part
        value = take_flat(flat_ref, start + 4 * chans + HID + block * LANES, LANES)
        bb_ref[at, :] = pick(row == lane, value)
    count = 9 * tall
    padded = -(-count // LANES) * LANES
    e_ref[...] = wide[0:count, :].astype(BF16)
    et_ref[...] = wide[0:padded, :].T[:, 0:count].astype(BF16)
    wide[...] = jnp.zeros_like(wide)
    for tap in range(9):
        for side in range(2):
            first = (tap * 2 + side) * tall
            wide[first : first + half, :] = exit_ref[tap, first_out + side * half : first_out + (side + 1) * half, :]
    count = 18 * tall
    padded = -(-count // LANES) * LANES
    f_ref[...] = wide[0:count, :].astype(BF16)
    ft_ref[...] = wide[0:padded, :].T[:, 0:count].astype(BF16)
    wb_ref[...] = middle_ref[level].astype(BF16)
    wbt_ref[...] = middle_ref[level].T.astype(BF16)


def prepare_two_kernel(
    flat_ref, entry_ref, middle_ref, exit_ref, chan1_ref, m1_ref, chan2_ref, m2_ref, m2t_ref, *rest
):
    outs, (lu, wide) = rest[:-2], rest[-2:]
    for level in range(2):
        chans, start, chan, lower, upper = level_tables(flat_ref, level, lu)
        product = high_dot(lower, upper)
        height = 16 * (level + 1)
        row, lane = iotas(height)
        natural, valid = natural_row(level, row)
        spread = ((lane == chans - 1 - natural) & valid).astype(F32)
        matrix = high_dot(spread, product)
        out_bias = pick((lane == natural) & valid, chan[3])
        if level == 0:
            m1_ref[...] = matrix
            shift, scale = pick(lane == row, chan[0]), pick((lane == row) & (row < CH), jnp.exp(chan[1]))
        else:
            source, target = iotas(LANES)
            place, used = natural_keep(target)
            matrix = high_dot(matrix, ((source == place) & used & (target < 32)).astype(F32))
            m2_ref[...] = matrix
            lu[...] = jnp.zeros_like(lu)
            lu[0:32, :] = matrix
            m2t_ref[...] = lu[...].T[0:32, :]
            place, used = natural_keep(row)
            shift = pick((lane == place) & used, chan[0])
            scale = pick((lane == place) & used, jnp.exp(chan[1]))
        chan_ref = chan1_ref if level == 0 else chan2_ref
        chan_ref[...] = (
            jnp.where(lane == 0, shift, 0.0) + jnp.where(lane == 1, scale, 0.0) + jnp.where(lane == 2, out_bias, 0.0)
        )
    prepare_level(1, flat_ref, entry_ref, middle_ref, exit_ref, outs, wide)


def prepare_one_kernel(flat_ref, entry_ref, middle_ref, exit_ref, prior_ref, wp_ref, wpt_ref, pbias_ref, *rest):
    outs, (lu, wide) = rest[:-2], rest[-2:]
    prepare_level(0, flat_ref, entry_ref, middle_ref, exit_ref, outs, wide)
    places = prior_places()
    blocks = [None] * 3
    for tap in range(9):
        moved = dot_nt(places, prior_ref[tap].astype(BF16)).astype(BF16)
        part = dot(moved, prior_lanes(tap))
        block = tap * 32 // LANES
        blocks[block] = part if blocks[block] is None else blocks[block] + part
    lu[...] = jnp.zeros_like(lu)
    for block, value in enumerate(blocks):
        width = min(LANES, 288 - block * LANES)
        at = slice(block * LANES, block * LANES + width)
        wp_ref[:, at] = value[:, 0:width].astype(BF16)
        lu[0:64, :] = value
        wpt_ref[at, :] = lu[...].T[0:width, 0:64].astype(BF16)
    row, lane = iotas(64)
    natural, valid = natural_keep(lax.rem(row, 32))
    pbias_ref[...] = pick((lane == natural + (row // 32) * 2 * CH) & valid, take_flat(flat_ref, PRIOR_START, 4 * CH))


def adamw(weight, grad, first, second):
    first_new = BETA_ONE * first + (1.0 - BETA_ONE) * grad
    second_new = BETA_TWO * second + (1.0 - BETA_TWO) * grad * grad
    first_hat = first_new / (1.0 - BETA_ONE**ADAM_STEP)
    second_hat = second_new / (1.0 - BETA_TWO**ADAM_STEP)
    updated = weight - LEARN_RATE * (first_hat / (jnp.sqrt(second_hat) + ADAM_EPS) + WEIGHT_DECAY * weight)
    return (updated, second_new)


def finish_kernel(
    count_ref,
    two_ref,
    one_ref,
    rest_ref,
    extra_ref,
    flat_ref,
    flat_first,
    flat_second,
    entry_ref,
    entry_first,
    entry_second,
    middle_ref,
    middle_first,
    middle_second,
    exit_ref,
    exit_first,
    exit_second,
    prior_ref,
    prior_first,
    prior_second,
    loss_ref,
    norm_ref,
    flat_new,
    flat_grad,
    flat_moment,
    entry_new,
    entry_grad,
    entry_moment,
    middle_new,
    middle_grad,
    middle_moment,
    exit_new,
    exit_grad,
    exit_moment,
    prior_new,
    prior_grad,
    prior_moment,
    bias_ref,
    two,
    one,
    rest,
    lu,
):
    two[...] = two_ref[WB_ROWS:, :].astype(F32)
    one[...] = one_ref[WB_ROWS:, :].astype(F32)
    rest[...] = rest_ref[...].astype(F32)
    extra = extra_ref[...].astype(F32)
    log_total = jnp.sum(extra[0:3], keepdims=True)
    count_two = jnp.sum(extra[3:6], keepdims=True)
    coef, count = coef_of(count_ref), jnp.sum(count_ref[...], keepdims=True)
    base = WB_ROWS
    squares = []
    pieces = {}
    consts = []
    for level in range(2):
        chans, start, chan, lower, upper = level_tables(flat_ref, level, lu)
        consts.append(jnp.sum(chan[1] + chan[2], keepdims=True))
        weight = coef * count if level == 0 else coef * count_two
        height = 16 * (level + 1)
        small = rest[REST_SMALL : REST_SMALL + 16, :] if level == 0 else two[TWO_SMALL - base : TWO_SMALL - base + 32, :]
        sum_lane = 16 * (level + 1)
        product = high_dot(lower, upper)
        row, lane = iotas(LANES, height)
        natural, valid = natural_row(level, lane)
        turned = high_dot(((row == chans - 1 - natural) & valid).astype(F32), small)
        row, lane = iotas(LANES)
        g_product = jnp.where(lane < sum_lane, turned, 0.0)
        if level == 1:
            place, used = natural_keep(row)
            g_product = high_dot(g_product, ((lane == place) & used & (row < 32)).astype(F32))
        else:
            g_product = jnp.where(lane < chans, g_product, 0.0)
        g_lower = high_dot(g_product, upper, (1, 1))
        g_upper = high_dot(lower.T, g_product)
        g_lu = jnp.where(row > lane, g_lower, 0.0) + jnp.where(row < lane, g_upper, 0.0)
        diagonal = jnp.sum(jnp.where(row == lane, g_upper, 0.0), axis=0, keepdims=True)
        shift = jnp.sum(turned[:, sum_lane : sum_lane + 1] * product, axis=0, keepdims=True)
        scale = jnp.sum(product * g_product, axis=0, keepdims=True)
        row, lane = iotas(height)
        natural, valid = natural_row(level, row)
        out_bias = jnp.where((lane == natural) & valid, small[:, sum_lane + 1 : sum_lane + 2], 0.0)
        put_flat(pieces, start, shift * jnp.exp(chan[1]), chans)
        put_flat(pieces, start + chans, scale + weight, chans)
        put_flat(pieces, start + 2 * chans, diagonal * jnp.exp(chan[2]) + weight, chans)
        put_flat(pieces, start + 3 * chans, jnp.sum(out_bias, axis=0, keepdims=True), chans)
        for i in range(chans):
            put_flat(pieces, start + 4 * chans + 2 * HID + i * chans, g_lu[i : i + 1, :], chans)
        for block in range(HID // LANES):
            if level == 0:
                value_a = rest[REST_A + block : REST_A + block + 1, :]
                value_b = one[ONE_B - base + block : ONE_B - base + block + 1, :]
            else:
                at = TWO_E - base + block * 144 + CH
                value_a = two[at : at + 1, :]
                value_b = two[TWO_B - base + block : TWO_B - base + block + 1, :]
            at = start + 4 * chans + block * LANES
            put_flat(pieces, at, value_a, LANES)
            put_flat(pieces, at + HID, value_b, LANES)
            bias_ref[2 * level : 2 * level + 1, block * LANES : (block + 1) * LANES] = value_a
            bias_ref[2 * level + 1 : 2 * level + 2, block * LANES : (block + 1) * LANES] = value_b
    row, lane = iotas(64)
    natural, valid = natural_keep(lax.rem(row, 32))
    column = one[ONE_P - base : ONE_P - base + 64, CH // 2 : CH // 2 + 1]
    prior_bias = jnp.where((lane == natural + (row // 32) * 2 * CH) & valid, column, 0.0)
    put_flat(pieces, PRIOR_START, jnp.sum(prior_bias, axis=0, keepdims=True), 4 * CH)
    for r in range(FLAT_ROWS):
        parts = pieces.get(r, [jnp.zeros((1, LANES), F32)])
        flat_grad[r : r + 1, :] = functools.reduce(jnp.add, parts)
    for tap in range(9):
        for block in range(HID // LANES):
            at = slice(block * LANES, (block + 1) * LANES)
            first = block * 56 + tap * 6
            entry_grad[tap, 0:6, at] = rest[first : first + 6, :]
            first = TWO_E - base + block * 144 + tap * 16
            entry_grad[tap, 6:18, at] = two[first : first + CH, :]
            first = ONE_F - base + block * 112 + tap * CH
            exit_grad[tap, 0:CH, at] = one[first : first + CH, :]
            first = TWO_F - base + block * 216 + tap * 2 * CH
            exit_grad[tap, CH : 3 * CH, at] = two[first : first + 2 * CH, :]
    places = prior_places()
    for tap in range(9):
        first = ONE_P - base + (tap * 32 // LANES) * 64
        block = one[first : first + 64, :].astype(BF16)
        moved = dot_nt(prior_lanes(tap), block).astype(BF16)
        prior_grad[tap, :, :] = dot(moved, places)
    for ref in (flat_grad, entry_grad, exit_grad, prior_grad):
        value = ref[...]
        squares.append(jnp.sum(value * value, keepdims=True).reshape(1, 1))
    for ref in (one_ref, two_ref):
        total = jnp.zeros((64, LANES), F32)
        for start in range(0, WB_ROWS, 64):
            value = ref[start : start + 64, :].astype(F32)
            total = total + value * value
        squares.append(jnp.sum(total, keepdims=True))
    norm = jnp.sqrt(functools.reduce(jnp.add, squares))
    clip = jnp.minimum(1.0, CLIP_NORM / (norm + 1e-06))
    total = log_total + consts[0] * count + count_two * (consts[1] - 2 * CH * LOG_TWO_PI)
    loss_ref[...] = coef * total + 8.0
    norm_ref[...] = norm
    bias_ref[...] = bias_ref[...] * clip

    def update(at, refs):
        weight, first, second, new, grad, moment = refs
        value = grad[at] * clip
        grad[at] = value
        new[at], moment[at] = adamw(weight[at], value, first[at], second[at])

    update(..., (flat_ref, flat_first, flat_second, flat_new, flat_grad, flat_moment))
    for tap in range(9):
        update(tap, (entry_ref, entry_first, entry_second, entry_new, entry_grad, entry_moment))
        update(tap, (exit_ref, exit_first, exit_second, exit_new, exit_grad, exit_moment))
        update(tap, (prior_ref, prior_first, prior_second, prior_new, prior_grad, prior_moment))
    size = 64
    for level, slab in enumerate((one_ref, two_ref)):

        @pl.loop(0, HID // size)
        def _(j):
            rows = pl.ds(pl.multiple_of(j * size, size), size)
            for block in range(HID // LANES):
                at = (level, rows, slice(block * LANES, (block + 1) * LANES))
                value = slab[pl.ds(pl.multiple_of(block * HID + j * size, size), size), :].astype(F32) * clip
                middle_grad[at] = value
                middle_new[at], middle_moment[at] = adamw(middle_ref[at], value, middle_first[at], middle_second[at])


def total_over(value, axes):
    for axis in axes:
        size = lax.axis_size(axis)
        distance = 1
        while distance < size:
            value = value + lax.ppermute(value, axis, [(i, i ^ distance) for i in range(size)])
            distance *= 2
    return value


def on_device(
    pixels,
    valid_mask,
    vectors,
    vectors_first,
    vectors_second,
    entry_taps,
    entry_first,
    entry_second,
    middle,
    middle_first,
    middle_second,
    exit_taps,
    exit_first,
    exit_second,
    prior_taps,
    prior_first,
    prior_second,
):
    bands = lax.axis_size("rows")
    rows, cols = valid_mask.shape[0], valid_mask.shape[1]
    dims = (rows, cols, bands)
    half_dims = (rows // 2, cols // 2, bands)
    size = rows * cols * LANES
    part = size // 4
    batches = lax.axis_size("batch")
    devices = batches * bands
    bits = [2**k for k in range((devices - 1).bit_length())]
    index = lax.axis_index("batch") * bands + lax.axis_index("rows")
    own = jnp.stack([lax.axis_index("rows"), index]).astype(jnp.int32)

    def trade(value, bit):
        return lax.ppermute(value, ("batch", "rows"), [(i, i ^ bit) for i in range(devices)])

    def after(value, *done):
        return lax.optimization_barrier((value, *done))[0]

    pixel_rows = (CH + 1) * rows * cols // bands
    piece_rows = pixel_rows + 16
    pieces = call(
        functools.partial(pack_kernel, bands),
        (own, pixels.reshape(-1, LANES), valid_mask.reshape(-1, LANES)),
        [shape((piece_rows, LANES), BF16)] * bands,
        [],
        1000,
    )
    bufs = [pieces[0]]
    for d in range(1, bands):
        bufs.append(lax.ppermute(pieces[d], "rows", [(i, i ^ d) for i in range(bands)]))

    def flat(value):
        return jnp.pad(value, (0, FLAT_ROWS * LANES - VEC)).reshape(FLAT_ROWS, LANES)

    vectors_flat = flat(vectors)

    def level_shapes(tall):
        return [
            shape((9 * tall, HID), BF16),
            shape((HID, 9 * tall), BF16),
            shape((18 * tall, HID), BF16),
            shape((HID, 18 * tall), BF16),
            shape((HID, HID), BF16),
            shape((HID, HID), BF16),
            shape((HID, 1)),
        ]

    square, tall_scratch = pltpu.VMEM((LANES, LANES), F32), pltpu.VMEM((384, HID), F32)
    rounds = iter(bits[bands.bit_length() - 1 :])

    def count_round(value, beside):
        bit = next(rounds, None)
        return value if bit is None else value + after(trade(value, bit), beside)

    chan_one, m_one, chan_two, m_two, m_two_t, e_two, e_two_t, f_two, f_two_t, wb_two, wb_two_t, bb_two = call(
        prepare_two_kernel,
        (after(vectors_flat, pieces[0]), entry_taps, middle, exit_taps),
        [shape((16, LANES)), shape((16, LANES)), shape((32, LANES)), shape((32, LANES)), shape((32, LANES))]
        + level_shapes(16),
        [square, tall_scratch],
        10**9,
    )
    bufs = [after(x, m_one) for x in bufs]
    count = sum(x[pixel_rows : pixel_rows + 1].astype(F32) for x in bufs)
    prior_turned = jnp.swapaxes(prior_taps, 1, 2)
    wp, wpt, prior_bias, e_one, e_one_t, f_one, f_one_t, wb_one, wb_one_t, bb_one = call(
        prepare_one_kernel,
        (after(vectors_flat, count), entry_taps, middle, exit_taps, prior_turned),
        [shape((64, 288), BF16), shape((288, 64), BF16), shape((64, 1))] + level_shapes(8),
        [square, tall_scratch],
        10**9,
    )
    count = count_round(count, prior_bias)

    ext_lanes = (rows // 2 + 2) * (cols // 2 + 2) * LANES
    (y1, mixed_one, mask, mask2, keep, y2, mixed_two) = call(
        functools.partial(unpack_kernel, dims),
        (own, *bufs, after(chan_one, count), m_one, chan_two, m_two),
        [
            shape((16, size)),
            shape((16, size)),
            shape((1, size)),
            shape((1, part)),
            shape((32, part)),
            shape((32, part)),
            shape((32, part)),
        ],
        [pltpu.VMEM((bands, piece_rows, LANES), F32), pltpu.VMEM((16, size), F32)],
        10**9,
    )
    count = count_round(count, mask2)
    (out_two, t_two, xcol_two, h1_two, h2_two, loss_two) = call(
        functools.partial(couple_two_forward, half_dims),
        (mixed_two, mask, mask2, after(chan_two, count), e_two_t, wb_two, f_two, bb_two),
        [
            shape((32, part)),
            shape((16, part)),
            shape((144, part), BF16),
            shape((HID, part), BF16),
            shape((HID, part), BF16),
            shape((8, LANES)),
        ],
        [pltpu.VMEM((16, ext_lanes), F32), pltpu.VMEM((32, ext_lanes), F32)],
        2 * HID * part * (144 + HID + 288),
    )
    for _ in bits:
        count = count_round(count, loss_two)
    half_two = shape((TWO_ROWS // 2, LANES))
    (kept_two, sent_two, gkeep_two) = call(
        functools.partial(couple_two_backward, half_dims),
        (own, count, mask2, y2, out_two, t_two, xcol_two, h1_two, h2_two, chan_two, m_two_t, e_two, wb_two_t, f_two_t),
        [half_two, half_two, shape((32, part))],
        [
            pltpu.VMEM((32, ext_lanes), F32),
            pltpu.VMEM((16, ext_lanes), F32),
            pltpu.VMEM((32, part), F32),
            pltpu.VMEM((HID, LANES), F32),
            pltpu.VMEM((144, HID), F32),
            pltpu.VMEM((288, HID), F32),
            pltpu.VMEM((32, 32, LANES), F32),
            pltpu.VMEM((TWO_ROWS, LANES), F32),
        ],
        4 * HID * part * (144 + HID + 288),
    )
    whole_lanes = (rows + 2) * (cols + 2) * LANES
    chunk = 1024
    steps = size // chunk
    smem = pl.BlockSpec(memory_space=pltpu.SMEM)

    def fixed(value):
        rank = len(value.shape)
        return pl.BlockSpec(value.shape, lambda j: (0,) * rank)

    def moving(height):
        return pl.BlockSpec((height, chunk), lambda j: (0, j))

    fwd_in = (
        count,
        mixed_one,
        mask,
        mask2,
        keep,
        gkeep_two,
        chan_one,
        e_one_t,
        wb_one,
        f_one,
        bb_one,
        wp,
        wpt,
        prior_bias,
    )
    fwd_out = [
        shape((72, size), BF16),
        shape((HID, size), BF16),
        shape((HID, size), BF16),
        shape((8, size)),
        shape((8, size)),
        shape((16, size)),
        shape((64, 288)),
        shape((8, LANES)),
    ]
    (xcol_one, h1_one, h2_one, res_one, t_one, gout_one, gwp, loss_one) = call(
        functools.partial(couple_one_forward, dims, chunk),
        fwd_in,
        fwd_out,
        [
            pltpu.VMEM((8, whole_lanes), F32),
            pltpu.VMEM((16, whole_lanes), F32),
            pltpu.VMEM((32, ext_lanes), F32),
            pltpu.VMEM((288, cols // 2 * LANES), BF16),
            pltpu.VMEM((32, ext_lanes), F32),
            pltpu.VMEM((32, part), F32),
        ],
        2 * HID * size * (72 + HID + 144),
        grid=(steps,),
        in_specs=[fixed(x) for x in fwd_in],
        out_specs=[moving(72), moving(HID), moving(HID)] + [fixed(x) for x in fwd_out[3:]],
    )
    first_bit, second_bit, third_bit = bits[0], bits[2], bits[1]
    total_two = kept_two + after(trade(sent_two, first_bit), loss_one)
    top_in = (own, after(count, total_two), mask, res_one, t_one, gout_one, f_one_t, gwp, loss_one, loss_two, h1_one, h2_one)
    half_a, half_b = shape((PART_A // 2, LANES)), shape(((ONE_ROWS - PART_A) // 2, LANES))
    top_out = [half_a, half_a, half_b, half_b] + [shape((8, size)), shape((16, LANES)), shape((HID, size), BF16)]
    (kept_a, sent_a, kept_b, sent_b, ghalf, gbc, gpre) = call(
        functools.partial(one_backward_top, dims, chunk, (second_bit, third_bit)),
        top_in,
        top_out,
        [
            pltpu.VMEM((16, whole_lanes), F32),
            pltpu.VMEM((144, HID), F32),
            pltpu.VMEM((HID, LANES), F32),
            pltpu.VMEM((ONE_ROWS, LANES), F32),
        ],
        2 * HID * size * (144 + HID + 144),
        grid=(steps,),
        in_specs=[smem] + [fixed(x) for x in top_in[1:10]] + [moving(HID), moving(HID)],
        out_specs=[fixed(x) for x in top_out[:6]] + [moving(HID)],
    )

    def halve(parts, bit, *beside):
        high = (index // bit) % 2
        halves = [x.shape[0] // 2 for x in parts]
        sent = [lax.dynamic_slice_in_dim(x, (1 - high) * h, h, 0) for x, h in zip(parts, halves)]
        kept = [lax.dynamic_slice_in_dim(x, high * h, h, 0) for x, h in zip(parts, halves)]
        got = after(trade(jnp.concatenate(sent) if len(sent) > 1 else sent[0], bit), *beside)
        results, first = [], 0
        for x, h in zip(kept, halves):
            results.append(x + got[first : first + h])
            first += h
        return results

    (total_two,) = halve([total_two], second_bit, gbc)
    low_in = (y1, ghalf, after(gbc, total_two), gout_one, e_one, wb_one_t, xcol_one, h1_one, gpre)
    (slab_rest,) = call(
        functools.partial(one_backward_bottom, dims, chunk),
        low_in,
        [shape((REST_ROWS, LANES))],
        [
            pltpu.VMEM((8, whole_lanes), F32),
            pltpu.VMEM((16, size), F32),
            pltpu.VMEM((72, HID), F32),
            pltpu.VMEM((CH, 16, LANES), F32),
        ],
        2 * HID * size * (72 + HID + 72),
        grid=(steps,),
        in_specs=[fixed(x) for x in low_in[:6]] + [moving(72), moving(HID), moving(HID)],
        out_specs=[fixed(shape((REST_ROWS, LANES)))],
    )

    total_a = kept_a + after(trade(sent_a, second_bit), slab_rest)
    total_b = kept_b + after(trade(sent_b, third_bit), slab_rest)
    (total_two,) = halve([total_two], third_bit, slab_rest)
    far = bits[3:]
    total_a, total_b, total_rest = halve([total_a, total_b, slab_rest], first_bit)
    total_a, total_rest = halve([total_a, total_rest], third_bit)
    (total_b,) = halve([total_b], second_bit)
    (total_rest,) = halve([total_rest], second_bit)
    shards = [total_two, total_a, total_b, total_rest]
    for bit in far:
        shards = halve(shards, bit)
    orders = [
        [first_bit, second_bit, third_bit] + far,
        [second_bit, first_bit, third_bit] + far,
        [third_bit, first_bit, second_bit] + far,
        [first_bit, third_bit, second_bit] + far,
    ]
    loss_part = shards[2]
    owner, loss_row = divmod(ONE_LOSS - PART_A, loss_part.shape[0])
    extra = []
    for row in range(2):
        value = loss_part[loss_row + row]
        for _ in range(3):
            high = lax.reduce_precision(value, 8, 7)
            extra.append(high)
            value = value - high
    extra = jnp.pad(jnp.stack(extra), ((0, 10), (0, 0)))
    spread = jnp.concatenate(shards + [extra]).astype(BF16)
    back = bits[::-1]
    for bit in back:
        other = trade(spread, bit)
        spread = jnp.where(
            (index // bit) % 2 == 0, jnp.concatenate([spread, other]), jnp.concatenate([other, spread])
        )
    spread = spread.reshape((2,) * len(bits) + (-1, LANES))
    totals = []
    first = 0
    for shard, order in zip(shards, orders):
        part_rows = spread[..., first : first + shard.shape[0], :]
        first += shard.shape[0]
        axes = [len(bits) - 1 - back.index(bit) for bit in order]
        totals.append(part_rows.transpose(axes + [len(bits), len(bits) + 1]).reshape(-1, LANES))
    place = [0] * len(bits)
    for k, bit in enumerate(orders[2]):
        place[len(bits) - 1 - back.index(bit)] = (owner >> (len(bits) - 1 - k)) & 1
    extra = spread[tuple(place)][first:]
    totals = [totals[0], jnp.concatenate(totals[1:3]), totals[3]]
    taps = [
        (entry_taps, entry_first, entry_second),
        (middle, middle_first, middle_second),
        (exit_taps, exit_first, exit_second),
        (prior_turned, jnp.swapaxes(prior_first, 1, 2), jnp.swapaxes(prior_second, 1, 2)),
    ]
    flats = (vectors_flat, flat(vectors_first), flat(vectors_second))
    outs = [shape((1, 1)), shape((1, 1))] + [shape((FLAT_ROWS, LANES))] * 3
    for group in taps:
        outs += [shape(group[0].shape)] * 3
    outs.append(shape((4, HID)))
    results = call(
        finish_kernel,
        (count, *totals, extra, *flats, *[x for group in taps for x in group]),
        outs,
        [
            pltpu.VMEM((TWO_ROWS - WB_ROWS, LANES), F32),
            pltpu.VMEM((ONE_ROWS - WB_ROWS, LANES), F32),
            pltpu.VMEM((REST_ROWS, LANES), F32),
            pltpu.VMEM((LANES, LANES), F32),
        ],
        10**8,
    )
    results = list(results)
    for k in range(2):
        results[k] = results[k].reshape(())
    for k in range(2, 5):
        results[k] = results[k].reshape(-1)[:VEC]
    for k in range(14, 17):
        results[k] = jnp.swapaxes(results[k], 1, 2)
    return tuple(results)


def solution(mesh):
    replicated = (P(),) * 15
    return jax.shard_map(
        on_device,
        mesh=mesh,
        in_specs=(P(None, "rows", None, "batch"), P("rows", None, "batch")) + replicated,
        out_specs=(P(),) * 18,
        check_vma=False,
    )
```

time: 376 us -> 165 us (0.44)
  waiting for transfers between devices: 137 us -> 52.7 us
  blocking collectives: 43.8 us -> 0 us
  other arithmetic: 35.5 us -> 2.9 us
  between operations: 30.5 us -> 1.87 us
  local copies, waits for them, and re-layouts: 47.8 us -> 20.9 us
  starting transfers between devices: 15.5 us -> 19.5 us
    psum x1 -> x0, waiting for transfers between devices: 135 us -> none  [on_device(): pieces_small, big = lax.psum((pieces_small, big), ('batch', 'rows'))]
    ppermute x5 -> x19, waiting for transfers between devices: 2.08 us -> 52.7 us  [trade(): lax.ppermute(value, ('batch', 'rows'), [(i, i ^ bit) for i in range(devic...]
    psum x1 -> x0, blocking collectives: 43.8 us -> none  [on_device(): pieces_small, big = lax.psum((pieces_small, big), ('batch', 'rows'))]
    reduce_sum x19 -> x0, other arithmetic: 15.7 us -> none  [the longest x5 3.88 us: on_device(): grad_norm = jnp.sqrt(sum((jnp.sum(grad * grad) for grad in grads)))]
    unnamed x104 -> x101, local copies, waits for them, and re-layouts: 7.16 us -> 19.6 us
    sub x5 -> x0, other arithmetic: 10.9 us -> none  [adamw(): weight - LEARN_RATE * (first_hat / (jnp.sqrt(second_hat) + ADAM_EPS) + WE...]
    reshape x36 -> x2, local copies, waits for them, and re-layouts: 9.93 us -> 0.72 us  [flat(): jnp.pad(value, (0, FLAT_ROWS * LANES - VEC)).reshape(FLAT_ROWS, LANES)]
    slice x14 -> x2, local copies, waits for them, and re-layouts: 7.72 us -> 0.02 us  [the longest x1 0.01 us: on_device(): part_rows = spread[..., first:first + shard.shape[0], :]]
  transfers between devices with their start and end apart: 9 -> 22, of which waited for: 5 -> 12; matrix products, arithmetic and copies ran while one was open for 11% -> 1% of each run, Pallas kernels for 1% -> 29%
where the time goes in v2:
time: 165 us; the launch traced here: 164 us
  Pallas kernels  66.1 us (40%)
  waiting for transfers between devices  52.7 us (32%)
  local copies, waits for them, and re-layouts  20.9 us (13%)
  starting transfers between devices  19.5 us (12%)
  other arithmetic  2.9 us (2%)
  between operations  1.87 us (1%)
    pallas_call x10, Pallas kernels, call(): pl.pallas_call(kernel, out_shape=outputs, in_specs=in_specs, out_specs=ou...  66.1 us
    ppermute x19, waiting for transfers between devices, trade(): lax.ppermute(value, ('batch', 'rows'), [(i, i ^ bit) for i in range(devic...  52.7 us
    unnamed x101, local copies, waits for them, and re-layouts  19.6 us
    ppermute x19, starting transfers between devices, trade(): lax.ppermute(value, ('batch', 'rows'), [(i, i ^ bit) for i in range(devic...  16.4 us
  transfers between devices with their start and end apart: 22, of which 12 were waited for; matrix products, arithmetic and copies ran while one was open for 1% of the time, Pallas kernels for 29%

profile of v2, /device:TPU:0, one launch (start us, length us, event | category | flops | bytes accessed | tf_op | source)
XLA Modules:
  0.0 164.1 jit_solution(11926884348787427817)
XLA Ops:
  0.7 1.0 copy-done.12
  1.7 0.8 copy-done.16
  2.5 0.8 shard_map.304
  3.3 2.5 %collective-permute-start.2 = (bf16[224,128]{1,0:T(8,128)(2,1)S(1)}, bf16[224,128]{1,0:T(8,128)(2,1)S(1)}, u32[]{:S(2)}, u32[]{:S(2)}) collective-permute-start(bf16[224,128]{1,0:T(8,128)(2,1)S(1)} %get-tuple-element.119), channel_id=1, source_target_pairs={{0,3},{1,2},{2,1},{3,0},{4,7},{5,6},{6,5},{7,4},{8,11},{9,10},{10,... | collective-permute-start | bytes 172040 | tf_op jit(solution)/shard_map/ppermute | solution.py:1096
  6.5 0.7 pad_bitcast_fusion.2.flat_ref
  7.2 1.6 copy-done
  8.8 1.1 copy-done.4
  9.9 1.0 copy-done.8
  10.9 1.1 shard_map.305
  12.0 1.8 %collective-permute-start.3 = (f32[1,128]{1,0:T(1,128)S(1)}, f32[1,128]{1,0:T(1,128)S(1)}, u32[]{:S(2)}, u32[]{:S(2)}) collective-permute-start(f32[1,128]{1,0:T(1,128)S(1)} %convert_add_fusion), channel_id=1, source_target_pairs={{0,4},{1,5},{2,6},{3,7},{4,0},{5,1},{6,2},{7,3},{8,12},{9,13},{10,... | collective-permute-start | bytes 1544 | tf_op jit(solution)/shard_map/ppermute | solution.py:1080
  13.8 0.8 shard_map.306
  14.7 0.9 collective-permute-done.3
  15.7 1.8 %collective-permute-start.4 = (f32[1,128]{1,0:T(1,128)S(1)}, f32[1,128]{1,0:T(1,128)S(1)}, u32[]{:S(2)}, u32[]{:S(2)}) collective-permute-start(f32[1,128]{1,0:T(1,128)S(1)} %add.224), channel_id=1, source_target_pairs={{0,8},{1,9},{2,10},{3,11},{4,12},{5,13},{6,14},{7,15},{8,0},{9,1},... | collective-permute-start | bytes 1544 | tf_op jit(solution)/shard_map/ppermute | solution.py:1080
  17.5 2.5 %shard_map.307 = (f32[16,8192]{1,0:T(8,128)S(1)}, f32[16,8192]{1,0:T(8,128)S(1)}, f32[1,8192]{1,0:T(1,128)S(1)}, f32[1,2048]{1,0:T(1,128)S(1)}, f32[32,2048]{1,0...) custom-call(s32[2]{0:T(128)S(1)} %pad_add_fusion.index_ref, bf16[224,128]{1,0:T(8,128)(2,1)S(1)} %get-tuple-element.114.b0, ...), custom_call_target="tpu_custom_call" | custom-call | flops 1000000000 | bytes 2154504 | tf_op jit(solution)/shard_map/pallas_call | solution.py:673
  20.8 2.7 %collective-permute-start.5 = (f32[1,128]{1,0:T(1,128)S(1)}, f32[1,128]{1,0:T(1,128)S(1)}, u32[]{:S(2)}, u32[]{:S(2)}) collective-permute-start(f32[1,128]{1,0:T(1,128)S(1)} %add.225), channel_id=1, source_target_pairs={{0,16},{1,17},{2,18},{3,19},{4,20},{5,21},{6,22},{7,23},{8,24},{9,... | collective-permute-start | bytes 1544 | tf_op jit(solution)/shard_map/ppermute | solution.py:1080
  23.4 2.7 %shard_map.308 = (f32[32,2048]{1,0:T(8,128)S(1)}, f32[16,2048]{1,0:T(8,128)S(1)}, bf16[144,2048]{1,0:T(8,128)(2,1)S(1)}, bf16[512,2048]{1,0:T(8,128)(2,1)S(1)}, ...) custom-call(f32[32,2048]{1,0:T(8,128)S(1)} %get-tuple-element.130.mix2_ref, ...), custom_call_target="tpu_custom_call" | custom-call | flops 1979711488 | bytes 6469632 | tf_op jit(solution)/shard_map/pallas_call | solution.py:673
  26.7 8.0 %shard_map.309 = (f32[1792,128]{1,0:T(8,128)S(1)}, f32[1792,128]{1,0:T(8,128)S(1)}, f32[32,2048]{1,0:T(8,128)S(1)}) custom-call(s32[2]{0:T(128)S(1)} %pad_add_fusion.index_ref, f32[1,128]{1,0:T(1,128)S(1)} %add.226.count_ref, f32[1,2048]{1,0:T(1,128)S(1)} %get-tuple-element.128.mask2_ref, f32[32,2048]{1,0:T(8,128)S(1)} %get-tuple-element.139.y2_ref, ...), custom_call_target="tpu_custom_call" | custom-call | flops 3959422976 | bytes 8544776 | tf_op jit(solution)/shard_map/pallas_call | solution.py:673
  35.4 0.9 copy-done.20
  36.4 0.9 copy-done.22
  37.3 0.9 copy-done.24
  38.2 0.9 copy-done.28
  39.1 0.8 copy-done.30
  39.9 0.8 copy-done.32
  40.6 1.0 copy-done.34
  41.7 0.9 copy-done.36
  42.6 0.9 copy-done.38
  43.6 0.8 copy-done.40
  44.3 12.5 %shard_map.310 = (bf16[72,8192]{1,0:T(8,128)(2,1)S(1)}, bf16[512,8192]{1,0:T(8,128)(2,1)S(1)}, bf16[512,8192]{1,0:T(8,128)(2,1)S(1)}, f32[8,8192]{1,0:T(8,128)S(...) custom-call(f32[1,128]{1,0:T(1,128)S(1)} %add.226.count_ref, ...), custom_call_target="tpu_custom_call" | custom-call | flops 6106906624 | bytes 21003008 | tf_op jit(solution)/shard_map/pallas_call | solution.py:673
  56.8 1.3 add.232
  58.2 1.6 collective-permute-start.7
  59.8 15.6 %shard_map.311 = (f32[768,128]{1,0:T(8,128)S(1)}, f32[768,128]{1,0:T(8,128)S(1)}, f32[640,128]{1,0:T(8,128)S(1)}, f32[640,128]{1,0:T(8,128)S(1)}, f32[8,8192]{1,...) custom-call(s32[2]{0:T(128)S(1)} %pad_add_fusion.index_ref, f32[1,128]{1,0:T(1,128)S(1)} %add.226.count_ref, ...), custom_call_target="tpu_custom_call" | custom-call | flops 6710886400 | bytes 28189192 | tf_op jit(solution)/shard_map/pallas_call | solution.py:673
  75.4 1.6 collective-permute-start.10
  77.6 12.8 %shard_map.312 = f32[256,128]{1,0:T(8,128)S(1)} custom-call(f32[16,8192]{1,0:T(8,128)S(1)} %get-tuple-element.172.y1_ref, f32[8,8192]{1,0:T(8,128)S(1)} %get-tuple-element.173.ghalf_ref, f32[16,128]{1,0:T(8,128)S(1)} %get-tuple-element.174.gbc_ref, f32[16,8192]{1,0:T(8,128)S(1)} %get-tuple-element.165.gout_ref, bf16[72,512]{1,0:T(8,128)(2,1)S(1)} %copy-done.26, ...), custom_call_target="tpu_custom_call" | custom-call | flops 5502926848 | bytes 20004864 | tf_op jit(solution)/shard_map/pallas_call | solution.py:673
  91.5 6.2 %collective-permute-done.8 = f32[448,128]{1,0:T(8,128)S(1)} collective-permute-done((f32[448,128]{1,0:T(8,128)S(1)}, f32[448,128]{1,0:T(8,128)S(1)}, u32[]{:S(2)}, u32[]{:S(2)}) %collective-permute-start.8) | collective-permute-done | bytes 229408 | tf_op jit(solution)/shard_map/ppermute | solution.py:1080
  97.9 1.6 collective-permute-start.13
  100.0 2.3 %collective-permute-done.13 = f32[160,128]{1,0:T(8,128)S(1)} collective-permute-done((f32[160,128]{1,0:T(8,128)S(1)}, f32[160,128]{1,0:T(8,128)S(1)}, u32[]{:S(2)}, u32[]{:S(2)}) %collective-permute-start.13) | collective-permute-done | bytes 81952 | tf_op jit(solution)/shard_map/ppermute | solution.py:1080
  102.4 2.1 %collective-permute-done.12 = f32[256,128]{1,0:T(8,128)S(1)} collective-permute-done((f32[256,128]{1,0:T(8,128)S(1)}, f32[256,128]{1,0:T(8,128)S(1)}, u32[]{:S(2)}, u32[]{:S(2)}) %collective-permute-start.12) | collective-permute-done | bytes 131104 | tf_op jit(solution)/shard_map/ppermute | solution.py:1080
  105.1 3.2 %collective-permute-done.14 = f32[32,128]{1,0:T(8,128)S(1)} collective-permute-done((f32[32,128]{1,0:T(8,128)S(1)}, f32[32,128]{1,0:T(8,128)S(1)}, u32[]{:S(2)}, u32[]{:S(2)}) %collective-permute-start.14) | collective-permute-done | bytes 16416 | tf_op jit(solution)/shard_map/ppermute | solution.py:1080
  108.8 6.3 %collective-permute-done.15 = f32[416,128]{1,0:T(8,128)S(1)} collective-permute-done((f32[416,128]{1,0:T(8,128)S(1)}, f32[416,128]{1,0:T(8,128)S(1)}, u32[]{:S(2)}, u32[]{:S(2)}) %collective-permute-start.15) | collective-permute-done | bytes 213024 | tf_op jit(solution)/shard_map/ppermute | solution.py:1080
  115.3 1.4 collective-permute-start.16
  116.8 5.7 %collective-permute-done.16 = f32[208,128]{1,0:T(8,128)S(1)} collective-permute-done((f32[208,128]{1,0:T(8,128)S(1)}, f32[208,128]{1,0:T(8,128)S(1)}, u32[]{:S(2)}, u32[]{:S(2)}) %collective-permute-start.16) | collective-permute-done | bytes 106528 | tf_op jit(solution)/shard_map/ppermute | solution.py:1080
  122.8 5.1 %collective-permute-done.17 = bf16[224,128]{1,0:T(8,128)(2,1)S(1)} collective-permute-done((bf16[224,128]{1,0:T(8,128)(2,1)S(1)}, bf16[224,128]{1,0:T(8,128)(2,1)S(1)}, u32[]{:S(2)}, u32[]{:S(2)}) %collective-permute-start.17) | collective-permute-done | bytes 57376 | tf_op jit(solution)/shard_map/ppermute | solution.py:1080
  128.1 4.8 %collective-permute-done.18 = bf16[448,128]{1,0:T(8,128)(2,1)S(1)} collective-permute-done((bf16[448,128]{1,0:T(8,128)(2,1)S(1)}, bf16[448,128]{1,0:T(8,128)(2,1)S(1)}, u32[]{:S(2)}, u32[]{:S(2)}) %collective-permute-start.18) | collective-permute-done | bytes 114720 | tf_op jit(solution)/shard_map/ppermute | solution.py:1080
  133.3 5.7 %collective-permute-done.19 = bf16[896,128]{1,0:T(8,128)(2,1)S(1)} collective-permute-done((bf16[896,128]{1,0:T(8,128)(2,1)S(1)}, bf16[896,128]{1,0:T(8,128)(2,1)S(1)}, u32[]{:S(2)}, u32[]{:S(2)}) %collective-permute-start.19) | collective-permute-done | bytes 229408 | tf_op jit(solution)/shard_map/ppermute | solution.py:1080
  139.7 8.0 %collective-permute-done.20 = bf16[1792,128]{1,0:T(8,128)(2,1)S(1)} collective-permute-done((bf16[1792,128]{1,0:T(8,128)(2,1)S(1)}, bf16[1792,128]{1,0:T(8,128)(2,1)S(1)}, u32[]{:S(2)}, u32[]{:S(2)}) %collective-permute-start.20) | collective-permute-done | bytes 458784 | tf_op jit(solution)/shard_map/ppermute | solution.py:1080
  148.0 2.4 %collective-permute-done.21 = bf16[3584,128]{1,0:T(8,128)(2,1)S(1)} collective-permute-done((bf16[3584,128]{1,0:T(8,128)(2,1)S(1)}, bf16[3584,128]{1,0:T(8,128)(2,1)S(1)}, u32[]{:S(2)}, u32[]{:S(2)}) %collective-permute-start.21) | collective-permute-done | bytes 917536 | tf_op jit(solution)/shard_map/ppermute | solution.py:1080
  151.9 0.9 copy-done.3
  154.5 9.4 %shard_map.313 = (f32[1,1]{1,0:T(1,128)}, f32[1,1]{1,0:T(1,128)}, f32[24,128]{1,0:T(8,128)}, f32[24,128]{1,0:T(8,128)}, f32[24,128]{1,0:T(8,128)}, /*index=5*/f3...) custom-call(f32[1,128]{1,0:T(1,128)S(1)} %add.226.count_ref, ...), custom_call_target="tpu_custom_call" | custom-call | flops 100000000 | bytes 20594184 | tf_op jit(solution)/shard_map/pallas_call | solution.py:673
  (175 shorter events, 11.3 us)
Async XLA Ops:
  3.3 8.7 %collective-permute-start.2 = (bf16[224,128]{1,0:T(8,128)(2,1)S(1)}, bf16[224,128]{1,0:T(8,128)(2,1)S(1)}, u32[]{:S(2)}, u32[]{:S(2)}) collective-permute-start(bf16[224,128]{1,0:T(8,128)(2,1)S(1)} %get-tuple-element.119), channel_id=1, source_target_pairs={{0,3},{1,2},{2,1},{3,0},{4,7},{5,6},{6,5},{7,4},{8,11},{9,10},{10,... | collective-permute-start | bytes 172040 | tf_op jit(solution)/shard_map/ppermute | solution.py:1096
  5.8 6.2 %collective-permute-start.1 = (bf16[224,128]{1,0:T(8,128)(2,1)S(1)}, bf16[224,128]{1,0:T(8,128)(2,1)S(1)}, u32[]{:S(2)}, u32[]{:S(2)}) collective-permute-start(bf16[224,128]{1,0:T(8,128)(2,1)S(1)} %get-tuple-element.117), channel_id=1, source_target_pairs={{0,2},{1,3},{2,0},{3,1},{4,6},{5,7},{6,4},{7,5},{8,10},{9,11},{10,... | collective-permute-start | bytes 172040 | tf_op jit(solution)/shard_map/ppermute | solution.py:1096
  6.4 5.6 %collective-permute-start = (bf16[224,128]{1,0:T(8,128)(2,1)S(1)}, bf16[224,128]{1,0:T(8,128)(2,1)S(1)}, u32[]{:S(2)}, u32[]{:S(2)}) collective-permute-start(bf16[224,128]{1,0:T(8,128)(2,1)S(1)} %get-tuple-element.115), channel_id=1, source_target_pairs={{0,1},{1,0},{2,3},{3,2},{4,5},{5,4},{6,7},{7,6},{8,9},{9,8},{10,11... | collective-permute-start | bytes 172040 | tf_op jit(solution)/shard_map/ppermute | solution.py:1096
  7.2 1.6 copy-start
  10.9 2.9 %copy-start.13 = (f32[9,48,24]{1,2,0:T(8,128)S(1)}, f32[9,48,24]{1,2,0:T(8,128)}, u32[]{:S(2)}) copy-start(f32[9,48,24]{1,2,0:T(8,128)} %param.31) | copy-start | bytes 124420
  12.0 3.6 %collective-permute-start.3 = (f32[1,128]{1,0:T(1,128)S(1)}, f32[1,128]{1,0:T(1,128)S(1)}, u32[]{:S(2)}, u32[]{:S(2)}) collective-permute-start(f32[1,128]{1,0:T(1,128)S(1)} %convert_add_fusion), channel_id=1, source_target_pairs={{0,4},{1,5},{2,6},{3,7},{4,0},{5,1},{6,2},{7,3},{8,12},{9,13},{10,... | collective-permute-start | bytes 1544 | tf_op jit(solution)/shard_map/ppermute | solution.py:1080
  14.6 5.3 %copy-start.17 = (bf16[512,144]{1,0:T(8,128)(2,1)}, bf16[512,144]{1,0:T(8,128)(2,1)S(1)}, u32[]{:S(2)}) copy-start(bf16[512,144]{1,0:T(8,128)(2,1)S(1)} %get-tuple-element.166.ft_ref) | copy-start | bytes 442372
  14.6 5.3 %copy-start.19 = (f32[512,1]{1,0:T(8,128)}, f32[512,1]{1,0:T(8,128)S(1)}, u32[]{:S(2)}) copy-start(f32[512,1]{1,0:T(8,128)S(1)} %get-tuple-element.157.bias_ref) | copy-start | bytes 6148
  14.7 5.3 %copy-start.21 = (bf16[144,512]{1,0:T(8,128)(2,1)}, bf16[144,512]{1,0:T(8,128)(2,1)S(1)}, u32[]{:S(2)}) copy-start(bf16[144,512]{1,0:T(8,128)(2,1)S(1)} %get-tuple-element.156.f_ref) | copy-start | bytes 442372
  14.7 5.3 %copy-start.23 = (bf16[512,72]{1,0:T(8,128)(2,1)}, bf16[512,72]{1,0:T(8,128)(2,1)S(1)}, u32[]{:S(2)}) copy-start(bf16[512,72]{1,0:T(8,128)(2,1)S(1)} %get-tuple-element.154.et_ref) | copy-start | bytes 221188
  14.7 5.3 %copy-start.25 = (bf16[72,512]{1,0:T(8,128)(2,1)}, bf16[72,512]{1,0:T(8,128)(2,1)S(1)}, u32[]{:S(2)}) copy-start(bf16[72,512]{1,0:T(8,128)(2,1)S(1)} %get-tuple-element.175.e_ref) | copy-start | bytes 221188
  14.7 5.3 %copy-start.27 = (bf16[288,64]{1,0:T(8,128)(2,1)}, bf16[288,64]{1,0:T(8,128)(2,1)S(1)}, u32[]{:S(2)}) copy-start(bf16[288,64]{1,0:T(8,128)(2,1)S(1)} %get-tuple-element.159.wpt_ref) | copy-start | bytes 110596
  14.7 5.3 %copy-start.29 = (bf16[64,288]{1,0:T(8,128)(2,1)}, bf16[64,288]{1,0:T(8,128)(2,1)S(1)}, u32[]{:S(2)}) copy-start(bf16[64,288]{1,0:T(8,128)(2,1)S(1)} %get-tuple-element.158.wp_ref) | copy-start | bytes 110596
  14.7 5.3 %copy-start.31 = (f32[64,1]{1,0:T(8,128)}, f32[64,1]{1,0:T(8,128)S(1)}, u32[]{:S(2)}) copy-start(f32[64,1]{1,0:T(8,128)S(1)} %get-tuple-element.122.pbias_ref) | copy-start | bytes 772
  15.7 5.1 %collective-permute-start.4 = (f32[1,128]{1,0:T(1,128)S(1)}, f32[1,128]{1,0:T(1,128)S(1)}, u32[]{:S(2)}, u32[]{:S(2)}) collective-permute-start(f32[1,128]{1,0:T(1,128)S(1)} %add.224), channel_id=1, source_target_pairs={{0,8},{1,9},{2,10},{3,11},{4,12},{5,13},{6,14},{7,15},{8,0},{9,1},... | collective-permute-start | bytes 1544 | tf_op jit(solution)/shard_map/ppermute | solution.py:1080
  20.7 5.3 %copy-start.33 = (f32[16,8192]{1,0:T(8,128)}, f32[16,8192]{1,0:T(8,128)S(1)}, u32[]{:S(2)}) copy-start(f32[16,8192]{1,0:T(8,128)S(1)} %get-tuple-element.151.mix1_ref) | copy-start | bytes 1572868
  20.7 5.3 %copy-start.39 = (f32[1,8192]{1,0:T(1,128)}, f32[1,8192]{1,0:T(1,128)S(1)}, u32[]{:S(2)}) copy-start(f32[1,8192]{1,0:T(1,128)S(1)} %get-tuple-element.131.mask_ref) | copy-start | bytes 98308
  20.8 5.9 %collective-permute-start.5 = (f32[1,128]{1,0:T(1,128)S(1)}, f32[1,128]{1,0:T(1,128)S(1)}, u32[]{:S(2)}, u32[]{:S(2)}) collective-permute-start(f32[1,128]{1,0:T(1,128)S(1)} %add.225), channel_id=1, source_target_pairs={{0,16},{1,17},{2,18},{3,19},{4,20},{5,21},{6,22},{7,23},{8,24},{9,... | collective-permute-start | bytes 1544 | tf_op jit(solution)/shard_map/ppermute | solution.py:1080
  35.4 21.4 %collective-permute-start.6 = (f32[1792,128]{1,0:T(8,128)S(1)}, f32[1792,128]{1,0:T(8,128)}, u32[]{:S(2)}, u32[]{:S(2)}) collective-permute-start(f32[1792,128]{1,0:T(8,128)S(1)} %get-tuple-element.150), channel_id=1, source_target_pairs={{0,1},{1,0},{2,3},{3,2},{4,5},{5,4},{6,7},{7,6},{8,9},{9,8},{10,11... | collective-permute-start | bytes 2752520 | tf_op jit(solution)/shard_map/ppermute | solution.py:1080
  56.8 3.0 %copy-start.18 = (bf16[512,144]{1,0:T(8,128)(2,1)S(1)}, bf16[512,144]{1,0:T(8,128)(2,1)}, u32[]{:S(2)}) copy-start(bf16[512,144]{1,0:T(8,128)(2,1)} %copy-done.17) | copy-start | bytes 442372
  56.8 2.9 %copy-start.42 = (f32[8,128]{1,0:T(8,128)S(1)}, f32[8,128]{1,0:T(8,128)}, u32[]{:S(2)}) copy-start(f32[8,128]{1,0:T(8,128)} %copy-done.41) | copy-start | bytes 12292
  58.2 19.3 %collective-permute-start.7 = (f32[896,128]{1,0:T(8,128)S(1)}, f32[896,128]{1,0:T(8,128)S(1)}, u32[]{:S(2)}, u32[]{:S(2)}) collective-permute-start(f32[896,128]{1,0:T(8,128)S(1)} %constant_dynamic-slice_fusion.18), channel_id=1, source_target_pairs={{0,4},{1,5},{2,6},{3,7},{4,0},{5,1},{6,2},{7,3},{8,12},{9,13},{10,... | collective-permute-start | bytes 1376264 | tf_op jit(solution)/shard_map/ppermute | solution.py:1080
  59.8 17.8 %copy-start.26 = (bf16[72,512]{1,0:T(8,128)(2,1)S(1)}, bf16[72,512]{1,0:T(8,128)(2,1)}, u32[]{:S(2)}) copy-start(bf16[72,512]{1,0:T(8,128)(2,1)} %copy-done.25) | copy-start | bytes 221188
  75.4 15.0 %collective-permute-start.10 = (f32[640,128]{1,0:T(8,128)S(1)}, f32[640,128]{1,0:T(8,128)S(1)}, u32[]{:S(2)}, u32[]{:S(2)}) collective-permute-start(f32[640,128]{1,0:T(8,128)S(1)} %get-tuple-element.184), channel_id=1, source_target_pairs={{0,2},{1,3},{2,0},{3,1},{4,6},{5,7},{6,4},{7,5},{8,10},{9,11},{10,... | collective-permute-start | bytes 983048 | tf_op jit(solution)/shard_map/ppermute | solution.py:1080
  77.0 13.4 %collective-permute-start.9 = (f32[768,128]{1,0:T(8,128)S(1)}, f32[768,128]{1,0:T(8,128)S(1)}, u32[]{:S(2)}, u32[]{:S(2)}) collective-permute-start(f32[768,128]{1,0:T(8,128)S(1)} %get-tuple-element.181), channel_id=1, source_target_pairs={{0,4},{1,5},{2,6},{3,7},{4,0},{5,1},{6,2},{7,3},{8,12},{9,13},{10,... | collective-permute-start | bytes 1179656 | tf_op jit(solution)/shard_map/ppermute | solution.py:1080
  77.6 12.8 %copy-start.43 = (f32[896,128]{1,0:T(8,128)}, f32[896,128]{1,0:T(8,128)S(1)}, u32[]{:S(2)}) copy-start(f32[896,128]{1,0:T(8,128)S(1)} %dynamic-slice_add_fusion) | copy-start | bytes 1376260
  90.4 7.2 %collective-permute-start.8 = (f32[448,128]{1,0:T(8,128)S(1)}, f32[448,128]{1,0:T(8,128)S(1)}, u32[]{:S(2)}, u32[]{:S(2)}) collective-permute-start(f32[448,128]{1,0:T(8,128)S(1)} %constant_dynamic-slice_fusion.17), channel_id=1, source_target_pairs={{0,2},{1,3},{2,0},{3,1},{4,6},{5,7},{6,4},{7,5},{8,10},{9,11},{10,... | collective-permute-start | bytes 688136 | tf_op jit(solution)/shard_map/ppermute | solution.py:1080
  91.0 6.7 %copy-start.44 = (f32[896,128]{1,0:T(8,128)S(1)}, f32[896,128]{1,0:T(8,128)}, u32[]{:S(2)}) copy-start(f32[896,128]{1,0:T(8,128)} %copy-done.43) | copy-start | bytes 1376260
  91.2 6.5 %collective-permute-start.11 = (f32[832,128]{1,0:T(8,128)S(1)}, f32[832,128]{1,0:T(8,128)S(1)}, u32[]{:S(2)}, u32[]{:S(2)}) collective-permute-start(f32[832,128]{1,0:T(8,128)S(1)} %pad_maximum_fusion.1), channel_id=1, source_target_pairs={{0,1},{1,0},{2,3},{3,2},{4,5},{5,4},{6,7},{7,6},{8,9},{9,8},{10,11... | collective-permute-start | bytes 1277960 | tf_op jit(solution)/shard_map/ppermute | solution.py:1080
  97.9 4.5 %collective-permute-start.13 = (f32[160,128]{1,0:T(8,128)S(1)}, f32[160,128]{1,0:T(8,128)S(1)}, u32[]{:S(2)}, u32[]{:S(2)}) collective-permute-start(f32[160,128]{1,0:T(8,128)S(1)} %constant_dynamic-slice_fusion.9), channel_id=1, source_target_pairs={{0,4},{1,5},{2,6},{3,7},{4,0},{5,1},{6,2},{7,3},{8,12},{9,13},{10,... | collective-permute-start | bytes 245768 | tf_op jit(solution)/shard_map/ppermute | solution.py:1080
  99.4 5.0 %collective-permute-start.12 = (f32[256,128]{1,0:T(8,128)S(1)}, f32[256,128]{1,0:T(8,128)S(1)}, u32[]{:S(2)}, u32[]{:S(2)}) collective-permute-start(f32[256,128]{1,0:T(8,128)S(1)} %pad_maximum_fusion.3), channel_id=1, source_target_pairs={{0,2},{1,3},{2,0},{3,1},{4,6},{5,7},{6,4},{7,5},{8,10},{9,11},{10,... | collective-permute-start | bytes 393224 | tf_op jit(solution)/shard_map/ppermute | solution.py:1080
  104.5 3.8 %collective-permute-start.14 = (f32[32,128]{1,0:T(8,128)S(1)}, f32[32,128]{1,0:T(8,128)S(1)}, u32[]{:S(2)}, u32[]{:S(2)}) collective-permute-start(f32[32,128]{1,0:T(8,128)S(1)} %constant_dynamic-slice_fusion.7), channel_id=1, source_target_pairs={{0,4},{1,5},{2,6},{3,7},{4,0},{5,1},{6,2},{7,3},{8,12},{9,13},{10,... | collective-permute-start | bytes 49160 | tf_op jit(solution)/shard_map/ppermute | solution.py:1080
  108.3 6.8 %collective-permute-start.15 = (f32[416,128]{1,0:T(8,128)S(1)}, f32[416,128]{1,0:T(8,128)S(1)}, u32[]{:S(2)}, u32[]{:S(2)}) collective-permute-start(f32[416,128]{1,0:T(8,128)S(1)} %pad_maximum_fusion.2), channel_id=1, source_target_pairs={{0,8},{1,9},{2,10},{3,11},{4,12},{5,13},{6,14},{7,15},{8,0},{9,1},... | collective-permute-start | bytes 638984 | tf_op jit(solution)/shard_map/ppermute | solution.py:1080
  115.3 7.2 %collective-permute-start.16 = (f32[208,128]{1,0:T(8,128)S(1)}, f32[208,128]{1,0:T(8,128)S(1)}, u32[]{:S(2)}, u32[]{:S(2)}) collective-permute-start(f32[208,128]{1,0:T(8,128)S(1)} %pad_maximum_fusion.4), channel_id=1, source_target_pairs={{0,16},{1,17},{2,18},{3,19},{4,20},{5,21},{6,22},{7,23},{8,24},{9,... | collective-permute-start | bytes 319496 | tf_op jit(solution)/shard_map/ppermute | solution.py:1080
  122.7 5.1 %collective-permute-start.17 = (bf16[224,128]{1,0:T(8,128)(2,1)S(1)}, bf16[224,128]{1,0:T(8,128)(2,1)S(1)}, u32[]{:S(2)}, u32[]{:S(2)}) collective-permute-start(bf16[224,128]{1,0:T(8,128)(2,1)S(1)} %get-tuple-element.220), channel_id=1, source_target_pairs={{0,16},{1,17},{2,18},{3,19},{4,20},{5,21},{6,22},{7,23},{8,24},{9,... | collective-permute-start | bytes 172040 | tf_op jit(solution)/shard_map/ppermute | solution.py:1080
  127.9 20.1 %copy-start.45 = (f32[2960]{0:T(1024)S(1)}, f32[2960]{0:T(1024)}, u32[]{:S(2)}) copy-start(f32[2960]{0:T(1024)} %param.21) | copy-start | bytes 35524
  127.9 20.1 %copy-start.46 = (f32[2960]{0:T(1024)S(1)}, f32[2960]{0:T(1024)}, u32[]{:S(2)}) copy-start(f32[2960]{0:T(1024)} %param.20) | copy-start | bytes 35524
  128.0 4.9 %collective-permute-start.18 = (bf16[448,128]{1,0:T(8,128)(2,1)S(1)}, bf16[448,128]{1,0:T(8,128)(2,1)S(1)}, u32[]{:S(2)}, u32[]{:S(2)}) collective-permute-start(bf16[448,128]{1,0:T(8,128)(2,1)S(1)} %broadcast_select_fusion), channel_id=1, source_target_pairs={{0,8},{1,9},{2,10},{3,11},{4,12},{5,13},{6,14},{7,15},{8,0},{9,1},... | collective-permute-start | bytes 344072 | tf_op jit(solution)/shard_map/ppermute | solution.py:1080
  132.9 6.1 %collective-permute-start.19 = (bf16[896,128]{1,0:T(8,128)(2,1)S(1)}, bf16[896,128]{1,0:T(8,128)(2,1)S(1)}, u32[]{:S(2)}, u32[]{:S(2)}) collective-permute-start(bf16[896,128]{1,0:T(8,128)(2,1)S(1)} %maximum_select_fusion.3), channel_id=1, source_target_pairs={{0,4},{1,5},{2,6},{3,7},{4,0},{5,1},{6,2},{7,3},{8,12},{9,13},{10,... | collective-permute-start | bytes 688136 | tf_op jit(solution)/shard_map/ppermute | solution.py:1080
  139.1 8.5 %collective-permute-start.20 = (bf16[1792,128]{1,0:T(8,128)(2,1)S(1)}, bf16[1792,128]{1,0:T(8,128)(2,1)S(1)}, u32[]{:S(2)}, u32[]{:S(2)}) collective-permute-start(bf16[1792,128]{1,0:T(8,128)(2,1)S(1)} %maximum_select_fusion.2), channel_id=1, source_target_pairs={{0,2},{1,3},{2,0},{3,1},{4,6},{5,7},{6,4},{7,5},{8,10},{9,11},{10,... | collective-permute-start | bytes 1376264 | tf_op jit(solution)/shard_map/ppermute | solution.py:1080
  147.9 2.5 %collective-permute-start.21 = (bf16[3584,128]{1,0:T(8,128)(2,1)S(1)}, bf16[3584,128]{1,0:T(8,128)(2,1)S(1)}, u32[]{:S(2)}, u32[]{:S(2)}) collective-permute-start(bf16[3584,128]{1,0:T(8,128)(2,1)S(1)} %maximum_select_fusion.1), channel_id=1, source_target_pairs={{0,1},{1,0},{2,3},{3,2},{4,5},{5,4},{6,7},{7,6},{8,9},{9,8},{10,11... | collective-permute-start | bytes 2752520 | tf_op jit(solution)/shard_map/ppermute | solution.py:1080
  151.0 1.8 %copy-start.3 = (f32[2,512,512]{2,1,0:T(8,128)S(1)}, f32[2,512,512]{2,1,0:T(8,128)}, u32[]{:S(2)}) copy-start(f32[2,512,512]{2,1,0:T(8,128)} %middle_second.1) | copy-start | bytes 6291460
  151.0 2.0 %copy-start.6 = (f32[9,36,512]{2,1,0:T(8,128)S(1)}, f32[9,36,512]{2,1,0:T(8,128)}, u32[]{:S(2)}) copy-start(f32[9,36,512]{2,1,0:T(8,128)} %exit_first.1) | copy-start | bytes 1990660
  151.1 2.1 %copy-start.5 = (f32[9,36,512]{2,1,0:T(8,128)S(1)}, f32[9,36,512]{2,1,0:T(8,128)}, u32[]{:S(2)}) copy-start(f32[9,36,512]{2,1,0:T(8,128)} %exit_ref.5) | copy-start | bytes 1990660
  151.2 2.7 %copy-start.2 = (f32[2,512,512]{2,1,0:T(8,128)S(1)}, f32[2,512,512]{2,1,0:T(8,128)}, u32[]{:S(2)}) copy-start(f32[2,512,512]{2,1,0:T(8,128)} %middle_first.1) | copy-start | bytes 6291460
  151.3 3.2 %copy-start.1 = (f32[2,512,512]{2,1,0:T(8,128)S(1)}, f32[2,512,512]{2,1,0:T(8,128)}, u32[]{:S(2)}) copy-start(f32[2,512,512]{2,1,0:T(8,128)} %middle_ref.5) | copy-start | bytes 6291460
  151.3 3.2 %copy-start.14 = (f32[9,48,24]{1,2,0:T(8,128)S(1)}, f32[9,48,24]{1,2,0:T(8,128)}, u32[]{:S(2)}) copy-start(f32[9,48,24]{1,2,0:T(8,128)} %param.32) | copy-start | bytes 124420
  151.3 3.2 %copy-start.15 = (f32[9,48,24]{1,2,0:T(8,128)S(1)}, f32[9,48,24]{1,2,0:T(8,128)}, u32[]{:S(2)}) copy-start(f32[9,48,24]{1,2,0:T(8,128)} %param.33) | copy-start | bytes 124420
  (21 other events, 20.0 us)

commit v3 on v2

--- a/solution.py
+++ b/solution.py
@@ -130,6 +130,11 @@
     if turned:
         dy, dx = 2 - dy, 2 - dx
     return ((row + dy) * (cols + 2) + first_col + dx) * LANES
+
+
+def place_of(step, chunk, cols):
+    per_row = cols * LANES // chunk
+    return step // per_row, lax.rem(step, per_row) * (chunk // LANES), pl.ds(pl.multiple_of(step * chunk, chunk), chunk)
 
 
 def gather_cols(ext_ref, cols, row, first_col, size, turned=False):
@@ -430,88 +435,82 @@
     drop,
 ):
     rows, cols, bands = dims
-    step = pl.program_id(0)
-    per_row = cols * LANES // chunk
     iota = lax.broadcasted_iota(jnp.int32, (8, 1), 0)
     ones = jnp.where(iota == CH // 2, 1.0, 0.0)
-
-    @pl.when(step == 0)
-    def _():
-        fill_ext(ext, mix1_ref[0:8, :] + ones, rows, cols, bands, ones)
-        oacc[...] = jnp.zeros_like(oacc)
-
-    row = step // per_row
-    col = (step % per_row) * (chunk // LANES)
-    xcol = gather_cols(ext, cols, row, col, chunk)
-    xcol_ref[...] = xcol
-    hidden = jnp.maximum(dot(et_ref[...], xcol), 0.0).astype(BF16)
-    h1_ref[...] = hidden
-    hidden = jnp.maximum(dot(wb_ref[...], hidden) + bias_ref[...], 0.0).astype(BF16)
-    h2_ref[...] = hidden
-    scatter_cols(oacc, dot(f_ref[...], hidden), cols, row, col, chunk, True)
-
-    @pl.when(step == pl.num_programs(0) - 1)
-    def _():
-        line = cols * LANES
-        valid = row_mask(8, 8, CH // 2)
-        step_total = None
-        half_rows, half_cols = rows // 2, cols // 2
-        for s, piece in enumerate(fold_ext(oacc, rows, cols, bands)):
-            at = slice(s * line, (s + 1) * line)
-            output = piece + chan1_ref[:, 2:3]
-            second = output[8:] + 2.0
-            t_ref[:, at] = second
-            scale_log = log_sigmoid(second)
-            result = (mix1_ref[8:16, at] + output[:8]) * jnp.exp(scale_log)
-            res_ref[:, at] = result
-            part = fold_lanes(jnp.where(valid, scale_log, 0.0) * mask_ref[:, at])
-            step_total = part if step_total is None else step_total + part
-        for i in range(half_rows):
-            for j in range(half_cols):
-                at = slice((i * half_cols + j) * LANES, (i * half_cols + j + 1) * LANES)
-                for p in range(4):
-                    start = ((2 * i + p // 2) * cols + 2 * j + p % 2) * LANES
-                    drop[p * 8 : p * 8 + 8, at] = res_ref[:, start : start + LANES]
-        part_iota = lax.broadcasted_iota(jnp.int32, (32, 1), 0)
-        part_ones = jnp.where(part_iota == CH // 2, 1.0, 0.0)
-        fill_ext(kext, keep_ref[...] + part_ones, half_rows, half_cols, bands, part_ones)
-        part_line = half_cols * LANES
-        gkacc[...] = jnp.zeros_like(gkacc)
-        weight = coef_of(count_ref) * mask2_ref[...]
-        valid = row_mask(32, 8, CH // 2)
-        prior_total = None
-        for i in range(half_rows):
-            at = slice(i * part_line, (i + 1) * part_line)
-            columns = gather_cols(kext, half_cols, i, 0, part_line)
-            kcol[...] = columns
-            prior = dot(wp_ref[...], columns) + pbias_ref[...]
-            mean, logs = prior[:32], prior[32:]
-            inverse = jnp.exp(-logs)
-            scaled = (drop[:, at] - mean) * inverse
-            part = fold_lanes((-logs - 0.5 * scaled * scaled) * mask2_ref[:, at])
-            prior_total = part if prior_total is None else prior_total + part
-            g_mean = weight[:, at] * scaled * inverse
-            g_logs = jnp.where(valid, weight[:, at] * (scaled * scaled - 1.0), 0.0)
-            drop[:, at] = -g_mean
-            g_prior = jnp.concatenate([g_mean, g_logs], axis=0).astype(BF16)
-            g_wp = dot_nt(g_prior, kcol[...])
-            if i == 0:
-                gwp_ref[...] = g_wp
-            else:
-                gwp_ref[...] += g_wp
-            scatter_cols(gkacc, dot(wpt_ref[...], g_prior), half_cols, i, 0, part_line)
-        loss_ref[...] = jnp.zeros_like(loss_ref)
-        loss_ref[0:1, :] = jnp.sum(step_total, axis=0, keepdims=True) + jnp.sum(prior_total, axis=0, keepdims=True)
-        for i, piece in enumerate(fold_ext(gkacc, half_rows, half_cols, bands)):
-            at = slice(i * part_line, (i + 1) * part_line)
-            g_keep = piece + gkeep_in_ref[:, at]
-            g_drop = drop[:, at]
-            for j in range(half_cols):
-                inner = slice(j * LANES, (j + 1) * LANES)
-                for p in range(4):
-                    start = ((2 * i + p // 2) * cols + 2 * j + p % 2) * LANES
-                    gout_ref[0:8, start : start + LANES] = g_keep[p * 8 : p * 8 + 8, inner]
-                    gout_ref[8:16, start : start + LANES] = g_drop[p * 8 : p * 8 + 8, inner]
+    fill_ext(ext, mix1_ref[0:8, :] + ones, rows, cols, bands, ones)
+    oacc[...] = jnp.zeros_like(oacc)
+
+    @pl.loop(0, rows * cols * LANES // chunk)
+    def _(step):
+        row, col, at = place_of(step, chunk, cols)
+        xcol = gather_cols(ext, cols, row, col, chunk)
+        xcol_ref[:, at] = xcol
+        hidden = jnp.maximum(dot(et_ref[...], xcol), 0.0).astype(BF16)
+        h1_ref[:, at] = hidden
+        hidden = jnp.maximum(dot(wb_ref[...], hidden) + bias_ref[...], 0.0).astype(BF16)
+        h2_ref[:, at] = hidden
+        scatter_cols(oacc, dot(f_ref[...], hidden), cols, row, col, chunk, True)
+
+    line = cols * LANES
+    valid = row_mask(8, 8, CH // 2)
+    step_total = None
+    half_rows, half_cols = rows // 2, cols // 2
+    for s, piece in enumerate(fold_ext(oacc, rows, cols, bands)):
+        at = slice(s * line, (s + 1) * line)
+        output = piece + chan1_ref[:, 2:3]
+        second = output[8:] + 2.0
+        t_ref[:, at] = second
+        scale_log = log_sigmoid(second)
+        result = (mix1_ref[8:16, at] + output[:8]) * jnp.exp(scale_log)
+        res_ref[:, at] = result
+        part = fold_lanes(jnp.where(valid, scale_log, 0.0) * mask_ref[:, at])
+        step_total = part if step_total is None else step_total + part
+    for i in range(half_rows):
+        for j in range(half_cols):
+            at = slice((i * half_cols + j) * LANES, (i * half_cols + j + 1) * LANES)
+            for p in range(4):
+                start = ((2 * i + p // 2) * cols + 2 * j + p % 2) * LANES
+                drop[p * 8 : p * 8 + 8, at] = res_ref[:, start : start + LANES]
+    part_iota = lax.broadcasted_iota(jnp.int32, (32, 1), 0)
+    part_ones = jnp.where(part_iota == CH // 2, 1.0, 0.0)
+    fill_ext(kext, keep_ref[...] + part_ones, half_rows, half_cols, bands, part_ones)
+    part_line = half_cols * LANES
+    gkacc[...] = jnp.zeros_like(gkacc)
+    weight = coef_of(count_ref) * mask2_ref[...]
+    valid = row_mask(32, 8, CH // 2)
+    prior_total = None
+    for i in range(half_rows):
+        at = slice(i * part_line, (i + 1) * part_line)
+        columns = gather_cols(kext, half_cols, i, 0, part_line)
+        kcol[...] = columns
+        prior = dot(wp_ref[...], columns) + pbias_ref[...]
+        mean, logs = prior[:32], prior[32:]
+        inverse = jnp.exp(-logs)
+        scaled = (drop[:, at] - mean) * inverse
+        part = fold_lanes((-logs - 0.5 * scaled * scaled) * mask2_ref[:, at])
+        prior_total = part if prior_total is None else prior_total + part
+        g_mean = weight[:, at] * scaled * inverse
+        g_logs = jnp.where(valid, weight[:, at] * (scaled * scaled - 1.0), 0.0)
+        drop[:, at] = -g_mean
+        g_prior = jnp.concatenate([g_mean, g_logs], axis=0).astype(BF16)
+        g_wp = dot_nt(g_prior, kcol[...])
+        if i == 0:
+            gwp_ref[...] = g_wp
+        else:
+            gwp_ref[...] += g_wp
+        scatter_cols(gkacc, dot(wpt_ref[...], g_prior), half_cols, i, 0, part_line)
+    loss_ref[...] = jnp.zeros_like(loss_ref)
+    loss_ref[0:1, :] = jnp.sum(step_total, axis=0, keepdims=True) + jnp.sum(prior_total, axis=0, keepdims=True)
+    for i, piece in enumerate(fold_ext(gkacc, half_rows, half_cols, bands)):
+        at = slice(i * part_line, (i + 1) * part_line)
+        g_keep = piece + gkeep_in_ref[:, at]
+        g_drop = drop[:, at]
+        for j in range(half_cols):
+            inner = slice(j * LANES, (j + 1) * LANES)
+            for p in range(4):
+                start = ((2 * i + p // 2) * cols + 2 * j + p % 2) * LANES
+                gout_ref[0:8, start : start + LANES] = g_keep[p * 8 : p * 8 + 8, inner]
+                gout_ref[8:16, start : start + LANES] = g_drop[p * 8 : p * 8 + 8, inner]
 
 
 def put_rows(slab_ref, first, values, row, count):
@@ -550,68 +549,62 @@
     loss_two_ref,
     h1_ref,
     h2_ref,
+    gpre_ref,
     kept_a,
     sent_a,
     kept_b,
     sent_b,
     ghalf_ref,
     gbc_ref,
-    gpre_ref,
     ext,
     gf,
     bacc,
     slab_ref,
 ):
     rows, cols, bands = dims
-    step = pl.program_id(0)
-    per_row = cols * LANES // chunk
-
-    @pl.when(step == 0)
-    def _():
-        weight = coef_of(count_ref) * mask_ref[...]
-        second = t_ref[...]
-        result = res_ref[...]
-        g_result = gout_ref[8:16, :]
-        g_log = g_result * result + weight
-        g_second = g_log * sigmoid_minus(second)
-        g_half = g_result * jnp.exp(log_sigmoid(second))
-        ghalf_ref[...] = g_half
-        valid = row_mask(8, 8, CH // 2)
-        g_out = jnp.concatenate([g_half, jnp.where(valid, g_second, 0.0)], axis=0)
-        g_out = g_out.astype(BF16).astype(F32)
-        gbc_ref[...] = fold_lanes(g_out)
-        fill_ext(ext, g_out, rows, cols, bands, jnp.zeros((16, 1), F32))
-        gf[...] = jnp.zeros_like(gf)
-        slab_ref[...] = jnp.zeros_like(slab_ref)
-        bacc[...] = jnp.zeros_like(bacc)
-
-    row = step // per_row
-    col = (step % per_row) * (chunk // LANES)
-    gcol = gather_cols(ext, cols, row, col, chunk, True)
-    hidden_two = h2_ref[...]
-    g_pre = jnp.where(hidden_two > 0, dot(ft_ref[...], gcol), 0.0).astype(BF16)
-    gpre_ref[...] = g_pre
-    gf[...] += dot_nt(gcol, hidden_two)
-    g_wb = dot_nt(g_pre, h1_ref[...])
-    for block in range(HID // LANES):
-        slab_ref[block * HID : (block + 1) * HID, :] += g_wb[:, block * LANES : (block + 1) * LANES]
-    bacc[...] += fold_lanes(g_pre.astype(F32))
-
-    @pl.when(step == pl.num_programs(0) - 1)
-    def _():
-        bias = ones_sum(bacc)
-        put_rows(slab_ref, lambda block: ONE_B + block, bias, 0, 1)
-        for piece in range(18):
-            put_rows(slab_ref, lambda block: ONE_F + block * 112 + piece * 6, gf, piece * 8, 6)
-        for block in range(3):
-            width = min(LANES, 288 - block * LANES)
-            slab_ref[ONE_P + block * 64 : ONE_P + block * 64 + 64, 0:width] = gwp_ref[
-                :, block * LANES : block * LANES + width
-            ]
-        slab_ref[ONE_LOSS : ONE_LOSS + 1, :] = loss_one_ref[0:1, :] + loss_two_ref[0:1, :]
-        slab_ref[ONE_LOSS + 1 : ONE_LOSS + 2, :] = loss_two_ref[1:2, :]
-        part_out(slab_ref, 0, PART_A, index_ref[1], bits[0], kept_a, sent_a)
-        part_out(slab_ref, PART_A, ONE_ROWS - PART_A, index_ref[1], bits[1], kept_b, sent_b)
+    weight = coef_of(count_ref) * mask_ref[...]
+    second = t_ref[...]
+    result = res_ref[...]
+    g_result = gout_ref[8:16, :]
+    g_log = g_result * result + weight
+    g_second = g_log * sigmoid_minus(second)
+    g_half = g_result * jnp.exp(log_sigmoid(second))
+    ghalf_ref[...] = g_half
+    valid = row_mask(8, 8, CH // 2)
+    g_out = jnp.concatenate([g_half, jnp.where(valid, g_second, 0.0)], axis=0)
+    g_out = g_out.astype(BF16).astype(F32)
+    gbc_ref[...] = fold_lanes(g_out)
+    fill_ext(ext, g_out, rows, cols, bands, jnp.zeros((16, 1), F32))
+    gf[...] = jnp.zeros_like(gf)
+    slab_ref[...] = jnp.zeros_like(slab_ref)
+    bacc[...] = jnp.zeros_like(bacc)
+
+    @pl.loop(0, rows * cols * LANES // chunk)
+    def _(step):
+        row, col, at = place_of(step, chunk, cols)
+        gcol = gather_cols(ext, cols, row, col, chunk, True)
+        hidden_two = h2_ref[:, at]
+        g_pre = jnp.where(hidden_two > 0, dot(ft_ref[...], gcol), 0.0).astype(BF16)
+        gf[...] += dot_nt(gcol, hidden_two)
+        gpre_ref[:, at] = g_pre
+        g_wb = dot_nt(g_pre, h1_ref[:, at])
+        for block in range(HID // LANES):
+            slab_ref[block * HID : (block + 1) * HID, :] += g_wb[:, block * LANES : (block + 1) * LANES]
+        bacc[...] += fold_lanes(g_pre.astype(F32))
+
+    bias = ones_sum(bacc)
+    put_rows(slab_ref, lambda block: ONE_B + block, bias, 0, 1)
+    for piece in range(18):
+        put_rows(slab_ref, lambda block: ONE_F + block * 112 + piece * 6, gf, piece * 8, 6)
+    for block in range(3):
+        width = min(LANES, 288 - block * LANES)
+        slab_ref[ONE_P + block * 64 : ONE_P + block * 64 + 64, 0:width] = gwp_ref[
+            :, block * LANES : block * LANES + width
+        ]
+    slab_ref[ONE_LOSS : ONE_LOSS + 1, :] = loss_one_ref[0:1, :] + loss_two_ref[0:1, :]
+    slab_ref[ONE_LOSS + 1 : ONE_LOSS + 2, :] = loss_two_ref[1:2, :]
+    part_out(slab_ref, 0, PART_A, index_ref[1], bits[0], kept_a, sent_a)
+    part_out(slab_ref, PART_A, ONE_ROWS - PART_A, index_ref[1], bits[1], kept_b, sent_b)
 
 
 def one_backward_bottom(
@@ -633,52 +626,42 @@
     acc,
 ):
     rows, cols, bands = dims
-    step = pl.program_id(0)
-    per_row = cols * LANES // chunk
-
-    @pl.when(step == 0)
-    def _():
-        gacc[...] = jnp.zeros_like(gacc)
-        ge[...] = jnp.zeros_like(ge)
-        slab_ref[...] = jnp.zeros_like(slab_ref)
-
-    row = step // per_row
-    col = (step % per_row) * (chunk // LANES)
-    g_pre = jnp.where(h1_ref[...] > 0, dot(wbt_ref[...], gpre_ref[...]), 0.0).astype(BF16)
-    ge[...] += dot_nt(xcol_ref[...], g_pre)
-    scatter_cols(gacc, dot(e_ref[...], g_pre), cols, row, col, chunk)
-
-    @pl.when(step == pl.num_programs(0) - 1)
-    def _():
-        gmix[0:8, :] = gout_ref[0:8, :] + jnp.concatenate(fold_ext(gacc, rows, cols, bands), axis=1)
-        gmix[8:16, :] = ghalf_ref[...]
-        g_mixed = gmix[...]
-        acc[...] = jnp.zeros_like(acc)
-        gram(g_mixed, y1_ref, range(CH), acc)
-        stack = [(j, acc[j]) for j in range(CH)] + [(16, fold_lanes(g_mixed)), (17, gbc_ref[...])]
-        slab_ref[REST_SMALL : REST_SMALL + 16, :] = lane_sums(stack, CH)
-        for tap in range(9):
-            put_rows(slab_ref, lambda block: block * 56 + tap * 6, ge, tap * 8, 6)
-        put_rows(slab_ref, lambda block: REST_A + block, ge, 6, 1)
-
-
-def call(kernel, inputs, outputs, scratch, flops, grid=None, in_specs=None, out_specs=None):
+    gacc[...] = jnp.zeros_like(gacc)
+    ge[...] = jnp.zeros_like(ge)
+    slab_ref[...] = jnp.zeros_like(slab_ref)
+
+    @pl.loop(0, rows * cols * LANES // chunk)
+    def _(step):
+        row, col, at = place_of(step, chunk, cols)
+        g_pre = jnp.where(h1_ref[:, at] > 0, dot(wbt_ref[...], gpre_ref[:, at]), 0.0).astype(BF16)
+        ge[...] += dot_nt(xcol_ref[:, at], g_pre)
+        scatter_cols(gacc, dot(e_ref[...], g_pre), cols, row, col, chunk)
+
+    gmix[0:8, :] = gout_ref[0:8, :] + jnp.concatenate(fold_ext(gacc, rows, cols, bands), axis=1)
+    gmix[8:16, :] = ghalf_ref[...]
+    g_mixed = gmix[...]
+    acc[...] = jnp.zeros_like(acc)
+    gram(g_mixed, y1_ref, range(CH), acc)
+    stack = [(j, acc[j]) for j in range(CH)] + [(16, fold_lanes(g_mixed)), (17, gbc_ref[...])]
+    slab_ref[REST_SMALL : REST_SMALL + 16, :] = lane_sums(stack, CH)
+    for tap in range(9):
+        put_rows(slab_ref, lambda block: block * 56 + tap * 6, ge, tap * 8, 6)
+    put_rows(slab_ref, lambda block: REST_A + block, ge, 6, 1)
+
+
+def call(kernel, inputs, outputs, scratch, flops, aliases=None):
     whole = pl.BlockSpec(memory_space=pltpu.VMEM)
     smem = pl.BlockSpec(memory_space=pltpu.SMEM)
-    if in_specs is None:
-        in_specs = [smem if x.dtype == jnp.int32 and x.ndim == 1 else whole for x in inputs]
-        out_specs = [whole for _ in outputs]
-    spec = {} if grid is None else {"grid": grid}
     traffic = sum(x.size * x.dtype.itemsize for x in list(inputs) + list(outputs))
     return pl.pallas_call(
         kernel,
         out_shape=outputs,
-        in_specs=in_specs,
-        out_specs=out_specs,
+        in_specs=[smem if x.dtype == jnp.int32 and x.ndim == 1 else whole for x in inputs],
+        out_specs=[whole for _ in outputs],
         scratch_shapes=scratch,
+        input_output_aliases=aliases or {},
         compiler_params=pltpu.CompilerParams(vmem_limit_bytes=VMEM_LIMIT),
         cost_estimate=pl.CostEstimate(flops=flops, bytes_accessed=traffic, transcendentals=0),
-        **spec,
     )(*inputs)
 
 
@@ -863,8 +846,8 @@
 def adamw(weight, grad, first, second):
     first_new = BETA_ONE * first + (1.0 - BETA_ONE) * grad
     second_new = BETA_TWO * second + (1.0 - BETA_TWO) * grad * grad
-    first_hat = first_new / (1.0 - BETA_ONE**ADAM_STEP)
-    second_hat = second_new / (1.0 - BETA_TWO**ADAM_STEP)
+    first_hat = first_new * (1.0 / (1.0 - BETA_ONE**ADAM_STEP))
+    second_hat = second_new * (1.0 / (1.0 - BETA_TWO**ADAM_STEP))
     updated = weight - LEARN_RATE * (first_hat / (jnp.sqrt(second_hat) + ADAM_EPS) + WEIGHT_DECAY * weight)
     return (updated, second_new)
 
@@ -1079,6 +1062,9 @@
     def trade(value, bit):
         return lax.ppermute(value, ("batch", "rows"), [(i, i ^ bit) for i in range(devices)])
 
+    def in_hbm(value):
+        return pltpu.with_memory_space_constraint(value, pltpu.HBM)
+
     def after(value, *done):
         return lax.optimization_barrier((value, *done))[0]
 
@@ -1190,31 +1176,21 @@
     )
     whole_lanes = (rows + 2) * (cols + 2) * LANES
     chunk = 1024
-    steps = size // chunk
-    smem = pl.BlockSpec(memory_space=pltpu.SMEM)
-
-    def fixed(value):
-        rank = len(value.shape)
-        return pl.BlockSpec(value.shape, lambda j: (0,) * rank)
-
-    def moving(height):
-        return pl.BlockSpec((height, chunk), lambda j: (0, j))
-
     fwd_in = (
         count,
-        mixed_one,
+        in_hbm(mixed_one),
         mask,
         mask2,
-        keep,
-        gkeep_two,
+        in_hbm(keep),
+        in_hbm(gkeep_two),
         chan_one,
-        e_one_t,
-        wb_one,
-        f_one,
-        bb_one,
-        wp,
-        wpt,
-        prior_bias,
+        in_hbm(e_one_t),
+        in_hbm(wb_one),
+        in_hbm(f_one),
+        in_hbm(bb_one),
+        in_hbm(wp),
+        in_hbm(wpt),
+        in_hbm(prior_bias),
     )
     fwd_out = [
         shape((72, size), BF16),
@@ -1239,16 +1215,13 @@
             pltpu.VMEM((32, part), F32),
         ],
         2 * HID * size * (72 + HID + 144),
-        grid=(steps,),
-        in_specs=[fixed(x) for x in fwd_in],
-        out_specs=[moving(72), moving(HID), moving(HID)] + [fixed(x) for x in fwd_out[3:]],
-    )
-    first_bit, second_bit, third_bit = bits[0], bits[2], bits[1]
+    )
+    first_bit, second_bit, third_bit, fourth_bit = bits[0], bits[2], bits[1], bits[3]
     total_two = kept_two + after(trade(sent_two, first_bit), loss_one)
     top_in = (own, after(count, total_two), mask, res_one, t_one, gout_one, f_one_t, gwp, loss_one, loss_two, h1_one, h2_one)
     half_a, half_b = shape((PART_A // 2, LANES)), shape(((ONE_ROWS - PART_A) // 2, LANES))
-    top_out = [half_a, half_a, half_b, half_b] + [shape((8, size)), shape((16, LANES)), shape((HID, size), BF16)]
-    (kept_a, sent_a, kept_b, sent_b, ghalf, gbc, gpre) = call(
+    top_out = [shape((HID, size), BF16), half_a, half_a, half_b, half_b, shape((8, size)), shape((16, LANES))]
+    (gpre, kept_a, sent_a, kept_b, sent_b, ghalf, gbc) = call(
         functools.partial(one_backward_top, dims, chunk, (second_bit, third_bit)),
         top_in,
         top_out,
@@ -1259,9 +1232,7 @@
             pltpu.VMEM((ONE_ROWS, LANES), F32),
         ],
         2 * HID * size * (144 + HID + 144),
-        grid=(steps,),
-        in_specs=[smem] + [fixed(x) for x in top_in[1:10]] + [moving(HID), moving(HID)],
-        out_specs=[fixed(x) for x in top_out[:6]] + [moving(HID)],
+        aliases={11: 0},
     )
 
     def halve(parts, bit, *beside):
@@ -1289,24 +1260,23 @@
             pltpu.VMEM((CH, 16, LANES), F32),
         ],
         2 * HID * size * (72 + HID + 72),
-        grid=(steps,),
-        in_specs=[fixed(x) for x in low_in[:6]] + [moving(72), moving(HID), moving(HID)],
-        out_specs=[fixed(shape((REST_ROWS, LANES)))],
     )
 
     total_a = kept_a + after(trade(sent_a, second_bit), slab_rest)
     total_b = kept_b + after(trade(sent_b, third_bit), slab_rest)
-    (total_two,) = halve([total_two], third_bit, slab_rest)
+    (total_two,) = halve([total_two], fourth_bit, slab_rest)
     far = bits[3:]
-    total_a, total_b, total_rest = halve([total_a, total_b, slab_rest], first_bit)
+    total_a, total_b, total_rest = halve([total_a, total_b, after(slab_rest, total_two)], first_bit)
+    (total_two,) = halve([total_two], third_bit)
     total_a, total_rest = halve([total_a, total_rest], third_bit)
     (total_b,) = halve([total_b], second_bit)
     (total_rest,) = halve([total_rest], second_bit)
-    shards = [total_two, total_a, total_b, total_rest]
-    for bit in far:
+    shards = halve([total_a, total_b, total_rest], far[0])
+    shards = [total_two] + shards
+    for bit in far[1:]:
         shards = halve(shards, bit)
     orders = [
-        [first_bit, second_bit, third_bit] + far,
+        [first_bit, second_bit, fourth_bit, third_bit] + far[1:],
         [second_bit, first_bit, third_bit] + far,
         [third_bit, first_bit, second_bit] + far,
         [first_bit, third_bit, second_bit] + far,
@@ -1321,25 +1291,41 @@
             extra.append(high)
             value = value - high
     extra = jnp.pad(jnp.stack(extra), ((0, 10), (0, 0)))
-    spread = jnp.concatenate(shards + [extra]).astype(BF16)
-    back = bits[::-1]
-    for bit in back:
-        other = trade(spread, bit)
-        spread = jnp.where(
-            (index // bit) % 2 == 0, jnp.concatenate([spread, other]), jnp.concatenate([other, spread])
-        )
-    spread = spread.reshape((2,) * len(bits) + (-1, LANES))
-    totals = []
+    spread = [shards[0].astype(BF16), jnp.concatenate(shards[1:] + [extra]).astype(BF16)]
+    near = [[third_bit, second_bit, first_bit], [second_bit, third_bit, first_bit]]
+    backs = [far[::-1] + near[0], far[::-1] + near[1]]
+
+    def double(values, bit):
+        low = (index // bit) % 2 == 0
+        joined = jnp.concatenate(values) if len(values) > 1 else values[0]
+        other = trade(joined, bit)
+        results, first = [], 0
+        for value in values:
+            got = other[first : first + value.shape[0]]
+            first += value.shape[0]
+            results.append(jnp.where(low, jnp.concatenate([value, got]), jnp.concatenate([got, value])))
+        return results
+
+    for bit in far[::-1]:
+        spread = double(spread, bit)
+    for k in range(3):
+        spread = [double([value], order[k])[0] for value, order in zip(spread, near)]
+    count_bits = len(bits)
+    spread = [value.reshape((2,) * count_bits + (-1, LANES)) for value in spread]
+
+    def reorder(value, back, order):
+        axes = [count_bits - 1 - back.index(bit) for bit in order]
+        return value.transpose(axes + [count_bits, count_bits + 1]).reshape(-1, LANES)
+
+    totals = [reorder(spread[0], backs[0], orders[0])]
     first = 0
-    for shard, order in zip(shards, orders):
-        part_rows = spread[..., first : first + shard.shape[0], :]
+    for shard, order in zip(shards[1:], orders[1:]):
+        totals.append(reorder(spread[1][..., first : first + shard.shape[0], :], backs[1], order))
         first += shard.shape[0]
-        axes = [len(bits) - 1 - back.index(bit) for bit in order]
-        totals.append(part_rows.transpose(axes + [len(bits), len(bits) + 1]).reshape(-1, LANES))
-    place = [0] * len(bits)
+    place = [0] * count_bits
     for k, bit in enumerate(orders[2]):
-        place[len(bits) - 1 - back.index(bit)] = (owner >> (len(bits) - 1 - k)) & 1
-    extra = spread[tuple(place)][first:]
+        place[count_bits - 1 - backs[1].index(bit)] = (owner >> (count_bits - 1 - k)) & 1
+    extra = spread[1][tuple(place)][first:]
     totals = [totals[0], jnp.concatenate(totals[1:3]), totals[3]]
     taps = [
         (entry_taps, entry_first, entry_second),

time: 165 us -> 147 us (0.89)
  waiting for transfers between devices: 52.7 us -> 43.1 us
  local copies, waits for them, and re-layouts: 20.9 us -> 11.8 us
  starting transfers between devices: 19.5 us -> 23.3 us
  Pallas kernels: 66.1 us -> 63.6 us
    ppermute x19 -> x23, waiting for transfers between devices: 52.7 us -> 43.1 us  [trade(): lax.ppermute(value, ('batch', 'rows'), [(i, i ^ bit) for i in range(devic...]
    unnamed x101 -> x64, local copies, waits for them, and re-layouts: 19.6 us -> 10.6 us
    ppermute x19 -> x23, starting transfers between devices: 16.4 us -> 20.2 us  [trade(): lax.ppermute(value, ('batch', 'rows'), [(i, i ^ bit) for i in range(devic...]
    pallas_call x10, Pallas kernels: 66.1 us -> 63.6 us  [call(): pl.pallas_call(kernel, out_shape=outputs, in_specs=[smem if x.dtype == jn...]
  transfers between devices with their start and end apart: 22 -> 26, of which waited for: 12 -> 14; matrix products, arithmetic and copies ran while one was open for 1% -> 1% of each run, Pallas kernels for 29% -> 31%
where the time goes in v3:
time: 147 us; the launch traced here: 146 us
  Pallas kernels  63.6 us (43%)
  waiting for transfers between devices  43.1 us (29%)
  starting transfers between devices  23.3 us (16%)
  local copies, waits for them, and re-layouts  11.8 us (8%)
  other arithmetic  2.84 us (2%)
  between operations  1.58 us (1%)
    pallas_call x10, Pallas kernels, call(): pl.pallas_call(kernel, out_shape=outputs, in_specs=[smem if x.dtype == jn...  63.6 us
    ppermute x23, waiting for transfers between devices, trade(): lax.ppermute(value, ('batch', 'rows'), [(i, i ^ bit) for i in range(devic...  43.1 us
    ppermute x23, starting transfers between devices, trade(): lax.ppermute(value, ('batch', 'rows'), [(i, i ^ bit) for i in range(devic...  20.2 us
    unnamed x64, local copies, waits for them, and re-layouts  10.6 us
    ppermute x3, starting transfers between devices, on_device(): lax.ppermute(pieces[d], 'rows', [(i, i ^ d) for i in range(bands)])  3.15 us
  transfers between devices with their start and end apart: 26, of which 14 were waited for; matrix products, arithmetic and copies ran while one was open for 1% of the time, Pallas kernels for 31%

profile of v3, /device:TPU:0, one launch (start us, length us, event | category | flops | bytes accessed | tf_op | source)
XLA Modules:
  0.0 146.3 jit_solution(6104292062099319401)
XLA Ops:
  0.7 1.0 copy-done.12
  1.7 0.8 copy-done.16
  2.5 0.8 shard_map.304
  3.3 2.5 %collective-permute-start.2 = (bf16[224,128]{1,0:T(8,128)(2,1)S(1)}, bf16[224,128]{1,0:T(8,128)(2,1)S(1)}, u32[]{:S(2)}, u32[]{:S(2)}) collective-permute-start(bf16[224,128]{1,0:T(8,128)(2,1)S(1)} %get-tuple-element.120), channel_id=1, source_target_pairs={{0,3},{1,2},{2,1},{3,0},{4,7},{5,6},{6,5},{7,4},{8,11},{9,10},{10,... | collective-permute-start | bytes 172040 | tf_op jit(solution)/shard_map/ppermute | solution.py:1082
  5.8 0.6 collective-permute-start.1
  6.5 0.7 pad_bitcast_fusion.2.flat_ref
  7.2 1.6 %copy-done = f32[2,512,512]{2,1,0:T(8,128)S(1)} copy-done((f32[2,512,512]{2,1,0:T(8,128)S(1)}, f32[2,512,512]{2,1,0:T(8,128)}, u32[]{:S(2)}) %copy-start) | copy-done | bytes 2097176
  8.8 1.1 copy-done.4
  9.9 1.0 copy-done.8
  10.9 1.1 shard_map.305
  12.0 1.8 %collective-permute-start.3 = (f32[1,128]{1,0:T(1,128)S(1)}, f32[1,128]{1,0:T(1,128)S(1)}, u32[]{:S(2)}, u32[]{:S(2)}) collective-permute-start(f32[1,128]{1,0:T(1,128)S(1)} %convert_add_fusion), channel_id=1, source_target_pairs={{0,4},{1,5},{2,6},{3,7},{4,0},{5,1},{6,2},{7,3},{8,12},{9,13},{10,... | collective-permute-start | bytes 1544 | tf_op jit(solution)/shard_map/ppermute | solution.py:1063
  13.8 0.8 shard_map.306
  14.6 0.7 copy-done.19
  15.7 1.8 %collective-permute-start.4 = (f32[1,128]{1,0:T(1,128)S(1)}, f32[1,128]{1,0:T(1,128)S(1)}, u32[]{:S(2)}, u32[]{:S(2)}) collective-permute-start(f32[1,128]{1,0:T(1,128)S(1)} %add.228), channel_id=1, source_target_pairs={{0,8},{1,9},{2,10},{3,11},{4,12},{5,13},{6,14},{7,15},{8,0},{9,1},... | collective-permute-start | bytes 1544 | tf_op jit(solution)/shard_map/ppermute | solution.py:1063
  17.5 2.5 %shard_map.307 = (f32[16,8192]{1,0:T(8,128)S(1)}, f32[16,8192]{1,0:T(8,128)S(1)}, f32[1,8192]{1,0:T(1,128)S(1)}, f32[1,2048]{1,0:T(1,128)S(1)}, f32[32,2048]{1,0...) custom-call(s32[2]{0:T(128)S(1)} %pad_add_fusion.index_ref, bf16[224,128]{1,0:T(8,128)(2,1)S(1)} %get-tuple-element.115.b0, ...), custom_call_target="tpu_custom_call" | custom-call | flops 1000000000 | bytes 2154504 | tf_op jit(solution)/shard_map/pallas_call | solution.py:656
  20.0 0.7 copy-done.25
  20.7 2.7 %collective-permute-start.5 = (f32[1,128]{1,0:T(1,128)S(1)}, f32[1,128]{1,0:T(1,128)S(1)}, u32[]{:S(2)}, u32[]{:S(2)}) collective-permute-start(f32[1,128]{1,0:T(1,128)S(1)} %add.229), channel_id=1, source_target_pairs={{0,16},{1,17},{2,18},{3,19},{4,20},{5,21},{6,22},{7,23},{8,24},{9,... | collective-permute-start | bytes 1544 | tf_op jit(solution)/shard_map/ppermute | solution.py:1063
  23.4 2.7 %shard_map.308 = (f32[32,2048]{1,0:T(8,128)S(1)}, f32[16,2048]{1,0:T(8,128)S(1)}, bf16[144,2048]{1,0:T(8,128)(2,1)S(1)}, bf16[512,2048]{1,0:T(8,128)(2,1)S(1)}, ...) custom-call(f32[32,2048]{1,0:T(8,128)S(1)} %get-tuple-element.131.mix2_ref, ...), custom_call_target="tpu_custom_call" | custom-call | flops 1979711488 | bytes 6469632 | tf_op jit(solution)/shard_map/pallas_call | solution.py:656
  26.1 8.1 %shard_map.309 = (f32[1792,128]{1,0:T(8,128)S(1)}, f32[1792,128]{1,0:T(8,128)S(1)}, f32[32,2048]{1,0:T(8,128)S(1)}) custom-call(s32[2]{0:T(128)S(1)} %pad_add_fusion.index_ref, f32[1,128]{1,0:T(1,128)S(1)} %add.230.count_ref, f32[1,2048]{1,0:T(1,128)S(1)} %get-tuple-element.129.mask2_ref, f32[32,2048]{1,0:T(8,128)S(1)} %get-tuple-element.140.y2_ref, ...), custom_call_target="tpu_custom_call" | custom-call | flops 3959422976 | bytes 8544776 | tf_op jit(solution)/shard_map/pallas_call | solution.py:656
  34.2 0.7 copy-done.26
  34.9 12.6 %shard_map.310 = (bf16[72,8192]{1,0:T(8,128)(2,1)S(1)}, bf16[512,8192]{1,0:T(8,128)(2,1)S(1)}, bf16[512,8192]{1,0:T(8,128)(2,1)S(1)}, f32[8,8192]{1,0:T(8,128)S(...) custom-call(f32[1,128]{1,0:T(1,128)S(1)} %add.230.count_ref, ...), custom_call_target="tpu_custom_call" | custom-call | flops 6106906624 | bytes 21003008 | tf_op jit(solution)/shard_map/pallas_call | solution.py:656
  47.6 1.3 add.236
  48.9 1.6 %collective-permute-start.7 = (f32[896,128]{1,0:T(8,128)S(1)}, f32[896,128]{1,0:T(8,128)S(1)}, u32[]{:S(2)}, u32[]{:S(2)}) collective-permute-start(f32[896,128]{1,0:T(8,128)S(1)} %constant_dynamic-slice_fusion.18), channel_id=1, source_target_pairs={{0,4},{1,5},{2,6},{3,7},{4,0},{5,1},{6,2},{7,3},{8,12},{9,13},{10,... | collective-permute-start | bytes 1376264 | tf_op jit(solution)/shard_map/ppermute | solution.py:1063
  50.4 14.1 %shard_map.311 = (bf16[512,8192]{1,0:T(8,128)(2,1)S(1)}, f32[768,128]{1,0:T(8,128)S(1)}, f32[768,128]{1,0:T(8,128)S(1)}, f32[640,128]{1,0:T(8,128)S(1)}, f32[640...) custom-call(s32[2]{0:T(128)S(1)} %pad_add_fusion.index_ref, ...), custom_call_target="tpu_custom_call", output_to_operand_aliasing={{0}: (11, {})} | custom-call | flops 6710886400 | bytes 28189192 | tf_op jit(solution)/shard_map/pallas_call | solution.py:656
  64.6 1.6 %collective-permute-start.11 = (f32[640,128]{1,0:T(8,128)S(1)}, f32[640,128]{1,0:T(8,128)S(1)}, u32[]{:S(2)}, u32[]{:S(2)}) collective-permute-start(f32[640,128]{1,0:T(8,128)S(1)} %get-tuple-element.185), channel_id=1, source_target_pairs={{0,2},{1,3},{2,0},{3,1},{4,6},{5,7},{6,4},{7,5},{8,10},{9,11},{10,... | collective-permute-start | bytes 983048 | tf_op jit(solution)/shard_map/ppermute | solution.py:1063
  67.3 11.5 %shard_map.312 = f32[256,128]{1,0:T(8,128)S(1)} custom-call(f32[16,8192]{1,0:T(8,128)S(1)} %get-tuple-element.173.y1_ref, f32[8,8192]{1,0:T(8,128)S(1)} %get-tuple-element.174.ghalf_ref, f32[16,128]{1,0:T(8,128)S(1)} %get-tuple-element.175.gbc_ref, f32[16,8192]{1,0:T(8,128)S(1)} %get-tuple-element.166.gout_ref, ...), custom_call_target="tpu_custom_call" | custom-call | flops 5502926848 | bytes 20004864 | tf_op jit(solution)/shard_map/pallas_call | solution.py:656
  79.7 5.0 %collective-permute-done.9 = f32[224,128]{1,0:T(8,128)S(1)} collective-permute-done((f32[224,128]{1,0:T(8,128)S(1)}, f32[224,128]{1,0:T(8,128)S(1)}, u32[]{:S(2)}, u32[]{:S(2)}) %collective-permute-start.9) | collective-permute-done | bytes 114720 | tf_op jit(solution)/shard_map/ppermute | solution.py:1063
  84.9 1.6 %collective-permute-start.14 = (f32[160,128]{1,0:T(8,128)S(1)}, f32[160,128]{1,0:T(8,128)S(1)}, u32[]{:S(2)}, u32[]{:S(2)}) collective-permute-start(f32[160,128]{1,0:T(8,128)S(1)} %constant_dynamic-slice_fusion.8), channel_id=1, source_target_pairs={{0,4},{1,5},{2,6},{3,7},{4,0},{5,1},{6,2},{7,3},{8,12},{9,13},{10,... | collective-permute-start | bytes 245768 | tf_op jit(solution)/shard_map/ppermute | solution.py:1063
  86.5 0.6 collective-permute-start.13
  87.1 2.3 %collective-permute-done.14 = f32[160,128]{1,0:T(8,128)S(1)} collective-permute-done((f32[160,128]{1,0:T(8,128)S(1)}, f32[160,128]{1,0:T(8,128)S(1)}, u32[]{:S(2)}, u32[]{:S(2)}) %collective-permute-start.14) | collective-permute-done | bytes 81952 | tf_op jit(solution)/shard_map/ppermute | solution.py:1063
  89.5 2.1 %collective-permute-done.13 = f32[256,128]{1,0:T(8,128)S(1)} collective-permute-done((f32[256,128]{1,0:T(8,128)S(1)}, f32[256,128]{1,0:T(8,128)S(1)}, u32[]{:S(2)}, u32[]{:S(2)}) %collective-permute-start.13) | collective-permute-done | bytes 131104 | tf_op jit(solution)/shard_map/ppermute | solution.py:1063
  91.6 0.6 collective-permute-start.15
  92.2 3.2 %collective-permute-done.15 = f32[32,128]{1,0:T(8,128)S(1)} collective-permute-done((f32[32,128]{1,0:T(8,128)S(1)}, f32[32,128]{1,0:T(8,128)S(1)}, u32[]{:S(2)}, u32[]{:S(2)}) %collective-permute-start.15) | collective-permute-done | bytes 16416 | tf_op jit(solution)/shard_map/ppermute | solution.py:1063
  95.4 1.6 %collective-permute-start.16 = (f32[192,128]{1,0:T(8,128)S(1)}, f32[192,128]{1,0:T(8,128)S(1)}, u32[]{:S(2)}, u32[]{:S(2)}) collective-permute-start(f32[192,128]{1,0:T(8,128)S(1)} %pad_maximum_fusion.7), channel_id=1, source_target_pairs={{0,8},{1,9},{2,10},{3,11},{4,12},{5,13},{6,14},{7,15},{8,0},{9,1},... | collective-permute-start | bytes 294920 | tf_op jit(solution)/shard_map/ppermute | solution.py:1063
  97.0 4.2 %collective-permute-done.16 = f32[192,128]{1,0:T(8,128)S(1)} collective-permute-done((f32[192,128]{1,0:T(8,128)S(1)}, f32[192,128]{1,0:T(8,128)S(1)}, u32[]{:S(2)}, u32[]{:S(2)}) %collective-permute-start.16) | collective-permute-done | bytes 98336 | tf_op jit(solution)/shard_map/ppermute | solution.py:1063
  101.3 1.2 collective-permute-start.17
  102.6 6.2 %collective-permute-done.17 = f32[208,128]{1,0:T(8,128)S(1)} collective-permute-done((f32[208,128]{1,0:T(8,128)S(1)}, f32[208,128]{1,0:T(8,128)S(1)}, u32[]{:S(2)}, u32[]{:S(2)}) %collective-permute-start.17) | collective-permute-done | bytes 106528 | tf_op jit(solution)/shard_map/ppermute | solution.py:1063
  109.2 5.4 %collective-permute-done.18 = bf16[224,128]{1,0:T(8,128)(2,1)S(1)} collective-permute-done((bf16[224,128]{1,0:T(8,128)(2,1)S(1)}, bf16[224,128]{1,0:T(8,128)(2,1)S(1)}, u32[]{:S(2)}, u32[]{:S(2)}) %collective-permute-start.18) | collective-permute-done | bytes 57376 | tf_op jit(solution)/shard_map/ppermute | solution.py:1063
  114.9 4.7 %collective-permute-done.19 = bf16[448,128]{1,0:T(8,128)(2,1)S(1)} collective-permute-done((bf16[448,128]{1,0:T(8,128)(2,1)S(1)}, bf16[448,128]{1,0:T(8,128)(2,1)S(1)}, u32[]{:S(2)}, u32[]{:S(2)}) %collective-permute-start.19) | collective-permute-done | bytes 114720 | tf_op jit(solution)/shard_map/ppermute | solution.py:1063
  120.4 4.1 %collective-permute-done.23 = bf16[448,128]{1,0:T(8,128)(2,1)S(1)} collective-permute-done((bf16[448,128]{1,0:T(8,128)(2,1)S(1)}, bf16[448,128]{1,0:T(8,128)(2,1)S(1)}, u32[]{:S(2)}, u32[]{:S(2)}) %collective-permute-start.23) | collective-permute-done | bytes 114720 | tf_op jit(solution)/shard_map/ppermute | solution.py:1063
  124.5 0.6 collective-permute-start.24
  125.2 1.5 %collective-permute-start.21 = (bf16[896,128]{1,0:T(8,128)(2,1)S(1)}, bf16[896,128]{1,0:T(8,128)(2,1)S(1)}, u32[]{:S(2)}, u32[]{:S(2)}) collective-permute-start(bf16[896,128]{1,0:T(8,128)(2,1)S(1)} %maximum_select_fusion.4), channel_id=1, source_target_pairs={{0,4},{1,5},{2,6},{3,7},{4,0},{5,1},{6,2},{7,3},{8,12},{9,13},{10,... | collective-permute-start | bytes 688136 | tf_op jit(solution)/shard_map/ppermute | solution.py:1063
  126.7 3.9 %collective-permute-done.24 = bf16[896,128]{1,0:T(8,128)(2,1)S(1)} collective-permute-done((bf16[896,128]{1,0:T(8,128)(2,1)S(1)}, bf16[896,128]{1,0:T(8,128)(2,1)S(1)}, u32[]{:S(2)}, u32[]{:S(2)}) %collective-permute-start.24) | collective-permute-done | bytes 229408 | tf_op jit(solution)/shard_map/ppermute | solution.py:1063
  131.5 1.1 collective-permute-done.25
  134.6 0.8 copy-done.3
  135.4 0.7 copy-done.2
  136.1 0.6 copy-done.1
  136.7 9.4 %shard_map.313 = (f32[1,1]{1,0:T(1,128)}, f32[1,1]{1,0:T(1,128)}, f32[24,128]{1,0:T(8,128)}, f32[24,128]{1,0:T(8,128)}, f32[24,128]{1,0:T(8,128)}, /*index=5*/f3...) custom-call(f32[1,128]{1,0:T(1,128)S(1)} %add.230.count_ref, ...), custom_call_target="tpu_custom_call" | custom-call | flops 100000000 | bytes 20594184 | tf_op jit(solution)/shard_map/pallas_call | solution.py:656
  (150 shorter events, 7.2 us)
Async XLA Ops:
  3.3 8.7 %collective-permute-start.2 = (bf16[224,128]{1,0:T(8,128)(2,1)S(1)}, bf16[224,128]{1,0:T(8,128)(2,1)S(1)}, u32[]{:S(2)}, u32[]{:S(2)}) collective-permute-start(bf16[224,128]{1,0:T(8,128)(2,1)S(1)} %get-tuple-element.120), channel_id=1, source_target_pairs={{0,3},{1,2},{2,1},{3,0},{4,7},{5,6},{6,5},{7,4},{8,11},{9,10},{10,... | collective-permute-start | bytes 172040 | tf_op jit(solution)/shard_map/ppermute | solution.py:1082
  5.8 6.2 %collective-permute-start.1 = (bf16[224,128]{1,0:T(8,128)(2,1)S(1)}, bf16[224,128]{1,0:T(8,128)(2,1)S(1)}, u32[]{:S(2)}, u32[]{:S(2)}) collective-permute-start(bf16[224,128]{1,0:T(8,128)(2,1)S(1)} %get-tuple-element.118), channel_id=1, source_target_pairs={{0,2},{1,3},{2,0},{3,1},{4,6},{5,7},{6,4},{7,5},{8,10},{9,11},{10,... | collective-permute-start | bytes 172040 | tf_op jit(solution)/shard_map/ppermute | solution.py:1082
  6.4 5.6 %collective-permute-start = (bf16[224,128]{1,0:T(8,128)(2,1)S(1)}, bf16[224,128]{1,0:T(8,128)(2,1)S(1)}, u32[]{:S(2)}, u32[]{:S(2)}) collective-permute-start(bf16[224,128]{1,0:T(8,128)(2,1)S(1)} %get-tuple-element.116), channel_id=1, source_target_pairs={{0,1},{1,0},{2,3},{3,2},{4,5},{5,4},{6,7},{7,6},{8,9},{9,8},{10,11... | collective-permute-start | bytes 172040 | tf_op jit(solution)/shard_map/ppermute | solution.py:1082
  7.2 1.6 %copy-start = (f32[2,512,512]{2,1,0:T(8,128)S(1)}, f32[2,512,512]{2,1,0:T(8,128)}, u32[]{:S(2)}) copy-start(f32[2,512,512]{2,1,0:T(8,128)} %middle_ref.5) | copy-start | bytes 6291460
  10.9 2.9 %copy-start.13 = (f32[9,48,24]{1,2,0:T(8,128)S(1)}, f32[9,48,24]{1,2,0:T(8,128)}, u32[]{:S(2)}) copy-start(f32[9,48,24]{1,2,0:T(8,128)} %param.31) | copy-start | bytes 124420
  12.0 3.6 %collective-permute-start.3 = (f32[1,128]{1,0:T(1,128)S(1)}, f32[1,128]{1,0:T(1,128)S(1)}, u32[]{:S(2)}, u32[]{:S(2)}) collective-permute-start(f32[1,128]{1,0:T(1,128)S(1)} %convert_add_fusion), channel_id=1, source_target_pairs={{0,4},{1,5},{2,6},{3,7},{4,0},{5,1},{6,2},{7,3},{8,12},{9,13},{10,... | collective-permute-start | bytes 1544 | tf_op jit(solution)/shard_map/ppermute | solution.py:1063
  15.3 4.7 %copy-start.17 = (bf16[512,512]{1,0:T(8,128)(2,1)}, bf16[512,512]{1,0:T(8,128)(2,1)S(1)}, u32[]{:S(2)}) copy-start(bf16[512,512]{1,0:T(8,128)(2,1)S(1)} %get-tuple-element.156.wb_ref) | copy-start | bytes 1572868
  15.3 4.7 %copy-start.18 = (f32[512,1]{1,0:T(8,128)}, f32[512,1]{1,0:T(8,128)S(1)}, u32[]{:S(2)}) copy-start(f32[512,1]{1,0:T(8,128)S(1)} %get-tuple-element.158.bias_ref) | copy-start | bytes 6148
  15.3 4.7 %copy-start.20 = (bf16[512,72]{1,0:T(8,128)(2,1)}, bf16[512,72]{1,0:T(8,128)(2,1)S(1)}, u32[]{:S(2)}) copy-start(bf16[512,72]{1,0:T(8,128)(2,1)S(1)} %get-tuple-element.155.et_ref) | copy-start | bytes 221188
  15.3 4.7 %copy-start.21 = (bf16[288,64]{1,0:T(8,128)(2,1)}, bf16[288,64]{1,0:T(8,128)(2,1)S(1)}, u32[]{:S(2)}) copy-start(bf16[288,64]{1,0:T(8,128)(2,1)S(1)} %get-tuple-element.160.wpt_ref) | copy-start | bytes 110596
  15.3 4.7 %copy-start.22 = (bf16[64,288]{1,0:T(8,128)(2,1)}, bf16[64,288]{1,0:T(8,128)(2,1)S(1)}, u32[]{:S(2)}) copy-start(bf16[64,288]{1,0:T(8,128)(2,1)S(1)} %get-tuple-element.159.wp_ref) | copy-start | bytes 110596
  15.3 4.7 %copy-start.23 = (f32[64,1]{1,0:T(8,128)}, f32[64,1]{1,0:T(8,128)S(1)}, u32[]{:S(2)}) copy-start(f32[64,1]{1,0:T(8,128)S(1)} %get-tuple-element.123.pbias_ref) | copy-start | bytes 772
  15.7 5.1 %collective-permute-start.4 = (f32[1,128]{1,0:T(1,128)S(1)}, f32[1,128]{1,0:T(1,128)S(1)}, u32[]{:S(2)}, u32[]{:S(2)}) collective-permute-start(f32[1,128]{1,0:T(1,128)S(1)} %add.228), channel_id=1, source_target_pairs={{0,8},{1,9},{2,10},{3,11},{4,12},{5,13},{6,14},{7,15},{8,0},{9,1},... | collective-permute-start | bytes 1544 | tf_op jit(solution)/shard_map/ppermute | solution.py:1063
  20.7 5.3 %copy-start.24 = (f32[16,8192]{1,0:T(8,128)}, f32[16,8192]{1,0:T(8,128)S(1)}, u32[]{:S(2)}) copy-start(f32[16,8192]{1,0:T(8,128)S(1)} %get-tuple-element.152.mix1_ref) | copy-start | bytes 1572868
  20.7 5.3 %collective-permute-start.5 = (f32[1,128]{1,0:T(1,128)S(1)}, f32[1,128]{1,0:T(1,128)S(1)}, u32[]{:S(2)}, u32[]{:S(2)}) collective-permute-start(f32[1,128]{1,0:T(1,128)S(1)} %add.229), channel_id=1, source_target_pairs={{0,16},{1,17},{2,18},{3,19},{4,20},{5,21},{6,22},{7,23},{8,24},{9,... | collective-permute-start | bytes 1544 | tf_op jit(solution)/shard_map/ppermute | solution.py:1063
  34.9 12.6 %collective-permute-start.6 = (f32[1792,128]{1,0:T(8,128)S(1)}, f32[1792,128]{1,0:T(8,128)}, u32[]{:S(2)}, u32[]{:S(2)}) collective-permute-start(f32[1792,128]{1,0:T(8,128)S(1)} %get-tuple-element.151), channel_id=1, source_target_pairs={{0,1},{1,0},{2,3},{3,2},{4,5},{5,4},{6,7},{7,6},{8,9},{9,8},{10,11... | collective-permute-start | bytes 2752520 | tf_op jit(solution)/shard_map/ppermute | solution.py:1063
  48.9 17.8 %collective-permute-start.7 = (f32[896,128]{1,0:T(8,128)S(1)}, f32[896,128]{1,0:T(8,128)S(1)}, u32[]{:S(2)}, u32[]{:S(2)}) collective-permute-start(f32[896,128]{1,0:T(8,128)S(1)} %constant_dynamic-slice_fusion.18), channel_id=1, source_target_pairs={{0,4},{1,5},{2,6},{3,7},{4,0},{5,1},{6,2},{7,3},{8,12},{9,13},{10,... | collective-permute-start | bytes 1376264 | tf_op jit(solution)/shard_map/ppermute | solution.py:1063
  64.6 14.2 %collective-permute-start.11 = (f32[640,128]{1,0:T(8,128)S(1)}, f32[640,128]{1,0:T(8,128)S(1)}, u32[]{:S(2)}, u32[]{:S(2)}) collective-permute-start(f32[640,128]{1,0:T(8,128)S(1)} %get-tuple-element.185), channel_id=1, source_target_pairs={{0,2},{1,3},{2,0},{3,1},{4,6},{5,7},{6,4},{7,5},{8,10},{9,11},{10,... | collective-permute-start | bytes 983048 | tf_op jit(solution)/shard_map/ppermute | solution.py:1063
  66.1 12.7 %collective-permute-start.10 = (f32[768,128]{1,0:T(8,128)S(1)}, f32[768,128]{1,0:T(8,128)S(1)}, u32[]{:S(2)}, u32[]{:S(2)}) collective-permute-start(f32[768,128]{1,0:T(8,128)S(1)} %get-tuple-element.182), channel_id=1, source_target_pairs={{0,4},{1,5},{2,6},{3,7},{4,0},{5,1},{6,2},{7,3},{8,12},{9,13},{10,... | collective-permute-start | bytes 1179656 | tf_op jit(solution)/shard_map/ppermute | solution.py:1063
  66.8 12.2 %collective-permute-start.8 = (f32[448,128]{1,0:T(8,128)S(1)}, f32[448,128]{1,0:T(8,128)S(1)}, u32[]{:S(2)}, u32[]{:S(2)}) collective-permute-start(f32[448,128]{1,0:T(8,128)S(1)} %constant_dynamic-slice_fusion.17), channel_id=1, source_target_pairs={{0,8},{1,9},{2,10},{3,11},{4,12},{5,13},{6,14},{7,15},{8,0},{9,1},... | collective-permute-start | bytes 688136 | tf_op jit(solution)/shard_map/ppermute | solution.py:1063
  79.1 5.7 %collective-permute-start.12 = (f32[832,128]{1,0:T(8,128)S(1)}, f32[832,128]{1,0:T(8,128)S(1)}, u32[]{:S(2)}, u32[]{:S(2)}) collective-permute-start(f32[832,128]{1,0:T(8,128)S(1)} %pad_maximum_fusion.1), channel_id=1, source_target_pairs={{0,1},{1,0},{2,3},{3,2},{4,5},{5,4},{6,7},{7,6},{8,9},{9,8},{10,11... | collective-permute-start | bytes 1277960 | tf_op jit(solution)/shard_map/ppermute | solution.py:1063
  79.2 5.6 %collective-permute-start.9 = (f32[224,128]{1,0:T(8,128)S(1)}, f32[224,128]{1,0:T(8,128)S(1)}, u32[]{:S(2)}, u32[]{:S(2)}) collective-permute-start(f32[224,128]{1,0:T(8,128)S(1)} %constant_dynamic-slice_fusion.16), channel_id=1, source_target_pairs={{0,2},{1,3},{2,0},{3,1},{4,6},{5,7},{6,4},{7,5},{8,10},{9,11},{10,... | collective-permute-start | bytes 344072 | tf_op jit(solution)/shard_map/ppermute | solution.py:1063
  84.9 4.5 %collective-permute-start.14 = (f32[160,128]{1,0:T(8,128)S(1)}, f32[160,128]{1,0:T(8,128)S(1)}, u32[]{:S(2)}, u32[]{:S(2)}) collective-permute-start(f32[160,128]{1,0:T(8,128)S(1)} %constant_dynamic-slice_fusion.8), channel_id=1, source_target_pairs={{0,4},{1,5},{2,6},{3,7},{4,0},{5,1},{6,2},{7,3},{8,12},{9,13},{10,... | collective-permute-start | bytes 245768 | tf_op jit(solution)/shard_map/ppermute | solution.py:1063
  86.5 5.0 %collective-permute-start.13 = (f32[256,128]{1,0:T(8,128)S(1)}, f32[256,128]{1,0:T(8,128)S(1)}, u32[]{:S(2)}, u32[]{:S(2)}) collective-permute-start(f32[256,128]{1,0:T(8,128)S(1)} %pad_maximum_fusion.2), channel_id=1, source_target_pairs={{0,2},{1,3},{2,0},{3,1},{4,6},{5,7},{6,4},{7,5},{8,10},{9,11},{10,... | collective-permute-start | bytes 393224 | tf_op jit(solution)/shard_map/ppermute | solution.py:1063
  91.6 3.8 %collective-permute-start.15 = (f32[32,128]{1,0:T(8,128)S(1)}, f32[32,128]{1,0:T(8,128)S(1)}, u32[]{:S(2)}, u32[]{:S(2)}) collective-permute-start(f32[32,128]{1,0:T(8,128)S(1)} %constant_dynamic-slice_fusion.6), channel_id=1, source_target_pairs={{0,4},{1,5},{2,6},{3,7},{4,0},{5,1},{6,2},{7,3},{8,12},{9,13},{10,... | collective-permute-start | bytes 49160 | tf_op jit(solution)/shard_map/ppermute | solution.py:1063
  95.4 5.8 %collective-permute-start.16 = (f32[192,128]{1,0:T(8,128)S(1)}, f32[192,128]{1,0:T(8,128)S(1)}, u32[]{:S(2)}, u32[]{:S(2)}) collective-permute-start(f32[192,128]{1,0:T(8,128)S(1)} %pad_maximum_fusion.7), channel_id=1, source_target_pairs={{0,8},{1,9},{2,10},{3,11},{4,12},{5,13},{6,14},{7,15},{8,0},{9,1},... | collective-permute-start | bytes 294920 | tf_op jit(solution)/shard_map/ppermute | solution.py:1063
  101.3 7.4 %collective-permute-start.17 = (f32[208,128]{1,0:T(8,128)S(1)}, f32[208,128]{1,0:T(8,128)S(1)}, u32[]{:S(2)}, u32[]{:S(2)}) collective-permute-start(f32[208,128]{1,0:T(8,128)S(1)} %pad_maximum_fusion.6), channel_id=1, source_target_pairs={{0,16},{1,17},{2,18},{3,19},{4,20},{5,21},{6,22},{7,23},{8,24},{9,... | collective-permute-start | bytes 319496 | tf_op jit(solution)/shard_map/ppermute | solution.py:1063
  108.8 22.0 %copy-start.27 = (f32[2960]{0:T(1024)S(1)}, f32[2960]{0:T(1024)}, u32[]{:S(2)}) copy-start(f32[2960]{0:T(1024)} %param.21) | copy-start | bytes 35524
  108.8 22.0 %copy-start.28 = (f32[2960]{0:T(1024)S(1)}, f32[2960]{0:T(1024)}, u32[]{:S(2)}) copy-start(f32[2960]{0:T(1024)} %param.20) | copy-start | bytes 35524
  109.0 5.6 %collective-permute-start.18 = (bf16[224,128]{1,0:T(8,128)(2,1)S(1)}, bf16[224,128]{1,0:T(8,128)(2,1)S(1)}, u32[]{:S(2)}, u32[]{:S(2)}) collective-permute-start(bf16[224,128]{1,0:T(8,128)(2,1)S(1)} %get-tuple-element.226), channel_id=1, source_target_pairs={{0,16},{1,17},{2,18},{3,19},{4,20},{5,21},{6,22},{7,23},{8,24},{9,... | collective-permute-start | bytes 172040 | tf_op jit(solution)/shard_map/ppermute | solution.py:1063
  114.7 4.9 %collective-permute-start.19 = (bf16[448,128]{1,0:T(8,128)(2,1)S(1)}, bf16[448,128]{1,0:T(8,128)(2,1)S(1)}, u32[]{:S(2)}, u32[]{:S(2)}) collective-permute-start(bf16[448,128]{1,0:T(8,128)(2,1)S(1)} %pad_maximum_fusion.4), channel_id=1, source_target_pairs={{0,8},{1,9},{2,10},{3,11},{4,12},{5,13},{6,14},{7,15},{8,0},{9,1},... | collective-permute-start | bytes 344072 | tf_op jit(solution)/shard_map/ppermute | solution.py:1063
  119.6 4.9 %collective-permute-start.23 = (bf16[448,128]{1,0:T(8,128)(2,1)S(1)}, bf16[448,128]{1,0:T(8,128)(2,1)S(1)}, u32[]{:S(2)}, u32[]{:S(2)}) collective-permute-start(bf16[448,128]{1,0:T(8,128)(2,1)S(1)} %fusion.1), channel_id=1, source_target_pairs={{0,4},{1,5},{2,6},{3,7},{4,0},{5,1},{6,2},{7,3},{8,12},{9,13},{10,... | collective-permute-start | bytes 344072 | tf_op jit(solution)/shard_map/ppermute | solution.py:1063
  119.8 5.3 %collective-permute-start.20 = (bf16[448,128]{1,0:T(8,128)(2,1)S(1)}, bf16[448,128]{1,0:T(8,128)(2,1)S(1)}, u32[]{:S(2)}, u32[]{:S(2)}) collective-permute-start(bf16[448,128]{1,0:T(8,128)(2,1)S(1)} %fusion), channel_id=1, source_target_pairs={{0,2},{1,3},{2,0},{3,1},{4,6},{5,7},{6,4},{7,5},{8,10},{9,11},{10,... | collective-permute-start | bytes 344072 | tf_op jit(solution)/shard_map/ppermute | solution.py:1063
  124.5 6.1 %collective-permute-start.24 = (bf16[896,128]{1,0:T(8,128)(2,1)S(1)}, bf16[896,128]{1,0:T(8,128)(2,1)S(1)}, u32[]{:S(2)}, u32[]{:S(2)}) collective-permute-start(bf16[896,128]{1,0:T(8,128)(2,1)S(1)} %maximum_select_fusion.5), channel_id=1, source_target_pairs={{0,2},{1,3},{2,0},{3,1},{4,6},{5,7},{6,4},{7,5},{8,10},{9,11},{10,... | collective-permute-start | bytes 688136 | tf_op jit(solution)/shard_map/ppermute | solution.py:1063
  125.2 6.1 %collective-permute-start.21 = (bf16[896,128]{1,0:T(8,128)(2,1)S(1)}, bf16[896,128]{1,0:T(8,128)(2,1)S(1)}, u32[]{:S(2)}, u32[]{:S(2)}) collective-permute-start(bf16[896,128]{1,0:T(8,128)(2,1)S(1)} %maximum_select_fusion.4), channel_id=1, source_target_pairs={{0,4},{1,5},{2,6},{3,7},{4,0},{5,1},{6,2},{7,3},{8,12},{9,13},{10,... | collective-permute-start | bytes 688136 | tf_op jit(solution)/shard_map/ppermute | solution.py:1063
  130.6 3.2 %copy-start.15 = (f32[9,48,24]{1,2,0:T(8,128)S(1)}, f32[9,48,24]{1,2,0:T(8,128)}, u32[]{:S(2)}) copy-start(f32[9,48,24]{1,2,0:T(8,128)} %param.33) | copy-start | bytes 124420
  130.7 1.9 %collective-permute-start.25 = (bf16[1792,128]{1,0:T(8,128)(2,1)S(1)}, bf16[1792,128]{1,0:T(8,128)(2,1)S(1)}, u32[]{:S(2)}, u32[]{:S(2)}) collective-permute-start(bf16[1792,128]{1,0:T(8,128)(2,1)S(1)} %maximum_select_fusion.3), channel_id=1, source_target_pairs={{0,1},{1,0},{2,3},{3,2},{4,5},{5,4},{6,7},{7,6},{8,9},{9,8},{10,11... | collective-permute-start | bytes 1376264 | tf_op jit(solution)/shard_map/ppermute | solution.py:1063
  131.4 1.9 %collective-permute-start.22 = (bf16[1792,128]{1,0:T(8,128)(2,1)S(1)}, bf16[1792,128]{1,0:T(8,128)(2,1)S(1)}, u32[]{:S(2)}, u32[]{:S(2)}) collective-permute-start(bf16[1792,128]{1,0:T(8,128)(2,1)S(1)} %maximum_select_fusion.2), channel_id=1, source_target_pairs={{0,1},{1,0},{2,3},{3,2},{4,5},{5,4},{6,7},{7,6},{8,9},{9,8},{10,11... | collective-permute-start | bytes 1376264 | tf_op jit(solution)/shard_map/ppermute | solution.py:1063
  132.6 1.2 copy-start.7
  132.6 1.2 copy-start.9
  132.6 1.4 copy-start.10
  132.6 1.5 %copy-start.11 = (f32[9,18,512]{2,1,0:T(8,128)S(1)}, f32[9,18,512]{2,1,0:T(8,128)}, u32[]{:S(2)}) copy-start(f32[9,18,512]{2,1,0:T(8,128)} %entry_second.1) | copy-start | bytes 995332
  132.9 1.5 %copy-start.5 = (f32[9,36,512]{2,1,0:T(8,128)S(1)}, f32[9,36,512]{2,1,0:T(8,128)}, u32[]{:S(2)}) copy-start(f32[9,36,512]{2,1,0:T(8,128)} %exit_ref.5) | copy-start | bytes 1990660
  132.9 1.8 %copy-start.6 = (f32[9,36,512]{2,1,0:T(8,128)S(1)}, f32[9,36,512]{2,1,0:T(8,128)}, u32[]{:S(2)}) copy-start(f32[9,36,512]{2,1,0:T(8,128)} %exit_first.1) | copy-start | bytes 1990660
  133.3 2.2 %copy-start.3 = (f32[2,512,512]{2,1,0:T(8,128)S(1)}, f32[2,512,512]{2,1,0:T(8,128)}, u32[]{:S(2)}) copy-start(f32[2,512,512]{2,1,0:T(8,128)} %middle_second.1) | copy-start | bytes 6291460
  133.5 2.6 %copy-start.2 = (f32[2,512,512]{2,1,0:T(8,128)S(1)}, f32[2,512,512]{2,1,0:T(8,128)}, u32[]{:S(2)}) copy-start(f32[2,512,512]{2,1,0:T(8,128)} %middle_first.1) | copy-start | bytes 6291460
  133.6 3.1 %copy-start.1 = (f32[2,512,512]{2,1,0:T(8,128)S(1)}, f32[2,512,512]{2,1,0:T(8,128)}, u32[]{:S(2)}) copy-start(f32[2,512,512]{2,1,0:T(8,128)} %middle_ref.5) | copy-start | bytes 6291460
  133.6 3.1 %copy-start.14 = (f32[9,48,24]{1,2,0:T(8,128)S(1)}, f32[9,48,24]{1,2,0:T(8,128)}, u32[]{:S(2)}) copy-start(f32[9,48,24]{1,2,0:T(8,128)} %param.32) | copy-start | bytes 124420
  (7 other events, 6.0 us)

commit v4 on v3

--- a/solution.py
+++ b/solution.py
@@ -59,8 +59,6 @@
 
 def pack_kernel(bands, index_ref, pixels_ref, mask_ref, *out_refs):
     own = index_ref[0]
-    count = jnp.sum(mask_ref[...].astype(F32), axis=0, keepdims=True)
-    count = jnp.where(lax.broadcasted_iota(jnp.int32, (16, 1), 0) == 0, count, 0.0).astype(BF16)
     width = LANES // bands
     rows = pixels_ref.shape[0] // bands
     extra = mask_ref.shape[0] // bands
@@ -75,7 +73,6 @@
                 shift = lax.rem(e - target + bands, bands) * width
                 total = jnp.where(band == e, pltpu.roll(source[e], shift, 1), total)
             out_ref[first : first + size, :] = total.astype(BF16)
-        out_ref[rows + extra :, :] = count
 
 
 def fill_ext(ext_ref, field, rows, cols, bands, pattern):
@@ -179,10 +176,6 @@
     for start in range(LANES, value.shape[1], LANES):
         total = total + value[:, start : start + LANES]
     return total
-
-
-def coef_of(count_ref):
-    return -1.0 / (CH * jnp.sum(count_ref[...], keepdims=True) * math.log(2.0))
 
 
 def unpack_kernel(
@@ -318,8 +311,8 @@
 
 def couple_two_backward(
     dims,
+    bits,
     index_ref,
-    count_ref,
     mask2_ref,
     y2_ref,
     out2_ref,
@@ -332,8 +325,10 @@
     e_ref,
     wbt_ref,
     ft_ref,
-    kept_ref,
-    sent_ref,
+    kept_u,
+    sent_u,
+    kept_v,
+    sent_v,
     gkeep_ref,
     ext,
     gacc,
@@ -345,9 +340,7 @@
     slab_ref,
 ):
     rows, cols, bands = dims
-    coef = coef_of(count_ref)
-    mask2 = mask2_ref[...]
-    weight = coef * mask2
+    weight = -mask2_ref[...]
     second = t2_ref[...]
     result = out2_ref[16:, :]
     g_result = -weight * result
@@ -397,15 +390,82 @@
     gram(g_mixed, y2_ref, pairs, acc)
     stack = [(j, acc[j]) for j in pairs] + [(32, fold_lanes(g_mixed)), (33, out_sums)]
     slab_ref[TWO_SMALL : TWO_SMALL + 32, :] = lane_sums(stack, 32)
-    part_out(slab_ref, 0, TWO_ROWS, index_ref[1], 1, kept_ref, sent_ref)
+    part_out(slab_ref, 0, TWO_ROWS // 2, index_ref[1], bits[0], kept_u, sent_u)
+    part_out(slab_ref, TWO_ROWS // 2, TWO_ROWS // 2, index_ref[1], bits[1], kept_v, sent_v)
     valid_rows = [j for j in range(32) if j % 16 < CH]
     gkeep_ref[...] = mix(m2t_ref, gmix, 0, rows * chunk, valid_rows) * chan2_ref[:, 1:2]
+
+
+def level_two_kernel(
+    dims,
+    bits,
+    index_ref,
+    b0,
+    b1,
+    b2,
+    b3,
+    chan1_ref,
+    m1_ref,
+    chan2_ref,
+    m2_ref,
+    m2t_ref,
+    e_ref,
+    et_ref,
+    f_ref,
+    ft_ref,
+    wb_ref,
+    wbt_ref,
+    bias_ref,
+    y1_ref,
+    mix1_ref,
+    mask_ref,
+    mask2_ref,
+    keep_ref,
+    loss_ref,
+    gkeep_ref,
+    kept_u,
+    sent_u,
+    kept_v,
+    sent_v,
+    bufs,
+    xs,
+    y2,
+    mix2,
+    out2,
+    t2,
+    xcol,
+    h1,
+    h2,
+    ext_in,
+    oacc,
+    ext_out,
+    gacc,
+    gmix,
+    bacc,
+    ge,
+    gf,
+    acc,
+    slab,
+):
+    rows, cols, bands = dims
+    half = (rows // 2, cols // 2, bands)
+    unpack_kernel(
+        dims, index_ref, b0, b1, b2, b3, chan1_ref, m1_ref, chan2_ref, m2_ref,
+        y1_ref, mix1_ref, mask_ref, mask2_ref, keep_ref, y2, mix2, bufs, xs,
+    )
+    couple_two_forward(
+        half, mix2, mask_ref, mask2_ref, chan2_ref, et_ref, wb_ref, f_ref, bias_ref,
+        out2, t2, xcol, h1, h2, loss_ref, ext_in, oacc,
+    )
+    couple_two_backward(
+        half, bits, index_ref, mask2_ref, y2, out2, t2, xcol, h1, h2, chan2_ref, m2t_ref, e_ref, wbt_ref, ft_ref,
+        kept_u, sent_u, kept_v, sent_v, gkeep_ref, ext_out, gacc, gmix, bacc, ge, gf, acc, slab,
+    )
 
 
 def couple_one_forward(
     dims,
     chunk,
-    count_ref,
     mix1_ref,
     mask_ref,
     mask2_ref,
@@ -476,7 +536,7 @@
     fill_ext(kext, keep_ref[...] + part_ones, half_rows, half_cols, bands, part_ones)
     part_line = half_cols * LANES
     gkacc[...] = jnp.zeros_like(gkacc)
-    weight = coef_of(count_ref) * mask2_ref[...]
+    weight = -mask2_ref[...]
     valid = row_mask(32, 8, CH // 2)
     prior_total = None
     for i in range(half_rows):
@@ -538,7 +598,6 @@
     chunk,
     bits,
     index_ref,
-    count_ref,
     mask_ref,
     res_ref,
     t_ref,
@@ -562,7 +621,7 @@
     slab_ref,
 ):
     rows, cols, bands = dims
-    weight = coef_of(count_ref) * mask_ref[...]
+    weight = -mask_ref[...]
     second = t_ref[...]
     result = res_ref[...]
     g_result = gout_ref[8:16, :]
@@ -602,7 +661,7 @@
             :, block * LANES : block * LANES + width
         ]
     slab_ref[ONE_LOSS : ONE_LOSS + 1, :] = loss_one_ref[0:1, :] + loss_two_ref[0:1, :]
-    slab_ref[ONE_LOSS + 1 : ONE_LOSS + 2, :] = loss_two_ref[1:2, :]
+    slab_ref[ONE_LOSS + 1 : ONE_LOSS + 3, :] = loss_two_ref[1:3, :]
     part_out(slab_ref, 0, PART_A, index_ref[1], bits[0], kept_a, sent_a)
     part_out(slab_ref, PART_A, ONE_ROWS - PART_A, index_ref[1], bits[1], kept_b, sent_b)
 
@@ -649,15 +708,18 @@
     put_rows(slab_ref, lambda block: REST_A + block, ge, 6, 1)
 
 
-def call(kernel, inputs, outputs, scratch, flops, aliases=None):
+def call(kernel, inputs, outputs, scratch, flops, aliases=None, far_in=(), far_out=()):
     whole = pl.BlockSpec(memory_space=pltpu.VMEM)
     smem = pl.BlockSpec(memory_space=pltpu.SMEM)
+    far = pl.BlockSpec(memory_space=pl.ANY)
     traffic = sum(x.size * x.dtype.itemsize for x in list(inputs) + list(outputs))
     return pl.pallas_call(
         kernel,
         out_shape=outputs,
-        in_specs=[smem if x.dtype == jnp.int32 and x.ndim == 1 else whole for x in inputs],
-        out_specs=[whole for _ in outputs],
+        in_specs=[
+            far if k in far_in else smem if x.dtype == jnp.int32 and x.ndim == 1 else whole for k, x in enumerate(inputs)
+        ],
+        out_specs=[far if k in far_out else whole for k in range(len(outputs))],
         scratch_shapes=scratch,
         input_output_aliases=aliases or {},
         compiler_params=pltpu.CompilerParams(vmem_limit_bytes=VMEM_LIMIT),
@@ -787,10 +849,32 @@
     wbt_ref[...] = middle_ref[level].T.astype(BF16)
 
 
-def prepare_two_kernel(
-    flat_ref, entry_ref, middle_ref, exit_ref, chan1_ref, m1_ref, chan2_ref, m2_ref, m2t_ref, *rest
+def prepare_kernel(
+    flat_ref,
+    prior_ref,
+    entry_far,
+    middle_far,
+    exit_far,
+    chan1_ref,
+    m1_ref,
+    chan2_ref,
+    m2_ref,
+    m2t_ref,
+    wp_ref,
+    wpt_ref,
+    pbias_ref,
+    *refs,
 ):
-    outs, (lu, wide) = rest[:-2], rest[-2:]
+    outs_two, outs_one = refs[:7], refs[7:14]
+    lu, wide, entry_ref, middle_ref, exit_ref, sems = refs[14:]
+    copies = [
+        pltpu.make_async_copy(middle_far.at[1], middle_ref.at[1], sems.at[0]),
+        pltpu.make_async_copy(exit_far, exit_ref, sems.at[1]),
+        pltpu.make_async_copy(entry_far, entry_ref, sems.at[2]),
+        pltpu.make_async_copy(middle_far.at[0], middle_ref.at[0], sems.at[3]),
+    ]
+    for copy in copies:
+        copy.start()
     for level in range(2):
         chans, start, chan, lower, upper = level_tables(flat_ref, level, lu)
         product = high_dot(lower, upper)
@@ -818,12 +902,6 @@
         chan_ref[...] = (
             jnp.where(lane == 0, shift, 0.0) + jnp.where(lane == 1, scale, 0.0) + jnp.where(lane == 2, out_bias, 0.0)
         )
-    prepare_level(1, flat_ref, entry_ref, middle_ref, exit_ref, outs, wide)
-
-
-def prepare_one_kernel(flat_ref, entry_ref, middle_ref, exit_ref, prior_ref, wp_ref, wpt_ref, pbias_ref, *rest):
-    outs, (lu, wide) = rest[:-2], rest[-2:]
-    prepare_level(0, flat_ref, entry_ref, middle_ref, exit_ref, outs, wide)
     places = prior_places()
     blocks = [None] * 3
     for tap in range(9):
@@ -841,6 +919,11 @@
     row, lane = iotas(64)
     natural, valid = natural_keep(lax.rem(row, 32))
     pbias_ref[...] = pick((lane == natural + (row // 32) * 2 * CH) & valid, take_flat(flat_ref, PRIOR_START, 4 * CH))
+    for copy in copies[:3]:
+        copy.wait()
+    prepare_level(1, flat_ref, entry_ref, middle_ref, exit_ref, outs_two, wide)
+    copies[3].wait()
+    prepare_level(0, flat_ref, entry_ref, middle_ref, exit_ref, outs_one, wide)
 
 
 def adamw(weight, grad, first, second):
@@ -853,7 +936,6 @@
 
 
 def finish_kernel(
-    count_ref,
     two_ref,
     one_ref,
     rest_ref,
@@ -861,48 +943,46 @@
     flat_ref,
     flat_first,
     flat_second,
-    entry_ref,
-    entry_first,
-    entry_second,
-    middle_ref,
-    middle_first,
-    middle_second,
-    exit_ref,
-    exit_first,
-    exit_second,
-    prior_ref,
-    prior_first,
-    prior_second,
-    loss_ref,
-    norm_ref,
-    flat_new,
-    flat_grad,
-    flat_moment,
-    entry_new,
-    entry_grad,
-    entry_moment,
-    middle_new,
-    middle_grad,
-    middle_moment,
-    exit_new,
-    exit_grad,
-    exit_moment,
-    prior_new,
-    prior_grad,
-    prior_moment,
-    bias_ref,
-    two,
-    one,
-    rest,
-    lu,
+    *refs,
 ):
-    two[...] = two_ref[WB_ROWS:, :].astype(F32)
-    one[...] = one_ref[WB_ROWS:, :].astype(F32)
-    rest[...] = rest_ref[...].astype(F32)
+    far_in, refs = refs[:12], refs[12:]
+    (loss_ref, norm_ref, flat_new, flat_grad, flat_moment), refs = refs[:5], refs[5:]
+    far_out, refs = refs[:12], refs[12:]
+    bias_ref, two, one, rest, lu = refs[:5]
+    held, (in_sems, out_sems) = refs[5:21], refs[21:]
+    weights, firsts, seconds, grads = held[0:4], held[4:8], held[8:12], held[12:16]
+    entry_grad, _, exit_grad, prior_grad = grads
+    jobs = [(1, 0), (1, 1), (2, None), (0, None), (3, None)]
+
+    def part(ref, level):
+        return ref if level is None else ref.at[level]
+
+    def copies_in(k):
+        group, level = jobs[k]
+        return [
+            pltpu.make_async_copy(part(far_in[3 * group + j], level), part(near[group], level), in_sems.at[k, j])
+            for j, near in enumerate((weights, firsts, seconds))
+        ]
+
+    def copies_out(k):
+        group, level = jobs[k]
+        return [
+            pltpu.make_async_copy(part(near[group], level), part(far_out[3 * group + j], level), out_sems.at[k, j])
+            for j, near in enumerate((weights, grads, seconds))
+        ]
+
+    for k in range(len(jobs)):
+        for copy in copies_in(k):
+            copy.start()
     extra = extra_ref[...].astype(F32)
+    count = jnp.sum(extra[6:9], keepdims=True)
+    coef = -1.0 / (CH * count * math.log(2.0))
+    factor = -coef
+    two[...] = two_ref[WB_ROWS:, :].astype(F32) * factor
+    one[...] = one_ref[WB_ROWS:, :].astype(F32) * factor
+    rest[...] = rest_ref[...].astype(F32) * factor
     log_total = jnp.sum(extra[0:3], keepdims=True)
     count_two = jnp.sum(extra[3:6], keepdims=True)
-    coef, count = coef_of(count_ref), jnp.sum(count_ref[...], keepdims=True)
     base = WB_ROWS
     squares = []
     pieces = {}
@@ -974,10 +1054,9 @@
             exit_grad[tap, CH : 3 * CH, at] = two[first : first + 2 * CH, :]
     places = prior_places()
     for tap in range(9):
-        first = ONE_P - base + (tap * 32 // LANES) * 64
-        block = one[first : first + 64, :].astype(BF16)
-        moved = dot_nt(prior_lanes(tap), block).astype(BF16)
-        prior_grad[tap, :, :] = dot(moved, places)
+        first = ONE_P + (tap * 32 // LANES) * 64
+        moved = dot_nt(prior_lanes(tap), one_ref[first : first + 64, :]).astype(BF16)
+        prior_grad[tap, :, :] = dot(moved, places) * factor
     for ref in (flat_grad, entry_grad, exit_grad, prior_grad):
         value = ref[...]
         squares.append(jnp.sum(value * value, keepdims=True).reshape(1, 1))
@@ -986,7 +1065,7 @@
         for start in range(0, WB_ROWS, 64):
             value = ref[start : start + 64, :].astype(F32)
             total = total + value * value
-        squares.append(jnp.sum(total, keepdims=True))
+        squares.append(jnp.sum(total, keepdims=True) * factor * factor)
     norm = jnp.sqrt(functools.reduce(jnp.add, squares))
     clip = jnp.minimum(1.0, CLIP_NORM / (norm + 1e-06))
     total = log_total + consts[0] * count + count_two * (consts[1] - 2 * CH * LOG_TWO_PI)
@@ -994,38 +1073,37 @@
     norm_ref[...] = norm
     bias_ref[...] = bias_ref[...] * clip
 
-    def update(at, refs):
-        weight, first, second, new, grad, moment = refs
-        value = grad[at] * clip
-        grad[at] = value
-        new[at], moment[at] = adamw(weight[at], value, first[at], second[at])
-
-    update(..., (flat_ref, flat_first, flat_second, flat_new, flat_grad, flat_moment))
-    for tap in range(9):
-        update(tap, (entry_ref, entry_first, entry_second, entry_new, entry_grad, entry_moment))
-        update(tap, (exit_ref, exit_first, exit_second, exit_new, exit_grad, exit_moment))
-        update(tap, (prior_ref, prior_first, prior_second, prior_new, prior_grad, prior_moment))
+    middle_factor = factor * clip
+    value = flat_grad[...] * clip
+    flat_grad[...] = value
+    flat_new[...], flat_moment[...] = adamw(flat_ref[...], value, flat_first[...], flat_second[...])
     size = 64
-    for level, slab in enumerate((one_ref, two_ref)):
-
-        @pl.loop(0, HID // size)
-        def _(j):
-            rows = pl.ds(pl.multiple_of(j * size, size), size)
-            for block in range(HID // LANES):
-                at = (level, rows, slice(block * LANES, (block + 1) * LANES))
-                value = slab[pl.ds(pl.multiple_of(block * HID + j * size, size), size), :].astype(F32) * clip
-                middle_grad[at] = value
-                middle_new[at], middle_moment[at] = adamw(middle_ref[at], value, middle_first[at], middle_second[at])
-
-
-def total_over(value, axes):
-    for axis in axes:
-        size = lax.axis_size(axis)
-        distance = 1
-        while distance < size:
-            value = value + lax.ppermute(value, axis, [(i, i ^ distance) for i in range(size)])
-            distance *= 2
-    return value
+    for k, (group, level) in enumerate(jobs):
+        for copy in copies_in(k):
+            copy.wait()
+        weight, first, second, grad = weights[group], firsts[group], seconds[group], grads[group]
+        if level is None:
+            for tap in range(9):
+                value = grad[tap] * clip
+                grad[tap] = value
+                weight[tap], second[tap] = adamw(weight[tap], value, first[tap], second[tap])
+        else:
+            slab = (one_ref, two_ref)[level]
+
+            @pl.loop(0, HID // size)
+            def _(j):
+                rows = pl.ds(pl.multiple_of(j * size, size), size)
+                for block in range(HID // LANES):
+                    at = (level, rows, slice(block * LANES, (block + 1) * LANES))
+                    value = slab[pl.ds(pl.multiple_of(block * HID + j * size, size), size), :].astype(F32) * middle_factor
+                    grad[at] = value
+                    weight[at], second[at] = adamw(weight[at], value, first[at], second[at])
+
+        for copy in copies_out(k):
+            copy.start()
+    for k in range(len(jobs)):
+        for copy in copies_out(k):
+            copy.wait()
 
 
 def on_device(
@@ -1050,7 +1128,6 @@
     bands = lax.axis_size("rows")
     rows, cols = valid_mask.shape[0], valid_mask.shape[1]
     dims = (rows, cols, bands)
-    half_dims = (rows // 2, cols // 2, bands)
     size = rows * cols * LANES
     part = size // 4
     batches = lax.axis_size("batch")
@@ -1068,8 +1145,7 @@
     def after(value, *done):
         return lax.optimization_barrier((value, *done))[0]
 
-    pixel_rows = (CH + 1) * rows * cols // bands
-    piece_rows = pixel_rows + 16
+    piece_rows = (CH + 1) * rows * cols // bands
     pieces = call(
         functools.partial(pack_kernel, bands),
         (own, pixels.reshape(-1, LANES), valid_mask.reshape(-1, LANES)),
@@ -1097,72 +1173,62 @@
             shape((HID, 1)),
         ]
 
-    square, tall_scratch = pltpu.VMEM((LANES, LANES), F32), pltpu.VMEM((384, HID), F32)
-    rounds = iter(bits[bands.bit_length() - 1 :])
-
-    def count_round(value, beside):
-        bit = next(rounds, None)
-        return value if bit is None else value + after(trade(value, bit), beside)
-
-    chan_one, m_one, chan_two, m_two, m_two_t, e_two, e_two_t, f_two, f_two_t, wb_two, wb_two_t, bb_two = call(
-        prepare_two_kernel,
-        (after(vectors_flat, pieces[0]), entry_taps, middle, exit_taps),
+    prior_turned = jnp.swapaxes(prior_taps, 1, 2)
+    (
+        chan_one, m_one, chan_two, m_two, m_two_t, wp, wpt, prior_bias,
+        e_two, e_two_t, f_two, f_two_t, wb_two, wb_two_t, bb_two,
+        e_one, e_one_t, f_one, f_one_t, wb_one, wb_one_t, bb_one,
+    ) = call(
+        prepare_kernel,
+        (after(vectors_flat, pieces[0]), prior_turned, in_hbm(entry_taps), in_hbm(middle), in_hbm(exit_taps)),
         [shape((16, LANES)), shape((16, LANES)), shape((32, LANES)), shape((32, LANES)), shape((32, LANES))]
-        + level_shapes(16),
-        [square, tall_scratch],
+        + [shape((64, 288), BF16), shape((288, 64), BF16), shape((64, 1))]
+        + level_shapes(16)
+        + level_shapes(8),
+        [
+            pltpu.VMEM((LANES, LANES), F32),
+            pltpu.VMEM((384, HID), F32),
+            pltpu.VMEM(entry_taps.shape, F32),
+            pltpu.VMEM(middle.shape, F32),
+            pltpu.VMEM(exit_taps.shape, F32),
+            pltpu.SemaphoreType.DMA((4,)),
+        ],
         10**9,
-    )
-    bufs = [after(x, m_one) for x in bufs]
-    count = sum(x[pixel_rows : pixel_rows + 1].astype(F32) for x in bufs)
-    prior_turned = jnp.swapaxes(prior_taps, 1, 2)
-    wp, wpt, prior_bias, e_one, e_one_t, f_one, f_one_t, wb_one, wb_one_t, bb_one = call(
-        prepare_one_kernel,
-        (after(vectors_flat, count), entry_taps, middle, exit_taps, prior_turned),
-        [shape((64, 288), BF16), shape((288, 64), BF16), shape((64, 1))] + level_shapes(8),
-        [square, tall_scratch],
-        10**9,
-    )
-    count = count_round(count, prior_bias)
+        far_in=(2, 3, 4),
+    )
+
 
     ext_lanes = (rows // 2 + 2) * (cols // 2 + 2) * LANES
-    (y1, mixed_one, mask, mask2, keep, y2, mixed_two) = call(
-        functools.partial(unpack_kernel, dims),
-        (own, *bufs, after(chan_one, count), m_one, chan_two, m_two),
+    first_bit, second_bit, third_bit, fourth_bit = bits[0], bits[2], bits[1], bits[3]
+    quarter_two = shape((TWO_ROWS // 4, LANES))
+    (y1, mixed_one, mask, mask2, keep, loss_two, gkeep_two, kept_u, sent_u, kept_v, sent_v) = call(
+        functools.partial(level_two_kernel, dims, (second_bit, third_bit)),
+        (
+            own, *bufs, chan_one, m_one, chan_two, m_two, m_two_t,
+            e_two, e_two_t, f_two, f_two_t, wb_two, wb_two_t, bb_two,
+        ),
         [
             shape((16, size)),
             shape((16, size)),
             shape((1, size)),
             shape((1, part)),
             shape((32, part)),
+            shape((8, LANES)),
             shape((32, part)),
-            shape((32, part)),
-        ],
-        [pltpu.VMEM((bands, piece_rows, LANES), F32), pltpu.VMEM((16, size), F32)],
-        10**9,
-    )
-    count = count_round(count, mask2)
-    (out_two, t_two, xcol_two, h1_two, h2_two, loss_two) = call(
-        functools.partial(couple_two_forward, half_dims),
-        (mixed_two, mask, mask2, after(chan_two, count), e_two_t, wb_two, f_two, bb_two),
+        ]
+        + [quarter_two] * 4,
         [
-            shape((32, part)),
-            shape((16, part)),
-            shape((144, part), BF16),
-            shape((HID, part), BF16),
-            shape((HID, part), BF16),
-            shape((8, LANES)),
-        ],
-        [pltpu.VMEM((16, ext_lanes), F32), pltpu.VMEM((32, ext_lanes), F32)],
-        2 * HID * part * (144 + HID + 288),
-    )
-    for _ in bits:
-        count = count_round(count, loss_two)
-    half_two = shape((TWO_ROWS // 2, LANES))
-    (kept_two, sent_two, gkeep_two) = call(
-        functools.partial(couple_two_backward, half_dims),
-        (own, count, mask2, y2, out_two, t_two, xcol_two, h1_two, h2_two, chan_two, m_two_t, e_two, wb_two_t, f_two_t),
-        [half_two, half_two, shape((32, part))],
-        [
+            pltpu.VMEM((bands, piece_rows, LANES), F32),
+            pltpu.VMEM((16, size), F32),
+            pltpu.VMEM((32, part), F32),
+            pltpu.VMEM((32, part), F32),
+            pltpu.VMEM((32, part), F32),
+            pltpu.VMEM((16, part), F32),
+            pltpu.VMEM((144, part), BF16),
+            pltpu.VMEM((HID, part), BF16),
+            pltpu.VMEM((HID, part), BF16),
+            pltpu.VMEM((16, ext_lanes), F32),
+            pltpu.VMEM((32, ext_lanes), F32),
             pltpu.VMEM((32, ext_lanes), F32),
             pltpu.VMEM((16, ext_lanes), F32),
             pltpu.VMEM((32, part), F32),
@@ -1172,25 +1238,24 @@
             pltpu.VMEM((32, 32, LANES), F32),
             pltpu.VMEM((TWO_ROWS, LANES), F32),
         ],
-        4 * HID * part * (144 + HID + 288),
+        6 * HID * part * (144 + HID + 288),
     )
     whole_lanes = (rows + 2) * (cols + 2) * LANES
     chunk = 1024
     fwd_in = (
-        count,
-        in_hbm(mixed_one),
+        mixed_one,
         mask,
         mask2,
-        in_hbm(keep),
-        in_hbm(gkeep_two),
+        keep,
+        gkeep_two,
         chan_one,
-        in_hbm(e_one_t),
-        in_hbm(wb_one),
-        in_hbm(f_one),
-        in_hbm(bb_one),
-        in_hbm(wp),
-        in_hbm(wpt),
-        in_hbm(prior_bias),
+        e_one_t,
+        wb_one,
+        f_one,
+        bb_one,
+        wp,
+        wpt,
+        prior_bias,
     )
     fwd_out = [
         shape((72, size), BF16),
@@ -1216,9 +1281,9 @@
         ],
         2 * HID * size * (72 + HID + 144),
     )
-    first_bit, second_bit, third_bit, fourth_bit = bits[0], bits[2], bits[1], bits[3]
-    total_two = kept_two + after(trade(sent_two, first_bit), loss_one)
-    top_in = (own, after(count, total_two), mask, res_one, t_one, gout_one, f_one_t, gwp, loss_one, loss_two, h1_one, h2_one)
+    total_u = kept_u + after(trade(sent_u, second_bit), loss_one)
+    total_v = kept_v + after(trade(sent_v, third_bit), loss_one)
+    top_in = (own, after(mask, total_u, total_v), res_one, t_one, gout_one, f_one_t, gwp, loss_one, loss_two, h1_one, h2_one)
     half_a, half_b = shape((PART_A // 2, LANES)), shape(((ONE_ROWS - PART_A) // 2, LANES))
     top_out = [shape((HID, size), BF16), half_a, half_a, half_b, half_b, shape((8, size)), shape((16, LANES))]
     (gpre, kept_a, sent_a, kept_b, sent_b, ghalf, gbc) = call(
@@ -1232,7 +1297,7 @@
             pltpu.VMEM((ONE_ROWS, LANES), F32),
         ],
         2 * HID * size * (144 + HID + 144),
-        aliases={11: 0},
+        aliases={10: 0},
     )
 
     def halve(parts, bit, *beside):
@@ -1247,8 +1312,34 @@
             first += h
         return results
 
-    (total_two,) = halve([total_two], second_bit, gbc)
-    low_in = (y1, ghalf, after(gbc, total_two), gout_one, e_one, wb_one_t, xcol_one, h1_one, gpre)
+    def exchange(parts, near_parts, far_parts, near, far_bit):
+        code = 2 * ((index // near) % 2) + (index // far_bit) % 2
+        sizes = [x.shape[0] // 4 for x in parts]
+
+        def pieces_for(partner):
+            return [lax.dynamic_slice_in_dim(x, (code ^ partner) * h, h, 0) for x, h in zip(parts, sizes)]
+
+        totals = pieces_for(0)
+        others = []
+        for partner, bit, more in ((2, near, near_parts), (1, far_bit, far_parts), (3, near | far_bit, [])):
+            high = (index // bit) % 2
+            halves = [x.shape[0] // 2 for x in more]
+            sent = pieces_for(partner) + [
+                lax.dynamic_slice_in_dim(x, (1 - high) * h, h, 0) for x, h in zip(more, halves)
+            ]
+            got = trade(jnp.concatenate(sent) if len(sent) > 1 else sent[0], bit)
+            first = 0
+            for k, h in enumerate(sizes):
+                totals[k] = totals[k] + got[first : first + h]
+                first += h
+            for x, h in zip(more, halves):
+                others.append(lax.dynamic_slice_in_dim(x, high * h, h, 0) + got[first : first + h])
+                first += h
+        return totals + others
+
+    (total_u,) = halve([total_u], third_bit, gbc)
+    (total_v,) = halve([total_v], second_bit, gbc)
+    low_in = (y1, ghalf, after(gbc, total_u, total_v), gout_one, e_one, wb_one_t, xcol_one, h1_one, gpre)
     (slab_rest,) = call(
         functools.partial(one_backward_bottom, dims, chunk),
         low_in,
@@ -1264,34 +1355,36 @@
 
     total_a = kept_a + after(trade(sent_a, second_bit), slab_rest)
     total_b = kept_b + after(trade(sent_b, third_bit), slab_rest)
-    (total_two,) = halve([total_two], fourth_bit, slab_rest)
+    total_u, total_v = halve([total_u, total_v], fourth_bit, slab_rest)
     far = bits[3:]
-    total_a, total_b, total_rest = halve([total_a, total_b, after(slab_rest, total_two)], first_bit)
-    (total_two,) = halve([total_two], third_bit)
-    total_a, total_rest = halve([total_a, total_rest], third_bit)
-    (total_b,) = halve([total_b], second_bit)
-    (total_rest,) = halve([total_rest], second_bit)
-    shards = halve([total_a, total_b, total_rest], far[0])
-    shards = [total_two] + shards
-    for bit in far[1:]:
+    total_u, total_v, total_a, total_b, total_rest = halve(
+        [total_u, total_v, total_a, total_b, after(slab_rest, total_u, total_v)], first_bit
+    )
+    total_rest, total_a, total_b = exchange([total_rest], [total_a], [total_b], third_bit, second_bit)
+    total_a, total_b, total_rest, total_u, total_v = exchange(
+        [total_a, total_b, total_rest], [], [total_u, total_v], far[0], far[1]
+    )
+    shards = [total_u, total_v, total_a, total_b, total_rest]
+    for bit in far[2:]:
         shards = halve(shards, bit)
     orders = [
-        [first_bit, second_bit, fourth_bit, third_bit] + far[1:],
+        [second_bit, third_bit, fourth_bit, first_bit] + far[1:],
+        [third_bit, second_bit, fourth_bit, first_bit] + far[1:],
         [second_bit, first_bit, third_bit] + far,
         [third_bit, first_bit, second_bit] + far,
         [first_bit, third_bit, second_bit] + far,
     ]
-    loss_part = shards[2]
+    loss_part = shards[3]
     owner, loss_row = divmod(ONE_LOSS - PART_A, loss_part.shape[0])
     extra = []
-    for row in range(2):
+    for row in range(3):
         value = loss_part[loss_row + row]
         for _ in range(3):
             high = lax.reduce_precision(value, 8, 7)
             extra.append(high)
             value = value - high
-    extra = jnp.pad(jnp.stack(extra), ((0, 10), (0, 0)))
-    spread = [shards[0].astype(BF16), jnp.concatenate(shards[1:] + [extra]).astype(BF16)]
+    extra = jnp.pad(jnp.stack(extra), ((0, 7), (0, 0)))
+    spread = [jnp.concatenate(shards[:2]).astype(BF16), jnp.concatenate(shards[2:] + [extra]).astype(BF16)]
     near = [[third_bit, second_bit, first_bit], [second_bit, third_bit, first_bit]]
     backs = [far[::-1] + near[0], far[::-1] + near[1]]
 
@@ -1306,8 +1399,25 @@
             results.append(jnp.where(low, jnp.concatenate([value, got]), jnp.concatenate([got, value])))
         return results
 
-    for bit in far[::-1]:
+    for bit in far[:1:-1]:
         spread = double(spread, bit)
+    near_low, far_low = (index // far[0]) % 2 == 0, (index // far[1]) % 2 == 0
+    sizes = [value.shape[0] for value in spread]
+    joined = jnp.concatenate(spread)
+    from_far, from_near, from_both = (trade(joined, bit) for bit in (far[1], far[0], far[0] | far[1]))
+
+    def ordered(low, one, other):
+        return jnp.where(low, jnp.concatenate([one, other]), jnp.concatenate([other, one]))
+
+    quads = []
+    for first, size_of in ((0, sizes[0]), (sizes[0], sizes[1])):
+        own_part, far_part, near_part, both_part = (
+            x[first : first + size_of] for x in (joined, from_far, from_near, from_both)
+        )
+        quads.append(
+            ordered(near_low, ordered(far_low, own_part, far_part), ordered(far_low, near_part, both_part))
+        )
+    spread = quads
     for k in range(3):
         spread = [double([value], order[k])[0] for value, order in zip(spread, near)]
     count_bits = len(bits)
@@ -1317,16 +1427,18 @@
         axes = [count_bits - 1 - back.index(bit) for bit in order]
         return value.transpose(axes + [count_bits, count_bits + 1]).reshape(-1, LANES)
 
-    totals = [reorder(spread[0], backs[0], orders[0])]
+    totals = []
     first = 0
-    for shard, order in zip(shards[1:], orders[1:]):
-        totals.append(reorder(spread[1][..., first : first + shard.shape[0], :], backs[1], order))
+    for k, (shard, order) in enumerate(zip(shards, orders)):
+        first = 0 if k in (0, 2) else first
+        side = 0 if k < 2 else 1
+        totals.append(reorder(spread[side][..., first : first + shard.shape[0], :], backs[side], order))
         first += shard.shape[0]
     place = [0] * count_bits
-    for k, bit in enumerate(orders[2]):
+    for k, bit in enumerate(orders[3]):
         place[count_bits - 1 - backs[1].index(bit)] = (owner >> (count_bits - 1 - k)) & 1
     extra = spread[1][tuple(place)][first:]
-    totals = [totals[0], jnp.concatenate(totals[1:3]), totals[3]]
+    totals = [jnp.concatenate(totals[:2]), jnp.concatenate(totals[2:4]), totals[4]]
     taps = [
         (entry_taps, entry_first, entry_second),
         (middle, middle_first, middle_second),
@@ -1340,15 +1452,19 @@
     outs.append(shape((4, HID)))
     results = call(
         finish_kernel,
-        (count, *totals, extra, *flats, *[x for group in taps for x in group]),
+        (*totals, extra, *flats, *[in_hbm(x) for group in taps for x in group]),
         outs,
         [
             pltpu.VMEM((TWO_ROWS - WB_ROWS, LANES), F32),
             pltpu.VMEM((ONE_ROWS - WB_ROWS, LANES), F32),
             pltpu.VMEM((REST_ROWS, LANES), F32),
             pltpu.VMEM((LANES, LANES), F32),
-        ],
+        ]
+        + [pltpu.VMEM(group[0].shape, F32) for _ in range(4) for group in taps]
+        + [pltpu.SemaphoreType.DMA((5, 3))] * 2,
         10**8,
+        far_in=range(7, 19),
+        far_out=range(5, 17),
     )
     results = list(results)
     for k in range(2):

time: 147 us -> 122 us (0.83)
  waiting for transfers between devices: 43.1 us -> 21.7 us
  local copies, waits for them, and re-layouts: 11.8 us -> 4.07 us
  starting transfers between devices: 23.3 us -> 30.1 us
    ppermute x23, waiting for transfers between devices: 43.1 us -> 21.7 us  [trade(): lax.ppermute(value, ('batch', 'rows'), [(i, i ^ bit) for i in range(devic...]
    unnamed x64 -> x23, local copies, waits for them, and re-layouts: 10.6 us -> 2.89 us
    ppermute x23, starting transfers between devices: 20.2 us -> 26.9 us  [trade(): lax.ppermute(value, ('batch', 'rows'), [(i, i ^ bit) for i in range(devic...]
    pallas_call x10 -> x7, Pallas kernels: 63.6 us -> 62.7 us  [call(): pl.pallas_call(kernel, out_shape=outputs, in_specs=[far if k in far_in el...]
  transfers between devices with their start and end apart: 26 -> 26, of which waited for: 14 -> 14; matrix products, arithmetic and copies ran while one was open for 1% -> 2% of each run, Pallas kernels for 31% -> 34%
where the time goes in v4:
time: 122 us
  Pallas kernels  62.7 us (51%)
  starting transfers between devices  30.1 us (25%)
  waiting for transfers between devices  21.7 us (18%)
  local copies, waits for them, and re-layouts  4.07 us (3%)
  other arithmetic  1.73 us (1%)
  between operations  1.64 us (1%)
    pallas_call x7, Pallas kernels, call(): pl.pallas_call(kernel, out_shape=outputs, in_specs=[far if k in far_in el...  62.7 us
    ppermute x23, starting transfers between devices, trade(): lax.ppermute(value, ('batch', 'rows'), [(i, i ^ bit) for i in range(devic...  26.9 us
    ppermute x23, waiting for transfers between devices, trade(): lax.ppermute(value, ('batch', 'rows'), [(i, i ^ bit) for i in range(devic...  21.7 us
    ppermute x3, starting transfers between devices, on_device(): lax.ppermute(pieces[d], 'rows', [(i, i ^ d) for i in range(bands)])  3.18 us
    unnamed x23, local copies, waits for them, and re-layouts  2.89 us
  transfers between devices with their start and end apart: 26, of which 14 were waited for; matrix products, arithmetic and copies ran while one was open for 2% of the time, Pallas kernels for 34%

profile of v4, /device:TPU:0, one launch (start us, length us, event | category | flops | bytes accessed | tf_op | source)
XLA Modules:
  0.0 121.9 jit_solution(11766225542454383596)
XLA Ops:
  0.7 1.0 copy-done
  1.7 0.8 copy-done.2
  2.5 0.8 shard_map.304
  3.3 0.5 collective-permute-start
  3.8 2.6 %collective-permute-start.1 = (bf16[208,128]{1,0:T(8,128)(2,1)S(1)}, bf16[208,128]{1,0:T(8,128)(2,1)S(1)}, u32[]{:S(2)}, u32[]{:S(2)}) collective-permute-start(bf16[208,128]{1,0:T(8,128)(2,1)S(1)} %get-tuple-element.101), channel_id=1, source_target_pairs={{0,2},{1,3},{2,0},{3,1},{4,6},{5,7},{6,4},{7,5},{8,10},{9,11},{10,... | collective-permute-start | bytes 159752 | tf_op jit(solution)/shard_map/ppermute | solution.py:1158
  6.5 0.7 pad_bitcast_fusion.2.flat_ref
  7.2 0.9 copy-done.1
  8.1 4.1 %shard_map.305 = (f32[16,128]{1,0:T(8,128)S(1)}, f32[16,128]{1,0:T(8,128)S(1)}, f32[32,128]{1,0:T(8,128)S(1)}, f32[32,128]{1,0:T(8,128)S(1)}, f32[32,128]{1,0:T(...) custom-call(f32[24,128]{1,0:T(8,128)S(1)} %pad_bitcast_fusion.2.flat, ...), custom_call_target="tpu_custom_call" | custom-call | flops 1000000000 | bytes 6714112 | tf_op jit(solution)/shard_map/pallas_call | solution.py:716
  12.3 12.0 %shard_map.306 = (f32[16,8192]{1,0:T(8,128)S(1)}, f32[16,8192]{1,0:T(8,128)S(1)}, f32[1,8192]{1,0:T(1,128)S(1)}, f32[1,2048]{1,0:T(1,128)S(1)}, f32[32,2048]{1,0...) custom-call(s32[2]{0:T(128)S(1)} %pad_add_fusion.index_ref, ...), custom_call_target="tpu_custom_call" | custom-call | flops 5939134464 | bytes 5666824 | tf_op jit(solution)/shard_map/pallas_call | solution.py:716
  24.3 1.8 %collective-permute-start.3 = (f32[896,128]{1,0:T(8,128)S(1)}, f32[896,128]{1,0:T(8,128)S(1)}, u32[]{:S(2)}, u32[]{:S(2)}) collective-permute-start(f32[896,128]{1,0:T(8,128)S(1)} %get-tuple-element.117), channel_id=1, source_target_pairs={{0,4},{1,5},{2,6},{3,7},{4,0},{5,1},{6,2},{7,3},{8,12},{9,13},{10,... | collective-permute-start | bytes 1376264 | tf_op jit(solution)/shard_map/ppermute | solution.py:1140
  26.0 1.5 %collective-permute-start.5 = (f32[896,128]{1,0:T(8,128)S(1)}, f32[896,128]{1,0:T(8,128)S(1)}, u32[]{:S(2)}, u32[]{:S(2)}) collective-permute-start(f32[896,128]{1,0:T(8,128)S(1)} %get-tuple-element.133), channel_id=1, source_target_pairs={{0,2},{1,3},{2,0},{3,1},{4,6},{5,7},{6,4},{7,5},{8,10},{9,11},{10,... | collective-permute-start | bytes 1376264 | tf_op jit(solution)/shard_map/ppermute | solution.py:1140
  27.6 11.0 %shard_map.307 = (bf16[72,8192]{1,0:T(8,128)(2,1)S(1)}, bf16[512,8192]{1,0:T(8,128)(2,1)S(1)}, bf16[512,8192]{1,0:T(8,128)(2,1)S(1)}, f32[8,8192]{1,0:T(8,128)S(...) custom-call(f32[16,8192]{1,0:T(8,128)S(1)} %get-tuple-element.118.mix1_ref, ...), custom_call_target="tpu_custom_call" | custom-call | flops 6106906624 | bytes 21002496 | tf_op jit(solution)/shard_map/pallas_call | solution.py:716
  38.8 1.5 %collective-permute-start.4 = (f32[448,128]{1,0:T(8,128)S(1)}, f32[448,128]{1,0:T(8,128)S(1)}, u32[]{:S(2)}, u32[]{:S(2)}) collective-permute-start(f32[448,128]{1,0:T(8,128)S(1)} %constant_dynamic-slice_fusion.16), channel_id=1, source_target_pairs={{0,2},{1,3},{2,0},{3,1},{4,6},{5,7},{6,4},{7,5},{8,10},{9,11},{10,... | collective-permute-start | bytes 688136 | tf_op jit(solution)/shard_map/ppermute | solution.py:1140
  40.3 0.6 collective-permute-start.6
  40.9 14.2 %shard_map.308 = (bf16[512,8192]{1,0:T(8,128)(2,1)S(1)}, f32[768,128]{1,0:T(8,128)S(1)}, f32[768,128]{1,0:T(8,128)S(1)}, f32[640,128]{1,0:T(8,128)S(1)}, f32[640...) custom-call(s32[2]{0:T(128)S(1)} %pad_add_fusion.index_ref, ...), custom_call_target="tpu_custom_call", output_to_operand_aliasing={{0}: (10, {})} | custom-call | flops 6710886400 | bytes 28188680 | tf_op jit(solution)/shard_map/pallas_call | solution.py:716
  55.1 0.7 collective-permute-start.9
  55.8 1.5 %collective-permute-start.8 = (f32[768,128]{1,0:T(8,128)S(1)}, f32[768,128]{1,0:T(8,128)S(1)}, u32[]{:S(2)}, u32[]{:S(2)}) collective-permute-start(f32[768,128]{1,0:T(8,128)S(1)} %get-tuple-element.156), channel_id=1, source_target_pairs={{0,4},{1,5},{2,6},{3,7},{4,0},{5,1},{6,2},{7,3},{8,12},{9,13},{10,... | collective-permute-start | bytes 1179656 | tf_op jit(solution)/shard_map/ppermute | solution.py:1140
  57.5 1.6 %collective-permute-start.7 = (f32[448,128]{1,0:T(8,128)S(1)}, f32[448,128]{1,0:T(8,128)S(1)}, u32[]{:S(2)}, u32[]{:S(2)}) collective-permute-start(f32[448,128]{1,0:T(8,128)S(1)} %pad_maximum_fusion.2), channel_id=1, source_target_pairs={{0,8},{1,9},{2,10},{3,11},{4,12},{5,13},{6,14},{7,15},{8,0},{9,1},... | collective-permute-start | bytes 688136 | tf_op jit(solution)/shard_map/ppermute | solution.py:1140
  59.1 11.6 %shard_map.309 = f32[256,128]{1,0:T(8,128)S(1)} custom-call(f32[16,8192]{1,0:T(8,128)S(1)} %get-tuple-element.147.y1_ref, f32[8,8192]{1,0:T(8,128)S(1)} %get-tuple-element.148.ghalf_ref, f32[16,128]{1,0:T(8,128)S(1)} %get-tuple-element.149.gbc_ref, f32[16,8192]{1,0:T(8,128)S(1)} %get-tuple-element.138.gout_ref, ...), custom_call_target="tpu_custom_call" | custom-call | flops 5502926848 | bytes 20004864 | tf_op jit(solution)/shard_map/pallas_call | solution.py:716
  71.2 1.7 %collective-permute-done.10 = f32[1056,128]{1,0:T(8,128)S(1)} collective-permute-done((f32[1056,128]{1,0:T(8,128)S(1)}, f32[1056,128]{1,0:T(8,128)S(1)}, u32[]{:S(2)}, u32[]{:S(2)}) %collective-permute-start.10) | collective-permute-done | bytes 540704 | tf_op jit(solution)/shard_map/ppermute | solution.py:1140
  73.1 0.6 collective-permute-start.12
  73.7 1.5 %collective-permute-start.11 = (f32[224,128]{1,0:T(8,128)S(1)}, f32[224,128]{1,0:T(8,128)S(1)}, u32[]{:S(2)}, u32[]{:S(2)}) collective-permute-start(f32[224,128]{1,0:T(8,128)S(1)} %pad_maximum_fusion.3), channel_id=1, source_target_pairs={{0,2},{1,3},{2,0},{3,1},{4,6},{5,7},{6,4},{7,5},{8,10},{9,11},{10,... | collective-permute-start | bytes 344072 | tf_op jit(solution)/shard_map/ppermute | solution.py:1140
  75.2 1.6 %collective-permute-start.13 = (f32[32,128]{1,0:T(8,128)S(1)}, f32[32,128]{1,0:T(8,128)S(1)}, u32[]{:S(2)}, u32[]{:S(2)}) collective-permute-start(f32[32,128]{1,0:T(8,128)S(1)} %get-tuple-element.202), channel_id=1, source_target_pairs={{0,6},{1,7},{2,4},{3,5},{4,2},{5,3},{6,0},{7,1},{8,14},{9,15},{10,... | collective-permute-start | bytes 49160 | tf_op jit(solution)/shard_map/ppermute | solution.py:1140
  76.8 1.4 %collective-permute-done.12 = f32[192,128]{1,0:T(8,128)S(1)} collective-permute-done((f32[192,128]{1,0:T(8,128)S(1)}, f32[192,128]{1,0:T(8,128)S(1)}, u32[]{:S(2)}, u32[]{:S(2)}) %collective-permute-start.12) | collective-permute-done | bytes 98336 | tf_op jit(solution)/shard_map/ppermute | solution.py:1140
  78.2 0.6 collective-permute-done.11
  78.9 0.9 collective-permute-done.13
  79.9 2.7 %collective-permute-start.14 = (f32[208,128]{1,0:T(8,128)S(1)}, f32[208,128]{1,0:T(8,128)S(1)}, u32[]{:S(2)}, u32[]{:S(2)}) collective-permute-start(f32[208,128]{1,0:T(8,128)S(1)} %constant_dynamic-update-slice_fusion), channel_id=1, source_target_pairs={{0,16},{1,17},{2,18},{3,19},{4,20},{5,21},{6,22},{7,23},{8,24},{9,... | collective-permute-start | bytes 319496 | tf_op jit(solution)/shard_map/ppermute | solution.py:1140
  82.6 0.4 collective-permute-start.15
  83.0 1.3 %collective-permute-start.16 = (f32[96,128]{1,0:T(8,128)S(1)}, f32[96,128]{1,0:T(8,128)S(1)}, u32[]{:S(2)}, u32[]{:S(2)}) collective-permute-start(f32[96,128]{1,0:T(8,128)S(1)} %pad_maximum_fusion.6), channel_id=1, source_target_pairs={{0,24},{1,25},{2,26},{3,27},{4,28},{5,29},{6,30},{7,31},{8,16},{9,... | collective-permute-start | bytes 147464 | tf_op jit(solution)/shard_map/ppermute | solution.py:1140
  84.4 3.4 %collective-permute-done.15 = f32[96,128]{1,0:T(8,128)S(1)} collective-permute-done((f32[96,128]{1,0:T(8,128)S(1)}, f32[96,128]{1,0:T(8,128)S(1)}, u32[]{:S(2)}, u32[]{:S(2)}) %collective-permute-start.15) | collective-permute-done | bytes 49184 | tf_op jit(solution)/shard_map/ppermute | solution.py:1140
  87.7 1.2 collective-permute-done.16
  89.2 1.4 %collective-permute-start.17 = (bf16[224,128]{1,0:T(8,128)(2,1)S(1)}, bf16[224,128]{1,0:T(8,128)(2,1)S(1)}, u32[]{:S(2)}, u32[]{:S(2)}) collective-permute-start(bf16[224,128]{1,0:T(8,128)(2,1)S(1)} %get-tuple-element.225), channel_id=1, source_target_pairs={{0,16},{1,17},{2,18},{3,19},{4,20},{5,21},{6,22},{7,23},{8,24},{9,... | collective-permute-start | bytes 172040 | tf_op jit(solution)/shard_map/ppermute | solution.py:1140
  90.6 0.9 collective-permute-start.18
  91.5 2.1 %collective-permute-start.19 = (bf16[224,128]{1,0:T(8,128)(2,1)S(1)}, bf16[224,128]{1,0:T(8,128)(2,1)S(1)}, u32[]{:S(2)}, u32[]{:S(2)}) collective-permute-start(bf16[224,128]{1,0:T(8,128)(2,1)S(1)} %get-tuple-element.225), channel_id=1, source_target_pairs={{0,24},{1,25},{2,26},{3,27},{4,28},{5,29},{6,30},{7,31},{8,16},{9,... | collective-permute-start | bytes 172040 | tf_op jit(solution)/shard_map/ppermute | solution.py:1140
  93.6 1.0 collective-permute-done.17
  94.7 0.5 collective-permute-done.18
  95.2 2.3 %collective-permute-done.19 = bf16[224,128]{1,0:T(8,128)(2,1)S(1)} collective-permute-done((bf16[224,128]{1,0:T(8,128)(2,1)S(1)}, bf16[224,128]{1,0:T(8,128)(2,1)S(1)}, u32[]{:S(2)}, u32[]{:S(2)}) %collective-permute-start.19) | collective-permute-done | bytes 57376 | tf_op jit(solution)/shard_map/ppermute | solution.py:1140
  97.6 1.6 %collective-permute-start.23 = (bf16[448,128]{1,0:T(8,128)(2,1)S(1)}, bf16[448,128]{1,0:T(8,128)(2,1)S(1)}, u32[]{:S(2)}, u32[]{:S(2)}) collective-permute-start(bf16[448,128]{1,0:T(8,128)(2,1)S(1)} %maximum_select_fusion.7), channel_id=1, source_target_pairs={{0,4},{1,5},{2,6},{3,7},{4,0},{5,1},{6,2},{7,3},{8,12},{9,13},{10,... | collective-permute-start | bytes 344072 | tf_op jit(solution)/shard_map/ppermute | solution.py:1140
  99.2 0.9 collective-permute-start.20
  100.1 3.4 %collective-permute-done.23 = bf16[448,128]{1,0:T(8,128)(2,1)S(1)} collective-permute-done((bf16[448,128]{1,0:T(8,128)(2,1)S(1)}, bf16[448,128]{1,0:T(8,128)(2,1)S(1)}, u32[]{:S(2)}, u32[]{:S(2)}) %collective-permute-start.23) | collective-permute-done | bytes 114720 | tf_op jit(solution)/shard_map/ppermute | solution.py:1140
  103.5 0.5 collective-permute-start.24
  104.1 1.9 %collective-permute-start.21 = (bf16[896,128]{1,0:T(8,128)(2,1)S(1)}, bf16[896,128]{1,0:T(8,128)(2,1)S(1)}, u32[]{:S(2)}, u32[]{:S(2)}) collective-permute-start(bf16[896,128]{1,0:T(8,128)(2,1)S(1)} %maximum_select_fusion.4), channel_id=1, source_target_pairs={{0,4},{1,5},{2,6},{3,7},{4,0},{5,1},{6,2},{7,3},{8,12},{9,13},{10,... | collective-permute-start | bytes 688136 | tf_op jit(solution)/shard_map/ppermute | solution.py:1140
  106.0 3.6 %collective-permute-done.24 = bf16[896,128]{1,0:T(8,128)(2,1)S(1)} collective-permute-done((bf16[896,128]{1,0:T(8,128)(2,1)S(1)}, bf16[896,128]{1,0:T(8,128)(2,1)S(1)}, u32[]{:S(2)}, u32[]{:S(2)}) %collective-permute-start.24) | collective-permute-done | bytes 229408 | tf_op jit(solution)/shard_map/ppermute | solution.py:1140
  109.8 0.4 collective-permute-done.21
  110.5 1.1 collective-permute-done.25
  111.6 0.2 maximum_select_fusion.1
  112.3 0.2 maximum_select_fusion
  112.8 8.9 %shard_map.310 = (f32[1,1]{1,0:T(1,128)}, f32[1,1]{1,0:T(1,128)}, f32[24,128]{1,0:T(8,128)}, f32[24,128]{1,0:T(8,128)}, f32[24,128]{1,0:T(8,128)}, /*index=5*/f3...) custom-call(bf16[3584,128]{1,0:T(8,128)(2,1)S(1)} %pad_maximum_fusio, ...), custom_call_target="tpu_custom_call" | custom-call | flops 100000000 | bytes 20593672 | tf_op jit(solution)/shard_map/pallas_call | solution.py:716
  (100 shorter events, 2.7 us)
Async XLA Ops:
  0.7 1.0 copy-start
  1.7 0.8 copy-start.2
  3.3 8.9 %collective-permute-start = (bf16[208,128]{1,0:T(8,128)(2,1)S(1)}, bf16[208,128]{1,0:T(8,128)(2,1)S(1)}, u32[]{:S(2)}, u32[]{:S(2)}) collective-permute-start(bf16[208,128]{1,0:T(8,128)(2,1)S(1)} %get-tuple-element.100), channel_id=1, source_target_pairs={{0,1},{1,0},{2,3},{3,2},{4,5},{5,4},{6,7},{7,6},{8,9},{9,8},{10,11... | collective-permute-start | bytes 159752 | tf_op jit(solution)/shard_map/ppermute | solution.py:1158
  3.8 8.4 %collective-permute-start.1 = (bf16[208,128]{1,0:T(8,128)(2,1)S(1)}, bf16[208,128]{1,0:T(8,128)(2,1)S(1)}, u32[]{:S(2)}, u32[]{:S(2)}) collective-permute-start(bf16[208,128]{1,0:T(8,128)(2,1)S(1)} %get-tuple-element.101), channel_id=1, source_target_pairs={{0,2},{1,3},{2,0},{3,1},{4,6},{5,7},{6,4},{7,5},{8,10},{9,11},{10,... | collective-permute-start | bytes 159752 | tf_op jit(solution)/shard_map/ppermute | solution.py:1158
  6.4 5.8 %collective-permute-start.2 = (bf16[208,128]{1,0:T(8,128)(2,1)S(1)}, bf16[208,128]{1,0:T(8,128)(2,1)S(1)}, u32[]{:S(2)}, u32[]{:S(2)}) collective-permute-start(bf16[208,128]{1,0:T(8,128)(2,1)S(1)} %get-tuple-element.102), channel_id=1, source_target_pairs={{0,3},{1,2},{2,1},{3,0},{4,7},{5,6},{6,5},{7,4},{8,11},{9,10},{10,... | collective-permute-start | bytes 159752 | tf_op jit(solution)/shard_map/ppermute | solution.py:1158
  7.2 0.9 copy-start.1
  24.3 14.4 %collective-permute-start.3 = (f32[896,128]{1,0:T(8,128)S(1)}, f32[896,128]{1,0:T(8,128)S(1)}, u32[]{:S(2)}, u32[]{:S(2)}) collective-permute-start(f32[896,128]{1,0:T(8,128)S(1)} %get-tuple-element.117), channel_id=1, source_target_pairs={{0,4},{1,5},{2,6},{3,7},{4,0},{5,1},{6,2},{7,3},{8,12},{9,13},{10,... | collective-permute-start | bytes 1376264 | tf_op jit(solution)/shard_map/ppermute | solution.py:1140
  26.0 12.6 %collective-permute-start.5 = (f32[896,128]{1,0:T(8,128)S(1)}, f32[896,128]{1,0:T(8,128)S(1)}, u32[]{:S(2)}, u32[]{:S(2)}) collective-permute-start(f32[896,128]{1,0:T(8,128)S(1)} %get-tuple-element.133), channel_id=1, source_target_pairs={{0,2},{1,3},{2,0},{3,1},{4,6},{5,7},{6,4},{7,5},{8,10},{9,11},{10,... | collective-permute-start | bytes 1376264 | tf_op jit(solution)/shard_map/ppermute | solution.py:1140
  38.8 18.5 %collective-permute-start.4 = (f32[448,128]{1,0:T(8,128)S(1)}, f32[448,128]{1,0:T(8,128)S(1)}, u32[]{:S(2)}, u32[]{:S(2)}) collective-permute-start(f32[448,128]{1,0:T(8,128)S(1)} %constant_dynamic-slice_fusion.16), channel_id=1, source_target_pairs={{0,2},{1,3},{2,0},{3,1},{4,6},{5,7},{6,4},{7,5},{8,10},{9,11},{10,... | collective-permute-start | bytes 688136 | tf_op jit(solution)/shard_map/ppermute | solution.py:1140
  40.3 17.0 %collective-permute-start.6 = (f32[448,128]{1,0:T(8,128)S(1)}, f32[448,128]{1,0:T(8,128)S(1)}, u32[]{:S(2)}, u32[]{:S(2)}) collective-permute-start(f32[448,128]{1,0:T(8,128)S(1)} %constant_dynamic-slice_fusion.14), channel_id=1, source_target_pairs={{0,4},{1,5},{2,6},{3,7},{4,0},{5,1},{6,2},{7,3},{8,12},{9,13},{10,... | collective-permute-start | bytes 688136 | tf_op jit(solution)/shard_map/ppermute | solution.py:1140
  55.1 15.5 %collective-permute-start.9 = (f32[640,128]{1,0:T(8,128)S(1)}, f32[640,128]{1,0:T(8,128)S(1)}, u32[]{:S(2)}, u32[]{:S(2)}) collective-permute-start(f32[640,128]{1,0:T(8,128)S(1)} %get-tuple-element.159), channel_id=1, source_target_pairs={{0,2},{1,3},{2,0},{3,1},{4,6},{5,7},{6,4},{7,5},{8,10},{9,11},{10,... | collective-permute-start | bytes 983048 | tf_op jit(solution)/shard_map/ppermute | solution.py:1140
  55.8 14.9 %collective-permute-start.8 = (f32[768,128]{1,0:T(8,128)S(1)}, f32[768,128]{1,0:T(8,128)S(1)}, u32[]{:S(2)}, u32[]{:S(2)}) collective-permute-start(f32[768,128]{1,0:T(8,128)S(1)} %get-tuple-element.156), channel_id=1, source_target_pairs={{0,4},{1,5},{2,6},{3,7},{4,0},{5,1},{6,2},{7,3},{8,12},{9,13},{10,... | collective-permute-start | bytes 1179656 | tf_op jit(solution)/shard_map/ppermute | solution.py:1140
  57.5 13.3 %collective-permute-start.7 = (f32[448,128]{1,0:T(8,128)S(1)}, f32[448,128]{1,0:T(8,128)S(1)}, u32[]{:S(2)}, u32[]{:S(2)}) collective-permute-start(f32[448,128]{1,0:T(8,128)S(1)} %pad_maximum_fusion.2), channel_id=1, source_target_pairs={{0,8},{1,9},{2,10},{3,11},{4,12},{5,13},{6,14},{7,15},{8,0},{9,1},... | collective-permute-start | bytes 688136 | tf_op jit(solution)/shard_map/ppermute | solution.py:1140
  70.9 2.0 %collective-permute-start.10 = (f32[1056,128]{1,0:T(8,128)S(1)}, f32[1056,128]{1,0:T(8,128)S(1)}, u32[]{:S(2)}, u32[]{:S(2)}) collective-permute-start(f32[1056,128]{1,0:T(8,128)S(1)} %dynamic-slice_dynamic-update-slice_fusion.2), channel_id=1, source_target_pairs={{0,1},{1,0},{2,3},{3,2},{4,5},{5,4},{6,7},{7,6},{8,9},{9,8},{10,11... | collective-permute-start | bytes 1622024 | tf_op jit(solution)/shard_map/ppermute | solution.py:1140
  73.1 5.1 %collective-permute-start.12 = (f32[192,128]{1,0:T(8,128)S(1)}, f32[192,128]{1,0:T(8,128)S(1)}, u32[]{:S(2)}, u32[]{:S(2)}) collective-permute-start(f32[192,128]{1,0:T(8,128)S(1)} %pad_maximum_fusion.4), channel_id=1, source_target_pairs={{0,4},{1,5},{2,6},{3,7},{4,0},{5,1},{6,2},{7,3},{8,12},{9,13},{10,... | collective-permute-start | bytes 294920 | tf_op jit(solution)/shard_map/ppermute | solution.py:1140
  73.7 5.1 %collective-permute-start.11 = (f32[224,128]{1,0:T(8,128)S(1)}, f32[224,128]{1,0:T(8,128)S(1)}, u32[]{:S(2)}, u32[]{:S(2)}) collective-permute-start(f32[224,128]{1,0:T(8,128)S(1)} %pad_maximum_fusion.3), channel_id=1, source_target_pairs={{0,2},{1,3},{2,0},{3,1},{4,6},{5,7},{6,4},{7,5},{8,10},{9,11},{10,... | collective-permute-start | bytes 344072 | tf_op jit(solution)/shard_map/ppermute | solution.py:1140
  75.2 4.6 %collective-permute-start.13 = (f32[32,128]{1,0:T(8,128)S(1)}, f32[32,128]{1,0:T(8,128)S(1)}, u32[]{:S(2)}, u32[]{:S(2)}) collective-permute-start(f32[32,128]{1,0:T(8,128)S(1)} %get-tuple-element.202), channel_id=1, source_target_pairs={{0,6},{1,7},{2,4},{3,5},{4,2},{5,3},{6,0},{7,1},{8,14},{9,15},{10,... | collective-permute-start | bytes 49160 | tf_op jit(solution)/shard_map/ppermute | solution.py:1140
  79.9 9.0 %collective-permute-start.14 = (f32[208,128]{1,0:T(8,128)S(1)}, f32[208,128]{1,0:T(8,128)S(1)}, u32[]{:S(2)}, u32[]{:S(2)}) collective-permute-start(f32[208,128]{1,0:T(8,128)S(1)} %constant_dynamic-update-slice_fusion), channel_id=1, source_target_pairs={{0,16},{1,17},{2,18},{3,19},{4,20},{5,21},{6,22},{7,23},{8,24},{9,... | collective-permute-start | bytes 319496 | tf_op jit(solution)/shard_map/ppermute | solution.py:1140
  82.6 5.2 %collective-permute-start.15 = (f32[96,128]{1,0:T(8,128)S(1)}, f32[96,128]{1,0:T(8,128)S(1)}, u32[]{:S(2)}, u32[]{:S(2)}) collective-permute-start(f32[96,128]{1,0:T(8,128)S(1)} %pad_maximum_fusion.5), channel_id=1, source_target_pairs={{0,8},{1,9},{2,10},{3,11},{4,12},{5,13},{6,14},{7,15},{8,0},{9,1},... | collective-permute-start | bytes 147464 | tf_op jit(solution)/shard_map/ppermute | solution.py:1140
  83.0 5.9 %collective-permute-start.16 = (f32[96,128]{1,0:T(8,128)S(1)}, f32[96,128]{1,0:T(8,128)S(1)}, u32[]{:S(2)}, u32[]{:S(2)}) collective-permute-start(f32[96,128]{1,0:T(8,128)S(1)} %pad_maximum_fusion.6), channel_id=1, source_target_pairs={{0,24},{1,25},{2,26},{3,27},{4,28},{5,29},{6,30},{7,31},{8,16},{9,... | collective-permute-start | bytes 147464 | tf_op jit(solution)/shard_map/ppermute | solution.py:1140
  88.9 20.9 %copy-start.3 = (f32[2960]{0:T(1024)S(1)}, f32[2960]{0:T(1024)}, u32[]{:S(2)}) copy-start(f32[2960]{0:T(1024)} %param.21) | copy-start | bytes 35524
  88.9 20.9 %copy-start.4 = (f32[2960]{0:T(1024)S(1)}, f32[2960]{0:T(1024)}, u32[]{:S(2)}) copy-start(f32[2960]{0:T(1024)} %param.20) | copy-start | bytes 35524
  89.2 5.4 %collective-permute-start.17 = (bf16[224,128]{1,0:T(8,128)(2,1)S(1)}, bf16[224,128]{1,0:T(8,128)(2,1)S(1)}, u32[]{:S(2)}, u32[]{:S(2)}) collective-permute-start(bf16[224,128]{1,0:T(8,128)(2,1)S(1)} %get-tuple-element.225), channel_id=1, source_target_pairs={{0,16},{1,17},{2,18},{3,19},{4,20},{5,21},{6,22},{7,23},{8,24},{9,... | collective-permute-start | bytes 172040 | tf_op jit(solution)/shard_map/ppermute | solution.py:1140
  90.6 4.6 %collective-permute-start.18 = (bf16[224,128]{1,0:T(8,128)(2,1)S(1)}, bf16[224,128]{1,0:T(8,128)(2,1)S(1)}, u32[]{:S(2)}, u32[]{:S(2)}) collective-permute-start(bf16[224,128]{1,0:T(8,128)(2,1)S(1)} %get-tuple-element.225), channel_id=1, source_target_pairs={{0,8},{1,9},{2,10},{3,11},{4,12},{5,13},{6,14},{7,15},{8,0},{9,1},... | collective-permute-start | bytes 172040 | tf_op jit(solution)/shard_map/ppermute | solution.py:1140
  91.5 6.0 %collective-permute-start.19 = (bf16[224,128]{1,0:T(8,128)(2,1)S(1)}, bf16[224,128]{1,0:T(8,128)(2,1)S(1)}, u32[]{:S(2)}, u32[]{:S(2)}) collective-permute-start(bf16[224,128]{1,0:T(8,128)(2,1)S(1)} %get-tuple-element.225), channel_id=1, source_target_pairs={{0,24},{1,25},{2,26},{3,27},{4,28},{5,29},{6,30},{7,31},{8,16},{9,... | collective-permute-start | bytes 172040 | tf_op jit(solution)/shard_map/ppermute | solution.py:1140
  97.6 5.9 %collective-permute-start.23 = (bf16[448,128]{1,0:T(8,128)(2,1)S(1)}, bf16[448,128]{1,0:T(8,128)(2,1)S(1)}, u32[]{:S(2)}, u32[]{:S(2)}) collective-permute-start(bf16[448,128]{1,0:T(8,128)(2,1)S(1)} %maximum_select_fusion.7), channel_id=1, source_target_pairs={{0,4},{1,5},{2,6},{3,7},{4,0},{5,1},{6,2},{7,3},{8,12},{9,13},{10,... | collective-permute-start | bytes 344072 | tf_op jit(solution)/shard_map/ppermute | solution.py:1140
  99.2 4.9 %collective-permute-start.20 = (bf16[448,128]{1,0:T(8,128)(2,1)S(1)}, bf16[448,128]{1,0:T(8,128)(2,1)S(1)}, u32[]{:S(2)}, u32[]{:S(2)}) collective-permute-start(bf16[448,128]{1,0:T(8,128)(2,1)S(1)} %maximum_select_fusion.6), channel_id=1, source_target_pairs={{0,2},{1,3},{2,0},{3,1},{4,6},{5,7},{6,4},{7,5},{8,10},{9,11},{10,... | collective-permute-start | bytes 344072 | tf_op jit(solution)/shard_map/ppermute | solution.py:1140
  103.5 6.1 %collective-permute-start.24 = (bf16[896,128]{1,0:T(8,128)(2,1)S(1)}, bf16[896,128]{1,0:T(8,128)(2,1)S(1)}, u32[]{:S(2)}, u32[]{:S(2)}) collective-permute-start(bf16[896,128]{1,0:T(8,128)(2,1)S(1)} %maximum_select_fusion.5), channel_id=1, source_target_pairs={{0,2},{1,3},{2,0},{3,1},{4,6},{5,7},{6,4},{7,5},{8,10},{9,11},{10,... | collective-permute-start | bytes 688136 | tf_op jit(solution)/shard_map/ppermute | solution.py:1140
  104.1 6.1 %collective-permute-start.21 = (bf16[896,128]{1,0:T(8,128)(2,1)S(1)}, bf16[896,128]{1,0:T(8,128)(2,1)S(1)}, u32[]{:S(2)}, u32[]{:S(2)}) collective-permute-start(bf16[896,128]{1,0:T(8,128)(2,1)S(1)} %maximum_select_fusion.4), channel_id=1, source_target_pairs={{0,4},{1,5},{2,6},{3,7},{4,0},{5,1},{6,2},{7,3},{8,12},{9,13},{10,... | collective-permute-start | bytes 688136 | tf_op jit(solution)/shard_map/ppermute | solution.py:1140
  109.7 1.9 %collective-permute-start.25 = (bf16[1792,128]{1,0:T(8,128)(2,1)S(1)}, bf16[1792,128]{1,0:T(8,128)(2,1)S(1)}, u32[]{:S(2)}, u32[]{:S(2)}) collective-permute-start(bf16[1792,128]{1,0:T(8,128)(2,1)S(1)} %maximum_select_fusion.3), channel_id=1, source_target_pairs={{0,1},{1,0},{2,3},{3,2},{4,5},{5,4},{6,7},{7,6},{8,9},{9,8},{10,11... | collective-permute-start | bytes 1376264 | tf_op jit(solution)/shard_map/ppermute | solution.py:1140
  110.3 1.9 %collective-permute-start.22 = (bf16[1792,128]{1,0:T(8,128)(2,1)S(1)}, bf16[1792,128]{1,0:T(8,128)(2,1)S(1)}, u32[]{:S(2)}, u32[]{:S(2)}) collective-permute-start(bf16[1792,128]{1,0:T(8,128)(2,1)S(1)} %maximum_select_fusion.2), channel_id=1, source_target_pairs={{0,1},{1,0},{2,3},{3,2},{4,5},{5,4},{6,7},{7,6},{8,9},{9,8},{10,11... | collective-permute-start | bytes 1376264 | tf_op jit(solution)/shard_map/ppermute | solution.py:1140

commit v5 on v4

--- a/solution.py
+++ b/solution.py
@@ -39,7 +39,7 @@
 ONE_B = ONE_P + 3 * 64
 ONE_LOSS = ONE_B + 8
 ONE_ROWS = 2816
-PART_A = 1536
+PART_A = 768
 REST_A = 4 * 56
 REST_SMALL = REST_A + 8
 REST_ROWS = 256
@@ -311,7 +311,7 @@
 
 def couple_two_backward(
     dims,
-    bits,
+    bit,
     index_ref,
     mask2_ref,
     y2_ref,
@@ -325,10 +325,8 @@
     e_ref,
     wbt_ref,
     ft_ref,
-    kept_u,
-    sent_u,
-    kept_v,
-    sent_v,
+    kept_ref,
+    sent_ref,
     gkeep_ref,
     ext,
     gacc,
@@ -390,15 +388,14 @@
     gram(g_mixed, y2_ref, pairs, acc)
     stack = [(j, acc[j]) for j in pairs] + [(32, fold_lanes(g_mixed)), (33, out_sums)]
     slab_ref[TWO_SMALL : TWO_SMALL + 32, :] = lane_sums(stack, 32)
-    part_out(slab_ref, 0, TWO_ROWS // 2, index_ref[1], bits[0], kept_u, sent_u)
-    part_out(slab_ref, TWO_ROWS // 2, TWO_ROWS // 2, index_ref[1], bits[1], kept_v, sent_v)
+    part_out(slab_ref, 0, TWO_ROWS, index_ref[1], bit, kept_ref, sent_ref)
     valid_rows = [j for j in range(32) if j % 16 < CH]
     gkeep_ref[...] = mix(m2t_ref, gmix, 0, rows * chunk, valid_rows) * chan2_ref[:, 1:2]
 
 
 def level_two_kernel(
     dims,
-    bits,
+    bit,
     index_ref,
     b0,
     b1,
@@ -423,10 +420,8 @@
     keep_ref,
     loss_ref,
     gkeep_ref,
-    kept_u,
-    sent_u,
-    kept_v,
-    sent_v,
+    kept_ref,
+    sent_ref,
     bufs,
     xs,
     y2,
@@ -458,8 +453,8 @@
         out2, t2, xcol, h1, h2, loss_ref, ext_in, oacc,
     )
     couple_two_backward(
-        half, bits, index_ref, mask2_ref, y2, out2, t2, xcol, h1, h2, chan2_ref, m2t_ref, e_ref, wbt_ref, ft_ref,
-        kept_u, sent_u, kept_v, sent_v, gkeep_ref, ext_out, gacc, gmix, bacc, ge, gf, acc, slab,
+        half, bit, index_ref, mask2_ref, y2, out2, t2, xcol, h1, h2, chan2_ref, m2t_ref, e_ref, wbt_ref, ft_ref,
+        kept_ref, sent_ref, gkeep_ref, ext_out, gacc, gmix, bacc, ge, gf, acc, slab,
     )
 
 
@@ -616,6 +611,7 @@
     ghalf_ref,
     gbc_ref,
     ext,
+    gft,
     gf,
     bacc,
     slab_ref,
@@ -634,7 +630,7 @@
     g_out = g_out.astype(BF16).astype(F32)
     gbc_ref[...] = fold_lanes(g_out)
     fill_ext(ext, g_out, rows, cols, bands, jnp.zeros((16, 1), F32))
-    gf[...] = jnp.zeros_like(gf)
+    gft[...] = jnp.zeros_like(gft)
     slab_ref[...] = jnp.zeros_like(slab_ref)
     bacc[...] = jnp.zeros_like(bacc)
 
@@ -644,13 +640,15 @@
         gcol = gather_cols(ext, cols, row, col, chunk, True)
         hidden_two = h2_ref[:, at]
         g_pre = jnp.where(hidden_two > 0, dot(ft_ref[...], gcol), 0.0).astype(BF16)
-        gf[...] += dot_nt(gcol, hidden_two)
+        gft[...] += dot_nt(hidden_two, gcol)
         gpre_ref[:, at] = g_pre
         g_wb = dot_nt(g_pre, h1_ref[:, at])
         for block in range(HID // LANES):
             slab_ref[block * HID : (block + 1) * HID, :] += g_wb[:, block * LANES : (block + 1) * LANES]
         bacc[...] += fold_lanes(g_pre.astype(F32))
 
+    for first, count in ((0, LANES), (LANES, 16)):
+        gf[first : first + count, :] = gft[:, first : first + count].T
     bias = ones_sum(bacc)
     put_rows(slab_ref, lambda block: ONE_B + block, bias, 0, 1)
     for piece in range(18):
@@ -851,7 +849,7 @@
 
 def prepare_kernel(
     flat_ref,
-    prior_ref,
+    prior_far,
     entry_far,
     middle_far,
     exit_far,
@@ -866,12 +864,13 @@
     *refs,
 ):
     outs_two, outs_one = refs[:7], refs[7:14]
-    lu, wide, entry_ref, middle_ref, exit_ref, sems = refs[14:]
+    lu, wide, entry_ref, middle_ref, exit_ref, prior_ref, sems = refs[14:]
     copies = [
         pltpu.make_async_copy(middle_far.at[1], middle_ref.at[1], sems.at[0]),
         pltpu.make_async_copy(exit_far, exit_ref, sems.at[1]),
         pltpu.make_async_copy(entry_far, entry_ref, sems.at[2]),
         pltpu.make_async_copy(middle_far.at[0], middle_ref.at[0], sems.at[3]),
+        pltpu.make_async_copy(prior_far, prior_ref, sems.at[4]),
     ]
     for copy in copies:
         copy.start()
@@ -902,6 +901,7 @@
         chan_ref[...] = (
             jnp.where(lane == 0, shift, 0.0) + jnp.where(lane == 1, scale, 0.0) + jnp.where(lane == 2, out_bias, 0.0)
         )
+    copies[4].wait()
     places = prior_places()
     blocks = [None] * 3
     for tap in range(9):
@@ -1148,7 +1148,7 @@
     piece_rows = (CH + 1) * rows * cols // bands
     pieces = call(
         functools.partial(pack_kernel, bands),
-        (own, pixels.reshape(-1, LANES), valid_mask.reshape(-1, LANES)),
+        (own, in_hbm(pixels.reshape(-1, LANES)), in_hbm(valid_mask.reshape(-1, LANES))),
         [shape((piece_rows, LANES), BF16)] * bands,
         [],
         1000,
@@ -1180,7 +1180,7 @@
         e_one, e_one_t, f_one, f_one_t, wb_one, wb_one_t, bb_one,
     ) = call(
         prepare_kernel,
-        (after(vectors_flat, pieces[0]), prior_turned, in_hbm(entry_taps), in_hbm(middle), in_hbm(exit_taps)),
+        (after(vectors_flat, pieces[0]), in_hbm(prior_turned), in_hbm(entry_taps), in_hbm(middle), in_hbm(exit_taps)),
         [shape((16, LANES)), shape((16, LANES)), shape((32, LANES)), shape((32, LANES)), shape((32, LANES))]
         + [shape((64, 288), BF16), shape((288, 64), BF16), shape((64, 1))]
         + level_shapes(16)
@@ -1191,18 +1191,19 @@
             pltpu.VMEM(entry_taps.shape, F32),
             pltpu.VMEM(middle.shape, F32),
             pltpu.VMEM(exit_taps.shape, F32),
-            pltpu.SemaphoreType.DMA((4,)),
+            pltpu.VMEM(prior_turned.shape, F32),
+            pltpu.SemaphoreType.DMA((5,)),
         ],
         10**9,
-        far_in=(2, 3, 4),
+        far_in=(1, 2, 3, 4),
     )
 
 
     ext_lanes = (rows // 2 + 2) * (cols // 2 + 2) * LANES
     first_bit, second_bit, third_bit, fourth_bit = bits[0], bits[2], bits[1], bits[3]
-    quarter_two = shape((TWO_ROWS // 4, LANES))
-    (y1, mixed_one, mask, mask2, keep, loss_two, gkeep_two, kept_u, sent_u, kept_v, sent_v) = call(
-        functools.partial(level_two_kernel, dims, (second_bit, third_bit)),
+    half_two = shape((TWO_ROWS // 2, LANES))
+    (y1, mixed_one, mask, mask2, keep, loss_two, gkeep_two, kept_two, sent_two) = call(
+        functools.partial(level_two_kernel, dims, second_bit),
         (
             own, *bufs, chan_one, m_one, chan_two, m_two, m_two_t,
             e_two, e_two_t, f_two, f_two_t, wb_two, wb_two_t, bb_two,
@@ -1216,7 +1217,7 @@
             shape((8, LANES)),
             shape((32, part)),
         ]
-        + [quarter_two] * 4,
+        + [half_two] * 2,
         [
             pltpu.VMEM((bands, piece_rows, LANES), F32),
             pltpu.VMEM((16, size), F32),
@@ -1241,7 +1242,7 @@
         6 * HID * part * (144 + HID + 288),
     )
     whole_lanes = (rows + 2) * (cols + 2) * LANES
-    chunk = 1024
+    chunk = min(2048, size)
     fwd_in = (
         mixed_one,
         mask,
@@ -1281,17 +1282,16 @@
         ],
         2 * HID * size * (72 + HID + 144),
     )
-    total_u = kept_u + after(trade(sent_u, second_bit), loss_one)
-    total_v = kept_v + after(trade(sent_v, third_bit), loss_one)
-    top_in = (own, after(mask, total_u, total_v), res_one, t_one, gout_one, f_one_t, gwp, loss_one, loss_two, h1_one, h2_one)
+    top_in = (own, mask, res_one, t_one, gout_one, f_one_t, gwp, loss_one, loss_two, h1_one, h2_one)
     half_a, half_b = shape((PART_A // 2, LANES)), shape(((ONE_ROWS - PART_A) // 2, LANES))
     top_out = [shape((HID, size), BF16), half_a, half_a, half_b, half_b, shape((8, size)), shape((16, LANES))]
     (gpre, kept_a, sent_a, kept_b, sent_b, ghalf, gbc) = call(
-        functools.partial(one_backward_top, dims, chunk, (second_bit, third_bit)),
+        functools.partial(one_backward_top, dims, chunk // 2, (second_bit, third_bit)),
         top_in,
         top_out,
         [
             pltpu.VMEM((16, whole_lanes), F32),
+            pltpu.VMEM((HID, 144), F32),
             pltpu.VMEM((144, HID), F32),
             pltpu.VMEM((HID, LANES), F32),
             pltpu.VMEM((ONE_ROWS, LANES), F32),
@@ -1337,9 +1337,8 @@
                 first += h
         return totals + others
 
-    (total_u,) = halve([total_u], third_bit, gbc)
-    (total_v,) = halve([total_v], second_bit, gbc)
-    low_in = (y1, ghalf, after(gbc, total_u, total_v), gout_one, e_one, wb_one_t, xcol_one, h1_one, gpre)
+    total_two = kept_two + after(trade(sent_two, second_bit), gbc)
+    low_in = (y1, ghalf, after(gbc, total_two), gout_one, e_one, wb_one_t, xcol_one, h1_one, gpre)
     (slab_rest,) = call(
         functools.partial(one_backward_bottom, dims, chunk),
         low_in,
@@ -1355,26 +1354,27 @@
 
     total_a = kept_a + after(trade(sent_a, second_bit), slab_rest)
     total_b = kept_b + after(trade(sent_b, third_bit), slab_rest)
-    total_u, total_v = halve([total_u, total_v], fourth_bit, slab_rest)
+    (total_two,) = halve([total_two], fourth_bit, slab_rest)
     far = bits[3:]
-    total_u, total_v, total_a, total_b, total_rest = halve(
-        [total_u, total_v, total_a, total_b, after(slab_rest, total_u, total_v)], first_bit
-    )
-    total_rest, total_a, total_b = exchange([total_rest], [total_a], [total_b], third_bit, second_bit)
-    total_a, total_b, total_rest, total_u, total_v = exchange(
-        [total_a, total_b, total_rest], [], [total_u, total_v], far[0], far[1]
-    )
-    shards = [total_u, total_v, total_a, total_b, total_rest]
+    total_two, total_a, total_b, total_rest = halve(
+        [total_two, total_a, total_b, after(slab_rest, total_two)], first_bit
+    )
+    total_rest, total_a, total_two, total_b = exchange(
+        [total_rest], [total_a, total_two], [total_b], third_bit, second_bit
+    )
+    total_a, total_b, total_rest, total_two = exchange(
+        [total_a, total_b, total_rest], [], [total_two], far[0], far[1]
+    )
+    shards = [total_two, total_a, total_b, total_rest]
     for bit in far[2:]:
         shards = halve(shards, bit)
     orders = [
-        [second_bit, third_bit, fourth_bit, first_bit] + far[1:],
-        [third_bit, second_bit, fourth_bit, first_bit] + far[1:],
+        [second_bit, fourth_bit, first_bit, third_bit] + far[1:],
         [second_bit, first_bit, third_bit] + far,
         [third_bit, first_bit, second_bit] + far,
         [first_bit, third_bit, second_bit] + far,
     ]
-    loss_part = shards[3]
+    loss_part = shards[2]
     owner, loss_row = divmod(ONE_LOSS - PART_A, loss_part.shape[0])
     extra = []
     for row in range(3):
@@ -1384,7 +1384,7 @@
             extra.append(high)
             value = value - high
     extra = jnp.pad(jnp.stack(extra), ((0, 7), (0, 0)))
-    spread = [jnp.concatenate(shards[:2]).astype(BF16), jnp.concatenate(shards[2:] + [extra]).astype(BF16)]
+    spread = [shards[0].astype(BF16), jnp.concatenate(shards[1:] + [extra]).astype(BF16)]
     near = [[third_bit, second_bit, first_bit], [second_bit, third_bit, first_bit]]
     backs = [far[::-1] + near[0], far[::-1] + near[1]]
 
@@ -1430,15 +1430,15 @@
     totals = []
     first = 0
     for k, (shard, order) in enumerate(zip(shards, orders)):
-        first = 0 if k in (0, 2) else first
-        side = 0 if k < 2 else 1
+        first = 0 if k < 2 else first
+        side = 0 if k < 1 else 1
         totals.append(reorder(spread[side][..., first : first + shard.shape[0], :], backs[side], order))
         first += shard.shape[0]
     place = [0] * count_bits
-    for k, bit in enumerate(orders[3]):
+    for k, bit in enumerate(orders[2]):
         place[count_bits - 1 - backs[1].index(bit)] = (owner >> (count_bits - 1 - k)) & 1
     extra = spread[1][tuple(place)][first:]
-    totals = [jnp.concatenate(totals[:2]), jnp.concatenate(totals[2:4]), totals[4]]
+    totals = [totals[0], jnp.concatenate(totals[1:3]), totals[3]]
     taps = [
         (entry_taps, entry_first, entry_second),
         (middle, middle_first, middle_second),

time: 122 us -> 119 us (0.975)
  starting transfers between devices: 30.1 us -> 25.3 us
  waiting for transfers between devices: 21.7 us -> 26.1 us
  local copies, waits for them, and re-layouts: 4.07 us -> 1.35 us
    ppermute x23 -> x20, starting transfers between devices: 26.9 us -> 22.1 us  [trade(): lax.ppermute(value, ('batch', 'rows'), [(i, i ^ bit) for i in range(devic...]
    ppermute x23 -> x20, waiting for transfers between devices: 21.7 us -> 26.1 us  [trade(): lax.ppermute(value, ('batch', 'rows'), [(i, i ^ bit) for i in range(devic...]
    unnamed x23 -> x10, local copies, waits for them, and re-layouts: 2.89 us -> 0.08 us
  transfers between devices with their start and end apart: 26 -> 23, of which waited for: 14 -> 11; matrix products, arithmetic and copies ran while one was open for 2% -> 2% of each run, Pallas kernels for 34% -> 34%
where the time goes in v5:
time: 119 us
  Pallas kernels  62.5 us (53%)
  waiting for transfers between devices  26.1 us (22%)
  starting transfers between devices  25.3 us (21%)
  between operations  1.68 us (1%)
  other arithmetic  1.67 us (1%)
  local copies, waits for them, and re-layouts  1.35 us (1%)
    pallas_call x7, Pallas kernels, call(): pl.pallas_call(kernel, out_shape=outputs, in_specs=[far if k in far_in el...  62.5 us
    ppermute x20, waiting for transfers between devices, trade(): lax.ppermute(value, ('batch', 'rows'), [(i, i ^ bit) for i in range(devic...  26.1 us
    ppermute x20, starting transfers between devices, trade(): lax.ppermute(value, ('batch', 'rows'), [(i, i ^ bit) for i in range(devic...  22.1 us
    ppermute x3, starting transfers between devices, on_device(): lax.ppermute(pieces[d], 'rows', [(i, i ^ d) for i in range(bands)])  3.18 us
  transfers between devices with their start and end apart: 23, of which 11 were waited for; matrix products, arithmetic and copies ran while one was open for 2% of the time, Pallas kernels for 34%

profile of v5, /device:TPU:0, one launch (start us, length us, event | category | flops | bytes accessed | tf_op | source)
XLA Modules:
  0.0 118.6 jit_solution(6100849868511631196)
XLA Ops:
  0.7 0.1 pad_add_fusion.index_ref
  0.7 1.3 %shard_map.304 = (bf16[208,128]{1,0:T(8,128)(2,1)S(1)}, bf16[208,128]{1,0:T(8,128)(2,1)S(1)}, bf16[208,128]{1,0:T(8,128)(2,1)S(1)}, bf16[208,128]{1,0:T(8,128)(2,1)S(1)}) custom-call(s32[2]{0:T(128)S(1)} %pad_add_fusion.index_ref, s32[768,128]{1,0:T(8,128)} %bitcast.47, s32[64,128]{1,0:T(8,128)} %bitcast.52), custom_call_target="tpu_custom_call" | custom-call | flops 1000 | bytes 638984 | tf_op jit(solution)/shard_map/pallas_call | solution.py:714
  2.0 0.5 collective-permute-start
  2.6 2.6 %collective-permute-start.1 = (bf16[208,128]{1,0:T(8,128)(2,1)S(1)}, bf16[208,128]{1,0:T(8,128)(2,1)S(1)}, u32[]{:S(2)}, u32[]{:S(2)}) collective-permute-start(bf16[208,128]{1,0:T(8,128)(2,1)S(1)} %get-tuple-element.95), channel_id=1, source_target_pairs={{0,2},{1,3},{2,0},{3,1},{4,6},{5,7},{6,4},{7,5},{8,10},{9,11},{10,... | collective-permute-start | bytes 159752 | tf_op jit(solution)/shard_map/ppermute | solution.py:1158
  5.2 0.7 pad_bitcast_fusion.2.flat_ref
  5.9 5.1 %shard_map.305 = (f32[16,128]{1,0:T(8,128)S(1)}, f32[16,128]{1,0:T(8,128)S(1)}, f32[32,128]{1,0:T(8,128)S(1)}, f32[32,128]{1,0:T(8,128)S(1)}, f32[32,128]{1,0:T(...) custom-call(f32[24,128]{1,0:T(8,128)S(1)} %pad_bitcast_fusion.2.flat, ...), custom_call_target="tpu_custom_call" | custom-call | flops 1000000000 | bytes 6714112 | tf_op jit(solution)/shard_map/pallas_call | solution.py:714
  11.1 12.3 %shard_map.306 = (f32[16,8192]{1,0:T(8,128)S(1)}, f32[16,8192]{1,0:T(8,128)S(1)}, f32[1,8192]{1,0:T(1,128)S(1)}, f32[1,2048]{1,0:T(1,128)S(1)}, f32[32,2048]{1,0...) custom-call(s32[2]{0:T(128)S(1)} %pad_add_fusion.index_ref, ...), custom_call_target="tpu_custom_call" | custom-call | flops 5939134464 | bytes 5666824 | tf_op jit(solution)/shard_map/pallas_call | solution.py:714
  23.3 1.8 %collective-permute-start.3 = (f32[1792,128]{1,0:T(8,128)S(1)}, f32[1792,128]{1,0:T(8,128)S(1)}, u32[]{:S(2)}, u32[]{:S(2)}) collective-permute-start(f32[1792,128]{1,0:T(8,128)S(1)} %get-tuple-element.111), channel_id=1, source_target_pairs={{0,4},{1,5},{2,6},{3,7},{4,0},{5,1},{6,2},{7,3},{8,12},{9,13},{10,... | collective-permute-start | bytes 2752520 | tf_op jit(solution)/shard_map/ppermute | solution.py:1140
  25.1 10.5 %shard_map.307 = (bf16[72,8192]{1,0:T(8,128)(2,1)S(1)}, bf16[512,8192]{1,0:T(8,128)(2,1)S(1)}, bf16[512,8192]{1,0:T(8,128)(2,1)S(1)}, f32[8,8192]{1,0:T(8,128)S(...) custom-call(f32[16,8192]{1,0:T(8,128)S(1)} %get-tuple-element.113.mix1_ref, ...), custom_call_target="tpu_custom_call" | custom-call | flops 6106906624 | bytes 21002496 | tf_op jit(solution)/shard_map/pallas_call | solution.py:714
  35.6 13.3 %shard_map.308 = (bf16[512,8192]{1,0:T(8,128)(2,1)S(1)}, f32[384,128]{1,0:T(8,128)S(1)}, f32[384,128]{1,0:T(8,128)S(1)}, f32[1024,128]{1,0:T(8,128)S(1)}, f32[10...) custom-call(s32[2]{0:T(128)S(1)} %pad_add_fusion.index_ref, ...), custom_call_target="tpu_custom_call", output_to_operand_aliasing={{0}: (10, {})} | custom-call | flops 6710886400 | bytes 28188680 | tf_op jit(solution)/shard_map/pallas_call | solution.py:714
  48.9 0.4 collective-permute-start.5
  49.3 1.7 %collective-permute-start.6 = (f32[1024,128]{1,0:T(8,128)S(1)}, f32[1024,128]{1,0:T(8,128)S(1)}, u32[]{:S(2)}, u32[]{:S(2)}) collective-permute-start(f32[1024,128]{1,0:T(8,128)S(1)} %get-tuple-element.147), channel_id=1, source_target_pairs={{0,2},{1,3},{2,0},{3,1},{4,6},{5,7},{6,4},{7,5},{8,10},{9,11},{10,... | collective-permute-start | bytes 1572872 | tf_op jit(solution)/shard_map/ppermute | solution.py:1140
  51.0 0.1 add.230
  51.2 1.7 %collective-permute-start.4 = (f32[896,128]{1,0:T(8,128)S(1)}, f32[896,128]{1,0:T(8,128)S(1)}, u32[]{:S(2)}, u32[]{:S(2)}) collective-permute-start(f32[896,128]{1,0:T(8,128)S(1)} %constant_dynamic-slice_fusion.21), channel_id=1, source_target_pairs={{0,8},{1,9},{2,10},{3,11},{4,12},{5,13},{6,14},{7,15},{8,0},{9,1},... | collective-permute-start | bytes 1376264 | tf_op jit(solution)/shard_map/ppermute | solution.py:1140
  52.9 11.1 %shard_map.309 = f32[256,128]{1,0:T(8,128)S(1)} custom-call(f32[16,8192]{1,0:T(8,128)S(1)} %get-tuple-element.135.y1_ref, f32[8,8192]{1,0:T(8,128)S(1)} %get-tuple-element.136.ghalf_ref, f32[16,128]{1,0:T(8,128)S(1)} %get-tuple-element.137.gbc_ref, f32[16,8192]{1,0:T(8,128)S(1)} %get-tuple-element.126.gout_ref, ...), custom_call_target="tpu_custom_call" | custom-call | flops 5502926848 | bytes 20004864 | tf_op jit(solution)/shard_map/pallas_call | solution.py:714
  64.3 0.1 collective-permute-start.7
  64.6 1.8 %collective-permute-done.7 = f32[1280,128]{1,0:T(8,128)S(1)} collective-permute-done((f32[1280,128]{1,0:T(8,128)S(1)}, f32[1280,128]{1,0:T(8,128)S(1)}, u32[]{:S(2)}, u32[]{:S(2)}) %collective-permute-start.7) | collective-permute-done | bytes 655392 | tf_op jit(solution)/shard_map/ppermute | solution.py:1140
  66.6 1.6 %collective-permute-start.9 = (f32[288,128]{1,0:T(8,128)S(1)}, f32[288,128]{1,0:T(8,128)S(1)}, u32[]{:S(2)}, u32[]{:S(2)}) collective-permute-start(f32[288,128]{1,0:T(8,128)S(1)} %pad_maximum_fusion.3), channel_id=1, source_target_pairs={{0,4},{1,5},{2,6},{3,7},{4,0},{5,1},{6,2},{7,3},{8,12},{9,13},{10,... | collective-permute-start | bytes 442376 | tf_op jit(solution)/shard_map/ppermute | solution.py:1140
  68.3 0.8 collective-permute-start.8
  69.0 1.3 %collective-permute-start.10 = (f32[32,128]{1,0:T(8,128)S(1)}, f32[32,128]{1,0:T(8,128)S(1)}, u32[]{:S(2)}, u32[]{:S(2)}) collective-permute-start(f32[32,128]{1,0:T(8,128)S(1)} %get-tuple-element.180), channel_id=1, source_target_pairs={{0,6},{1,7},{2,4},{3,5},{4,2},{5,3},{6,0},{7,1},{8,14},{9,15},{10,... | collective-permute-start | bytes 49160 | tf_op jit(solution)/shard_map/ppermute | solution.py:1140
  70.3 2.5 %collective-permute-done.9 = f32[288,128]{1,0:T(8,128)S(1)} collective-permute-done((f32[288,128]{1,0:T(8,128)S(1)}, f32[288,128]{1,0:T(8,128)S(1)}, u32[]{:S(2)}, u32[]{:S(2)}) %collective-permute-start.9) | collective-permute-done | bytes 147488 | tf_op jit(solution)/shard_map/ppermute | solution.py:1140
  72.8 2.2 %collective-permute-done.8 = f32[352,128]{1,0:T(8,128)S(1)} collective-permute-done((f32[352,128]{1,0:T(8,128)S(1)}, f32[352,128]{1,0:T(8,128)S(1)}, u32[]{:S(2)}, u32[]{:S(2)}) %collective-permute-start.8) | collective-permute-done | bytes 180256 | tf_op jit(solution)/shard_map/ppermute | solution.py:1140
  75.1 2.7 %collective-permute-start.11 = (f32[208,128]{1,0:T(8,128)S(1)}, f32[208,128]{1,0:T(8,128)S(1)}, u32[]{:S(2)}, u32[]{:S(2)}) collective-permute-start(f32[208,128]{1,0:T(8,128)S(1)} %pad_maximum_fusion.4), channel_id=1, source_target_pairs={{0,16},{1,17},{2,18},{3,19},{4,20},{5,21},{6,22},{7,23},{8,24},{9,... | collective-permute-start | bytes 319496 | tf_op jit(solution)/shard_map/ppermute | solution.py:1140
  77.8 0.7 collective-permute-start.12
  78.6 1.0 collective-permute-start.13
  79.6 3.3 %collective-permute-done.12 = f32[96,128]{1,0:T(8,128)S(1)} collective-permute-done((f32[96,128]{1,0:T(8,128)S(1)}, f32[96,128]{1,0:T(8,128)S(1)}, u32[]{:S(2)}, u32[]{:S(2)}) %collective-permute-start.12) | collective-permute-done | bytes 49184 | tf_op jit(solution)/shard_map/ppermute | solution.py:1140
  82.9 1.5 %collective-permute-done.13 = f32[96,128]{1,0:T(8,128)S(1)} collective-permute-done((f32[96,128]{1,0:T(8,128)S(1)}, f32[96,128]{1,0:T(8,128)S(1)}, u32[]{:S(2)}, u32[]{:S(2)}) %collective-permute-start.13) | collective-permute-done | bytes 49184 | tf_op jit(solution)/shard_map/ppermute | solution.py:1140
  84.7 1.7 %collective-permute-start.14 = (bf16[224,128]{1,0:T(8,128)(2,1)S(1)}, bf16[224,128]{1,0:T(8,128)(2,1)S(1)}, u32[]{:S(2)}, u32[]{:S(2)}) collective-permute-start(bf16[224,128]{1,0:T(8,128)(2,1)S(1)} %get-tuple-element.205), channel_id=1, source_target_pairs={{0,16},{1,17},{2,18},{3,19},{4,20},{5,21},{6,22},{7,23},{8,24},{9,... | collective-permute-start | bytes 172040 | tf_op jit(solution)/shard_map/ppermute | solution.py:1140
  86.4 0.9 collective-permute-start.15
  87.3 1.9 %collective-permute-start.16 = (bf16[224,128]{1,0:T(8,128)(2,1)S(1)}, bf16[224,128]{1,0:T(8,128)(2,1)S(1)}, u32[]{:S(2)}, u32[]{:S(2)}) collective-permute-start(bf16[224,128]{1,0:T(8,128)(2,1)S(1)} %get-tuple-element.205), channel_id=1, source_target_pairs={{0,24},{1,25},{2,26},{3,27},{4,28},{5,29},{6,30},{7,31},{8,16},{9,... | collective-permute-start | bytes 172040 | tf_op jit(solution)/shard_map/ppermute | solution.py:1140
  89.1 2.0 %collective-permute-done.14 = bf16[224,128]{1,0:T(8,128)(2,1)S(1)} collective-permute-done((bf16[224,128]{1,0:T(8,128)(2,1)S(1)}, bf16[224,128]{1,0:T(8,128)(2,1)S(1)}, u32[]{:S(2)}, u32[]{:S(2)}) %collective-permute-start.14) | collective-permute-done | bytes 57376 | tf_op jit(solution)/shard_map/ppermute | solution.py:1140
  91.3 2.0 %collective-permute-done.16 = bf16[224,128]{1,0:T(8,128)(2,1)S(1)} collective-permute-done((bf16[224,128]{1,0:T(8,128)(2,1)S(1)}, bf16[224,128]{1,0:T(8,128)(2,1)S(1)}, u32[]{:S(2)}, u32[]{:S(2)}) %collective-permute-start.16) | collective-permute-done | bytes 57376 | tf_op jit(solution)/shard_map/ppermute | solution.py:1140
  93.3 0.6 collective-permute-start.20
  94.0 1.3 %collective-permute-start.17 = (bf16[448,128]{1,0:T(8,128)(2,1)S(1)}, bf16[448,128]{1,0:T(8,128)(2,1)S(1)}, u32[]{:S(2)}, u32[]{:S(2)}) collective-permute-start(bf16[448,128]{1,0:T(8,128)(2,1)S(1)} %maximum_select_fusion.6), channel_id=1, source_target_pairs={{0,2},{1,3},{2,0},{3,1},{4,6},{5,7},{6,4},{7,5},{8,10},{9,11},{10,... | collective-permute-start | bytes 344072 | tf_op jit(solution)/shard_map/ppermute | solution.py:1140
  95.3 3.7 %collective-permute-done.20 = bf16[448,128]{1,0:T(8,128)(2,1)S(1)} collective-permute-done((bf16[448,128]{1,0:T(8,128)(2,1)S(1)}, bf16[448,128]{1,0:T(8,128)(2,1)S(1)}, u32[]{:S(2)}, u32[]{:S(2)}) %collective-permute-start.20) | collective-permute-done | bytes 114720 | tf_op jit(solution)/shard_map/ppermute | solution.py:1140
  99.0 1.9 %collective-permute-start.21 = (bf16[896,128]{1,0:T(8,128)(2,1)S(1)}, bf16[896,128]{1,0:T(8,128)(2,1)S(1)}, u32[]{:S(2)}, u32[]{:S(2)}) collective-permute-start(bf16[896,128]{1,0:T(8,128)(2,1)S(1)} %maximum_select_fusion.5), channel_id=1, source_target_pairs={{0,2},{1,3},{2,0},{3,1},{4,6},{5,7},{6,4},{7,5},{8,10},{9,11},{10,... | collective-permute-start | bytes 688136 | tf_op jit(solution)/shard_map/ppermute | solution.py:1140
  101.0 0.1 collective-permute-start.18
  101.1 4.0 %collective-permute-done.21 = bf16[896,128]{1,0:T(8,128)(2,1)S(1)} collective-permute-done((bf16[896,128]{1,0:T(8,128)(2,1)S(1)}, bf16[896,128]{1,0:T(8,128)(2,1)S(1)}, u32[]{:S(2)}, u32[]{:S(2)}) %collective-permute-start.21) | collective-permute-done | bytes 229408 | tf_op jit(solution)/shard_map/ppermute | solution.py:1140
  105.1 0.1 maximum_select_fusion.3
  105.2 0.1 collective-permute-start.22
  105.4 1.8 %collective-permute-done.18 = bf16[896,128]{1,0:T(8,128)(2,1)S(1)} collective-permute-done((bf16[896,128]{1,0:T(8,128)(2,1)S(1)}, bf16[896,128]{1,0:T(8,128)(2,1)S(1)}, u32[]{:S(2)}, u32[]{:S(2)}) %collective-permute-start.18) | collective-permute-done | bytes 229408 | tf_op jit(solution)/shard_map/ppermute | solution.py:1140
  107.1 0.1 maximum_select_fusion.2
  107.2 0.1 collective-permute-start.19
  107.3 0.2 maximum_select_fusion.1
  107.8 1.3 %collective-permute-done.19 = bf16[1792,128]{1,0:T(8,128)(2,1)S(1)} collective-permute-done((bf16[1792,128]{1,0:T(8,128)(2,1)S(1)}, bf16[1792,128]{1,0:T(8,128)(2,1)S(1)}, u32[]{:S(2)}, u32[]{:S(2)}) %collective-permute-start.19) | collective-permute-done | bytes 458784 | tf_op jit(solution)/shard_map/ppermute | solution.py:1140
  109.1 0.2 maximum_select_fusion
  109.4 0.1 copy.37
  109.5 8.9 %shard_map.310 = (f32[1,1]{1,0:T(1,128)}, f32[1,1]{1,0:T(1,128)}, f32[24,128]{1,0:T(8,128)}, f32[24,128]{1,0:T(8,128)}, f32[24,128]{1,0:T(8,128)}, /*index=5*/f3...) custom-call(bf16[3584,128]{1,0:T(8,128)(2,1)S(1)} %bitcast.38, ...), custom_call_target="tpu_custom_call" | custom-call | flops 100000000 | bytes 20593672 | tf_op jit(solution)/shard_map/pallas_call | solution.py:714
  (79 shorter events, 1.4 us)
Async XLA Ops:
  2.0 9.0 %collective-permute-start = (bf16[208,128]{1,0:T(8,128)(2,1)S(1)}, bf16[208,128]{1,0:T(8,128)(2,1)S(1)}, u32[]{:S(2)}, u32[]{:S(2)}) collective-permute-start(bf16[208,128]{1,0:T(8,128)(2,1)S(1)} %get-tuple-element.94), channel_id=1, source_target_pairs={{0,1},{1,0},{2,3},{3,2},{4,5},{5,4},{6,7},{7,6},{8,9},{9,8},{10,11... | collective-permute-start | bytes 159752 | tf_op jit(solution)/shard_map/ppermute | solution.py:1158
  2.6 8.5 %collective-permute-start.1 = (bf16[208,128]{1,0:T(8,128)(2,1)S(1)}, bf16[208,128]{1,0:T(8,128)(2,1)S(1)}, u32[]{:S(2)}, u32[]{:S(2)}) collective-permute-start(bf16[208,128]{1,0:T(8,128)(2,1)S(1)} %get-tuple-element.95), channel_id=1, source_target_pairs={{0,2},{1,3},{2,0},{3,1},{4,6},{5,7},{6,4},{7,5},{8,10},{9,11},{10,... | collective-permute-start | bytes 159752 | tf_op jit(solution)/shard_map/ppermute | solution.py:1158
  5.2 5.9 %collective-permute-start.2 = (bf16[208,128]{1,0:T(8,128)(2,1)S(1)}, bf16[208,128]{1,0:T(8,128)(2,1)S(1)}, u32[]{:S(2)}, u32[]{:S(2)}) collective-permute-start(bf16[208,128]{1,0:T(8,128)(2,1)S(1)} %get-tuple-element.96), channel_id=1, source_target_pairs={{0,3},{1,2},{2,1},{3,0},{4,7},{5,6},{6,5},{7,4},{8,11},{9,10},{10,... | collective-permute-start | bytes 159752 | tf_op jit(solution)/shard_map/ppermute | solution.py:1158
  23.3 27.7 %collective-permute-start.3 = (f32[1792,128]{1,0:T(8,128)S(1)}, f32[1792,128]{1,0:T(8,128)S(1)}, u32[]{:S(2)}, u32[]{:S(2)}) collective-permute-start(f32[1792,128]{1,0:T(8,128)S(1)} %get-tuple-element.111), channel_id=1, source_target_pairs={{0,4},{1,5},{2,6},{3,7},{4,0},{5,1},{6,2},{7,3},{8,12},{9,13},{10,... | collective-permute-start | bytes 2752520 | tf_op jit(solution)/shard_map/ppermute | solution.py:1140
  48.9 15.0 %collective-permute-start.5 = (f32[384,128]{1,0:T(8,128)S(1)}, f32[384,128]{1,0:T(8,128)S(1)}, u32[]{:S(2)}, u32[]{:S(2)}) collective-permute-start(f32[384,128]{1,0:T(8,128)S(1)} %get-tuple-element.144), channel_id=1, source_target_pairs={{0,4},{1,5},{2,6},{3,7},{4,0},{5,1},{6,2},{7,3},{8,12},{9,13},{10,... | collective-permute-start | bytes 589832 | tf_op jit(solution)/shard_map/ppermute | solution.py:1140
  49.3 14.6 %collective-permute-start.6 = (f32[1024,128]{1,0:T(8,128)S(1)}, f32[1024,128]{1,0:T(8,128)S(1)}, u32[]{:S(2)}, u32[]{:S(2)}) collective-permute-start(f32[1024,128]{1,0:T(8,128)S(1)} %get-tuple-element.147), channel_id=1, source_target_pairs={{0,2},{1,3},{2,0},{3,1},{4,6},{5,7},{6,4},{7,5},{8,10},{9,11},{10,... | collective-permute-start | bytes 1572872 | tf_op jit(solution)/shard_map/ppermute | solution.py:1140
  51.2 12.9 %collective-permute-start.4 = (f32[896,128]{1,0:T(8,128)S(1)}, f32[896,128]{1,0:T(8,128)S(1)}, u32[]{:S(2)}, u32[]{:S(2)}) collective-permute-start(f32[896,128]{1,0:T(8,128)S(1)} %constant_dynamic-slice_fusion.21), channel_id=1, source_target_pairs={{0,8},{1,9},{2,10},{3,11},{4,12},{5,13},{6,14},{7,15},{8,0},{9,1},... | collective-permute-start | bytes 1376264 | tf_op jit(solution)/shard_map/ppermute | solution.py:1140
  64.3 2.2 %collective-permute-start.7 = (f32[1280,128]{1,0:T(8,128)S(1)}, f32[1280,128]{1,0:T(8,128)S(1)}, u32[]{:S(2)}, u32[]{:S(2)}) collective-permute-start(f32[1280,128]{1,0:T(8,128)S(1)} %pad_maximum_fusion.1), channel_id=1, source_target_pairs={{0,1},{1,0},{2,3},{3,2},{4,5},{5,4},{6,7},{7,6},{8,9},{9,8},{10,11... | collective-permute-start | bytes 1966088 | tf_op jit(solution)/shard_map/ppermute | solution.py:1140
  66.6 6.1 %collective-permute-start.9 = (f32[288,128]{1,0:T(8,128)S(1)}, f32[288,128]{1,0:T(8,128)S(1)}, u32[]{:S(2)}, u32[]{:S(2)}) collective-permute-start(f32[288,128]{1,0:T(8,128)S(1)} %pad_maximum_fusion.3), channel_id=1, source_target_pairs={{0,4},{1,5},{2,6},{3,7},{4,0},{5,1},{6,2},{7,3},{8,12},{9,13},{10,... | collective-permute-start | bytes 442376 | tf_op jit(solution)/shard_map/ppermute | solution.py:1140
  68.3 6.7 %collective-permute-start.8 = (f32[352,128]{1,0:T(8,128)S(1)}, f32[352,128]{1,0:T(8,128)S(1)}, u32[]{:S(2)}, u32[]{:S(2)}) collective-permute-start(f32[352,128]{1,0:T(8,128)S(1)} %pad_maximum_fusion.2), channel_id=1, source_target_pairs={{0,2},{1,3},{2,0},{3,1},{4,6},{5,7},{6,4},{7,5},{8,10},{9,11},{10,... | collective-permute-start | bytes 540680 | tf_op jit(solution)/shard_map/ppermute | solution.py:1140
  69.0 6.0 %collective-permute-start.10 = (f32[32,128]{1,0:T(8,128)S(1)}, f32[32,128]{1,0:T(8,128)S(1)}, u32[]{:S(2)}, u32[]{:S(2)}) collective-permute-start(f32[32,128]{1,0:T(8,128)S(1)} %get-tuple-element.180), channel_id=1, source_target_pairs={{0,6},{1,7},{2,4},{3,5},{4,2},{5,3},{6,0},{7,1},{8,14},{9,15},{10,... | collective-permute-start | bytes 49160 | tf_op jit(solution)/shard_map/ppermute | solution.py:1140
  75.1 9.3 %collective-permute-start.11 = (f32[208,128]{1,0:T(8,128)S(1)}, f32[208,128]{1,0:T(8,128)S(1)}, u32[]{:S(2)}, u32[]{:S(2)}) collective-permute-start(f32[208,128]{1,0:T(8,128)S(1)} %pad_maximum_fusion.4), channel_id=1, source_target_pairs={{0,16},{1,17},{2,18},{3,19},{4,20},{5,21},{6,22},{7,23},{8,24},{9,... | collective-permute-start | bytes 319496 | tf_op jit(solution)/shard_map/ppermute | solution.py:1140
  77.8 5.1 %collective-permute-start.12 = (f32[96,128]{1,0:T(8,128)S(1)}, f32[96,128]{1,0:T(8,128)S(1)}, u32[]{:S(2)}, u32[]{:S(2)}) collective-permute-start(f32[96,128]{1,0:T(8,128)S(1)} %pad_maximum_fusion.5), channel_id=1, source_target_pairs={{0,8},{1,9},{2,10},{3,11},{4,12},{5,13},{6,14},{7,15},{8,0},{9,1},... | collective-permute-start | bytes 147464 | tf_op jit(solution)/shard_map/ppermute | solution.py:1140
  78.6 5.9 %collective-permute-start.13 = (f32[96,128]{1,0:T(8,128)S(1)}, f32[96,128]{1,0:T(8,128)S(1)}, u32[]{:S(2)}, u32[]{:S(2)}) collective-permute-start(f32[96,128]{1,0:T(8,128)S(1)} %pad_maximum_fusion.6), channel_id=1, source_target_pairs={{0,24},{1,25},{2,26},{3,27},{4,28},{5,29},{6,30},{7,31},{8,16},{9,... | collective-permute-start | bytes 147464 | tf_op jit(solution)/shard_map/ppermute | solution.py:1140
  84.5 20.8 %copy-start = (f32[2960]{0:T(1024)S(1)}, f32[2960]{0:T(1024)}, u32[]{:S(2)}) copy-start(f32[2960]{0:T(1024)} %param.21) | copy-start | bytes 35524
  84.5 20.8 %copy-start.1 = (f32[2960]{0:T(1024)S(1)}, f32[2960]{0:T(1024)}, u32[]{:S(2)}) copy-start(f32[2960]{0:T(1024)} %param.20) | copy-start | bytes 35524
  84.7 6.5 %collective-permute-start.14 = (bf16[224,128]{1,0:T(8,128)(2,1)S(1)}, bf16[224,128]{1,0:T(8,128)(2,1)S(1)}, u32[]{:S(2)}, u32[]{:S(2)}) collective-permute-start(bf16[224,128]{1,0:T(8,128)(2,1)S(1)} %get-tuple-element.205), channel_id=1, source_target_pairs={{0,16},{1,17},{2,18},{3,19},{4,20},{5,21},{6,22},{7,23},{8,24},{9,... | collective-permute-start | bytes 172040 | tf_op jit(solution)/shard_map/ppermute | solution.py:1140
  86.4 4.9 %collective-permute-start.15 = (bf16[224,128]{1,0:T(8,128)(2,1)S(1)}, bf16[224,128]{1,0:T(8,128)(2,1)S(1)}, u32[]{:S(2)}, u32[]{:S(2)}) collective-permute-start(bf16[224,128]{1,0:T(8,128)(2,1)S(1)} %get-tuple-element.205), channel_id=1, source_target_pairs={{0,8},{1,9},{2,10},{3,11},{4,12},{5,13},{6,14},{7,15},{8,0},{9,1},... | collective-permute-start | bytes 172040 | tf_op jit(solution)/shard_map/ppermute | solution.py:1140
  87.3 6.0 %collective-permute-start.16 = (bf16[224,128]{1,0:T(8,128)(2,1)S(1)}, bf16[224,128]{1,0:T(8,128)(2,1)S(1)}, u32[]{:S(2)}, u32[]{:S(2)}) collective-permute-start(bf16[224,128]{1,0:T(8,128)(2,1)S(1)} %get-tuple-element.205), channel_id=1, source_target_pairs={{0,24},{1,25},{2,26},{3,27},{4,28},{5,29},{6,30},{7,31},{8,16},{9,... | collective-permute-start | bytes 172040 | tf_op jit(solution)/shard_map/ppermute | solution.py:1140
  93.3 5.6 %collective-permute-start.20 = (bf16[448,128]{1,0:T(8,128)(2,1)S(1)}, bf16[448,128]{1,0:T(8,128)(2,1)S(1)}, u32[]{:S(2)}, u32[]{:S(2)}) collective-permute-start(bf16[448,128]{1,0:T(8,128)(2,1)S(1)} %maximum_select_fusion.7), channel_id=1, source_target_pairs={{0,4},{1,5},{2,6},{3,7},{4,0},{5,1},{6,2},{7,3},{8,12},{9,13},{10,... | collective-permute-start | bytes 344072 | tf_op jit(solution)/shard_map/ppermute | solution.py:1140
  94.0 7.0 %collective-permute-start.17 = (bf16[448,128]{1,0:T(8,128)(2,1)S(1)}, bf16[448,128]{1,0:T(8,128)(2,1)S(1)}, u32[]{:S(2)}, u32[]{:S(2)}) collective-permute-start(bf16[448,128]{1,0:T(8,128)(2,1)S(1)} %maximum_select_fusion.6), channel_id=1, source_target_pairs={{0,2},{1,3},{2,0},{3,1},{4,6},{5,7},{6,4},{7,5},{8,10},{9,11},{10,... | collective-permute-start | bytes 344072 | tf_op jit(solution)/shard_map/ppermute | solution.py:1140
  99.0 6.1 %collective-permute-start.21 = (bf16[896,128]{1,0:T(8,128)(2,1)S(1)}, bf16[896,128]{1,0:T(8,128)(2,1)S(1)}, u32[]{:S(2)}, u32[]{:S(2)}) collective-permute-start(bf16[896,128]{1,0:T(8,128)(2,1)S(1)} %maximum_select_fusion.5), channel_id=1, source_target_pairs={{0,2},{1,3},{2,0},{3,1},{4,6},{5,7},{6,4},{7,5},{8,10},{9,11},{10,... | collective-permute-start | bytes 688136 | tf_op jit(solution)/shard_map/ppermute | solution.py:1140
  101.0 6.1 %collective-permute-start.18 = (bf16[896,128]{1,0:T(8,128)(2,1)S(1)}, bf16[896,128]{1,0:T(8,128)(2,1)S(1)}, u32[]{:S(2)}, u32[]{:S(2)}) collective-permute-start(bf16[896,128]{1,0:T(8,128)(2,1)S(1)} %maximum_select_fusion.4), channel_id=1, source_target_pairs={{0,4},{1,5},{2,6},{3,7},{4,0},{5,1},{6,2},{7,3},{8,12},{9,13},{10,... | collective-permute-start | bytes 688136 | tf_op jit(solution)/shard_map/ppermute | solution.py:1140
  105.2 2.1 %collective-permute-start.22 = (bf16[1792,128]{1,0:T(8,128)(2,1)S(1)}, bf16[1792,128]{1,0:T(8,128)(2,1)S(1)}, u32[]{:S(2)}, u32[]{:S(2)}) collective-permute-start(bf16[1792,128]{1,0:T(8,128)(2,1)S(1)} %maximum_select_fusion.3), channel_id=1, source_target_pairs={{0,1},{1,0},{2,3},{3,2},{4,5},{5,4},{6,7},{7,6},{8,9},{9,8},{10,11... | collective-permute-start | bytes 1376264 | tf_op jit(solution)/shard_map/ppermute | solution.py:1140
  107.2 1.9 %collective-permute-start.19 = (bf16[1792,128]{1,0:T(8,128)(2,1)S(1)}, bf16[1792,128]{1,0:T(8,128)(2,1)S(1)}, u32[]{:S(2)}, u32[]{:S(2)}) collective-permute-start(bf16[1792,128]{1,0:T(8,128)(2,1)S(1)} %maximum_select_fusion.2), channel_id=1, source_target_pairs={{0,1},{1,0},{2,3},{3,2},{4,5},{5,4},{6,7},{7,6},{8,9},{9,8},{10,11... | collective-permute-start | bytes 1376264 | tf_op jit(solution)/shard_map/ppermute | solution.py:1140

commit v6 on v5

--- a/solution.py
+++ b/solution.py
@@ -32,7 +32,6 @@
 WB_ROWS = 4 * HID
 TWO_F, TWO_E = WB_ROWS, WB_ROWS + 4 * 216
 TWO_B = TWO_E + 4 * 144
-TWO_SMALL = TWO_B + 8
 TWO_ROWS = 3584
 ONE_F = WB_ROWS
 ONE_P = ONE_F + 4 * 112
@@ -277,9 +276,9 @@
         at = slice(i * chunk, (i + 1) * chunk)
         xcol = gather_cols(ext, half_cols, i, 0, chunk)
         xcol_ref[:, at] = xcol
-        hidden = jnp.maximum(dot(et_ref[...], xcol), 0.0).astype(BF16)
+        hidden = jnp.maximum(dot(et_ref[...], xcol).astype(BF16), jnp.zeros((), BF16))
         h1_ref[:, at] = hidden
-        hidden = jnp.maximum(dot(wb_ref[...], hidden) + bias_ref[...], 0.0).astype(BF16)
+        hidden = jnp.maximum((dot(wb_ref[...], hidden) + bias_ref[...]).astype(BF16), jnp.zeros((), BF16))
         h2_ref[:, at] = hidden
         scatter_cols(oacc, dot(f_ref[...], hidden), half_cols, i, 0, chunk, True)
     output = jnp.concatenate(fold_ext(oacc, half_rows, half_cols, bands), axis=1) + chan2_ref[:, 2:3]
@@ -327,6 +326,7 @@
     ft_ref,
     kept_ref,
     sent_ref,
+    small_ref,
     gkeep_ref,
     ext,
     gacc,
@@ -359,11 +359,11 @@
         gcol = gather_cols(ext, cols, i, 0, chunk, True)
         hidden_two = h2_ref[:, at]
         hidden_one = h1_ref[:, at]
-        g_pre = jnp.where(hidden_two > 0, dot(ft_ref[...], gcol), 0.0).astype(BF16)
+        g_pre = jnp.where(hidden_two > 0, dot(ft_ref[...], gcol).astype(BF16), jnp.zeros((), BF16))
         g_f = dot_nt(gcol, hidden_two)
         g_wb = dot_nt(g_pre, hidden_one)
         folded = fold_lanes(g_pre.astype(F32))
-        g_pre = jnp.where(hidden_one > 0, dot(wbt_ref[...], g_pre), 0.0).astype(BF16)
+        g_pre = jnp.where(hidden_one > 0, dot(wbt_ref[...], g_pre).astype(BF16), jnp.zeros((), BF16))
         g_e = dot_nt(xcol_ref[:, at], g_pre)
         scatter_cols(gacc, dot(e_ref[...], g_pre), cols, i, 0, chunk)
         if i == 0:
@@ -387,7 +387,7 @@
     acc[...] = jnp.zeros_like(acc)
     gram(g_mixed, y2_ref, pairs, acc)
     stack = [(j, acc[j]) for j in pairs] + [(32, fold_lanes(g_mixed)), (33, out_sums)]
-    slab_ref[TWO_SMALL : TWO_SMALL + 32, :] = lane_sums(stack, 32)
+    small_ref[...] = lane_sums(stack, 32)
     part_out(slab_ref, 0, TWO_ROWS, index_ref[1], bit, kept_ref, sent_ref)
     valid_rows = [j for j in range(32) if j % 16 < CH]
     gkeep_ref[...] = mix(m2t_ref, gmix, 0, rows * chunk, valid_rows) * chan2_ref[:, 1:2]
@@ -422,6 +422,7 @@
     gkeep_ref,
     kept_ref,
     sent_ref,
+    small_ref,
     bufs,
     xs,
     y2,
@@ -454,7 +455,7 @@
     )
     couple_two_backward(
         half, bit, index_ref, mask2_ref, y2, out2, t2, xcol, h1, h2, chan2_ref, m2t_ref, e_ref, wbt_ref, ft_ref,
-        kept_ref, sent_ref, gkeep_ref, ext_out, gacc, gmix, bacc, ge, gf, acc, slab,
+        kept_ref, sent_ref, small_ref, gkeep_ref, ext_out, gacc, gmix, bacc, ge, gf, acc, slab,
     )
 
 
@@ -500,9 +501,9 @@
         row, col, at = place_of(step, chunk, cols)
         xcol = gather_cols(ext, cols, row, col, chunk)
         xcol_ref[:, at] = xcol
-        hidden = jnp.maximum(dot(et_ref[...], xcol), 0.0).astype(BF16)
+        hidden = jnp.maximum(dot(et_ref[...], xcol).astype(BF16), jnp.zeros((), BF16))
         h1_ref[:, at] = hidden
-        hidden = jnp.maximum(dot(wb_ref[...], hidden) + bias_ref[...], 0.0).astype(BF16)
+        hidden = jnp.maximum((dot(wb_ref[...], hidden) + bias_ref[...]).astype(BF16), jnp.zeros((), BF16))
         h2_ref[:, at] = hidden
         scatter_cols(oacc, dot(f_ref[...], hidden), cols, row, col, chunk, True)
 
@@ -639,7 +640,7 @@
         row, col, at = place_of(step, chunk, cols)
         gcol = gather_cols(ext, cols, row, col, chunk, True)
         hidden_two = h2_ref[:, at]
-        g_pre = jnp.where(hidden_two > 0, dot(ft_ref[...], gcol), 0.0).astype(BF16)
+        g_pre = jnp.where(hidden_two > 0, dot(ft_ref[...], gcol).astype(BF16), jnp.zeros((), BF16))
         gft[...] += dot_nt(hidden_two, gcol)
         gpre_ref[:, at] = g_pre
         g_wb = dot_nt(g_pre, h1_ref[:, at])
@@ -658,8 +659,8 @@
         slab_ref[ONE_P + block * 64 : ONE_P + block * 64 + 64, 0:width] = gwp_ref[
             :, block * LANES : block * LANES + width
         ]
-    slab_ref[ONE_LOSS : ONE_LOSS + 1, :] = loss_one_ref[0:1, :] + loss_two_ref[0:1, :]
-    slab_ref[ONE_LOSS + 1 : ONE_LOSS + 3, :] = loss_two_ref[1:3, :]
+    scalars = [(0, loss_one_ref[0:1, :] + loss_two_ref[0:1, :]), (1, loss_two_ref[1:2, :]), (2, loss_two_ref[2:3, :])]
+    slab_ref[ONE_LOSS : ONE_LOSS + 1, :] = lane_sums(scalars, 3)
     part_out(slab_ref, 0, PART_A, index_ref[1], bits[0], kept_a, sent_a)
     part_out(slab_ref, PART_A, ONE_ROWS - PART_A, index_ref[1], bits[1], kept_b, sent_b)
 
@@ -676,6 +677,7 @@
     xcol_ref,
     h1_ref,
     gpre_ref,
+    small_ref,
     slab_ref,
     gacc,
     gmix,
@@ -690,7 +692,7 @@
     @pl.loop(0, rows * cols * LANES // chunk)
     def _(step):
         row, col, at = place_of(step, chunk, cols)
-        g_pre = jnp.where(h1_ref[:, at] > 0, dot(wbt_ref[...], gpre_ref[:, at]), 0.0).astype(BF16)
+        g_pre = jnp.where(h1_ref[:, at] > 0, dot(wbt_ref[...], gpre_ref[:, at]).astype(BF16), jnp.zeros((), BF16))
         ge[...] += dot_nt(xcol_ref[:, at], g_pre)
         scatter_cols(gacc, dot(e_ref[...], g_pre), cols, row, col, chunk)
 
@@ -700,7 +702,9 @@
     acc[...] = jnp.zeros_like(acc)
     gram(g_mixed, y1_ref, range(CH), acc)
     stack = [(j, acc[j]) for j in range(CH)] + [(16, fold_lanes(g_mixed)), (17, gbc_ref[...])]
-    slab_ref[REST_SMALL : REST_SMALL + 16, :] = lane_sums(stack, CH)
+    slab_ref[REST_SMALL : REST_SMALL + 16, :] = (
+        lane_sums(stack, CH) + pltpu.roll(small_ref[0:16, :], 32, 1) + pltpu.roll(small_ref[16:32, :], 66, 1)
+    )
     for tap in range(9):
         put_rows(slab_ref, lambda block: block * 56 + tap * 6, ge, tap * 8, 6)
     put_rows(slab_ref, lambda block: REST_A + block, ge, 6, 1)
@@ -865,12 +869,13 @@
 ):
     outs_two, outs_one = refs[:7], refs[7:14]
     lu, wide, entry_ref, middle_ref, exit_ref, prior_ref, sems = refs[14:]
+    pieces = [(middle_far, middle_ref, (1, slice(k * LANES, (k + 1) * LANES))) for k in range(4)]
+    pieces += [(exit_far, exit_ref, (slice(3 * k, 3 * k + 3),)) for k in range(3)]
+    pieces += [(entry_far, entry_ref, (slice(3 * k, 3 * k + 3),)) for k in range(3)]
+    pieces += [(middle_far, middle_ref, (0, slice(k * LANES, (k + 1) * LANES))) for k in range(4)]
+    pieces += [(prior_far, prior_ref, (slice(0, 9),))]
     copies = [
-        pltpu.make_async_copy(middle_far.at[1], middle_ref.at[1], sems.at[0]),
-        pltpu.make_async_copy(exit_far, exit_ref, sems.at[1]),
-        pltpu.make_async_copy(entry_far, entry_ref, sems.at[2]),
-        pltpu.make_async_copy(middle_far.at[0], middle_ref.at[0], sems.at[3]),
-        pltpu.make_async_copy(prior_far, prior_ref, sems.at[4]),
+        pltpu.make_async_copy(source.at[at], target.at[at], sems.at[k]) for k, (source, target, at) in enumerate(pieces)
     ]
     for copy in copies:
         copy.start()
@@ -901,7 +906,7 @@
         chan_ref[...] = (
             jnp.where(lane == 0, shift, 0.0) + jnp.where(lane == 1, scale, 0.0) + jnp.where(lane == 2, out_bias, 0.0)
         )
-    copies[4].wait()
+    copies[14].wait()
     places = prior_places()
     blocks = [None] * 3
     for tap in range(9):
@@ -919,10 +924,11 @@
     row, lane = iotas(64)
     natural, valid = natural_keep(lax.rem(row, 32))
     pbias_ref[...] = pick((lane == natural + (row // 32) * 2 * CH) & valid, take_flat(flat_ref, PRIOR_START, 4 * CH))
-    for copy in copies[:3]:
+    for copy in copies[:10]:
         copy.wait()
     prepare_level(1, flat_ref, entry_ref, middle_ref, exit_ref, outs_two, wide)
-    copies[3].wait()
+    for copy in copies[10:14]:
+        copy.wait()
     prepare_level(0, flat_ref, entry_ref, middle_ref, exit_ref, outs_one, wide)
 
 
@@ -939,6 +945,7 @@
     two_ref,
     one_ref,
     rest_ref,
+    low_ref,
     extra_ref,
     flat_ref,
     flat_first,
@@ -975,14 +982,13 @@
         for copy in copies_in(k):
             copy.start()
     extra = extra_ref[...].astype(F32)
-    count = jnp.sum(extra[6:9], keepdims=True)
+    _, lane = iotas(extra.shape[0])
+    log_total, count_two, count = (jnp.sum(jnp.where(lane == k, extra, 0.0), keepdims=True) for k in range(3))
     coef = -1.0 / (CH * count * math.log(2.0))
     factor = -coef
     two[...] = two_ref[WB_ROWS:, :].astype(F32) * factor
     one[...] = one_ref[WB_ROWS:, :].astype(F32) * factor
-    rest[...] = rest_ref[...].astype(F32) * factor
-    log_total = jnp.sum(extra[0:3], keepdims=True)
-    count_two = jnp.sum(extra[3:6], keepdims=True)
+    rest[...] = (rest_ref[...].astype(F32) + low_ref[...].astype(F32)) * factor
     base = WB_ROWS
     squares = []
     pieces = {}
@@ -992,7 +998,9 @@
         consts.append(jnp.sum(chan[1] + chan[2], keepdims=True))
         weight = coef * count if level == 0 else coef * count_two
         height = 16 * (level + 1)
-        small = rest[REST_SMALL : REST_SMALL + 16, :] if level == 0 else two[TWO_SMALL - base : TWO_SMALL - base + 32, :]
+        small = rest[REST_SMALL : REST_SMALL + 16, :]
+        if level == 1:
+            small = jnp.concatenate([pltpu.roll(small, LANES - 32, 1), pltpu.roll(small, LANES - 66, 1)], axis=0)
         sum_lane = 16 * (level + 1)
         product = high_dot(lower, upper)
         row, lane = iotas(LANES, height)
@@ -1192,7 +1200,7 @@
             pltpu.VMEM(middle.shape, F32),
             pltpu.VMEM(exit_taps.shape, F32),
             pltpu.VMEM(prior_turned.shape, F32),
-            pltpu.SemaphoreType.DMA((5,)),
+            pltpu.SemaphoreType.DMA((15,)),
         ],
         10**9,
         far_in=(1, 2, 3, 4),
@@ -1202,7 +1210,7 @@
     ext_lanes = (rows // 2 + 2) * (cols // 2 + 2) * LANES
     first_bit, second_bit, third_bit, fourth_bit = bits[0], bits[2], bits[1], bits[3]
     half_two = shape((TWO_ROWS // 2, LANES))
-    (y1, mixed_one, mask, mask2, keep, loss_two, gkeep_two, kept_two, sent_two) = call(
+    (y1, mixed_one, mask, mask2, keep, loss_two, gkeep_two, kept_two, sent_two, small_two) = call(
         functools.partial(level_two_kernel, dims, second_bit),
         (
             own, *bufs, chan_one, m_one, chan_two, m_two, m_two_t,
@@ -1217,7 +1225,8 @@
             shape((8, LANES)),
             shape((32, part)),
         ]
-        + [half_two] * 2,
+        + [half_two] * 2
+        + [shape((32, LANES))],
         [
             pltpu.VMEM((bands, piece_rows, LANES), F32),
             pltpu.VMEM((16, size), F32),
@@ -1338,7 +1347,7 @@
         return totals + others
 
     total_two = kept_two + after(trade(sent_two, second_bit), gbc)
-    low_in = (y1, ghalf, after(gbc, total_two), gout_one, e_one, wb_one_t, xcol_one, h1_one, gpre)
+    low_in = (y1, ghalf, after(gbc, total_two), gout_one, e_one, wb_one_t, xcol_one, h1_one, gpre, small_two)
     (slab_rest,) = call(
         functools.partial(one_backward_bottom, dims, chunk),
         low_in,
@@ -1377,13 +1386,14 @@
     loss_part = shards[2]
     owner, loss_row = divmod(ONE_LOSS - PART_A, loss_part.shape[0])
     extra = []
-    for row in range(3):
-        value = loss_part[loss_row + row]
-        for _ in range(3):
-            high = lax.reduce_precision(value, 8, 7)
-            extra.append(high)
-            value = value - high
-    extra = jnp.pad(jnp.stack(extra), ((0, 7), (0, 0)))
+    value = loss_part[loss_row : loss_row + 1]
+    for _ in range(3):
+        high = lax.reduce_precision(value, 8, 7)
+        extra.append(high)
+        value = value - high
+    extra.append(shards[3] - lax.reduce_precision(shards[3], 8, 7))
+    extra = jnp.concatenate(extra)
+    extra = jnp.pad(extra, ((0, -extra.shape[0] % 16), (0, 0)))
     spread = [shards[0].astype(BF16), jnp.concatenate(shards[1:] + [extra]).astype(BF16)]
     near = [[third_bit, second_bit, first_bit], [second_bit, third_bit, first_bit]]
     backs = [far[::-1] + near[0], far[::-1] + near[1]]
@@ -1437,7 +1447,8 @@
     place = [0] * count_bits
     for k, bit in enumerate(orders[2]):
         place[count_bits - 1 - backs[1].index(bit)] = (owner >> (count_bits - 1 - k)) & 1
-    extra = spread[1][tuple(place)][first:]
+    extra = spread[1][tuple(place)][first : first + 3]
+    low_rest = reorder(spread[1][..., first + 3 : first + 3 + shards[3].shape[0], :], backs[1], orders[3])
     totals = [totals[0], jnp.concatenate(totals[1:3]), totals[3]]
     taps = [
         (entry_taps, entry_first, entry_second),
@@ -1452,7 +1463,7 @@
     outs.append(shape((4, HID)))
     results = call(
         finish_kernel,
-        (*totals, extra, *flats, *[in_hbm(x) for group in taps for x in group]),
+        (*totals, low_rest, extra, *flats, *[in_hbm(x) for group in taps for x in group]),
         outs,
         [
             pltpu.VMEM((TWO_ROWS - WB_ROWS, LANES), F32),
@@ -1463,7 +1474,7 @@
         + [pltpu.VMEM(group[0].shape, F32) for _ in range(4) for group in taps]
         + [pltpu.SemaphoreType.DMA((5, 3))] * 2,
         10**8,
-        far_in=range(7, 19),
+        far_in=range(8, 20),
         far_out=range(5, 17),
     )
     results = list(results)

time: 119 us -> 116 us (0.975)
  Pallas kernels: 62.5 us -> 59.1 us
  starting transfers between devices: 25.3 us -> 26.5 us
    pallas_call x7, Pallas kernels: 62.5 us -> 59.1 us  [call(): pl.pallas_call(kernel, out_shape=outputs, in_specs=[far if k in far_in el...]
  transfers between devices with their start and end apart: 23 -> 23, of which waited for: 11 -> 13; matrix products, arithmetic and copies ran while one was open for 2% -> 2% of each run, Pallas kernels for 34% -> 32%
where the time goes in v6:
time: 116 us
  Pallas kernels  59.1 us (51%)
  starting transfers between devices  26.5 us (23%)
  waiting for transfers between devices  25.9 us (22%)
  other arithmetic  1.73 us (1%)
  between operations  1.65 us (1%)
  local copies, waits for them, and re-layouts  1.26 us (1%)
    pallas_call x7, Pallas kernels, call(): pl.pallas_call(kernel, out_shape=outputs, in_specs=[far if k in far_in el...  59.1 us
    ppermute x20, waiting for transfers between devices, trade(): lax.ppermute(value, ('batch', 'rows'), [(i, i ^ bit) for i in range(devic...  25.9 us
    ppermute x20, starting transfers between devices, trade(): lax.ppermute(value, ('batch', 'rows'), [(i, i ^ bit) for i in range(devic...  23.3 us
    ppermute x3, starting transfers between devices, on_device(): lax.ppermute(pieces[d], 'rows', [(i, i ^ d) for i in range(bands)])  3.18 us
  transfers between devices with their start and end apart: 23, of which 13 were waited for; matrix products, arithmetic and copies ran while one was open for 2% of the time, Pallas kernels for 32%

profile of v6, /device:TPU:0, one launch (start us, length us, event | category | flops | bytes accessed | tf_op | source)
XLA Modules:
  0.0 116.1 jit_solution(1296075200817907043)
XLA Ops:
  0.7 0.1 pad_add_fusion.index_ref
  0.7 1.3 %shard_map.304 = (bf16[208,128]{1,0:T(8,128)(2,1)S(1)}, bf16[208,128]{1,0:T(8,128)(2,1)S(1)}, bf16[208,128]{1,0:T(8,128)(2,1)S(1)}, bf16[208,128]{1,0:T(8,128)(2,1)S(1)}) custom-call(s32[2]{0:T(128)S(1)} %pad_add_fusion.index_ref, s32[768,128]{1,0:T(8,128)} %bitcast.49, s32[64,128]{1,0:T(8,128)} %bitcast.54), custom_call_target="tpu_custom_call" | custom-call | flops 1000 | bytes 638984 | tf_op jit(solution)/shard_map/pallas_call | solution.py:718
  2.0 0.5 collective-permute-start
  2.6 2.6 %collective-permute-start.1 = (bf16[208,128]{1,0:T(8,128)(2,1)S(1)}, bf16[208,128]{1,0:T(8,128)(2,1)S(1)}, u32[]{:S(2)}, u32[]{:S(2)}) collective-permute-start(bf16[208,128]{1,0:T(8,128)(2,1)S(1)} %get-tuple-element.96), channel_id=1, source_target_pairs={{0,2},{1,3},{2,0},{3,1},{4,6},{5,7},{6,4},{7,5},{8,10},{9,11},{10,... | collective-permute-start | bytes 159752 | tf_op jit(solution)/shard_map/ppermute | solution.py:1166
  5.2 0.7 pad_bitcast_fusion.2.flat_ref
  5.9 5.0 %shard_map.305 = (f32[16,128]{1,0:T(8,128)S(1)}, f32[16,128]{1,0:T(8,128)S(1)}, f32[32,128]{1,0:T(8,128)S(1)}, f32[32,128]{1,0:T(8,128)S(1)}, f32[32,128]{1,0:T(...) custom-call(f32[24,128]{1,0:T(8,128)S(1)} %pad_bitcast_fusion.2.flat, ...), custom_call_target="tpu_custom_call" | custom-call | flops 1000000000 | bytes 6714112 | tf_op jit(solution)/shard_map/pallas_call | solution.py:718
  11.0 11.4 %shard_map.306 = (f32[16,8192]{1,0:T(8,128)S(1)}, f32[16,8192]{1,0:T(8,128)S(1)}, f32[1,8192]{1,0:T(1,128)S(1)}, f32[1,2048]{1,0:T(1,128)S(1)}, f32[32,2048]{1,0...) custom-call(s32[2]{0:T(128)S(1)} %pad_add_fusion.index_ref, ...), custom_call_target="tpu_custom_call" | custom-call | flops 5939134464 | bytes 5683208 | tf_op jit(solution)/shard_map/pallas_call | solution.py:718
  22.4 1.8 %collective-permute-start.3 = (f32[1792,128]{1,0:T(8,128)S(1)}, f32[1792,128]{1,0:T(8,128)S(1)}, u32[]{:S(2)}, u32[]{:S(2)}) collective-permute-start(f32[1792,128]{1,0:T(8,128)S(1)} %get-tuple-element.112), channel_id=1, source_target_pairs={{0,4},{1,5},{2,6},{3,7},{4,0},{5,1},{6,2},{7,3},{8,12},{9,13},{10,... | collective-permute-start | bytes 2752520 | tf_op jit(solution)/shard_map/ppermute | solution.py:1148
  24.2 10.5 %shard_map.307 = (bf16[72,8192]{1,0:T(8,128)(2,1)S(1)}, bf16[512,8192]{1,0:T(8,128)(2,1)S(1)}, bf16[512,8192]{1,0:T(8,128)(2,1)S(1)}, f32[8,8192]{1,0:T(8,128)S(...) custom-call(f32[16,8192]{1,0:T(8,128)S(1)} %get-tuple-element.114.mix1_ref, ...), custom_call_target="tpu_custom_call" | custom-call | flops 6106906624 | bytes 21002496 | tf_op jit(solution)/shard_map/pallas_call | solution.py:718
  34.7 11.8 %shard_map.308 = (bf16[512,8192]{1,0:T(8,128)(2,1)S(1)}, f32[384,128]{1,0:T(8,128)S(1)}, f32[384,128]{1,0:T(8,128)S(1)}, f32[1024,128]{1,0:T(8,128)S(1)}, f32[10...) custom-call(s32[2]{0:T(128)S(1)} %pad_add_fusion.index_ref, ...), custom_call_target="tpu_custom_call", output_to_operand_aliasing={{0}: (10, {})} | custom-call | flops 6710886400 | bytes 28188680 | tf_op jit(solution)/shard_map/pallas_call | solution.py:718
  46.5 0.4 collective-permute-start.5
  46.9 1.7 %collective-permute-start.6 = (f32[1024,128]{1,0:T(8,128)S(1)}, f32[1024,128]{1,0:T(8,128)S(1)}, u32[]{:S(2)}, u32[]{:S(2)}) collective-permute-start(f32[1024,128]{1,0:T(8,128)S(1)} %get-tuple-element.149), channel_id=1, source_target_pairs={{0,2},{1,3},{2,0},{3,1},{4,6},{5,7},{6,4},{7,5},{8,10},{9,11},{10,... | collective-permute-start | bytes 1572872 | tf_op jit(solution)/shard_map/ppermute | solution.py:1148
  48.6 0.1 add.230
  48.7 1.6 %collective-permute-start.4 = (f32[896,128]{1,0:T(8,128)S(1)}, f32[896,128]{1,0:T(8,128)S(1)}, u32[]{:S(2)}, u32[]{:S(2)}) collective-permute-start(f32[896,128]{1,0:T(8,128)S(1)} %constant_dynamic-slice_fusion.21), channel_id=1, source_target_pairs={{0,8},{1,9},{2,10},{3,11},{4,12},{5,13},{6,14},{7,15},{8,0},{9,1},... | collective-permute-start | bytes 1376264 | tf_op jit(solution)/shard_map/ppermute | solution.py:1148
  50.4 10.1 %shard_map.309 = f32[256,128]{1,0:T(8,128)S(1)} custom-call(f32[16,8192]{1,0:T(8,128)S(1)} %get-tuple-element.136.y1_ref, f32[8,8192]{1,0:T(8,128)S(1)} %get-tuple-element.137.ghalf_ref, f32[16,128]{1,0:T(8,128)S(1)} %get-tuple-element.138.gbc_ref, f32[16,8192]{1,0:T(8,128)S(1)} %get-tuple-element.127.gout_ref, ...), custom_call_target="tpu_custom_call" | custom-call | flops 5502926848 | bytes 20021248 | tf_op jit(solution)/shard_map/pallas_call | solution.py:718
  60.7 0.1 collective-permute-done.4
  60.9 0.1 collective-permute-start.7
  61.2 1.8 %collective-permute-done.7 = f32[1280,128]{1,0:T(8,128)S(1)} collective-permute-done((f32[1280,128]{1,0:T(8,128)S(1)}, f32[1280,128]{1,0:T(8,128)S(1)}, u32[]{:S(2)}, u32[]{:S(2)}) %collective-permute-start.7) | collective-permute-done | bytes 655392 | tf_op jit(solution)/shard_map/ppermute | solution.py:1148
  63.2 1.7 %collective-permute-start.9 = (f32[288,128]{1,0:T(8,128)S(1)}, f32[288,128]{1,0:T(8,128)S(1)}, u32[]{:S(2)}, u32[]{:S(2)}) collective-permute-start(f32[288,128]{1,0:T(8,128)S(1)} %pad_maximum_fusion.3), channel_id=1, source_target_pairs={{0,4},{1,5},{2,6},{3,7},{4,0},{5,1},{6,2},{7,3},{8,12},{9,13},{10,... | collective-permute-start | bytes 442376 | tf_op jit(solution)/shard_map/ppermute | solution.py:1148
  65.0 1.6 %collective-permute-start.8 = (f32[352,128]{1,0:T(8,128)S(1)}, f32[352,128]{1,0:T(8,128)S(1)}, u32[]{:S(2)}, u32[]{:S(2)}) collective-permute-start(f32[352,128]{1,0:T(8,128)S(1)} %pad_maximum_fusion.2), channel_id=1, source_target_pairs={{0,2},{1,3},{2,0},{3,1},{4,6},{5,7},{6,4},{7,5},{8,10},{9,11},{10,... | collective-permute-start | bytes 540680 | tf_op jit(solution)/shard_map/ppermute | solution.py:1148
  66.6 0.4 collective-permute-start.10
  66.9 2.5 %collective-permute-done.9 = f32[288,128]{1,0:T(8,128)S(1)} collective-permute-done((f32[288,128]{1,0:T(8,128)S(1)}, f32[288,128]{1,0:T(8,128)S(1)}, u32[]{:S(2)}, u32[]{:S(2)}) %collective-permute-start.9) | collective-permute-done | bytes 147488 | tf_op jit(solution)/shard_map/ppermute | solution.py:1148
  69.4 2.3 %collective-permute-done.8 = f32[352,128]{1,0:T(8,128)S(1)} collective-permute-done((f32[352,128]{1,0:T(8,128)S(1)}, f32[352,128]{1,0:T(8,128)S(1)}, u32[]{:S(2)}, u32[]{:S(2)}) %collective-permute-start.8) | collective-permute-done | bytes 180256 | tf_op jit(solution)/shard_map/ppermute | solution.py:1148
  71.9 2.6 %collective-permute-start.11 = (f32[208,128]{1,0:T(8,128)S(1)}, f32[208,128]{1,0:T(8,128)S(1)}, u32[]{:S(2)}, u32[]{:S(2)}) collective-permute-start(f32[208,128]{1,0:T(8,128)S(1)} %pad_maximum_fusion.4), channel_id=1, source_target_pairs={{0,16},{1,17},{2,18},{3,19},{4,20},{5,21},{6,22},{7,23},{8,24},{9,... | collective-permute-start | bytes 319496 | tf_op jit(solution)/shard_map/ppermute | solution.py:1148
  74.5 1.6 %collective-permute-start.12 = (f32[96,128]{1,0:T(8,128)S(1)}, f32[96,128]{1,0:T(8,128)S(1)}, u32[]{:S(2)}, u32[]{:S(2)}) collective-permute-start(f32[96,128]{1,0:T(8,128)S(1)} %pad_maximum_fusion.5), channel_id=1, source_target_pairs={{0,8},{1,9},{2,10},{3,11},{4,12},{5,13},{6,14},{7,15},{8,0},{9,1},... | collective-permute-start | bytes 147464 | tf_op jit(solution)/shard_map/ppermute | solution.py:1148
  76.1 0.2 collective-permute-start.13
  76.3 2.3 %collective-permute-done.12 = f32[96,128]{1,0:T(8,128)S(1)} collective-permute-done((f32[96,128]{1,0:T(8,128)S(1)}, f32[96,128]{1,0:T(8,128)S(1)}, u32[]{:S(2)}, u32[]{:S(2)}) %collective-permute-start.12) | collective-permute-done | bytes 49184 | tf_op jit(solution)/shard_map/ppermute | solution.py:1148
  78.6 3.4 %collective-permute-done.13 = f32[96,128]{1,0:T(8,128)S(1)} collective-permute-done((f32[96,128]{1,0:T(8,128)S(1)}, f32[96,128]{1,0:T(8,128)S(1)}, u32[]{:S(2)}, u32[]{:S(2)}) %collective-permute-start.13) | collective-permute-done | bytes 49184 | tf_op jit(solution)/shard_map/ppermute | solution.py:1148
  82.2 1.6 %collective-permute-start.14 = (bf16[224,128]{1,0:T(8,128)(2,1)S(1)}, bf16[224,128]{1,0:T(8,128)(2,1)S(1)}, u32[]{:S(2)}, u32[]{:S(2)}) collective-permute-start(bf16[224,128]{1,0:T(8,128)(2,1)S(1)} %get-tuple-element.203), channel_id=1, source_target_pairs={{0,16},{1,17},{2,18},{3,19},{4,20},{5,21},{6,22},{7,23},{8,24},{9,... | collective-permute-start | bytes 172040 | tf_op jit(solution)/shard_map/ppermute | solution.py:1148
  83.7 0.9 collective-permute-start.15
  84.7 2.0 %collective-permute-start.16 = (bf16[224,128]{1,0:T(8,128)(2,1)S(1)}, bf16[224,128]{1,0:T(8,128)(2,1)S(1)}, u32[]{:S(2)}, u32[]{:S(2)}) collective-permute-start(bf16[224,128]{1,0:T(8,128)(2,1)S(1)} %get-tuple-element.203), channel_id=1, source_target_pairs={{0,24},{1,25},{2,26},{3,27},{4,28},{5,29},{6,30},{7,31},{8,16},{9,... | collective-permute-start | bytes 172040 | tf_op jit(solution)/shard_map/ppermute | solution.py:1148
  86.6 1.6 %collective-permute-done.14 = bf16[224,128]{1,0:T(8,128)(2,1)S(1)} collective-permute-done((bf16[224,128]{1,0:T(8,128)(2,1)S(1)}, bf16[224,128]{1,0:T(8,128)(2,1)S(1)}, u32[]{:S(2)}, u32[]{:S(2)}) %collective-permute-start.14) | collective-permute-done | bytes 57376 | tf_op jit(solution)/shard_map/ppermute | solution.py:1148
  88.3 0.3 collective-permute-done.15
  88.6 2.0 %collective-permute-done.16 = bf16[224,128]{1,0:T(8,128)(2,1)S(1)} collective-permute-done((bf16[224,128]{1,0:T(8,128)(2,1)S(1)}, bf16[224,128]{1,0:T(8,128)(2,1)S(1)}, u32[]{:S(2)}, u32[]{:S(2)}) %collective-permute-start.16) | collective-permute-done | bytes 57376 | tf_op jit(solution)/shard_map/ppermute | solution.py:1148
  90.7 0.6 collective-permute-start.20
  91.4 1.6 %collective-permute-start.17 = (bf16[448,128]{1,0:T(8,128)(2,1)S(1)}, bf16[448,128]{1,0:T(8,128)(2,1)S(1)}, u32[]{:S(2)}, u32[]{:S(2)}) collective-permute-start(bf16[448,128]{1,0:T(8,128)(2,1)S(1)} %maximum_select_fusion.6), channel_id=1, source_target_pairs={{0,2},{1,3},{2,0},{3,1},{4,6},{5,7},{6,4},{7,5},{8,10},{9,11},{10,... | collective-permute-start | bytes 344072 | tf_op jit(solution)/shard_map/ppermute | solution.py:1148
  93.0 2.6 %collective-permute-done.20 = bf16[448,128]{1,0:T(8,128)(2,1)S(1)} collective-permute-done((bf16[448,128]{1,0:T(8,128)(2,1)S(1)}, bf16[448,128]{1,0:T(8,128)(2,1)S(1)}, u32[]{:S(2)}, u32[]{:S(2)}) %collective-permute-start.20) | collective-permute-done | bytes 114720 | tf_op jit(solution)/shard_map/ppermute | solution.py:1148
  95.6 2.8 %collective-permute-start.21 = (bf16[896,128]{1,0:T(8,128)(2,1)S(1)}, bf16[896,128]{1,0:T(8,128)(2,1)S(1)}, u32[]{:S(2)}, u32[]{:S(2)}) collective-permute-start(bf16[896,128]{1,0:T(8,128)(2,1)S(1)} %maximum_select_fusion.5), channel_id=1, source_target_pairs={{0,2},{1,3},{2,0},{3,1},{4,6},{5,7},{6,4},{7,5},{8,10},{9,11},{10,... | collective-permute-start | bytes 688136 | tf_op jit(solution)/shard_map/ppermute | solution.py:1148
  98.5 0.1 collective-permute-start.18
  98.6 3.8 %collective-permute-done.21 = bf16[896,128]{1,0:T(8,128)(2,1)S(1)} collective-permute-done((bf16[896,128]{1,0:T(8,128)(2,1)S(1)}, bf16[896,128]{1,0:T(8,128)(2,1)S(1)}, u32[]{:S(2)}, u32[]{:S(2)}) %collective-permute-start.21) | collective-permute-done | bytes 229408 | tf_op jit(solution)/shard_map/ppermute | solution.py:1148
  102.4 0.1 maximum_select_fusion.3
  102.7 1.9 %collective-permute-done.18 = bf16[896,128]{1,0:T(8,128)(2,1)S(1)} collective-permute-done((bf16[896,128]{1,0:T(8,128)(2,1)S(1)}, bf16[896,128]{1,0:T(8,128)(2,1)S(1)}, u32[]{:S(2)}, u32[]{:S(2)}) %collective-permute-start.18) | collective-permute-done | bytes 229408 | tf_op jit(solution)/shard_map/ppermute | solution.py:1148
  104.6 0.1 maximum_select_fusion.2
  104.8 0.2 maximum_select_fusion.1
  105.3 1.3 %collective-permute-done.19 = bf16[1792,128]{1,0:T(8,128)(2,1)S(1)} collective-permute-done((bf16[1792,128]{1,0:T(8,128)(2,1)S(1)}, bf16[1792,128]{1,0:T(8,128)(2,1)S(1)}, u32[]{:S(2)}, u32[]{:S(2)}) %collective-permute-start.19) | collective-permute-done | bytes 458784 | tf_op jit(solution)/shard_map/ppermute | solution.py:1148
  106.6 0.2 maximum_select_fusion
  106.8 0.1 copy.37
  107.0 9.0 %shard_map.310 = (f32[1,1]{1,0:T(1,128)}, f32[1,1]{1,0:T(1,128)}, f32[24,128]{1,0:T(8,128)}, f32[24,128]{1,0:T(8,128)}, f32[24,128]{1,0:T(8,128)}, /*index=5*/f3...) custom-call(bf16[3584,128]{1,0:T(8,128)(2,1)S(1)} %bitcast.39, ...), custom_call_target="tpu_custom_call" | custom-call | flops 100000000 | bytes 20655880 | tf_op jit(solution)/shard_map/pallas_call | solution.py:718
  (79 shorter events, 1.6 us)
Async XLA Ops:
  2.0 8.9 %collective-permute-start = (bf16[208,128]{1,0:T(8,128)(2,1)S(1)}, bf16[208,128]{1,0:T(8,128)(2,1)S(1)}, u32[]{:S(2)}, u32[]{:S(2)}) collective-permute-start(bf16[208,128]{1,0:T(8,128)(2,1)S(1)} %get-tuple-element.95), channel_id=1, source_target_pairs={{0,1},{1,0},{2,3},{3,2},{4,5},{5,4},{6,7},{7,6},{8,9},{9,8},{10,11... | collective-permute-start | bytes 159752 | tf_op jit(solution)/shard_map/ppermute | solution.py:1166
  2.6 8.4 %collective-permute-start.1 = (bf16[208,128]{1,0:T(8,128)(2,1)S(1)}, bf16[208,128]{1,0:T(8,128)(2,1)S(1)}, u32[]{:S(2)}, u32[]{:S(2)}) collective-permute-start(bf16[208,128]{1,0:T(8,128)(2,1)S(1)} %get-tuple-element.96), channel_id=1, source_target_pairs={{0,2},{1,3},{2,0},{3,1},{4,6},{5,7},{6,4},{7,5},{8,10},{9,11},{10,... | collective-permute-start | bytes 159752 | tf_op jit(solution)/shard_map/ppermute | solution.py:1166
  5.2 5.8 %collective-permute-start.2 = (bf16[208,128]{1,0:T(8,128)(2,1)S(1)}, bf16[208,128]{1,0:T(8,128)(2,1)S(1)}, u32[]{:S(2)}, u32[]{:S(2)}) collective-permute-start(bf16[208,128]{1,0:T(8,128)(2,1)S(1)} %get-tuple-element.97), channel_id=1, source_target_pairs={{0,3},{1,2},{2,1},{3,0},{4,7},{5,6},{6,5},{7,4},{8,11},{9,10},{10,... | collective-permute-start | bytes 159752 | tf_op jit(solution)/shard_map/ppermute | solution.py:1166
  22.4 26.2 %collective-permute-start.3 = (f32[1792,128]{1,0:T(8,128)S(1)}, f32[1792,128]{1,0:T(8,128)S(1)}, u32[]{:S(2)}, u32[]{:S(2)}) collective-permute-start(f32[1792,128]{1,0:T(8,128)S(1)} %get-tuple-element.112), channel_id=1, source_target_pairs={{0,4},{1,5},{2,6},{3,7},{4,0},{5,1},{6,2},{7,3},{8,12},{9,13},{10,... | collective-permute-start | bytes 2752520 | tf_op jit(solution)/shard_map/ppermute | solution.py:1148
  46.5 14.0 %collective-permute-start.5 = (f32[384,128]{1,0:T(8,128)S(1)}, f32[384,128]{1,0:T(8,128)S(1)}, u32[]{:S(2)}, u32[]{:S(2)}) collective-permute-start(f32[384,128]{1,0:T(8,128)S(1)} %get-tuple-element.146), channel_id=1, source_target_pairs={{0,4},{1,5},{2,6},{3,7},{4,0},{5,1},{6,2},{7,3},{8,12},{9,13},{10,... | collective-permute-start | bytes 589832 | tf_op jit(solution)/shard_map/ppermute | solution.py:1148
  46.9 13.7 %collective-permute-start.6 = (f32[1024,128]{1,0:T(8,128)S(1)}, f32[1024,128]{1,0:T(8,128)S(1)}, u32[]{:S(2)}, u32[]{:S(2)}) collective-permute-start(f32[1024,128]{1,0:T(8,128)S(1)} %get-tuple-element.149), channel_id=1, source_target_pairs={{0,2},{1,3},{2,0},{3,1},{4,6},{5,7},{6,4},{7,5},{8,10},{9,11},{10,... | collective-permute-start | bytes 1572872 | tf_op jit(solution)/shard_map/ppermute | solution.py:1148
  48.7 12.0 %collective-permute-start.4 = (f32[896,128]{1,0:T(8,128)S(1)}, f32[896,128]{1,0:T(8,128)S(1)}, u32[]{:S(2)}, u32[]{:S(2)}) collective-permute-start(f32[896,128]{1,0:T(8,128)S(1)} %constant_dynamic-slice_fusion.21), channel_id=1, source_target_pairs={{0,8},{1,9},{2,10},{3,11},{4,12},{5,13},{6,14},{7,15},{8,0},{9,1},... | collective-permute-start | bytes 1376264 | tf_op jit(solution)/shard_map/ppermute | solution.py:1148
  60.9 2.2 %collective-permute-start.7 = (f32[1280,128]{1,0:T(8,128)S(1)}, f32[1280,128]{1,0:T(8,128)S(1)}, u32[]{:S(2)}, u32[]{:S(2)}) collective-permute-start(f32[1280,128]{1,0:T(8,128)S(1)} %pad_maximum_fusion.1), channel_id=1, source_target_pairs={{0,1},{1,0},{2,3},{3,2},{4,5},{5,4},{6,7},{7,6},{8,9},{9,8},{10,11... | collective-permute-start | bytes 1966088 | tf_op jit(solution)/shard_map/ppermute | solution.py:1148
  63.2 6.1 %collective-permute-start.9 = (f32[288,128]{1,0:T(8,128)S(1)}, f32[288,128]{1,0:T(8,128)S(1)}, u32[]{:S(2)}, u32[]{:S(2)}) collective-permute-start(f32[288,128]{1,0:T(8,128)S(1)} %pad_maximum_fusion.3), channel_id=1, source_target_pairs={{0,4},{1,5},{2,6},{3,7},{4,0},{5,1},{6,2},{7,3},{8,12},{9,13},{10,... | collective-permute-start | bytes 442376 | tf_op jit(solution)/shard_map/ppermute | solution.py:1148
  65.0 6.7 %collective-permute-start.8 = (f32[352,128]{1,0:T(8,128)S(1)}, f32[352,128]{1,0:T(8,128)S(1)}, u32[]{:S(2)}, u32[]{:S(2)}) collective-permute-start(f32[352,128]{1,0:T(8,128)S(1)} %pad_maximum_fusion.2), channel_id=1, source_target_pairs={{0,2},{1,3},{2,0},{3,1},{4,6},{5,7},{6,4},{7,5},{8,10},{9,11},{10,... | collective-permute-start | bytes 540680 | tf_op jit(solution)/shard_map/ppermute | solution.py:1148
  66.6 5.2 %collective-permute-start.10 = (f32[32,128]{1,0:T(8,128)S(1)}, f32[32,128]{1,0:T(8,128)S(1)}, u32[]{:S(2)}, u32[]{:S(2)}) collective-permute-start(f32[32,128]{1,0:T(8,128)S(1)} %get-tuple-element.184), channel_id=1, source_target_pairs={{0,6},{1,7},{2,4},{3,5},{4,2},{5,3},{6,0},{7,1},{8,14},{9,15},{10,... | collective-permute-start | bytes 49160 | tf_op jit(solution)/shard_map/ppermute | solution.py:1148
  71.9 10.1 %collective-permute-start.11 = (f32[208,128]{1,0:T(8,128)S(1)}, f32[208,128]{1,0:T(8,128)S(1)}, u32[]{:S(2)}, u32[]{:S(2)}) collective-permute-start(f32[208,128]{1,0:T(8,128)S(1)} %pad_maximum_fusion.4), channel_id=1, source_target_pairs={{0,16},{1,17},{2,18},{3,19},{4,20},{5,21},{6,22},{7,23},{8,24},{9,... | collective-permute-start | bytes 319496 | tf_op jit(solution)/shard_map/ppermute | solution.py:1148
  74.5 4.1 %collective-permute-start.12 = (f32[96,128]{1,0:T(8,128)S(1)}, f32[96,128]{1,0:T(8,128)S(1)}, u32[]{:S(2)}, u32[]{:S(2)}) collective-permute-start(f32[96,128]{1,0:T(8,128)S(1)} %pad_maximum_fusion.5), channel_id=1, source_target_pairs={{0,8},{1,9},{2,10},{3,11},{4,12},{5,13},{6,14},{7,15},{8,0},{9,1},... | collective-permute-start | bytes 147464 | tf_op jit(solution)/shard_map/ppermute | solution.py:1148
  76.1 5.9 %collective-permute-start.13 = (f32[96,128]{1,0:T(8,128)S(1)}, f32[96,128]{1,0:T(8,128)S(1)}, u32[]{:S(2)}, u32[]{:S(2)}) collective-permute-start(f32[96,128]{1,0:T(8,128)S(1)} %pad_maximum_fusion.6), channel_id=1, source_target_pairs={{0,24},{1,25},{2,26},{3,27},{4,28},{5,29},{6,30},{7,31},{8,16},{9,... | collective-permute-start | bytes 147464 | tf_op jit(solution)/shard_map/ppermute | solution.py:1148
  82.0 20.6 %copy-start = (f32[2960]{0:T(1024)S(1)}, f32[2960]{0:T(1024)}, u32[]{:S(2)}) copy-start(f32[2960]{0:T(1024)} %param.21) | copy-start | bytes 35524
  82.0 20.6 %copy-start.1 = (f32[2960]{0:T(1024)S(1)}, f32[2960]{0:T(1024)}, u32[]{:S(2)}) copy-start(f32[2960]{0:T(1024)} %param.20) | copy-start | bytes 35524
  82.2 6.0 %collective-permute-start.14 = (bf16[224,128]{1,0:T(8,128)(2,1)S(1)}, bf16[224,128]{1,0:T(8,128)(2,1)S(1)}, u32[]{:S(2)}, u32[]{:S(2)}) collective-permute-start(bf16[224,128]{1,0:T(8,128)(2,1)S(1)} %get-tuple-element.203), channel_id=1, source_target_pairs={{0,16},{1,17},{2,18},{3,19},{4,20},{5,21},{6,22},{7,23},{8,24},{9,... | collective-permute-start | bytes 172040 | tf_op jit(solution)/shard_map/ppermute | solution.py:1148
  83.7 4.9 %collective-permute-start.15 = (bf16[224,128]{1,0:T(8,128)(2,1)S(1)}, bf16[224,128]{1,0:T(8,128)(2,1)S(1)}, u32[]{:S(2)}, u32[]{:S(2)}) collective-permute-start(bf16[224,128]{1,0:T(8,128)(2,1)S(1)} %get-tuple-element.203), channel_id=1, source_target_pairs={{0,8},{1,9},{2,10},{3,11},{4,12},{5,13},{6,14},{7,15},{8,0},{9,1},... | collective-permute-start | bytes 172040 | tf_op jit(solution)/shard_map/ppermute | solution.py:1148
  84.7 6.0 %collective-permute-start.16 = (bf16[224,128]{1,0:T(8,128)(2,1)S(1)}, bf16[224,128]{1,0:T(8,128)(2,1)S(1)}, u32[]{:S(2)}, u32[]{:S(2)}) collective-permute-start(bf16[224,128]{1,0:T(8,128)(2,1)S(1)} %get-tuple-element.203), channel_id=1, source_target_pairs={{0,24},{1,25},{2,26},{3,27},{4,28},{5,29},{6,30},{7,31},{8,16},{9,... | collective-permute-start | bytes 172040 | tf_op jit(solution)/shard_map/ppermute | solution.py:1148
  90.7 4.9 %collective-permute-start.20 = (bf16[448,128]{1,0:T(8,128)(2,1)S(1)}, bf16[448,128]{1,0:T(8,128)(2,1)S(1)}, u32[]{:S(2)}, u32[]{:S(2)}) collective-permute-start(bf16[448,128]{1,0:T(8,128)(2,1)S(1)} %maximum_select_fusion.7), channel_id=1, source_target_pairs={{0,4},{1,5},{2,6},{3,7},{4,0},{5,1},{6,2},{7,3},{8,12},{9,13},{10,... | collective-permute-start | bytes 344072 | tf_op jit(solution)/shard_map/ppermute | solution.py:1148
  91.4 7.1 %collective-permute-start.17 = (bf16[448,128]{1,0:T(8,128)(2,1)S(1)}, bf16[448,128]{1,0:T(8,128)(2,1)S(1)}, u32[]{:S(2)}, u32[]{:S(2)}) collective-permute-start(bf16[448,128]{1,0:T(8,128)(2,1)S(1)} %maximum_select_fusion.6), channel_id=1, source_target_pairs={{0,2},{1,3},{2,0},{3,1},{4,6},{5,7},{6,4},{7,5},{8,10},{9,11},{10,... | collective-permute-start | bytes 344072 | tf_op jit(solution)/shard_map/ppermute | solution.py:1148
  95.6 6.8 %collective-permute-start.21 = (bf16[896,128]{1,0:T(8,128)(2,1)S(1)}, bf16[896,128]{1,0:T(8,128)(2,1)S(1)}, u32[]{:S(2)}, u32[]{:S(2)}) collective-permute-start(bf16[896,128]{1,0:T(8,128)(2,1)S(1)} %maximum_select_fusion.5), channel_id=1, source_target_pairs={{0,2},{1,3},{2,0},{3,1},{4,6},{5,7},{6,4},{7,5},{8,10},{9,11},{10,... | collective-permute-start | bytes 688136 | tf_op jit(solution)/shard_map/ppermute | solution.py:1148
  98.5 6.1 %collective-permute-start.18 = (bf16[896,128]{1,0:T(8,128)(2,1)S(1)}, bf16[896,128]{1,0:T(8,128)(2,1)S(1)}, u32[]{:S(2)}, u32[]{:S(2)}) collective-permute-start(bf16[896,128]{1,0:T(8,128)(2,1)S(1)} %maximum_select_fusion.4), channel_id=1, source_target_pairs={{0,4},{1,5},{2,6},{3,7},{4,0},{5,1},{6,2},{7,3},{8,12},{9,13},{10,... | collective-permute-start | bytes 688136 | tf_op jit(solution)/shard_map/ppermute | solution.py:1148
  102.6 2.2 %collective-permute-start.22 = (bf16[1792,128]{1,0:T(8,128)(2,1)S(1)}, bf16[1792,128]{1,0:T(8,128)(2,1)S(1)}, u32[]{:S(2)}, u32[]{:S(2)}) collective-permute-start(bf16[1792,128]{1,0:T(8,128)(2,1)S(1)} %maximum_select_fusion.3), channel_id=1, source_target_pairs={{0,1},{1,0},{2,3},{3,2},{4,5},{5,4},{6,7},{7,6},{8,9},{9,8},{10,11... | collective-permute-start | bytes 1376264 | tf_op jit(solution)/shard_map/ppermute | solution.py:1148
  104.7 1.9 %collective-permute-start.19 = (bf16[1792,128]{1,0:T(8,128)(2,1)S(1)}, bf16[1792,128]{1,0:T(8,128)(2,1)S(1)}, u32[]{:S(2)}, u32[]{:S(2)}) collective-permute-start(bf16[1792,128]{1,0:T(8,128)(2,1)S(1)} %maximum_select_fusion.2), channel_id=1, source_target_pairs={{0,1},{1,0},{2,3},{3,2},{4,5},{5,4},{6,7},{7,6},{8,9},{9,8},{10,11... | collective-permute-start | bytes 1376264 | tf_op jit(solution)/shard_map/ppermute | solution.py:1148

commit v7 on v6

--- a/solution.py
+++ b/solution.py
@@ -272,15 +272,15 @@
     fill_ext(ext, mixed[:16] + ones, half_rows, half_cols, bands, ones)
     oacc[...] = jnp.zeros_like(oacc)
     chunk = half_cols * LANES
+    xcol = jnp.concatenate([gather_cols(ext, half_cols, i, 0, chunk) for i in range(half_rows)], axis=1)
+    xcol_ref[...] = xcol
+    hidden = jnp.maximum(dot(et_ref[...], xcol).astype(BF16), jnp.zeros((), BF16))
+    h1_ref[...] = hidden
+    hidden = jnp.maximum((dot(wb_ref[...], hidden) + bias_ref[...]).astype(BF16), jnp.zeros((), BF16))
+    h2_ref[...] = hidden
+    outputs = dot(f_ref[...], hidden)
     for i in range(half_rows):
-        at = slice(i * chunk, (i + 1) * chunk)
-        xcol = gather_cols(ext, half_cols, i, 0, chunk)
-        xcol_ref[:, at] = xcol
-        hidden = jnp.maximum(dot(et_ref[...], xcol).astype(BF16), jnp.zeros((), BF16))
-        h1_ref[:, at] = hidden
-        hidden = jnp.maximum((dot(wb_ref[...], hidden) + bias_ref[...]).astype(BF16), jnp.zeros((), BF16))
-        h2_ref[:, at] = hidden
-        scatter_cols(oacc, dot(f_ref[...], hidden), half_cols, i, 0, chunk, True)
+        scatter_cols(oacc, outputs[:, i * chunk : (i + 1) * chunk], half_cols, i, 0, chunk, True)
     output = jnp.concatenate(fold_ext(oacc, half_rows, half_cols, bands), axis=1) + chan2_ref[:, 2:3]
     second = output[16:] + 2.0
     t2_ref[...] = second
@@ -354,28 +354,20 @@
     fill_ext(ext, g_out, rows, cols, bands, jnp.zeros((32, 1), F32))
     gacc[...] = jnp.zeros_like(gacc)
     chunk = cols * LANES
+    gcol = jnp.concatenate([gather_cols(ext, cols, i, 0, chunk, True) for i in range(rows)], axis=1)
+    hidden_two = h2_ref[...]
+    hidden_one = h1_ref[...]
+    g_pre = jnp.where(hidden_two > 0, dot(ft_ref[...], gcol).astype(BF16), jnp.zeros((), BF16))
+    gf[...] = dot_nt(gcol, hidden_two)
+    g_wb = dot_nt(g_pre, hidden_one)
+    for block in range(HID // LANES):
+        slab_ref[block * HID : (block + 1) * HID, :] = g_wb[:, block * LANES : (block + 1) * LANES]
+    bacc[...] = fold_lanes(g_pre.astype(F32))
+    g_pre = jnp.where(hidden_one > 0, dot(wbt_ref[...], g_pre).astype(BF16), jnp.zeros((), BF16))
+    ge[...] = dot_nt(xcol_ref[...], g_pre)
+    inputs = dot(e_ref[...], g_pre)
     for i in range(rows):
-        at = slice(i * chunk, (i + 1) * chunk)
-        gcol = gather_cols(ext, cols, i, 0, chunk, True)
-        hidden_two = h2_ref[:, at]
-        hidden_one = h1_ref[:, at]
-        g_pre = jnp.where(hidden_two > 0, dot(ft_ref[...], gcol).astype(BF16), jnp.zeros((), BF16))
-        g_f = dot_nt(gcol, hidden_two)
-        g_wb = dot_nt(g_pre, hidden_one)
-        folded = fold_lanes(g_pre.astype(F32))
-        g_pre = jnp.where(hidden_one > 0, dot(wbt_ref[...], g_pre).astype(BF16), jnp.zeros((), BF16))
-        g_e = dot_nt(xcol_ref[:, at], g_pre)
-        scatter_cols(gacc, dot(e_ref[...], g_pre), cols, i, 0, chunk)
-        if i == 0:
-            gf[...], ge[...], bacc[...] = g_f, g_e, folded
-        else:
-            gf[...] += g_f
-            ge[...] += g_e
-            bacc[...] += folded
-        for block in range(HID // LANES):
-            at = slice(block * HID, (block + 1) * HID)
-            part = g_wb[:, block * LANES : (block + 1) * LANES]
-            slab_ref[at, :] = part if i == 0 else slab_ref[at, :] + part
+        scatter_cols(gacc, inputs[:, i * chunk : (i + 1) * chunk], cols, i, 0, chunk)
     slab_ref[TWO_B:TWO_ROWS, :] = jnp.zeros((TWO_ROWS - TWO_B, LANES), F32)
     put_rows(slab_ref, lambda block: TWO_B + block, ones_sum(bacc), 0, 1)
     for piece in range(18):
@@ -1295,7 +1287,7 @@
     half_a, half_b = shape((PART_A // 2, LANES)), shape(((ONE_ROWS - PART_A) // 2, LANES))
     top_out = [shape((HID, size), BF16), half_a, half_a, half_b, half_b, shape((8, size)), shape((16, LANES))]
     (gpre, kept_a, sent_a, kept_b, sent_b, ghalf, gbc) = call(
-        functools.partial(one_backward_top, dims, chunk // 2, (second_bit, third_bit)),
+        functools.partial(one_backward_top, dims, chunk, (second_bit, third_bit)),
         top_in,
         top_out,
         [

time: 116 us -> 116 us (level)
  no operation moved by 1% of the time
where the time goes in v7:
time: 116 us
  Pallas kernels  58.9 us (51%)
  starting transfers between devices  26.5 us (23%)
  waiting for transfers between devices  26 us (22%)
  other arithmetic  1.73 us (1%)
  between operations  1.65 us (1%)
  local copies, waits for them, and re-layouts  1.26 us (1%)
    pallas_call x7, Pallas kernels, call(): pl.pallas_call(kernel, out_shape=outputs, in_specs=[far if k in far_in el...  58.9 us
    ppermute x20, waiting for transfers between devices, trade(): lax.ppermute(value, ('batch', 'rows'), [(i, i ^ bit) for i in range(devic...  26 us
    ppermute x20, starting transfers between devices, trade(): lax.ppermute(value, ('batch', 'rows'), [(i, i ^ bit) for i in range(devic...  23.3 us
    ppermute x3, starting transfers between devices, on_device(): lax.ppermute(pieces[d], 'rows', [(i, i ^ d) for i in range(bands)])  3.18 us
  transfers between devices with their start and end apart: 23, of which 13 were waited for; matrix products, arithmetic and copies ran while one was open for 2% of the time, Pallas kernels for 32%

profile of v7, /device:TPU:0, one launch (start us, length us, event | category | flops | bytes accessed | tf_op | source)
XLA Modules:
  0.0 116.0 jit_solution(14226366034251918954)
XLA Ops:
  0.7 0.1 pad_add_fusion.index_ref
  0.7 1.3 %shard_map.304 = (bf16[208,128]{1,0:T(8,128)(2,1)S(1)}, bf16[208,128]{1,0:T(8,128)(2,1)S(1)}, bf16[208,128]{1,0:T(8,128)(2,1)S(1)}, bf16[208,128]{1,0:T(8,128)(2,1)S(1)}) custom-call(s32[2]{0:T(128)S(1)} %pad_add_fusion.index_ref, s32[768,128]{1,0:T(8,128)} %bitcast.49, s32[64,128]{1,0:T(8,128)} %bitcast.54), custom_call_target="tpu_custom_call" | custom-call | flops 1000 | bytes 638984 | tf_op jit(solution)/shard_map/pallas_call | solution.py:710
  2.0 0.5 collective-permute-start
  2.6 2.6 %collective-permute-start.1 = (bf16[208,128]{1,0:T(8,128)(2,1)S(1)}, bf16[208,128]{1,0:T(8,128)(2,1)S(1)}, u32[]{:S(2)}, u32[]{:S(2)}) collective-permute-start(bf16[208,128]{1,0:T(8,128)(2,1)S(1)} %get-tuple-element.96), channel_id=1, source_target_pairs={{0,2},{1,3},{2,0},{3,1},{4,6},{5,7},{6,4},{7,5},{8,10},{9,11},{10,... | collective-permute-start | bytes 159752 | tf_op jit(solution)/shard_map/ppermute | solution.py:1158
  5.2 0.7 pad_bitcast_fusion.2.flat_ref
  5.9 5.0 %shard_map.305 = (f32[16,128]{1,0:T(8,128)S(1)}, f32[16,128]{1,0:T(8,128)S(1)}, f32[32,128]{1,0:T(8,128)S(1)}, f32[32,128]{1,0:T(8,128)S(1)}, f32[32,128]{1,0:T(...) custom-call(f32[24,128]{1,0:T(8,128)S(1)} %pad_bitcast_fusion.2.flat, ...), custom_call_target="tpu_custom_call" | custom-call | flops 1000000000 | bytes 6714112 | tf_op jit(solution)/shard_map/pallas_call | solution.py:710
  11.0 11.6 %shard_map.306 = (f32[16,8192]{1,0:T(8,128)S(1)}, f32[16,8192]{1,0:T(8,128)S(1)}, f32[1,8192]{1,0:T(1,128)S(1)}, f32[1,2048]{1,0:T(1,128)S(1)}, f32[32,2048]{1,0...) custom-call(s32[2]{0:T(128)S(1)} %pad_add_fusion.index_ref, ...), custom_call_target="tpu_custom_call" | custom-call | flops 5939134464 | bytes 5683208 | tf_op jit(solution)/shard_map/pallas_call | solution.py:710
  22.5 1.8 %collective-permute-start.3 = (f32[1792,128]{1,0:T(8,128)S(1)}, f32[1792,128]{1,0:T(8,128)S(1)}, u32[]{:S(2)}, u32[]{:S(2)}) collective-permute-start(f32[1792,128]{1,0:T(8,128)S(1)} %get-tuple-element.112), channel_id=1, source_target_pairs={{0,4},{1,5},{2,6},{3,7},{4,0},{5,1},{6,2},{7,3},{8,12},{9,13},{10,... | collective-permute-start | bytes 2752520 | tf_op jit(solution)/shard_map/ppermute | solution.py:1140
  24.3 10.5 %shard_map.307 = (bf16[72,8192]{1,0:T(8,128)(2,1)S(1)}, bf16[512,8192]{1,0:T(8,128)(2,1)S(1)}, bf16[512,8192]{1,0:T(8,128)(2,1)S(1)}, f32[8,8192]{1,0:T(8,128)S(...) custom-call(f32[16,8192]{1,0:T(8,128)S(1)} %get-tuple-element.114.mix1_ref, ...), custom_call_target="tpu_custom_call" | custom-call | flops 6106906624 | bytes 21002496 | tf_op jit(solution)/shard_map/pallas_call | solution.py:710
  34.8 11.5 %shard_map.308 = (bf16[512,8192]{1,0:T(8,128)(2,1)S(1)}, f32[384,128]{1,0:T(8,128)S(1)}, f32[384,128]{1,0:T(8,128)S(1)}, f32[1024,128]{1,0:T(8,128)S(1)}, f32[10...) custom-call(s32[2]{0:T(128)S(1)} %pad_add_fusion.index_ref, ...), custom_call_target="tpu_custom_call", output_to_operand_aliasing={{0}: (10, {})} | custom-call | flops 6710886400 | bytes 28188680 | tf_op jit(solution)/shard_map/pallas_call | solution.py:710
  46.3 0.4 collective-permute-start.5
  46.7 1.7 %collective-permute-start.6 = (f32[1024,128]{1,0:T(8,128)S(1)}, f32[1024,128]{1,0:T(8,128)S(1)}, u32[]{:S(2)}, u32[]{:S(2)}) collective-permute-start(f32[1024,128]{1,0:T(8,128)S(1)} %get-tuple-element.149), channel_id=1, source_target_pairs={{0,2},{1,3},{2,0},{3,1},{4,6},{5,7},{6,4},{7,5},{8,10},{9,11},{10,... | collective-permute-start | bytes 1572872 | tf_op jit(solution)/shard_map/ppermute | solution.py:1140
  48.4 0.1 add.230
  48.6 1.6 %collective-permute-start.4 = (f32[896,128]{1,0:T(8,128)S(1)}, f32[896,128]{1,0:T(8,128)S(1)}, u32[]{:S(2)}, u32[]{:S(2)}) collective-permute-start(f32[896,128]{1,0:T(8,128)S(1)} %constant_dynamic-slice_fusion.21), channel_id=1, source_target_pairs={{0,8},{1,9},{2,10},{3,11},{4,12},{5,13},{6,14},{7,15},{8,0},{9,1},... | collective-permute-start | bytes 1376264 | tf_op jit(solution)/shard_map/ppermute | solution.py:1140
  50.2 10.1 %shard_map.309 = f32[256,128]{1,0:T(8,128)S(1)} custom-call(f32[16,8192]{1,0:T(8,128)S(1)} %get-tuple-element.136.y1_ref, f32[8,8192]{1,0:T(8,128)S(1)} %get-tuple-element.137.ghalf_ref, f32[16,128]{1,0:T(8,128)S(1)} %get-tuple-element.138.gbc_ref, f32[16,8192]{1,0:T(8,128)S(1)} %get-tuple-element.127.gout_ref, ...), custom_call_target="tpu_custom_call" | custom-call | flops 5502926848 | bytes 20021248 | tf_op jit(solution)/shard_map/pallas_call | solution.py:710
  60.7 0.1 collective-permute-start.7
  61.0 1.8 %collective-permute-done.7 = f32[1280,128]{1,0:T(8,128)S(1)} collective-permute-done((f32[1280,128]{1,0:T(8,128)S(1)}, f32[1280,128]{1,0:T(8,128)S(1)}, u32[]{:S(2)}, u32[]{:S(2)}) %collective-permute-start.7) | collective-permute-done | bytes 655392 | tf_op jit(solution)/shard_map/ppermute | solution.py:1140
  63.0 1.7 %collective-permute-start.9 = (f32[288,128]{1,0:T(8,128)S(1)}, f32[288,128]{1,0:T(8,128)S(1)}, u32[]{:S(2)}, u32[]{:S(2)}) collective-permute-start(f32[288,128]{1,0:T(8,128)S(1)} %pad_maximum_fusion.3), channel_id=1, source_target_pairs={{0,4},{1,5},{2,6},{3,7},{4,0},{5,1},{6,2},{7,3},{8,12},{9,13},{10,... | collective-permute-start | bytes 442376 | tf_op jit(solution)/shard_map/ppermute | solution.py:1140
  64.8 1.6 %collective-permute-start.8 = (f32[352,128]{1,0:T(8,128)S(1)}, f32[352,128]{1,0:T(8,128)S(1)}, u32[]{:S(2)}, u32[]{:S(2)}) collective-permute-start(f32[352,128]{1,0:T(8,128)S(1)} %pad_maximum_fusion.2), channel_id=1, source_target_pairs={{0,2},{1,3},{2,0},{3,1},{4,6},{5,7},{6,4},{7,5},{8,10},{9,11},{10,... | collective-permute-start | bytes 540680 | tf_op jit(solution)/shard_map/ppermute | solution.py:1140
  66.4 0.3 collective-permute-start.10
  66.7 2.5 %collective-permute-done.9 = f32[288,128]{1,0:T(8,128)S(1)} collective-permute-done((f32[288,128]{1,0:T(8,128)S(1)}, f32[288,128]{1,0:T(8,128)S(1)}, u32[]{:S(2)}, u32[]{:S(2)}) %collective-permute-start.9) | collective-permute-done | bytes 147488 | tf_op jit(solution)/shard_map/ppermute | solution.py:1140
  69.2 2.3 %collective-permute-done.8 = f32[352,128]{1,0:T(8,128)S(1)} collective-permute-done((f32[352,128]{1,0:T(8,128)S(1)}, f32[352,128]{1,0:T(8,128)S(1)}, u32[]{:S(2)}, u32[]{:S(2)}) %collective-permute-start.8) | collective-permute-done | bytes 180256 | tf_op jit(solution)/shard_map/ppermute | solution.py:1140
  71.7 2.6 %collective-permute-start.11 = (f32[208,128]{1,0:T(8,128)S(1)}, f32[208,128]{1,0:T(8,128)S(1)}, u32[]{:S(2)}, u32[]{:S(2)}) collective-permute-start(f32[208,128]{1,0:T(8,128)S(1)} %pad_maximum_fusion.4), channel_id=1, source_target_pairs={{0,16},{1,17},{2,18},{3,19},{4,20},{5,21},{6,22},{7,23},{8,24},{9,... | collective-permute-start | bytes 319496 | tf_op jit(solution)/shard_map/ppermute | solution.py:1140
  74.3 1.6 %collective-permute-start.12 = (f32[96,128]{1,0:T(8,128)S(1)}, f32[96,128]{1,0:T(8,128)S(1)}, u32[]{:S(2)}, u32[]{:S(2)}) collective-permute-start(f32[96,128]{1,0:T(8,128)S(1)} %pad_maximum_fusion.5), channel_id=1, source_target_pairs={{0,8},{1,9},{2,10},{3,11},{4,12},{5,13},{6,14},{7,15},{8,0},{9,1},... | collective-permute-start | bytes 147464 | tf_op jit(solution)/shard_map/ppermute | solution.py:1140
  75.9 0.2 collective-permute-start.13
  76.2 2.3 %collective-permute-done.12 = f32[96,128]{1,0:T(8,128)S(1)} collective-permute-done((f32[96,128]{1,0:T(8,128)S(1)}, f32[96,128]{1,0:T(8,128)S(1)}, u32[]{:S(2)}, u32[]{:S(2)}) %collective-permute-start.12) | collective-permute-done | bytes 49184 | tf_op jit(solution)/shard_map/ppermute | solution.py:1140
  78.4 3.4 %collective-permute-done.13 = f32[96,128]{1,0:T(8,128)S(1)} collective-permute-done((f32[96,128]{1,0:T(8,128)S(1)}, f32[96,128]{1,0:T(8,128)S(1)}, u32[]{:S(2)}, u32[]{:S(2)}) %collective-permute-start.13) | collective-permute-done | bytes 49184 | tf_op jit(solution)/shard_map/ppermute | solution.py:1140
  82.0 1.6 %collective-permute-start.14 = (bf16[224,128]{1,0:T(8,128)(2,1)S(1)}, bf16[224,128]{1,0:T(8,128)(2,1)S(1)}, u32[]{:S(2)}, u32[]{:S(2)}) collective-permute-start(bf16[224,128]{1,0:T(8,128)(2,1)S(1)} %get-tuple-element.203), channel_id=1, source_target_pairs={{0,16},{1,17},{2,18},{3,19},{4,20},{5,21},{6,22},{7,23},{8,24},{9,... | collective-permute-start | bytes 172040 | tf_op jit(solution)/shard_map/ppermute | solution.py:1140
  83.6 0.9 collective-permute-start.15
  84.5 2.0 %collective-permute-start.16 = (bf16[224,128]{1,0:T(8,128)(2,1)S(1)}, bf16[224,128]{1,0:T(8,128)(2,1)S(1)}, u32[]{:S(2)}, u32[]{:S(2)}) collective-permute-start(bf16[224,128]{1,0:T(8,128)(2,1)S(1)} %get-tuple-element.203), channel_id=1, source_target_pairs={{0,24},{1,25},{2,26},{3,27},{4,28},{5,29},{6,30},{7,31},{8,16},{9,... | collective-permute-start | bytes 172040 | tf_op jit(solution)/shard_map/ppermute | solution.py:1140
  86.5 1.6 %collective-permute-done.14 = bf16[224,128]{1,0:T(8,128)(2,1)S(1)} collective-permute-done((bf16[224,128]{1,0:T(8,128)(2,1)S(1)}, bf16[224,128]{1,0:T(8,128)(2,1)S(1)}, u32[]{:S(2)}, u32[]{:S(2)}) %collective-permute-start.14) | collective-permute-done | bytes 57376 | tf_op jit(solution)/shard_map/ppermute | solution.py:1140
  88.2 0.3 collective-permute-done.15
  88.5 2.0 %collective-permute-done.16 = bf16[224,128]{1,0:T(8,128)(2,1)S(1)} collective-permute-done((bf16[224,128]{1,0:T(8,128)(2,1)S(1)}, bf16[224,128]{1,0:T(8,128)(2,1)S(1)}, u32[]{:S(2)}, u32[]{:S(2)}) %collective-permute-start.16) | collective-permute-done | bytes 57376 | tf_op jit(solution)/shard_map/ppermute | solution.py:1140
  90.5 0.6 collective-permute-start.20
  91.2 1.6 %collective-permute-start.17 = (bf16[448,128]{1,0:T(8,128)(2,1)S(1)}, bf16[448,128]{1,0:T(8,128)(2,1)S(1)}, u32[]{:S(2)}, u32[]{:S(2)}) collective-permute-start(bf16[448,128]{1,0:T(8,128)(2,1)S(1)} %maximum_select_fusion.6), channel_id=1, source_target_pairs={{0,2},{1,3},{2,0},{3,1},{4,6},{5,7},{6,4},{7,5},{8,10},{9,11},{10,... | collective-permute-start | bytes 344072 | tf_op jit(solution)/shard_map/ppermute | solution.py:1140
  92.8 2.6 %collective-permute-done.20 = bf16[448,128]{1,0:T(8,128)(2,1)S(1)} collective-permute-done((bf16[448,128]{1,0:T(8,128)(2,1)S(1)}, bf16[448,128]{1,0:T(8,128)(2,1)S(1)}, u32[]{:S(2)}, u32[]{:S(2)}) %collective-permute-start.20) | collective-permute-done | bytes 114720 | tf_op jit(solution)/shard_map/ppermute | solution.py:1140
  95.5 2.8 %collective-permute-start.21 = (bf16[896,128]{1,0:T(8,128)(2,1)S(1)}, bf16[896,128]{1,0:T(8,128)(2,1)S(1)}, u32[]{:S(2)}, u32[]{:S(2)}) collective-permute-start(bf16[896,128]{1,0:T(8,128)(2,1)S(1)} %maximum_select_fusion.5), channel_id=1, source_target_pairs={{0,2},{1,3},{2,0},{3,1},{4,6},{5,7},{6,4},{7,5},{8,10},{9,11},{10,... | collective-permute-start | bytes 688136 | tf_op jit(solution)/shard_map/ppermute | solution.py:1140
  98.3 0.1 collective-permute-start.18
  98.4 3.8 %collective-permute-done.21 = bf16[896,128]{1,0:T(8,128)(2,1)S(1)} collective-permute-done((bf16[896,128]{1,0:T(8,128)(2,1)S(1)}, bf16[896,128]{1,0:T(8,128)(2,1)S(1)}, u32[]{:S(2)}, u32[]{:S(2)}) %collective-permute-start.21) | collective-permute-done | bytes 229408 | tf_op jit(solution)/shard_map/ppermute | solution.py:1140
  102.3 0.1 maximum_select_fusion.3
  102.4 0.1 collective-permute-start.22
  102.5 1.9 %collective-permute-done.18 = bf16[896,128]{1,0:T(8,128)(2,1)S(1)} collective-permute-done((bf16[896,128]{1,0:T(8,128)(2,1)S(1)}, bf16[896,128]{1,0:T(8,128)(2,1)S(1)}, u32[]{:S(2)}, u32[]{:S(2)}) %collective-permute-start.18) | collective-permute-done | bytes 229408 | tf_op jit(solution)/shard_map/ppermute | solution.py:1140
  104.4 0.1 maximum_select_fusion.2
  104.6 0.2 maximum_select_fusion.1
  105.1 1.3 %collective-permute-done.19 = bf16[1792,128]{1,0:T(8,128)(2,1)S(1)} collective-permute-done((bf16[1792,128]{1,0:T(8,128)(2,1)S(1)}, bf16[1792,128]{1,0:T(8,128)(2,1)S(1)}, u32[]{:S(2)}, u32[]{:S(2)}) %collective-permute-start.19) | collective-permute-done | bytes 458784 | tf_op jit(solution)/shard_map/ppermute | solution.py:1140
  106.4 0.2 maximum_select_fusion
  106.7 0.1 copy.37
  106.8 9.0 %shard_map.310 = (f32[1,1]{1,0:T(1,128)}, f32[1,1]{1,0:T(1,128)}, f32[24,128]{1,0:T(8,128)}, f32[24,128]{1,0:T(8,128)}, f32[24,128]{1,0:T(8,128)}, /*index=5*/f3...) custom-call(bf16[3584,128]{1,0:T(8,128)(2,1)S(1)} %bitcast.39, ...), custom_call_target="tpu_custom_call" | custom-call | flops 100000000 | bytes 20655880 | tf_op jit(solution)/shard_map/pallas_call | solution.py:710
  (79 shorter events, 1.6 us)
Async XLA Ops:
  2.0 8.9 %collective-permute-start = (bf16[208,128]{1,0:T(8,128)(2,1)S(1)}, bf16[208,128]{1,0:T(8,128)(2,1)S(1)}, u32[]{:S(2)}, u32[]{:S(2)}) collective-permute-start(bf16[208,128]{1,0:T(8,128)(2,1)S(1)} %get-tuple-element.95), channel_id=1, source_target_pairs={{0,1},{1,0},{2,3},{3,2},{4,5},{5,4},{6,7},{7,6},{8,9},{9,8},{10,11... | collective-permute-start | bytes 159752 | tf_op jit(solution)/shard_map/ppermute | solution.py:1158
  2.6 8.4 %collective-permute-start.1 = (bf16[208,128]{1,0:T(8,128)(2,1)S(1)}, bf16[208,128]{1,0:T(8,128)(2,1)S(1)}, u32[]{:S(2)}, u32[]{:S(2)}) collective-permute-start(bf16[208,128]{1,0:T(8,128)(2,1)S(1)} %get-tuple-element.96), channel_id=1, source_target_pairs={{0,2},{1,3},{2,0},{3,1},{4,6},{5,7},{6,4},{7,5},{8,10},{9,11},{10,... | collective-permute-start | bytes 159752 | tf_op jit(solution)/shard_map/ppermute | solution.py:1158
  5.2 5.8 %collective-permute-start.2 = (bf16[208,128]{1,0:T(8,128)(2,1)S(1)}, bf16[208,128]{1,0:T(8,128)(2,1)S(1)}, u32[]{:S(2)}, u32[]{:S(2)}) collective-permute-start(bf16[208,128]{1,0:T(8,128)(2,1)S(1)} %get-tuple-element.97), channel_id=1, source_target_pairs={{0,3},{1,2},{2,1},{3,0},{4,7},{5,6},{6,5},{7,4},{8,11},{9,10},{10,... | collective-permute-start | bytes 159752 | tf_op jit(solution)/shard_map/ppermute | solution.py:1158
  22.5 25.9 %collective-permute-start.3 = (f32[1792,128]{1,0:T(8,128)S(1)}, f32[1792,128]{1,0:T(8,128)S(1)}, u32[]{:S(2)}, u32[]{:S(2)}) collective-permute-start(f32[1792,128]{1,0:T(8,128)S(1)} %get-tuple-element.112), channel_id=1, source_target_pairs={{0,4},{1,5},{2,6},{3,7},{4,0},{5,1},{6,2},{7,3},{8,12},{9,13},{10,... | collective-permute-start | bytes 2752520 | tf_op jit(solution)/shard_map/ppermute | solution.py:1140
  46.3 14.0 %collective-permute-start.5 = (f32[384,128]{1,0:T(8,128)S(1)}, f32[384,128]{1,0:T(8,128)S(1)}, u32[]{:S(2)}, u32[]{:S(2)}) collective-permute-start(f32[384,128]{1,0:T(8,128)S(1)} %get-tuple-element.146), channel_id=1, source_target_pairs={{0,4},{1,5},{2,6},{3,7},{4,0},{5,1},{6,2},{7,3},{8,12},{9,13},{10,... | collective-permute-start | bytes 589832 | tf_op jit(solution)/shard_map/ppermute | solution.py:1140
  46.7 13.7 %collective-permute-start.6 = (f32[1024,128]{1,0:T(8,128)S(1)}, f32[1024,128]{1,0:T(8,128)S(1)}, u32[]{:S(2)}, u32[]{:S(2)}) collective-permute-start(f32[1024,128]{1,0:T(8,128)S(1)} %get-tuple-element.149), channel_id=1, source_target_pairs={{0,2},{1,3},{2,0},{3,1},{4,6},{5,7},{6,4},{7,5},{8,10},{9,11},{10,... | collective-permute-start | bytes 1572872 | tf_op jit(solution)/shard_map/ppermute | solution.py:1140
  48.6 12.0 %collective-permute-start.4 = (f32[896,128]{1,0:T(8,128)S(1)}, f32[896,128]{1,0:T(8,128)S(1)}, u32[]{:S(2)}, u32[]{:S(2)}) collective-permute-start(f32[896,128]{1,0:T(8,128)S(1)} %constant_dynamic-slice_fusion.21), channel_id=1, source_target_pairs={{0,8},{1,9},{2,10},{3,11},{4,12},{5,13},{6,14},{7,15},{8,0},{9,1},... | collective-permute-start | bytes 1376264 | tf_op jit(solution)/shard_map/ppermute | solution.py:1140
  60.7 2.2 %collective-permute-start.7 = (f32[1280,128]{1,0:T(8,128)S(1)}, f32[1280,128]{1,0:T(8,128)S(1)}, u32[]{:S(2)}, u32[]{:S(2)}) collective-permute-start(f32[1280,128]{1,0:T(8,128)S(1)} %pad_maximum_fusion.1), channel_id=1, source_target_pairs={{0,1},{1,0},{2,3},{3,2},{4,5},{5,4},{6,7},{7,6},{8,9},{9,8},{10,11... | collective-permute-start | bytes 1966088 | tf_op jit(solution)/shard_map/ppermute | solution.py:1140
  63.0 6.1 %collective-permute-start.9 = (f32[288,128]{1,0:T(8,128)S(1)}, f32[288,128]{1,0:T(8,128)S(1)}, u32[]{:S(2)}, u32[]{:S(2)}) collective-permute-start(f32[288,128]{1,0:T(8,128)S(1)} %pad_maximum_fusion.3), channel_id=1, source_target_pairs={{0,4},{1,5},{2,6},{3,7},{4,0},{5,1},{6,2},{7,3},{8,12},{9,13},{10,... | collective-permute-start | bytes 442376 | tf_op jit(solution)/shard_map/ppermute | solution.py:1140
  64.8 6.7 %collective-permute-start.8 = (f32[352,128]{1,0:T(8,128)S(1)}, f32[352,128]{1,0:T(8,128)S(1)}, u32[]{:S(2)}, u32[]{:S(2)}) collective-permute-start(f32[352,128]{1,0:T(8,128)S(1)} %pad_maximum_fusion.2), channel_id=1, source_target_pairs={{0,2},{1,3},{2,0},{3,1},{4,6},{5,7},{6,4},{7,5},{8,10},{9,11},{10,... | collective-permute-start | bytes 540680 | tf_op jit(solution)/shard_map/ppermute | solution.py:1140
  66.4 5.2 %collective-permute-start.10 = (f32[32,128]{1,0:T(8,128)S(1)}, f32[32,128]{1,0:T(8,128)S(1)}, u32[]{:S(2)}, u32[]{:S(2)}) collective-permute-start(f32[32,128]{1,0:T(8,128)S(1)} %get-tuple-element.184), channel_id=1, source_target_pairs={{0,6},{1,7},{2,4},{3,5},{4,2},{5,3},{6,0},{7,1},{8,14},{9,15},{10,... | collective-permute-start | bytes 49160 | tf_op jit(solution)/shard_map/ppermute | solution.py:1140
  71.7 10.1 %collective-permute-start.11 = (f32[208,128]{1,0:T(8,128)S(1)}, f32[208,128]{1,0:T(8,128)S(1)}, u32[]{:S(2)}, u32[]{:S(2)}) collective-permute-start(f32[208,128]{1,0:T(8,128)S(1)} %pad_maximum_fusion.4), channel_id=1, source_target_pairs={{0,16},{1,17},{2,18},{3,19},{4,20},{5,21},{6,22},{7,23},{8,24},{9,... | collective-permute-start | bytes 319496 | tf_op jit(solution)/shard_map/ppermute | solution.py:1140
  74.3 4.1 %collective-permute-start.12 = (f32[96,128]{1,0:T(8,128)S(1)}, f32[96,128]{1,0:T(8,128)S(1)}, u32[]{:S(2)}, u32[]{:S(2)}) collective-permute-start(f32[96,128]{1,0:T(8,128)S(1)} %pad_maximum_fusion.5), channel_id=1, source_target_pairs={{0,8},{1,9},{2,10},{3,11},{4,12},{5,13},{6,14},{7,15},{8,0},{9,1},... | collective-permute-start | bytes 147464 | tf_op jit(solution)/shard_map/ppermute | solution.py:1140
  75.9 5.9 %collective-permute-start.13 = (f32[96,128]{1,0:T(8,128)S(1)}, f32[96,128]{1,0:T(8,128)S(1)}, u32[]{:S(2)}, u32[]{:S(2)}) collective-permute-start(f32[96,128]{1,0:T(8,128)S(1)} %pad_maximum_fusion.6), channel_id=1, source_target_pairs={{0,24},{1,25},{2,26},{3,27},{4,28},{5,29},{6,30},{7,31},{8,16},{9,... | collective-permute-start | bytes 147464 | tf_op jit(solution)/shard_map/ppermute | solution.py:1140
  81.9 20.6 %copy-start = (f32[2960]{0:T(1024)S(1)}, f32[2960]{0:T(1024)}, u32[]{:S(2)}) copy-start(f32[2960]{0:T(1024)} %param.21) | copy-start | bytes 35524
  81.9 20.6 %copy-start.1 = (f32[2960]{0:T(1024)S(1)}, f32[2960]{0:T(1024)}, u32[]{:S(2)}) copy-start(f32[2960]{0:T(1024)} %param.20) | copy-start | bytes 35524
  82.0 6.0 %collective-permute-start.14 = (bf16[224,128]{1,0:T(8,128)(2,1)S(1)}, bf16[224,128]{1,0:T(8,128)(2,1)S(1)}, u32[]{:S(2)}, u32[]{:S(2)}) collective-permute-start(bf16[224,128]{1,0:T(8,128)(2,1)S(1)} %get-tuple-element.203), channel_id=1, source_target_pairs={{0,16},{1,17},{2,18},{3,19},{4,20},{5,21},{6,22},{7,23},{8,24},{9,... | collective-permute-start | bytes 172040 | tf_op jit(solution)/shard_map/ppermute | solution.py:1140
  83.6 4.9 %collective-permute-start.15 = (bf16[224,128]{1,0:T(8,128)(2,1)S(1)}, bf16[224,128]{1,0:T(8,128)(2,1)S(1)}, u32[]{:S(2)}, u32[]{:S(2)}) collective-permute-start(bf16[224,128]{1,0:T(8,128)(2,1)S(1)} %get-tuple-element.203), channel_id=1, source_target_pairs={{0,8},{1,9},{2,10},{3,11},{4,12},{5,13},{6,14},{7,15},{8,0},{9,1},... | collective-permute-start | bytes 172040 | tf_op jit(solution)/shard_map/ppermute | solution.py:1140
  84.5 6.0 %collective-permute-start.16 = (bf16[224,128]{1,0:T(8,128)(2,1)S(1)}, bf16[224,128]{1,0:T(8,128)(2,1)S(1)}, u32[]{:S(2)}, u32[]{:S(2)}) collective-permute-start(bf16[224,128]{1,0:T(8,128)(2,1)S(1)} %get-tuple-element.203), channel_id=1, source_target_pairs={{0,24},{1,25},{2,26},{3,27},{4,28},{5,29},{6,30},{7,31},{8,16},{9,... | collective-permute-start | bytes 172040 | tf_op jit(solution)/shard_map/ppermute | solution.py:1140
  90.5 4.9 %collective-permute-start.20 = (bf16[448,128]{1,0:T(8,128)(2,1)S(1)}, bf16[448,128]{1,0:T(8,128)(2,1)S(1)}, u32[]{:S(2)}, u32[]{:S(2)}) collective-permute-start(bf16[448,128]{1,0:T(8,128)(2,1)S(1)} %maximum_select_fusion.7), channel_id=1, source_target_pairs={{0,4},{1,5},{2,6},{3,7},{4,0},{5,1},{6,2},{7,3},{8,12},{9,13},{10,... | collective-permute-start | bytes 344072 | tf_op jit(solution)/shard_map/ppermute | solution.py:1140
  91.2 7.1 %collective-permute-start.17 = (bf16[448,128]{1,0:T(8,128)(2,1)S(1)}, bf16[448,128]{1,0:T(8,128)(2,1)S(1)}, u32[]{:S(2)}, u32[]{:S(2)}) collective-permute-start(bf16[448,128]{1,0:T(8,128)(2,1)S(1)} %maximum_select_fusion.6), channel_id=1, source_target_pairs={{0,2},{1,3},{2,0},{3,1},{4,6},{5,7},{6,4},{7,5},{8,10},{9,11},{10,... | collective-permute-start | bytes 344072 | tf_op jit(solution)/shard_map/ppermute | solution.py:1140
  95.5 6.8 %collective-permute-start.21 = (bf16[896,128]{1,0:T(8,128)(2,1)S(1)}, bf16[896,128]{1,0:T(8,128)(2,1)S(1)}, u32[]{:S(2)}, u32[]{:S(2)}) collective-permute-start(bf16[896,128]{1,0:T(8,128)(2,1)S(1)} %maximum_select_fusion.5), channel_id=1, source_target_pairs={{0,2},{1,3},{2,0},{3,1},{4,6},{5,7},{6,4},{7,5},{8,10},{9,11},{10,... | collective-permute-start | bytes 688136 | tf_op jit(solution)/shard_map/ppermute | solution.py:1140
  98.3 6.1 %collective-permute-start.18 = (bf16[896,128]{1,0:T(8,128)(2,1)S(1)}, bf16[896,128]{1,0:T(8,128)(2,1)S(1)}, u32[]{:S(2)}, u32[]{:S(2)}) collective-permute-start(bf16[896,128]{1,0:T(8,128)(2,1)S(1)} %maximum_select_fusion.4), channel_id=1, source_target_pairs={{0,4},{1,5},{2,6},{3,7},{4,0},{5,1},{6,2},{7,3},{8,12},{9,13},{10,... | collective-permute-start | bytes 688136 | tf_op jit(solution)/shard_map/ppermute | solution.py:1140
  102.4 2.2 %collective-permute-start.22 = (bf16[1792,128]{1,0:T(8,128)(2,1)S(1)}, bf16[1792,128]{1,0:T(8,128)(2,1)S(1)}, u32[]{:S(2)}, u32[]{:S(2)}) collective-permute-start(bf16[1792,128]{1,0:T(8,128)(2,1)S(1)} %maximum_select_fusion.3), channel_id=1, source_target_pairs={{0,1},{1,0},{2,3},{3,2},{4,5},{5,4},{6,7},{7,6},{8,9},{9,8},{10,11... | collective-permute-start | bytes 1376264 | tf_op jit(solution)/shard_map/ppermute | solution.py:1140
  104.6 1.9 %collective-permute-start.19 = (bf16[1792,128]{1,0:T(8,128)(2,1)S(1)}, bf16[1792,128]{1,0:T(8,128)(2,1)S(1)}, u32[]{:S(2)}, u32[]{:S(2)}) collective-permute-start(bf16[1792,128]{1,0:T(8,128)(2,1)S(1)} %maximum_select_fusion.2), channel_id=1, source_target_pairs={{0,1},{1,0},{2,3},{3,2},{4,5},{5,4},{6,7},{7,6},{8,9},{9,8},{10,11... | collective-permute-start | bytes 1376264 | tf_op jit(solution)/shard_map/ppermute | solution.py:1140

commit v8 on v7

--- a/solution.py
+++ b/solution.py
@@ -763,10 +763,14 @@
     pieces.setdefault(row, []).append(value)
 
 
-def level_tables(flat_ref, level, lu):
+def level_rows(flat_ref, level):
     chans = CH * (level + 1)
     start = ONE_START - 4 * CH if level == 0 else TWO_START
-    chan = [take_flat(flat_ref, start + k * chans, chans) for k in range(4)]
+    return chans, start, [take_flat(flat_ref, start + k * chans, chans) for k in range(4)]
+
+
+def level_tables(flat_ref, level, lu):
+    chans, start, chan = level_rows(flat_ref, level)
     first = start + 4 * chans + 2 * HID
     lu[...] = jnp.zeros_like(lu)
     for i in range(chans):
@@ -857,6 +861,7 @@
     wp_ref,
     wpt_ref,
     pbias_ref,
+    tables_ref,
     *refs,
 ):
     outs_two, outs_one = refs[:7], refs[7:14]
@@ -874,6 +879,8 @@
     for level in range(2):
         chans, start, chan, lower, upper = level_tables(flat_ref, level, lu)
         product = high_dot(lower, upper)
+        for k, table in enumerate((product, lower.T, upper)):
+            tables_ref[3 * level + k] = table
         height = 16 * (level + 1)
         row, lane = iotas(height)
         natural, valid = natural_row(level, row)
@@ -939,6 +946,7 @@
     rest_ref,
     low_ref,
     extra_ref,
+    tables_ref,
     flat_ref,
     flat_first,
     flat_second,
@@ -947,8 +955,8 @@
     far_in, refs = refs[:12], refs[12:]
     (loss_ref, norm_ref, flat_new, flat_grad, flat_moment), refs = refs[:5], refs[5:]
     far_out, refs = refs[:12], refs[12:]
-    bias_ref, two, one, rest, lu = refs[:5]
-    held, (in_sems, out_sems) = refs[5:21], refs[21:]
+    bias_ref, two, one, rest = refs[:4]
+    held, (in_sems, out_sems) = refs[4:20], refs[20:]
     weights, firsts, seconds, grads = held[0:4], held[4:8], held[8:12], held[12:16]
     entry_grad, _, exit_grad, prior_grad = grads
     jobs = [(1, 0), (1, 1), (2, None), (0, None), (3, None)]
@@ -986,7 +994,8 @@
     pieces = {}
     consts = []
     for level in range(2):
-        chans, start, chan, lower, upper = level_tables(flat_ref, level, lu)
+        chans, start, chan = level_rows(flat_ref, level)
+        product, lower_turned, upper = (tables_ref[3 * level + k] for k in range(3))
         consts.append(jnp.sum(chan[1] + chan[2], keepdims=True))
         weight = coef * count if level == 0 else coef * count_two
         height = 16 * (level + 1)
@@ -994,7 +1003,6 @@
         if level == 1:
             small = jnp.concatenate([pltpu.roll(small, LANES - 32, 1), pltpu.roll(small, LANES - 66, 1)], axis=0)
         sum_lane = 16 * (level + 1)
-        product = high_dot(lower, upper)
         row, lane = iotas(LANES, height)
         natural, valid = natural_row(level, lane)
         turned = high_dot(((row == chans - 1 - natural) & valid).astype(F32), small)
@@ -1006,7 +1014,7 @@
         else:
             g_product = jnp.where(lane < chans, g_product, 0.0)
         g_lower = high_dot(g_product, upper, (1, 1))
-        g_upper = high_dot(lower.T, g_product)
+        g_upper = high_dot(lower_turned, g_product)
         g_lu = jnp.where(row > lane, g_lower, 0.0) + jnp.where(row < lane, g_upper, 0.0)
         diagonal = jnp.sum(jnp.where(row == lane, g_upper, 0.0), axis=0, keepdims=True)
         shift = jnp.sum(turned[:, sum_lane : sum_lane + 1] * product, axis=0, keepdims=True)
@@ -1053,10 +1061,13 @@
             first = TWO_F - base + block * 216 + tap * 2 * CH
             exit_grad[tap, CH : 3 * CH, at] = two[first : first + 2 * CH, :]
     places = prior_places()
-    for tap in range(9):
-        first = ONE_P + (tap * 32 // LANES) * 64
-        moved = dot_nt(prior_lanes(tap), one_ref[first : first + 64, :]).astype(BF16)
-        prior_grad[tap, :, :] = dot(moved, places) * factor
+    for block in range(3):
+        taps = [tap for tap in range(9) if tap * 32 // LANES == block]
+        lanes = jnp.concatenate([prior_lanes(tap).astype(F32) for tap in taps], axis=0).astype(BF16)
+        moved = dot_nt(lanes, one_ref[ONE_P + block * 64 : ONE_P + block * 64 + 64, :]).astype(BF16)
+        moved = dot(moved, places) * factor
+        for k, tap in enumerate(taps):
+            prior_grad[tap, :, :] = moved[k * 2 * CH : (k + 1) * 2 * CH]
     for ref in (flat_grad, entry_grad, exit_grad, prior_grad):
         value = ref[...]
         squares.append(jnp.sum(value * value, keepdims=True).reshape(1, 1))
@@ -1083,10 +1094,13 @@
             copy.wait()
         weight, first, second, grad = weights[group], firsts[group], seconds[group], grads[group]
         if level is None:
-            for tap in range(9):
+
+            @pl.loop(0, 9)
+            def _(tap):
                 value = grad[tap] * clip
                 grad[tap] = value
                 weight[tap], second[tap] = adamw(weight[tap], value, first[tap], second[tap])
+
         else:
             slab = (one_ref, two_ref)[level]
 
@@ -1175,14 +1189,14 @@
 
     prior_turned = jnp.swapaxes(prior_taps, 1, 2)
     (
-        chan_one, m_one, chan_two, m_two, m_two_t, wp, wpt, prior_bias,
+        chan_one, m_one, chan_two, m_two, m_two_t, wp, wpt, prior_bias, tables,
         e_two, e_two_t, f_two, f_two_t, wb_two, wb_two_t, bb_two,
         e_one, e_one_t, f_one, f_one_t, wb_one, wb_one_t, bb_one,
     ) = call(
         prepare_kernel,
         (after(vectors_flat, pieces[0]), in_hbm(prior_turned), in_hbm(entry_taps), in_hbm(middle), in_hbm(exit_taps)),
         [shape((16, LANES)), shape((16, LANES)), shape((32, LANES)), shape((32, LANES)), shape((32, LANES))]
-        + [shape((64, 288), BF16), shape((288, 64), BF16), shape((64, 1))]
+        + [shape((64, 288), BF16), shape((288, 64), BF16), shape((64, 1)), shape((6, LANES, LANES))]
         + level_shapes(16)
         + level_shapes(8),
         [
@@ -1455,18 +1469,17 @@
     outs.append(shape((4, HID)))
     results = call(
         finish_kernel,
-        (*totals, low_rest, extra, *flats, *[in_hbm(x) for group in taps for x in group]),
+        (*totals, low_rest, extra, tables, *flats, *[in_hbm(x) for group in taps for x in group]),
         outs,
         [
             pltpu.VMEM((TWO_ROWS - WB_ROWS, LANES), F32),
             pltpu.VMEM((ONE_ROWS - WB_ROWS, LANES), F32),
             pltpu.VMEM((REST_ROWS, LANES), F32),
-            pltpu.VMEM((LANES, LANES), F32),
         ]
         + [pltpu.VMEM(group[0].shape, F32) for _ in range(4) for group in taps]
         + [pltpu.SemaphoreType.DMA((5, 3))] * 2,
         10**8,
-        far_in=range(8, 20),
+        far_in=range(9, 21),
         far_out=range(5, 17),
     )
     results = list(results)

time: 116 us -> 116 us (level)
  no operation moved by 1% of the time
where the time goes in v8:
time: 116 us
  Pallas kernels  58.7 us (51%)
  starting transfers between devices  26.5 us (23%)
  waiting for transfers between devices  26 us (22%)
  other arithmetic  1.73 us (1%)
  between operations  1.65 us (1%)
  local copies, waits for them, and re-layouts  1.25 us (1%)
    pallas_call x7, Pallas kernels, call(): pl.pallas_call(kernel, out_shape=outputs, in_specs=[far if k in far_in el...  58.7 us
    ppermute x20, waiting for transfers between devices, trade(): lax.ppermute(value, ('batch', 'rows'), [(i, i ^ bit) for i in range(devic...  26 us
    ppermute x20, starting transfers between devices, trade(): lax.ppermute(value, ('batch', 'rows'), [(i, i ^ bit) for i in range(devic...  23.3 us
    ppermute x3, starting transfers between devices, on_device(): lax.ppermute(pieces[d], 'rows', [(i, i ^ d) for i in range(bands)])  3.18 us
  transfers between devices with their start and end apart: 23, of which 13 were waited for; matrix products, arithmetic and copies ran while one was open for 2% of the time, Pallas kernels for 32%

profile of v8, /device:TPU:0, one launch (start us, length us, event | category | flops | bytes accessed | tf_op | source)
XLA Modules:
  0.0 115.8 jit_solution(14489167603255331704)
XLA Ops:
  0.7 0.1 pad_add_fusion.index_ref
  0.7 1.3 %shard_map.304 = (bf16[208,128]{1,0:T(8,128)(2,1)S(1)}, bf16[208,128]{1,0:T(8,128)(2,1)S(1)}, bf16[208,128]{1,0:T(8,128)(2,1)S(1)}, bf16[208,128]{1,0:T(8,128)(2,1)S(1)}) custom-call(s32[2]{0:T(128)S(1)} %pad_add_fusion.index_ref, s32[768,128]{1,0:T(8,128)} %bitcast.49, s32[64,128]{1,0:T(8,128)} %bitcast.54), custom_call_target="tpu_custom_call" | custom-call | flops 1000 | bytes 638984 | tf_op jit(solution)/shard_map/pallas_call | solution.py:710
  2.0 0.5 collective-permute-start
  2.6 2.6 %collective-permute-start.1 = (bf16[208,128]{1,0:T(8,128)(2,1)S(1)}, bf16[208,128]{1,0:T(8,128)(2,1)S(1)}, u32[]{:S(2)}, u32[]{:S(2)}) collective-permute-start(bf16[208,128]{1,0:T(8,128)(2,1)S(1)} %get-tuple-element.97), channel_id=1, source_target_pairs={{0,2},{1,3},{2,0},{3,1},{4,6},{5,7},{6,4},{7,5},{8,10},{9,11},{10,... | collective-permute-start | bytes 159752 | tf_op jit(solution)/shard_map/ppermute | solution.py:1172
  5.2 0.7 pad_bitcast_fusion.2.flat_ref
  5.9 5.1 %shard_map.305 = (f32[16,128]{1,0:T(8,128)S(1)}, f32[16,128]{1,0:T(8,128)S(1)}, f32[32,128]{1,0:T(8,128)S(1)}, f32[32,128]{1,0:T(8,128)S(1)}, f32[32,128]{1,0:T(...) custom-call(f32[24,128]{1,0:T(8,128)S(1)} %pad_bitcast_fusion.2.flat, ...), custom_call_target="tpu_custom_call" | custom-call | flops 1000000000 | bytes 7107328 | tf_op jit(solution)/shard_map/pallas_call | solution.py:710
  11.1 11.6 %shard_map.306 = (f32[16,8192]{1,0:T(8,128)S(1)}, f32[16,8192]{1,0:T(8,128)S(1)}, f32[1,8192]{1,0:T(1,128)S(1)}, f32[1,2048]{1,0:T(1,128)S(1)}, f32[32,2048]{1,0...) custom-call(s32[2]{0:T(128)S(1)} %pad_add_fusion.index_ref, ...), custom_call_target="tpu_custom_call" | custom-call | flops 5939134464 | bytes 5683208 | tf_op jit(solution)/shard_map/pallas_call | solution.py:710
  22.6 1.8 %collective-permute-start.3 = (f32[1792,128]{1,0:T(8,128)S(1)}, f32[1792,128]{1,0:T(8,128)S(1)}, u32[]{:S(2)}, u32[]{:S(2)}) collective-permute-start(f32[1792,128]{1,0:T(8,128)S(1)} %get-tuple-element.113), channel_id=1, source_target_pairs={{0,4},{1,5},{2,6},{3,7},{4,0},{5,1},{6,2},{7,3},{8,12},{9,13},{10,... | collective-permute-start | bytes 2752520 | tf_op jit(solution)/shard_map/ppermute | solution.py:1154
  24.4 10.5 %shard_map.307 = (bf16[72,8192]{1,0:T(8,128)(2,1)S(1)}, bf16[512,8192]{1,0:T(8,128)(2,1)S(1)}, bf16[512,8192]{1,0:T(8,128)(2,1)S(1)}, f32[8,8192]{1,0:T(8,128)S(...) custom-call(f32[16,8192]{1,0:T(8,128)S(1)} %get-tuple-element.115.mix1_ref, ...), custom_call_target="tpu_custom_call" | custom-call | flops 6106906624 | bytes 21002496 | tf_op jit(solution)/shard_map/pallas_call | solution.py:710
  34.9 11.3 %shard_map.308 = (bf16[512,8192]{1,0:T(8,128)(2,1)S(1)}, f32[384,128]{1,0:T(8,128)S(1)}, f32[384,128]{1,0:T(8,128)S(1)}, f32[1024,128]{1,0:T(8,128)S(1)}, f32[10...) custom-call(s32[2]{0:T(128)S(1)} %pad_add_fusion.index_ref, ...), custom_call_target="tpu_custom_call", output_to_operand_aliasing={{0}: (10, {})} | custom-call | flops 6710886400 | bytes 28188680 | tf_op jit(solution)/shard_map/pallas_call | solution.py:710
  46.2 0.4 collective-permute-start.5
  46.6 1.7 %collective-permute-start.6 = (f32[1024,128]{1,0:T(8,128)S(1)}, f32[1024,128]{1,0:T(8,128)S(1)}, u32[]{:S(2)}, u32[]{:S(2)}) collective-permute-start(f32[1024,128]{1,0:T(8,128)S(1)} %get-tuple-element.150), channel_id=1, source_target_pairs={{0,2},{1,3},{2,0},{3,1},{4,6},{5,7},{6,4},{7,5},{8,10},{9,11},{10,... | collective-permute-start | bytes 1572872 | tf_op jit(solution)/shard_map/ppermute | solution.py:1154
  48.3 0.1 add.230
  48.5 1.6 %collective-permute-start.4 = (f32[896,128]{1,0:T(8,128)S(1)}, f32[896,128]{1,0:T(8,128)S(1)}, u32[]{:S(2)}, u32[]{:S(2)}) collective-permute-start(f32[896,128]{1,0:T(8,128)S(1)} %constant_dynamic-slice_fusion.21), channel_id=1, source_target_pairs={{0,8},{1,9},{2,10},{3,11},{4,12},{5,13},{6,14},{7,15},{8,0},{9,1},... | collective-permute-start | bytes 1376264 | tf_op jit(solution)/shard_map/ppermute | solution.py:1154
  50.1 10.1 %shard_map.309 = f32[256,128]{1,0:T(8,128)S(1)} custom-call(f32[16,8192]{1,0:T(8,128)S(1)} %get-tuple-element.137.y1_ref, f32[8,8192]{1,0:T(8,128)S(1)} %get-tuple-element.138.ghalf_ref, f32[16,128]{1,0:T(8,128)S(1)} %get-tuple-element.139.gbc_ref, f32[16,8192]{1,0:T(8,128)S(1)} %get-tuple-element.128.gout_ref, ...), custom_call_target="tpu_custom_call" | custom-call | flops 5502926848 | bytes 20021248 | tf_op jit(solution)/shard_map/pallas_call | solution.py:710
  60.4 0.1 collective-permute-done.4
  60.6 0.1 collective-permute-start.7
  61.0 1.8 %collective-permute-done.7 = f32[1280,128]{1,0:T(8,128)S(1)} collective-permute-done((f32[1280,128]{1,0:T(8,128)S(1)}, f32[1280,128]{1,0:T(8,128)S(1)}, u32[]{:S(2)}, u32[]{:S(2)}) %collective-permute-start.7) | collective-permute-done | bytes 655392 | tf_op jit(solution)/shard_map/ppermute | solution.py:1154
  63.0 1.7 %collective-permute-start.9 = (f32[288,128]{1,0:T(8,128)S(1)}, f32[288,128]{1,0:T(8,128)S(1)}, u32[]{:S(2)}, u32[]{:S(2)}) collective-permute-start(f32[288,128]{1,0:T(8,128)S(1)} %pad_maximum_fusion.3), channel_id=1, source_target_pairs={{0,4},{1,5},{2,6},{3,7},{4,0},{5,1},{6,2},{7,3},{8,12},{9,13},{10,... | collective-permute-start | bytes 442376 | tf_op jit(solution)/shard_map/ppermute | solution.py:1154
  64.7 1.6 %collective-permute-start.8 = (f32[352,128]{1,0:T(8,128)S(1)}, f32[352,128]{1,0:T(8,128)S(1)}, u32[]{:S(2)}, u32[]{:S(2)}) collective-permute-start(f32[352,128]{1,0:T(8,128)S(1)} %pad_maximum_fusion.2), channel_id=1, source_target_pairs={{0,2},{1,3},{2,0},{3,1},{4,6},{5,7},{6,4},{7,5},{8,10},{9,11},{10,... | collective-permute-start | bytes 540680 | tf_op jit(solution)/shard_map/ppermute | solution.py:1154
  66.3 0.4 collective-permute-start.10
  66.7 2.5 %collective-permute-done.9 = f32[288,128]{1,0:T(8,128)S(1)} collective-permute-done((f32[288,128]{1,0:T(8,128)S(1)}, f32[288,128]{1,0:T(8,128)S(1)}, u32[]{:S(2)}, u32[]{:S(2)}) %collective-permute-start.9) | collective-permute-done | bytes 147488 | tf_op jit(solution)/shard_map/ppermute | solution.py:1154
  69.2 2.3 %collective-permute-done.8 = f32[352,128]{1,0:T(8,128)S(1)} collective-permute-done((f32[352,128]{1,0:T(8,128)S(1)}, f32[352,128]{1,0:T(8,128)S(1)}, u32[]{:S(2)}, u32[]{:S(2)}) %collective-permute-start.8) | collective-permute-done | bytes 180256 | tf_op jit(solution)/shard_map/ppermute | solution.py:1154
  71.6 2.7 %collective-permute-start.11 = (f32[208,128]{1,0:T(8,128)S(1)}, f32[208,128]{1,0:T(8,128)S(1)}, u32[]{:S(2)}, u32[]{:S(2)}) collective-permute-start(f32[208,128]{1,0:T(8,128)S(1)} %pad_maximum_fusion.4), channel_id=1, source_target_pairs={{0,16},{1,17},{2,18},{3,19},{4,20},{5,21},{6,22},{7,23},{8,24},{9,... | collective-permute-start | bytes 319496 | tf_op jit(solution)/shard_map/ppermute | solution.py:1154
  74.3 1.6 %collective-permute-start.12 = (f32[96,128]{1,0:T(8,128)S(1)}, f32[96,128]{1,0:T(8,128)S(1)}, u32[]{:S(2)}, u32[]{:S(2)}) collective-permute-start(f32[96,128]{1,0:T(8,128)S(1)} %pad_maximum_fusion.5), channel_id=1, source_target_pairs={{0,8},{1,9},{2,10},{3,11},{4,12},{5,13},{6,14},{7,15},{8,0},{9,1},... | collective-permute-start | bytes 147464 | tf_op jit(solution)/shard_map/ppermute | solution.py:1154
  75.8 0.2 collective-permute-start.13
  76.1 2.3 %collective-permute-done.12 = f32[96,128]{1,0:T(8,128)S(1)} collective-permute-done((f32[96,128]{1,0:T(8,128)S(1)}, f32[96,128]{1,0:T(8,128)S(1)}, u32[]{:S(2)}, u32[]{:S(2)}) %collective-permute-start.12) | collective-permute-done | bytes 49184 | tf_op jit(solution)/shard_map/ppermute | solution.py:1154
  78.4 3.4 %collective-permute-done.13 = f32[96,128]{1,0:T(8,128)S(1)} collective-permute-done((f32[96,128]{1,0:T(8,128)S(1)}, f32[96,128]{1,0:T(8,128)S(1)}, u32[]{:S(2)}, u32[]{:S(2)}) %collective-permute-start.13) | collective-permute-done | bytes 49184 | tf_op jit(solution)/shard_map/ppermute | solution.py:1154
  81.9 1.6 %collective-permute-start.14 = (bf16[224,128]{1,0:T(8,128)(2,1)S(1)}, bf16[224,128]{1,0:T(8,128)(2,1)S(1)}, u32[]{:S(2)}, u32[]{:S(2)}) collective-permute-start(bf16[224,128]{1,0:T(8,128)(2,1)S(1)} %get-tuple-element.205), channel_id=1, source_target_pairs={{0,16},{1,17},{2,18},{3,19},{4,20},{5,21},{6,22},{7,23},{8,24},{9,... | collective-permute-start | bytes 172040 | tf_op jit(solution)/shard_map/ppermute | solution.py:1154
  83.5 0.9 collective-permute-start.15
  84.4 2.0 %collective-permute-start.16 = (bf16[224,128]{1,0:T(8,128)(2,1)S(1)}, bf16[224,128]{1,0:T(8,128)(2,1)S(1)}, u32[]{:S(2)}, u32[]{:S(2)}) collective-permute-start(bf16[224,128]{1,0:T(8,128)(2,1)S(1)} %get-tuple-element.205), channel_id=1, source_target_pairs={{0,24},{1,25},{2,26},{3,27},{4,28},{5,29},{6,30},{7,31},{8,16},{9,... | collective-permute-start | bytes 172040 | tf_op jit(solution)/shard_map/ppermute | solution.py:1154
  86.4 1.6 %collective-permute-done.14 = bf16[224,128]{1,0:T(8,128)(2,1)S(1)} collective-permute-done((bf16[224,128]{1,0:T(8,128)(2,1)S(1)}, bf16[224,128]{1,0:T(8,128)(2,1)S(1)}, u32[]{:S(2)}, u32[]{:S(2)}) %collective-permute-start.14) | collective-permute-done | bytes 57376 | tf_op jit(solution)/shard_map/ppermute | solution.py:1154
  88.1 0.3 collective-permute-done.15
  88.4 2.0 %collective-permute-done.16 = bf16[224,128]{1,0:T(8,128)(2,1)S(1)} collective-permute-done((bf16[224,128]{1,0:T(8,128)(2,1)S(1)}, bf16[224,128]{1,0:T(8,128)(2,1)S(1)}, u32[]{:S(2)}, u32[]{:S(2)}) %collective-permute-start.16) | collective-permute-done | bytes 57376 | tf_op jit(solution)/shard_map/ppermute | solution.py:1154
  90.5 0.6 collective-permute-start.20
  91.1 1.6 %collective-permute-start.17 = (bf16[448,128]{1,0:T(8,128)(2,1)S(1)}, bf16[448,128]{1,0:T(8,128)(2,1)S(1)}, u32[]{:S(2)}, u32[]{:S(2)}) collective-permute-start(bf16[448,128]{1,0:T(8,128)(2,1)S(1)} %maximum_select_fusion.6), channel_id=1, source_target_pairs={{0,2},{1,3},{2,0},{3,1},{4,6},{5,7},{6,4},{7,5},{8,10},{9,11},{10,... | collective-permute-start | bytes 344072 | tf_op jit(solution)/shard_map/ppermute | solution.py:1154
  92.7 2.6 %collective-permute-done.20 = bf16[448,128]{1,0:T(8,128)(2,1)S(1)} collective-permute-done((bf16[448,128]{1,0:T(8,128)(2,1)S(1)}, bf16[448,128]{1,0:T(8,128)(2,1)S(1)}, u32[]{:S(2)}, u32[]{:S(2)}) %collective-permute-start.20) | collective-permute-done | bytes 114720 | tf_op jit(solution)/shard_map/ppermute | solution.py:1154
  95.4 2.8 %collective-permute-start.21 = (bf16[896,128]{1,0:T(8,128)(2,1)S(1)}, bf16[896,128]{1,0:T(8,128)(2,1)S(1)}, u32[]{:S(2)}, u32[]{:S(2)}) collective-permute-start(bf16[896,128]{1,0:T(8,128)(2,1)S(1)} %maximum_select_fusion.5), channel_id=1, source_target_pairs={{0,2},{1,3},{2,0},{3,1},{4,6},{5,7},{6,4},{7,5},{8,10},{9,11},{10,... | collective-permute-start | bytes 688136 | tf_op jit(solution)/shard_map/ppermute | solution.py:1154
  98.3 0.1 collective-permute-start.18
  98.3 3.8 %collective-permute-done.21 = bf16[896,128]{1,0:T(8,128)(2,1)S(1)} collective-permute-done((bf16[896,128]{1,0:T(8,128)(2,1)S(1)}, bf16[896,128]{1,0:T(8,128)(2,1)S(1)}, u32[]{:S(2)}, u32[]{:S(2)}) %collective-permute-start.21) | collective-permute-done | bytes 229408 | tf_op jit(solution)/shard_map/ppermute | solution.py:1154
  102.2 0.1 maximum_select_fusion.3
  102.4 1.9 %collective-permute-done.18 = bf16[896,128]{1,0:T(8,128)(2,1)S(1)} collective-permute-done((bf16[896,128]{1,0:T(8,128)(2,1)S(1)}, bf16[896,128]{1,0:T(8,128)(2,1)S(1)}, u32[]{:S(2)}, u32[]{:S(2)}) %collective-permute-start.18) | collective-permute-done | bytes 229408 | tf_op jit(solution)/shard_map/ppermute | solution.py:1154
  104.3 0.1 maximum_select_fusion.2
  104.6 0.2 maximum_select_fusion.1
  105.0 1.3 %collective-permute-done.19 = bf16[1792,128]{1,0:T(8,128)(2,1)S(1)} collective-permute-done((bf16[1792,128]{1,0:T(8,128)(2,1)S(1)}, bf16[1792,128]{1,0:T(8,128)(2,1)S(1)}, u32[]{:S(2)}, u32[]{:S(2)}) %collective-permute-start.19) | collective-permute-done | bytes 458784 | tf_op jit(solution)/shard_map/ppermute | solution.py:1154
  106.3 0.2 maximum_select_fusion
  106.6 0.1 copy.37
  106.7 8.9 %shard_map.310 = (f32[1,1]{1,0:T(1,128)}, f32[1,1]{1,0:T(1,128)}, f32[24,128]{1,0:T(8,128)}, f32[24,128]{1,0:T(8,128)}, f32[24,128]{1,0:T(8,128)}, /*index=5*/f3...) custom-call(bf16[3584,128]{1,0:T(8,128)(2,1)S(1)} %bitcast.39, ...), custom_call_target="tpu_custom_call" | custom-call | flops 100000000 | bytes 21049096 | tf_op jit(solution)/shard_map/pallas_call | solution.py:710
  (79 shorter events, 1.6 us)
Async XLA Ops:
  2.0 9.0 %collective-permute-start = (bf16[208,128]{1,0:T(8,128)(2,1)S(1)}, bf16[208,128]{1,0:T(8,128)(2,1)S(1)}, u32[]{:S(2)}, u32[]{:S(2)}) collective-permute-start(bf16[208,128]{1,0:T(8,128)(2,1)S(1)} %get-tuple-element.96), channel_id=1, source_target_pairs={{0,1},{1,0},{2,3},{3,2},{4,5},{5,4},{6,7},{7,6},{8,9},{9,8},{10,11... | collective-permute-start | bytes 159752 | tf_op jit(solution)/shard_map/ppermute | solution.py:1172
  2.6 8.5 %collective-permute-start.1 = (bf16[208,128]{1,0:T(8,128)(2,1)S(1)}, bf16[208,128]{1,0:T(8,128)(2,1)S(1)}, u32[]{:S(2)}, u32[]{:S(2)}) collective-permute-start(bf16[208,128]{1,0:T(8,128)(2,1)S(1)} %get-tuple-element.97), channel_id=1, source_target_pairs={{0,2},{1,3},{2,0},{3,1},{4,6},{5,7},{6,4},{7,5},{8,10},{9,11},{10,... | collective-permute-start | bytes 159752 | tf_op jit(solution)/shard_map/ppermute | solution.py:1172
  5.2 5.9 %collective-permute-start.2 = (bf16[208,128]{1,0:T(8,128)(2,1)S(1)}, bf16[208,128]{1,0:T(8,128)(2,1)S(1)}, u32[]{:S(2)}, u32[]{:S(2)}) collective-permute-start(bf16[208,128]{1,0:T(8,128)(2,1)S(1)} %get-tuple-element.98), channel_id=1, source_target_pairs={{0,3},{1,2},{2,1},{3,0},{4,7},{5,6},{6,5},{7,4},{8,11},{9,10},{10,... | collective-permute-start | bytes 159752 | tf_op jit(solution)/shard_map/ppermute | solution.py:1172
  22.6 25.7 %collective-permute-start.3 = (f32[1792,128]{1,0:T(8,128)S(1)}, f32[1792,128]{1,0:T(8,128)S(1)}, u32[]{:S(2)}, u32[]{:S(2)}) collective-permute-start(f32[1792,128]{1,0:T(8,128)S(1)} %get-tuple-element.113), channel_id=1, source_target_pairs={{0,4},{1,5},{2,6},{3,7},{4,0},{5,1},{6,2},{7,3},{8,12},{9,13},{10,... | collective-permute-start | bytes 2752520 | tf_op jit(solution)/shard_map/ppermute | solution.py:1154
  46.2 14.0 %collective-permute-start.5 = (f32[384,128]{1,0:T(8,128)S(1)}, f32[384,128]{1,0:T(8,128)S(1)}, u32[]{:S(2)}, u32[]{:S(2)}) collective-permute-start(f32[384,128]{1,0:T(8,128)S(1)} %get-tuple-element.147), channel_id=1, source_target_pairs={{0,4},{1,5},{2,6},{3,7},{4,0},{5,1},{6,2},{7,3},{8,12},{9,13},{10,... | collective-permute-start | bytes 589832 | tf_op jit(solution)/shard_map/ppermute | solution.py:1154
  46.6 13.6 %collective-permute-start.6 = (f32[1024,128]{1,0:T(8,128)S(1)}, f32[1024,128]{1,0:T(8,128)S(1)}, u32[]{:S(2)}, u32[]{:S(2)}) collective-permute-start(f32[1024,128]{1,0:T(8,128)S(1)} %get-tuple-element.150), channel_id=1, source_target_pairs={{0,2},{1,3},{2,0},{3,1},{4,6},{5,7},{6,4},{7,5},{8,10},{9,11},{10,... | collective-permute-start | bytes 1572872 | tf_op jit(solution)/shard_map/ppermute | solution.py:1154
  48.5 12.0 %collective-permute-start.4 = (f32[896,128]{1,0:T(8,128)S(1)}, f32[896,128]{1,0:T(8,128)S(1)}, u32[]{:S(2)}, u32[]{:S(2)}) collective-permute-start(f32[896,128]{1,0:T(8,128)S(1)} %constant_dynamic-slice_fusion.21), channel_id=1, source_target_pairs={{0,8},{1,9},{2,10},{3,11},{4,12},{5,13},{6,14},{7,15},{8,0},{9,1},... | collective-permute-start | bytes 1376264 | tf_op jit(solution)/shard_map/ppermute | solution.py:1154
  60.6 2.2 %collective-permute-start.7 = (f32[1280,128]{1,0:T(8,128)S(1)}, f32[1280,128]{1,0:T(8,128)S(1)}, u32[]{:S(2)}, u32[]{:S(2)}) collective-permute-start(f32[1280,128]{1,0:T(8,128)S(1)} %pad_maximum_fusion.1), channel_id=1, source_target_pairs={{0,1},{1,0},{2,3},{3,2},{4,5},{5,4},{6,7},{7,6},{8,9},{9,8},{10,11... | collective-permute-start | bytes 1966088 | tf_op jit(solution)/shard_map/ppermute | solution.py:1154
  63.0 6.1 %collective-permute-start.9 = (f32[288,128]{1,0:T(8,128)S(1)}, f32[288,128]{1,0:T(8,128)S(1)}, u32[]{:S(2)}, u32[]{:S(2)}) collective-permute-start(f32[288,128]{1,0:T(8,128)S(1)} %pad_maximum_fusion.3), channel_id=1, source_target_pairs={{0,4},{1,5},{2,6},{3,7},{4,0},{5,1},{6,2},{7,3},{8,12},{9,13},{10,... | collective-permute-start | bytes 442376 | tf_op jit(solution)/shard_map/ppermute | solution.py:1154
  64.7 6.7 %collective-permute-start.8 = (f32[352,128]{1,0:T(8,128)S(1)}, f32[352,128]{1,0:T(8,128)S(1)}, u32[]{:S(2)}, u32[]{:S(2)}) collective-permute-start(f32[352,128]{1,0:T(8,128)S(1)} %pad_maximum_fusion.2), channel_id=1, source_target_pairs={{0,2},{1,3},{2,0},{3,1},{4,6},{5,7},{6,4},{7,5},{8,10},{9,11},{10,... | collective-permute-start | bytes 540680 | tf_op jit(solution)/shard_map/ppermute | solution.py:1154
  66.3 5.2 %collective-permute-start.10 = (f32[32,128]{1,0:T(8,128)S(1)}, f32[32,128]{1,0:T(8,128)S(1)}, u32[]{:S(2)}, u32[]{:S(2)}) collective-permute-start(f32[32,128]{1,0:T(8,128)S(1)} %get-tuple-element.186), channel_id=1, source_target_pairs={{0,6},{1,7},{2,4},{3,5},{4,2},{5,3},{6,0},{7,1},{8,14},{9,15},{10,... | collective-permute-start | bytes 49160 | tf_op jit(solution)/shard_map/ppermute | solution.py:1154
  71.6 10.1 %collective-permute-start.11 = (f32[208,128]{1,0:T(8,128)S(1)}, f32[208,128]{1,0:T(8,128)S(1)}, u32[]{:S(2)}, u32[]{:S(2)}) collective-permute-start(f32[208,128]{1,0:T(8,128)S(1)} %pad_maximum_fusion.4), channel_id=1, source_target_pairs={{0,16},{1,17},{2,18},{3,19},{4,20},{5,21},{6,22},{7,23},{8,24},{9,... | collective-permute-start | bytes 319496 | tf_op jit(solution)/shard_map/ppermute | solution.py:1154
  74.3 4.1 %collective-permute-start.12 = (f32[96,128]{1,0:T(8,128)S(1)}, f32[96,128]{1,0:T(8,128)S(1)}, u32[]{:S(2)}, u32[]{:S(2)}) collective-permute-start(f32[96,128]{1,0:T(8,128)S(1)} %pad_maximum_fusion.5), channel_id=1, source_target_pairs={{0,8},{1,9},{2,10},{3,11},{4,12},{5,13},{6,14},{7,15},{8,0},{9,1},... | collective-permute-start | bytes 147464 | tf_op jit(solution)/shard_map/ppermute | solution.py:1154
  75.8 5.9 %collective-permute-start.13 = (f32[96,128]{1,0:T(8,128)S(1)}, f32[96,128]{1,0:T(8,128)S(1)}, u32[]{:S(2)}, u32[]{:S(2)}) collective-permute-start(f32[96,128]{1,0:T(8,128)S(1)} %pad_maximum_fusion.6), channel_id=1, source_target_pairs={{0,24},{1,25},{2,26},{3,27},{4,28},{5,29},{6,30},{7,31},{8,16},{9,... | collective-permute-start | bytes 147464 | tf_op jit(solution)/shard_map/ppermute | solution.py:1154
  81.8 20.6 %copy-start = (f32[2960]{0:T(1024)S(1)}, f32[2960]{0:T(1024)}, u32[]{:S(2)}) copy-start(f32[2960]{0:T(1024)} %param.21) | copy-start | bytes 35524
  81.8 20.6 %copy-start.1 = (f32[2960]{0:T(1024)S(1)}, f32[2960]{0:T(1024)}, u32[]{:S(2)}) copy-start(f32[2960]{0:T(1024)} %param.20) | copy-start | bytes 35524
  81.9 6.0 %collective-permute-start.14 = (bf16[224,128]{1,0:T(8,128)(2,1)S(1)}, bf16[224,128]{1,0:T(8,128)(2,1)S(1)}, u32[]{:S(2)}, u32[]{:S(2)}) collective-permute-start(bf16[224,128]{1,0:T(8,128)(2,1)S(1)} %get-tuple-element.205), channel_id=1, source_target_pairs={{0,16},{1,17},{2,18},{3,19},{4,20},{5,21},{6,22},{7,23},{8,24},{9,... | collective-permute-start | bytes 172040 | tf_op jit(solution)/shard_map/ppermute | solution.py:1154
  83.5 4.9 %collective-permute-start.15 = (bf16[224,128]{1,0:T(8,128)(2,1)S(1)}, bf16[224,128]{1,0:T(8,128)(2,1)S(1)}, u32[]{:S(2)}, u32[]{:S(2)}) collective-permute-start(bf16[224,128]{1,0:T(8,128)(2,1)S(1)} %get-tuple-element.205), channel_id=1, source_target_pairs={{0,8},{1,9},{2,10},{3,11},{4,12},{5,13},{6,14},{7,15},{8,0},{9,1},... | collective-permute-start | bytes 172040 | tf_op jit(solution)/shard_map/ppermute | solution.py:1154
  84.4 6.0 %collective-permute-start.16 = (bf16[224,128]{1,0:T(8,128)(2,1)S(1)}, bf16[224,128]{1,0:T(8,128)(2,1)S(1)}, u32[]{:S(2)}, u32[]{:S(2)}) collective-permute-start(bf16[224,128]{1,0:T(8,128)(2,1)S(1)} %get-tuple-element.205), channel_id=1, source_target_pairs={{0,24},{1,25},{2,26},{3,27},{4,28},{5,29},{6,30},{7,31},{8,16},{9,... | collective-permute-start | bytes 172040 | tf_op jit(solution)/shard_map/ppermute | solution.py:1154
  90.5 4.9 %collective-permute-start.20 = (bf16[448,128]{1,0:T(8,128)(2,1)S(1)}, bf16[448,128]{1,0:T(8,128)(2,1)S(1)}, u32[]{:S(2)}, u32[]{:S(2)}) collective-permute-start(bf16[448,128]{1,0:T(8,128)(2,1)S(1)} %maximum_select_fusion.7), channel_id=1, source_target_pairs={{0,4},{1,5},{2,6},{3,7},{4,0},{5,1},{6,2},{7,3},{8,12},{9,13},{10,... | collective-permute-start | bytes 344072 | tf_op jit(solution)/shard_map/ppermute | solution.py:1154
  91.1 7.1 %collective-permute-start.17 = (bf16[448,128]{1,0:T(8,128)(2,1)S(1)}, bf16[448,128]{1,0:T(8,128)(2,1)S(1)}, u32[]{:S(2)}, u32[]{:S(2)}) collective-permute-start(bf16[448,128]{1,0:T(8,128)(2,1)S(1)} %maximum_select_fusion.6), channel_id=1, source_target_pairs={{0,2},{1,3},{2,0},{3,1},{4,6},{5,7},{6,4},{7,5},{8,10},{9,11},{10,... | collective-permute-start | bytes 344072 | tf_op jit(solution)/shard_map/ppermute | solution.py:1154
  95.4 6.8 %collective-permute-start.21 = (bf16[896,128]{1,0:T(8,128)(2,1)S(1)}, bf16[896,128]{1,0:T(8,128)(2,1)S(1)}, u32[]{:S(2)}, u32[]{:S(2)}) collective-permute-start(bf16[896,128]{1,0:T(8,128)(2,1)S(1)} %maximum_select_fusion.5), channel_id=1, source_target_pairs={{0,2},{1,3},{2,0},{3,1},{4,6},{5,7},{6,4},{7,5},{8,10},{9,11},{10,... | collective-permute-start | bytes 688136 | tf_op jit(solution)/shard_map/ppermute | solution.py:1154
  98.3 6.1 %collective-permute-start.18 = (bf16[896,128]{1,0:T(8,128)(2,1)S(1)}, bf16[896,128]{1,0:T(8,128)(2,1)S(1)}, u32[]{:S(2)}, u32[]{:S(2)}) collective-permute-start(bf16[896,128]{1,0:T(8,128)(2,1)S(1)} %maximum_select_fusion.4), channel_id=1, source_target_pairs={{0,4},{1,5},{2,6},{3,7},{4,0},{5,1},{6,2},{7,3},{8,12},{9,13},{10,... | collective-permute-start | bytes 688136 | tf_op jit(solution)/shard_map/ppermute | solution.py:1154
  102.3 2.2 %collective-permute-start.22 = (bf16[1792,128]{1,0:T(8,128)(2,1)S(1)}, bf16[1792,128]{1,0:T(8,128)(2,1)S(1)}, u32[]{:S(2)}, u32[]{:S(2)}) collective-permute-start(bf16[1792,128]{1,0:T(8,128)(2,1)S(1)} %maximum_select_fusion.3), channel_id=1, source_target_pairs={{0,1},{1,0},{2,3},{3,2},{4,5},{5,4},{6,7},{7,6},{8,9},{9,8},{10,11... | collective-permute-start | bytes 1376264 | tf_op jit(solution)/shard_map/ppermute | solution.py:1154
  104.5 1.9 %collective-permute-start.19 = (bf16[1792,128]{1,0:T(8,128)(2,1)S(1)}, bf16[1792,128]{1,0:T(8,128)(2,1)S(1)}, u32[]{:S(2)}, u32[]{:S(2)}) collective-permute-start(bf16[1792,128]{1,0:T(8,128)(2,1)S(1)} %maximum_select_fusion.2), channel_id=1, source_target_pairs={{0,1},{1,0},{2,3},{3,2},{4,5},{5,4},{6,7},{7,6},{8,9},{9,8},{10,11... | collective-permute-start | bytes 1376264 | tf_op jit(solution)/shard_map/ppermute | solution.py:1154
